TPU v7x, 32 devices: a whole 2x2x4 slice. The times are simulated.
32 devices in a mesh: expert: 4 (over y, x), tensor: 8 (over z, core).
Axes of the slice: x: 2, y: 2, z: 4, core: 2. Of those that a mesh axis runs over, the one named last changes fastest.
Arguments:
- tokens: bfloat16 [512, 7168], P('expert', 'tensor'), may hold values from -6 to 6
- gate_weights: bfloat16 [512, 1], P('expert'), may hold values from 0.099609375 to 1
- expert_ids: int32 [512, 1], P('expert'), may hold values from 0 to 3; in each aligned block of 128 rows (0 to 127, 128 to 255, ...) at most 48 rows name the same one
- w_gate: bfloat16 [4, 7168, 2048], P('expert', 'tensor'), may hold values from -0.0625 to 0.0625
- w_up: bfloat16 [4, 7168, 2048], P('expert', 'tensor'), may hold values from -0.0625 to 0.0625
- w_down: bfloat16 [4, 2048, 7168], P('expert', None, 'tensor'), may hold values from -0.125 to 0.125
- grad_out: bfloat16 [512, 7168], P('expert', 'tensor'), may hold values from -6 to 6
Outputs:
- mixed: bfloat16 [512, 7168], P('expert', 'tensor')
- grad_tokens: bfloat16 [512, 7168], P('expert', 'tensor')
- grad_w_gate: bfloat16 [4, 7168, 2048], P('expert', 'tensor')
- grad_w_up: bfloat16 [4, 7168, 2048], P('expert', 'tensor')
- grad_w_down: bfloat16 [4, 2048, 7168], P('expert', None, 'tensor')
Inputs may be any that keep to these rules, and one draw needn't show every extreme that they name: `expert_ids`: the 1 expert of a token differ. The tokens of one expert index (aligned blocks of 128 rows) name one expert at most 48 times, a bound that some block reaches.
All inputs are finite; a program needn't handle non-finite values.
Results may differ from a plain program's by a relative error of at most 0.0058.
Values may be sent and summed in bfloat16 or wider, within the bound.
No kernel may reach another device: no remote copies, remote signals or barrier semaphores. Data moves between devices by JAX's collectives and lax.ppermute only.
A program may use at most 64 MiB of HBM per device.

v0:
```python
import jax
import jax.numpy as jnp
from jax import lax
from jax.sharding import PartitionSpec as P


def spread_units(function, share):
    return lax.psum_scatter(
        function(jnp.int32(0), share * lax.axis_size("tensor")),
        "tensor",
        scatter_dimension=0,
        tiled=True,
    )


def local(tokens, gate_weights, expert_ids, w_gate, w_up, w_down, grad_out):
    members = lax.axis_size("expert")
    tensor_count = lax.axis_size("tensor")
    tok_rows = tokens.shape[0]
    routes = expert_ids.shape[1]
    width = tokens.shape[1]
    slot = 3 * routes * tok_rows // (2 * members)
    total = members * slot
    flat_ids = expert_ids.reshape(-1)
    counted = (flat_ids[:, None] == jnp.arange(members, dtype=jnp.int32)[None, :]).astype(jnp.int32)
    ranks = jnp.cumsum(counted, axis=0) - 1
    position = jnp.sum(counted * ranks, axis=1)
    target = (flat_ids * slot + position).reshape(tok_rows, routes)
    matched = target[None, :, :] == jnp.arange(total, dtype=jnp.int32)[:, None, None]
    place = jnp.sum(matched.astype(jnp.float32), axis=2).astype(jnp.bfloat16)
    weighted = jnp.sum(
        jnp.where(matched, gate_weights.astype(jnp.float32)[None], 0.0), axis=2
    ).astype(jnp.bfloat16)
    x_slots = jnp.dot(place, tokens, preferred_element_type=jnp.float32).astype(jnp.bfloat16)
    dy_slots = jnp.dot(weighted, grad_out, preferred_element_type=jnp.float32).astype(jnp.bfloat16)
    outgoing = jnp.stack(
        [x_slots.reshape(members, slot, width), dy_slots.reshape(members, slot, width)], axis=1
    )
    arrived = lax.all_to_all(outgoing, "expert", split_axis=0, concat_axis=0, tiled=True)
    x_rows = arrived[:, 0].reshape(total, width)
    dy_rows = arrived[:, 1].reshape(total, width)
    weight_gate = w_gate[0]
    weight_up = w_up[0]
    weight_down = w_down[0]
    share = weight_gate.shape[1] // tensor_count

    def gate_terms(start, count):
        gate_part = lax.dot_general(
            weight_gate, x_rows, (((0,), (1,)), ((), ())), preferred_element_type=jnp.float32
        )
        up_part = lax.dot_general(
            weight_up, x_rows, (((0,), (1,)), ((), ())), preferred_element_type=jnp.float32
        )
        return jnp.concatenate([gate_part, up_part], axis=1)

    summed = spread_units(gate_terms, share)
    gate_t = summed[:, :total]
    up_t = summed[:, total:]
    sigma = jax.nn.sigmoid(gate_t)
    active = gate_t * sigma
    hidden_t = (active * up_t).astype(jnp.bfloat16)
    hidden_full = lax.all_gather(hidden_t, "tensor", axis=0, tiled=True)
    out_rows = lax.dot_general(
        hidden_full, weight_down, (((0,), (0,)), ((), ())), preferred_element_type=jnp.float32
    ).astype(jnp.bfloat16)
    out_slots = out_rows.reshape(members, slot, width)
    out_back = lax.all_to_all(out_slots, "expert", split_axis=0, concat_axis=0, tiled=True)

    def grad_terms(start, count):
        return lax.dot_general(
            weight_down, dy_rows, (((1,), (1,)), ((), ())), preferred_element_type=jnp.float32
        )

    d_hidden = spread_units(grad_terms, share)
    d_gate_t = (d_hidden * up_t * sigma * (1.0 + gate_t * (1.0 - sigma))).astype(jnp.bfloat16)
    d_up_t = (d_hidden * active).astype(jnp.bfloat16)
    d_gate_full, d_up_full = (
        lax.all_gather(d_gate_t, "tensor", axis=0, tiled=True),
        lax.all_gather(d_up_t, "tensor", axis=0, tiled=True),
    )
    back_rows = (
        lax.dot_general(
            d_gate_full, weight_gate, (((0,), (1,)), ((), ())), preferred_element_type=jnp.float32
        )
        + lax.dot_general(
            d_up_full, weight_up, (((0,), (1,)), ((), ())), preferred_element_type=jnp.float32
        )
    ).astype(jnp.bfloat16)
    grad_w_gate = lax.dot_general(
        x_rows, d_gate_full, (((0,), (1,)), ((), ())), preferred_element_type=jnp.float32
    ).astype(jnp.bfloat16)[None]
    grad_w_up = lax.dot_general(
        x_rows, d_up_full, (((0,), (1,)), ((), ())), preferred_element_type=jnp.float32
    ).astype(jnp.bfloat16)[None]
    grad_w_down = lax.dot_general(
        hidden_full, dy_rows, (((1,), (0,)), ((), ())), preferred_element_type=jnp.float32
    ).astype(jnp.bfloat16)[None]
    back_slots = back_rows.reshape(members, slot, width)
    grad_back = lax.all_to_all(back_slots, "expert", split_axis=0, concat_axis=0, tiled=True)
    mixed = lax.dot_general(
        weighted,
        out_back.reshape(total, width),
        (((0,), (0,)), ((), ())),
        preferred_element_type=jnp.float32,
    ).astype(jnp.bfloat16)
    grad_tokens = lax.dot_general(
        place,
        grad_back.reshape(total, width),
        (((0,), (0,)), ((), ())),
        preferred_element_type=jnp.float32,
    ).astype(jnp.bfloat16)
    return (mixed, grad_tokens, grad_w_gate, grad_w_up, grad_w_down)


def solution(mesh):
    in_specs = (
        P("expert", "tensor"),
        P("expert", None),
        P("expert", None),
        P("expert", "tensor", None),
        P("expert", "tensor", None),
        P("expert", None, "tensor"),
        P("expert", "tensor"),
    )
    out_specs = (
        P("expert", "tensor"),
        P("expert", "tensor"),
        P("expert", "tensor", None),
        P("expert", "tensor", None),
        P("expert", None, "tensor"),
    )
    return jax.shard_map(local, mesh=mesh, in_specs=in_specs, out_specs=out_specs, check_vma=False)
```

profile of v0, /device:TPU:0, one launch (start us, length us, event | category | flops | bytes accessed | tf_op | source)
XLA Modules:
  0.0 191.4 jit_solution(5882674442447173989)
XLA Ops:
  7.2 0.0 copy-start
  7.2 0.0 reduce-scatter.5.cloned.1.call-start
  7.2 0.8 fusion.31
  8.0 0.2 reduce_window_sum.11
  8.2 0.0 copy-start.3
  8.2 1.0 select_reduce_fusion
  9.2 0.8 multiply_add_fusion
  10.0 0.0 copy-done
  10.0 0.2 convolution_convert_fusion.1
  10.2 1.2 convolution_convert_fusion
  11.4 0.1 pad_maximum_fusion.1
  11.5 15.5 %all_to_all.15 = bf16[4,2,48,896]{3,2,1,0:T(8,128)(2,1)S(1)} all-to-all(bf16[4,2,48,896]{3,2,1,0:T(8,128)(2,1)S(1)} %pad_maximum_fusion.1), channel_id=1, replica_groups=mesh['expert'=4,'tensor'=8] {'expert'}, dimensions={0} | all-to-all | bytes 1376256 | tf_op jit(solution)/shard_map/all_to_all | solution.py:39
  27.1 0.1 fusion.46
  27.1 0.0 copy-done.3
  27.1 2.5 %fusion.18 = f32[2048,192]{0,1:T(8,128)} fusion(bf16[192,896]{1,0:T(8,128)(2,1)S(1)} %bitcast.87, bf16[1,2048,896]{2,1,0:T(8,128)(2,1)S(1)} %copy-done.3), kind=kOutput, calls=%fused_computation.18 | convolution fusion | flops 704643072 | bytes 5586944 | tf_op jit(solution)/shard_map/dot_general | solution.py:70
  29.6 0.0 reduce-scatter.5.cloned.1.call-update
  29.7 0.0 reduce-scatter.3.cloned.1.call-start
  29.7 0.0 copy-start.1
  29.7 3.2 %fusion.15 = f32[2048,192]{0,1:T(8,128)S(1)} fusion(bf16[192,896]{1,0:T(8,128)(2,1)S(1)} %bitcast.79, bf16[1,896,2048]{2,1,0:T(8,128)(2,1)} %param.11), kind=kOutput, calls=%fused_computation.17 | convolution fusion | flops 704643072 | bytes 5586944 | tf_op jit(solution)/shard_map/dot_general | solution.py:51
  32.9 0.0 copy-done.1
  32.9 1.0 fusion.12
  34.0 2.0 %pad_maximum_fusion = f32[2048,384]{0,1:T(8,128)} fusion(f32[2048,192]{0,1:T(8,128)S(1)} %fusion.15, f32[2048,192]{0,1:T(8,128)S(1)} %fusion.12), kind=kLoop, calls=%fused_computation.15 | loop fusion | flops 786432 | bytes 6291456 | tf_op jit(solution)/shard_map/concatenate | solution.py:54
  36.0 0.0 reduce-scatter.3.cloned.1.call-update
  36.0 27.5 %reduce-scatter.5.cloned.1.call-done = f32[256,192]{0,1:T(8,128)} async-done(((f32[2048,192]{0,1:T(8,128)}), f32[256,192]{0,1:T(8,128)}) %reduce-scatter.5.cloned.1.call-update) | async-done | bytes 196624 | tf_op jit(solution)/shard_map/reduce_scatter | solution.py:8
  63.5 41.8 %reduce-scatter.3.cloned.1.call-done = f32[256,384]{0,1:T(8,128)} async-done(((f32[2048,384]{0,1:T(8,128)}), f32[256,384]{0,1:T(8,128)}) %reduce-scatter.3.cloned.1.call-update) | async-done | bytes 393232 | tf_op jit(solution)/shard_map/reduce_scatter | solution.py:8
  105.2 1.2 multiply_convert_fusion.1
  106.5 15.2 %all_gather.10 = bf16[2048,192]{0,1:T(8,128)(2,1)S(1)} all-gather(bf16[256,192]{0,1:T(8,128)(2,1)S(1)} %get-tuple-element.7), channel_id=1, replica_groups=mesh['expert'=4,'tensor'=8] {'tensor'}, dimensions={0}, use_global_device_ids=true | all-gather | bytes 884736 | tf_op jit(solution)/shard_map/all_gather | solution.py:78
  121.6 0.0 copy-start.2
  121.6 16.3 %all_gather.11 = bf16[2048,192]{0,1:T(8,128)(2,1)S(1)} all-gather(bf16[256,192]{0,1:T(8,128)(2,1)S(1)} %get-tuple-element.8), channel_id=1, replica_groups=mesh['expert'=4,'tensor'=8] {'tensor'}, dimensions={0}, use_global_device_ids=true | all-gather | bytes 884736 | tf_op jit(solution)/shard_map/all_gather | solution.py:79
  138.0 3.4 %fusion.4 = f32[192,896]{1,0:T(8,128)S(1)} fusion(bf16[2048,192]{0,1:T(8,128)(2,1)S(1)} %all_gather.11, bf16[1,896,2048]{2,1,0:T(8,128)(2,1)} %param.11), kind=kOutput, calls=%fused_computation.4 | convolution fusion | flops 704643072 | bytes 5144576 | tf_op jit(solution)/shard_map/dot_general | solution.py:85
  141.4 0.0 copy-done.2
  141.4 2.1 %fusion.24 = bf16[192,896]{1,0:T(8,128)(2,1)} fusion(f32[192,896]{1,0:T(8,128)S(1)} %fusion.4, bf16[2048,192]{0,1:T(8,128)(2,1)S(1)} %all_gather.10, bf16[1,896,2048]{2,1,0:T(8,128)(2,1)S(1)} %copy-done.2), kind=kOutput, calls=%fused_computation.20 | convolution fusion | flops 704987136 | bytes 5488640 | tf_op jit(solution)/shard_map/dot_general | solution.py:82
  143.5 3.7 %all-to-all-start.2 = ((bf16[4,48,896]{2,1,0:T(8,128)(2,1)}), bf16[4,48,896]{2,1,0:T(8,128)(2,1)S(1)}, u32[]{:S(2)}, u32[]{:S(2)}) async-start(bf16[4,48,896]{2,1,0:T(8,128)(2,1)} %bitcast.19), calls=%async_computation.4 | async-start | bytes 688128 | tf_op jit(solution)/shard_map/all_to_all | solution.py:99
  147.2 15.9 %all_gather.9 = bf16[2048,192]{0,1:T(8,128)(2,1)S(1)} all-gather(bf16[256,192]{0,1:T(8,128)(2,1)S(1)} %get-tuple-element.9), channel_id=1, replica_groups=mesh['expert'=4,'tensor'=8] {'tensor'}, dimensions={0}, use_global_device_ids=true | all-gather | bytes 884736 | tf_op jit(solution)/shard_map/all_gather | solution.py:62
  163.1 3.8 %fusion.27 = bf16[192,896]{1,0:T(8,128)(2,1)} fusion(bf16[2048,192]{0,1:T(8,128)(2,1)S(1)} %all_gather.9, bf16[1,2048,896]{2,1,0:T(8,128)(2,1)} %param.12), kind=kOutput, calls=%fused_computation.21 | convolution fusion | flops 704815104 | bytes 4800512 | tf_op jit(solution)/shard_map/dot_general | solution.py:63
  166.9 3.1 %convert_bitcast_fusion = bf16[1,2048,896]{2,1,0:T(8,128)(2,1)} fusion(bf16[2048,192]{0,1:T(8,128)(2,1)S(1)} %all_gather.9, bf16[192,896]{1,0:T(8,128)(2,1)S(1)} %bitcast.88), kind=kOutput, calls=%fused_computation.12 | convolution fusion | flops 706478080 | bytes 4800512 | tf_op jit(solution)/shard_map/dot_general | solution.py:95
  170.1 3.0 %convert_bitcast_fusion.2 = bf16[1,896,2048]{2,1,0:T(8,128)(2,1)} fusion(bf16[192,896]{1,0:T(8,128)(2,1)S(1)} %bitcast.81, bf16[2048,192]{0,1:T(8,128)(2,1)S(1)} %all_gather.10), kind=kOutput, calls=%fused_computation.14 | convolution fusion | flops 706478080 | bytes 4800512 | tf_op jit(solution)/shard_map/dot_general | solution.py:89
  173.1 0.0 copy-start.4
  173.1 0.0 all-to-all-done.2
  173.1 4.0 %all-to-all-start.1 = ((bf16[4,48,896]{2,1,0:T(8,128)(2,1)}), bf16[4,48,896]{2,1,0:T(8,128)(2,1)S(1)}, u32[]{:S(2)}, u32[]{:S(2)}) async-start(bf16[4,48,896]{2,1,0:T(8,128)(2,1)} %bitcast.14), calls=%async_computation.2 | async-start | bytes 688128 | tf_op jit(solution)/shard_map/all_to_all | solution.py:67
  177.1 3.0 %convert_bitcast_fusion.1 = bf16[1,896,2048]{2,1,0:T(8,128)(2,1)} fusion(bf16[192,896]{1,0:T(8,128)(2,1)S(1)} %bitcast.82, bf16[2048,192]{0,1:T(8,128)(2,1)S(1)} %all_gather.11), kind=kOutput, calls=%fused_computation.13 | convolution fusion | flops 706478080 | bytes 4800512 | tf_op jit(solution)/shard_map/dot_general | solution.py:92
  180.1 0.9 convolution_convert_fusion.2
  181.0 2.6 %all-to-all-done.1 = bf16[4,48,896]{2,1,0:T(8,128)(2,1)S(1)} async-done(((bf16[4,48,896]{2,1,0:T(8,128)(2,1)}), bf16[4,48,896]{2,1,0:T(8,128)(2,1)S(1)}, u32[]{:S(2)}, u32[]{:S(2)}) %all-to-all-start.1) | async-done | bytes 344096 | tf_op jit(solution)/shard_map/all_to_all | solution.py:67
  183.7 0.0 copy-done.4
  183.7 0.9 convolution_convert_fusion.3
Async XLA Ops:
  7.2 2.8 %copy-start = (bf16[128,896]{1,0:T(8,128)(2,1)S(1)}, bf16[128,896]{1,0:T(8,128)(2,1)}, u32[]{:S(2)}) copy-start(bf16[128,896]{1,0:T(8,128)(2,1)} %param.7) | copy-start | bytes 688132
  7.2 56.3 %reduce-scatter.5.cloned.1.call-start = ((), (), s32[]{:S(2)}) async-start(), calls=%async_computation.6 | async-start | bytes 1769472 | tf_op jit(solution)/shard_map/reduce_scatter | solution.py:8
  8.2 18.9 %copy-start.3 = (bf16[1,2048,896]{2,1,0:T(8,128)(2,1)S(1)}, bf16[1,2048,896]{2,1,0:T(8,128)(2,1)}, u32[]{:S(2)}) copy-start(bf16[1,2048,896]{2,1,0:T(8,128)(2,1)} %param.12) | copy-start | bytes 11010052
  29.7 75.6 %reduce-scatter.3.cloned.1.call-start = ((), (), s32[]{:S(2)}) async-start(), calls=%async_computation.5 | async-start | bytes 3538944 | tf_op jit(solution)/shard_map/reduce_scatter | solution.py:8
  29.7 3.2 %copy-start.1 = (bf16[1,896,2048]{2,1,0:T(8,128)(2,1)S(1)}, bf16[1,896,2048]{2,1,0:T(8,128)(2,1)}, u32[]{:S(2)}) copy-start(bf16[1,896,2048]{2,1,0:T(8,128)(2,1)} %param.10) | copy-start | bytes 11010052
  121.6 19.7 %copy-start.2 = (bf16[1,896,2048]{2,1,0:T(8,128)(2,1)S(1)}, bf16[1,896,2048]{2,1,0:T(8,128)(2,1)}, u32[]{:S(2)}) copy-start(bf16[1,896,2048]{2,1,0:T(8,128)(2,1)} %param.10) | copy-start | bytes 11010052
  143.5 29.5 %all-to-all-start.2 = ((bf16[4,48,896]{2,1,0:T(8,128)(2,1)}), bf16[4,48,896]{2,1,0:T(8,128)(2,1)S(1)}, u32[]{:S(2)}, u32[]{:S(2)}) async-start(bf16[4,48,896]{2,1,0:T(8,128)(2,1)} %bitcast.19), calls=%async_computation.4 | async-start | bytes 688128 | tf_op jit(solution)/shard_map/all_to_all | solution.py:99
  173.1 10.6 %copy-start.4 = (bf16[128,1]{0,1:T(2,128)(2,1)S(1)}, bf16[128,1]{0,1:T(2,128)(2,1)}, u32[]{:S(2)}) copy-start(bf16[128,1]{0,1:T(2,128)(2,1)} %param.8) | copy-start | bytes 772
  173.1 10.6 %all-to-all-start.1 = ((bf16[4,48,896]{2,1,0:T(8,128)(2,1)}), bf16[4,48,896]{2,1,0:T(8,128)(2,1)S(1)}, u32[]{:S(2)}, u32[]{:S(2)}) async-start(bf16[4,48,896]{2,1,0:T(8,128)(2,1)} %bitcast.14), calls=%async_computation.2 | async-start | bytes 688128 | tf_op jit(solution)/shard_map/all_to_all | solution.py:67
Sparse Core Ops, SparseCore 0:
  29.8 33.6 reduce-scatter.4
  66.3 38.8 reduce-scatter.2
where the time goes:
time: 192 us; the launch traced here: 191 us
  waiting for transfers between devices  71.9 us (37%)
  blocking collectives  63 us (33%)
  matrix products  28.5 us (15%)
  between operations  14.2 us (7%)
  starting transfers between devices  7.81 us (4%)
  other arithmetic  6.05 us (3%)
    reduce_scatter x2, waiting for transfers between devices, spread_units(): lax.psum_scatter(function(jnp.int32(0), share * lax.axis_size('tensor')),...  69.2 us
    all_gather x1, blocking collectives, local(): lax.all_gather(d_up_t, 'tensor', axis=0, tiled=True)  16.3 us
    all_gather x1, blocking collectives, local(): hidden_full = lax.all_gather(hidden_t, 'tensor', axis=0, tiled=True)  15.9 us
    all_to_all x1, blocking collectives, local(): lax.all_to_all(outgoing, 'expert', split_axis=0, concat_axis=0, tiled=True)  15.5 us
    all_gather x1, blocking collectives, local(): lax.all_gather(d_gate_t, 'tensor', axis=0, tiled=True)  15.2 us
    all_to_all x1, starting transfers between devices, local(): lax.all_to_all(out_slots, 'expert', split_axis=0, concat_axis=0, tiled=True)  4.03 us
  transfers between devices with their start and end apart: 4, of which 3 were waited for; matrix products, arithmetic and copies ran while one was open for 10% of the time, Pallas kernels for 0%

commit v1 on v0

v1 whole, which is shorter than its diff:
```python
import functools

import jax
import jax.numpy as jnp
from jax import lax
from jax.experimental import pallas as pl
from jax.experimental.pallas import tpu as pltpu
from jax.sharding import PartitionSpec as P

F32 = jnp.float32
BF16 = jnp.bfloat16


def spread_units(function):
    return lax.psum_scatter(function(), "tensor", scatter_dimension=0, tiled=True)


def general(tokens, gate_weights, expert_ids, w_gate, w_up, w_down, grad_out):
    members = lax.axis_size("expert")
    tok_rows = tokens.shape[0]
    routes = expert_ids.shape[1]
    width = tokens.shape[1]
    slot = 3 * routes * tok_rows // (2 * members)
    total = members * slot
    flat_ids = expert_ids.reshape(-1)
    counted = (flat_ids[:, None] == jnp.arange(members, dtype=jnp.int32)[None, :]).astype(jnp.int32)
    ranks = jnp.cumsum(counted, axis=0) - 1
    position = jnp.sum(counted * ranks, axis=1)
    target = (flat_ids * slot + position).reshape(tok_rows, routes)
    matched = target[None, :, :] == jnp.arange(total, dtype=jnp.int32)[:, None, None]
    place = jnp.sum(matched.astype(F32), axis=2).astype(BF16)
    weighted = jnp.sum(jnp.where(matched, gate_weights.astype(F32)[None], 0.0), axis=2).astype(BF16)
    x_slots = jnp.dot(place, tokens, preferred_element_type=F32).astype(BF16)
    dy_slots = jnp.dot(weighted, grad_out, preferred_element_type=F32).astype(BF16)
    outgoing = jnp.stack(
        [x_slots.reshape(members, slot, width), dy_slots.reshape(members, slot, width)], axis=1
    )
    arrived = lax.all_to_all(outgoing, "expert", split_axis=0, concat_axis=0, tiled=True)
    x_rows = arrived[:, 0].reshape(total, width)
    dy_rows = arrived[:, 1].reshape(total, width)
    weight_gate, weight_up, weight_down = w_gate[0], w_up[0], w_down[0]
    dot = functools.partial(lax.dot_general, preferred_element_type=F32)

    def gate_terms():
        return jnp.concatenate(
            [dot(w, x_rows, (((0,), (1,)), ((), ()))) for w in (weight_gate, weight_up)], axis=1
        )

    summed = spread_units(gate_terms)
    gate_t, up_t = summed[:, :total], summed[:, total:]
    sigma = jax.nn.sigmoid(gate_t)
    active = gate_t * sigma
    hidden_t = (active * up_t).astype(BF16)
    hidden = lax.all_gather(hidden_t, "tensor", axis=0, tiled=True)
    out_rows = dot(hidden, weight_down, (((0,), (0,)), ((), ()))).astype(BF16)
    swap = functools.partial(
        lax.all_to_all, axis_name="expert", split_axis=0, concat_axis=0, tiled=True
    )
    out_back = swap(out_rows.reshape(members, slot, width))
    d_hidden = spread_units(lambda: dot(weight_down, dy_rows, (((1,), (1,)), ((), ()))))
    d_gate_t = (d_hidden * up_t * sigma * (1.0 + gate_t * (1.0 - sigma))).astype(BF16)
    d_up_t = (d_hidden * active).astype(BF16)
    d_gate = lax.all_gather(d_gate_t, "tensor", axis=0, tiled=True)
    d_up = lax.all_gather(d_up_t, "tensor", axis=0, tiled=True)
    back_rows = (
        dot(d_gate, weight_gate, (((0,), (1,)), ((), ())))
        + dot(d_up, weight_up, (((0,), (1,)), ((), ())))
    ).astype(BF16)
    grad_w_gate = dot(x_rows, d_gate, (((0,), (1,)), ((), ()))).astype(BF16)[None]
    grad_w_up = dot(x_rows, d_up, (((0,), (1,)), ((), ()))).astype(BF16)[None]
    grad_w_down = dot(hidden, dy_rows, (((1,), (0,)), ((), ()))).astype(BF16)[None]
    grad_back = swap(back_rows.reshape(members, slot, width))
    mixed = dot(weighted, out_back.reshape(total, width), (((0,), (0,)), ((), ()))).astype(BF16)
    grad_tokens = dot(place, grad_back.reshape(total, width), (((0,), (0,)), ((), ()))).astype(BF16)
    return (mixed, grad_tokens, grad_w_gate, grad_w_up, grad_w_down)


NT = (((1,), (1,)), ((), ()))
TN = (((0,), (0,)), ((), ()))
NN = (((1,), (0,)), ((), ()))


def mm(a, b, dims=NN):
    return lax.dot_general(a, b, dims, preferred_element_type=F32)


def params(mib=24):
    return pltpu.CompilerParams(vmem_limit_bytes=mib * 2**20)


def cost(flops, nbytes):
    return pl.CostEstimate(flops=int(flops), bytes_accessed=int(nbytes), transcendentals=0)


def placement(ids, here, members, slot, total):
    count = ids.shape[1]
    lanes = lax.broadcasted_iota(jnp.int32, (max(members, 8), count), 0)
    chosen = (lanes == ids).astype(F32)
    before = lax.broadcasted_iota(jnp.int32, (count, count), 0) < lax.broadcasted_iota(
        jnp.int32, (count, count), 1
    )
    ranks = mm(chosen.astype(BF16), before.astype(F32).astype(BF16))
    rank = jnp.sum(chosen * ranks, axis=0, keepdims=True).astype(jnp.int32)
    target = (ids ^ here) * slot + rank
    return lax.broadcasted_iota(jnp.int32, (total, count), 0) == target


def dispatch(ids, here, data, gates, members, slot):
    total, width = members * slot, data.shape[1]

    def kernel(here_ref, ids_ref, *refs):
        data_ref, out_refs = refs[-members - 1], refs[-members:]
        mask = placement(ids_ref[...], here_ref[0], members, slot, total)
        value = 1.0 if gates is None else refs[0][...].astype(F32)
        rows = mm(jnp.where(mask, value, 0.0).astype(BF16), data_ref[...]).astype(BF16)
        for m, ref in enumerate(out_refs):
            ref[...] = rows[m * slot : (m + 1) * slot]

    vmem = pl.BlockSpec(memory_space=pltpu.VMEM)
    extra = () if gates is None else (gates,)
    return pl.pallas_call(
        kernel,
        out_shape=[jax.ShapeDtypeStruct((slot, width), BF16)] * members,
        in_specs=[pl.BlockSpec(memory_space=pltpu.SMEM), vmem] + [vmem] * len(extra) + [vmem],
        out_specs=[vmem] * members,
        compiler_params=params(8),
        cost_estimate=cost(2 * total * data.size, 4 * data.size),
        name="dispatch",
    )(here, ids, *extra, data)


def collect(ids, here, rows, gates, members, slot):
    total, width, count = members * slot, rows[0].shape[1], ids.shape[1]

    def kernel(here_ref, ids_ref, *refs):
        row_refs, out_ref, joined = refs[-members - 2 : -2], refs[-2], refs[-1]
        for m, ref in enumerate(row_refs):
            joined[m * slot : (m + 1) * slot, :] = ref[...]
        mask = placement(ids_ref[...], here_ref[0], members, slot, total)
        value = 1.0 if gates is None else refs[0][...].astype(F32)
        pick = jnp.where(mask, value, 0.0).astype(BF16)
        out_ref[...] = mm(pick, joined[...], TN).astype(BF16)

    vmem = pl.BlockSpec(memory_space=pltpu.VMEM)
    extra = () if gates is None else (gates,)
    return pl.pallas_call(
        kernel,
        out_shape=jax.ShapeDtypeStruct((count, width), BF16),
        in_specs=[pl.BlockSpec(memory_space=pltpu.SMEM), vmem] + [vmem] * (len(extra) + members),
        out_specs=vmem,
        scratch_shapes=[pltpu.VMEM((total, width), BF16)],
        compiler_params=params(8),
        cost_estimate=cost(2 * count * total * width, 4 * total * width),
        name="collect",
    )(here, ids, *extra, *rows)


def partial_units(order, rows, weights, unit, down, kept=None, first=0):
    members, slot, width = len(rows), rows[0].shape[0], rows[0].shape[1]
    total, n, blocks = members * slot, len(weights), order.shape[0]

    def kernel(order_ref, *refs):
        row_refs, w_refs = refs[:members], refs[members : members + n]
        rest, joined = refs[members + n : -1], refs[-1]
        j = pl.program_id(0)

        @pl.when(j == 0)
        def _():
            for m, ref in enumerate(row_refs):
                joined[m * slot : (m + 1) * slot, :] = ref[...]

        for i, w_ref in enumerate(w_refs):
            term = mm(joined[...], w_ref[...], NT if down else NN)
            if kept is None:
                rest[0][0, i] = term.astype(BF16)
            else:
                term = term + rest[0][0, i].astype(F32)

                @pl.when(j < first)
                def _():
                    rest[1][0, i] = term.astype(BF16)

                @pl.when(j >= first)
                def _():
                    rest[2][0, i] = term

    whole = pl.BlockSpec((slot, width), lambda j, o: (0, 0))
    w_spec = (
        pl.BlockSpec((unit, width), lambda j, o: (o[j], 0))
        if down
        else pl.BlockSpec((width, unit), lambda j, o: (0, o[j]))
    )
    block = (1, n, total, unit)
    if kept is None:
        extra, extra_specs = (), []
        shapes = [jax.ShapeDtypeStruct((blocks, n, total, unit), BF16)]
        out_specs = [pl.BlockSpec(block, lambda j, o: (j, 0, 0, 0))]
    else:
        extra = (kept,)
        extra_specs = [pl.BlockSpec(block, lambda j, o: ((j + first) % blocks, 0, 0, 0))]
        shapes = [
            jax.ShapeDtypeStruct((first, n, total, unit), BF16),
            jax.ShapeDtypeStruct((blocks - first, n, total, unit), F32),
        ]
        out_specs = [
            pl.BlockSpec(block, lambda j, o: (jnp.minimum(j, first - 1), 0, 0, 0)),
            pl.BlockSpec(block, lambda j, o: (jnp.maximum(j - first, 0), 0, 0, 0)),
        ]
    return pl.pallas_call(
        kernel,
        out_shape=shapes,
        grid_spec=pltpu.PrefetchScalarGridSpec(
            num_scalar_prefetch=1,
            grid=(blocks,),
            in_specs=[whole] * members + [w_spec] * n + extra_specs,
            out_specs=out_specs,
            scratch_shapes=[pltpu.VMEM((total, width), BF16)],
        ),
        compiler_params=params(),
        cost_estimate=cost(
            2 * n * blocks * total * width * unit, 2 * n * blocks * unit * (width + 2 * total)
        ),
        name="partial_units",
    )(order, *rows, *weights)[0] if kept is None else pl.pallas_call(
        kernel,
        out_shape=shapes,
        grid_spec=pltpu.PrefetchScalarGridSpec(
            num_scalar_prefetch=1,
            grid=(blocks,),
            in_specs=[whole] * members + [w_spec] * n + extra_specs,
            out_specs=out_specs,
            scratch_shapes=[pltpu.VMEM((total, width), BF16)],
        ),
        compiler_params=params(),
        cost_estimate=cost(
            2 * n * blocks * total * width * unit, 2 * n * blocks * unit * (width + 4 * total)
        ),
        name="partial_units",
    )(order, *rows, *weights, *extra)


def full_units(order, pieces, weights, slot, unit, down):
    n, total = pieces[0].shape[1], pieces[0].shape[2]
    width = weights[0].shape[1] if down else weights[0].shape[0]
    members, blocks = total // slot, order.shape[0]
    starts = [sum(p.shape[0] for p in pieces[:i]) for i in range(len(pieces))]

    def kernel(order_ref, *refs):
        piece_refs, w_refs = refs[: len(pieces)], refs[len(pieces) : len(pieces) + n]
        out_refs, acc = refs[len(pieces) + n : -1], refs[-1]
        j = pl.program_id(0)

        @pl.when(j == 0)
        def _():
            acc[...] = jnp.zeros_like(acc)

        for p, ref in enumerate(piece_refs):

            @pl.when((j >= starts[p]) & (j < starts[p] + pieces[p].shape[0]))
            def _():
                term = mm(ref[0, 0], w_refs[0][...], NN if down else NT)
                for i in range(1, n):
                    term = term + mm(ref[0, i], w_refs[i][...], NN if down else NT)
                acc[...] += term

        @pl.when(j == blocks - 1)
        def _():
            for m, ref in enumerate(out_refs):
                ref[...] = acc[m * slot : (m + 1) * slot, :].astype(BF16)

    w_spec = (
        pl.BlockSpec((unit, width), lambda j, o: (o[j], 0))
        if down
        else pl.BlockSpec((width, unit), lambda j, o: (0, o[j]))
    )
    return pl.pallas_call(
        kernel,
        out_shape=[jax.ShapeDtypeStruct((slot, width), BF16)] * members,
        grid_spec=pltpu.PrefetchScalarGridSpec(
            num_scalar_prefetch=1,
            grid=(blocks,),
            in_specs=[piece_spec(p, s, total, unit) for p, s in zip(pieces, starts)]
            + [w_spec] * n,
            out_specs=[pl.BlockSpec((slot, width), lambda j, o: (0, 0))] * members,
            scratch_shapes=[pltpu.VMEM((total, width), F32)],
        ),
        compiler_params=params(),
        cost_estimate=cost(
            2 * n * blocks * total * width * unit, 2 * n * blocks * unit * (width + total)
        ),
        name="full_units",
    )(order, *pieces, *weights)


def piece_spec(piece, start, total, unit):
    last = piece.shape[0] - 1
    return pl.BlockSpec(
        (1, piece.shape[1], total, unit),
        lambda j, o: (jnp.clip(j - start, 0, last), 0, 0, 0),
    )


def weight_grads(order, pieces, rows, unit, down):
    n, total = pieces[0].shape[1], pieces[0].shape[2]
    members, slot, width = len(rows), rows[0].shape[0], rows[0].shape[1]
    blocks = order.shape[0]
    starts = [sum(p.shape[0] for p in pieces[:i]) for i in range(len(pieces))]

    def kernel(order_ref, *refs):
        piece_refs, row_refs = refs[: len(pieces)], refs[len(pieces) : len(pieces) + members]
        out_refs, joined = refs[len(pieces) + members : -1], refs[-1]
        j = pl.program_id(0)

        @pl.when(j == 0)
        def _():
            for m, ref in enumerate(row_refs):
                joined[m * slot : (m + 1) * slot, :] = ref[...]

        for p, ref in enumerate(piece_refs):

            @pl.when((j >= starts[p]) & (j < starts[p] + pieces[p].shape[0]))
            def _():
                for i, out_ref in enumerate(out_refs):
                    if down:
                        out_ref[0] = mm(ref[0, i], joined[...], TN).astype(BF16)
                    else:
                        out_ref[0] = mm(joined[...], ref[0, i], TN).astype(BF16)

    whole = pl.BlockSpec((slot, width), lambda j, o: (0, 0))
    if down:
        shape = (1, blocks * unit, width)
        out_spec = pl.BlockSpec((1, unit, width), lambda j, o: (0, o[j], 0))
    else:
        shape = (1, width, blocks * unit)
        out_spec = pl.BlockSpec((1, width, unit), lambda j, o: (0, 0, o[j]))
    return pl.pallas_call(
        kernel,
        out_shape=[jax.ShapeDtypeStruct(shape, BF16)] * n,
        grid_spec=pltpu.PrefetchScalarGridSpec(
            num_scalar_prefetch=1,
            grid=(blocks,),
            in_specs=[piece_spec(p, s, total, unit) for p, s in zip(pieces, starts)]
            + [whole] * members,
            out_specs=[out_spec] * n,
            scratch_shapes=[pltpu.VMEM((total, width), BF16)],
        ),
        compiler_params=params(),
        cost_estimate=cost(
            2 * n * blocks * total * width * unit, 2 * n * blocks * unit * (width + total)
        ),
        name="weight_grads",
    )(order, *pieces, *rows)


def hypercube(tokens, gate_weights, expert_ids, w_gate, w_up, w_down, grad_out):
    members = lax.axis_size("expert")
    parts = lax.axis_size("tensor")
    bits = (parts // 2).bit_length() - 1
    count = tokens.shape[0]
    slot = 3 * count // (2 * members)
    weight_gate, weight_up, weight_down = w_gate[0], w_up[0], w_down[0]
    unit = weight_gate.shape[1] // parts
    half = parts // 2

    own = lax.axis_index("expert")
    here = own.reshape(1)
    ids = expert_ids.reshape(1, count)
    gates = gate_weights.reshape(1, count)

    t = lax.axis_index("tensor")
    core, chip = t % 2, t // 2
    orders = (tuple(range(bits)), tuple(reversed(range(bits))))

    def pairs(step):
        return [(d, d ^ (2 << orders[d % 2][step])) for d in range(parts)]

    def step_swap(x, step):
        return lax.ppermute(x, "tensor", pairs(step))

    def core_swap(x):
        return lax.ppermute(x, "tensor", [(d, d ^ 1) for d in range(parts)])

    def block_ids(c):
        out = []
        for rel in range(half):
            place = [jnp.int32(0), jnp.int32(0)]
            for k in range(2):
                for step in range(bits):
                    bit = (chip >> orders[k][step]) & 1
                    flip = (rel >> (bits - 1 - step)) & 1
                    place[k] = place[k] * 2 + (bit ^ flip)
            out.append(half * c + jnp.where(c == 0, place[0], place[1]))
        return jnp.stack(out).astype(jnp.int32)

    mine, other = block_ids(core), block_ids(1 - core)
    first = half // 2
    send_first = jnp.concatenate([mine[first:], mine[:first]])
    every = jnp.concatenate([mine, other])

    def expert_swap(rows):
        return [rows[0]] + [
            lax.ppermute(rows[m], "expert", [(d, d ^ m) for d in range(members)])
            for m in range(1, members)
        ]

    def reduce_units(rows, weights, down):
        away = partial_units(other, rows, weights, unit, down)
        arrived = core_swap(away)
        send, keep = partial_units(send_first, rows, weights, unit, down, arrived, first)
        size = first
        for step in range(bits):
            got = step_swap(send, step)
            total = keep + got.astype(F32)
            size //= 2
            if step < bits - 1:
                send, keep = total[size:].astype(BF16), total[:size]
        return total[0]

    def gather_units(x):
        for step in reversed(range(bits)):
            x = jnp.concatenate([x, step_swap(x, step)], axis=0)
        return [x, core_swap(x)]

    x_rows = expert_swap(dispatch(ids, here, tokens, None, members, slot))
    dy_rows = expert_swap(dispatch(ids, here, grad_out, gates, members, slot))

    gate, up = reduce_units(x_rows, (weight_gate, weight_up), False)
    (d_hidden,) = reduce_units(dy_rows, (weight_down,), True)

    sigma = jax.nn.sigmoid(gate)
    active = gate * sigma
    hidden = (active * up).astype(BF16)
    d_gate = (d_hidden * up * sigma * (1.0 + gate * (1.0 - sigma))).astype(BF16)
    d_up = (d_hidden * active).astype(BF16)

    hidden_all = gather_units(hidden[None, None])
    out_rows = full_units(every, hidden_all, (weight_down,), slot, unit, True)
    out_back = expert_swap(out_rows)
    (grad_w_down,) = weight_grads(every, hidden_all, dy_rows, unit, True)

    d_all = gather_units(jnp.stack([d_gate, d_up])[None])
    back_rows = full_units(every, d_all, (weight_gate, weight_up), slot, unit, False)
    grad_back = expert_swap(back_rows)
    grad_w_gate, grad_w_up = weight_grads(every, d_all, x_rows, unit, False)

    mixed = collect(ids, here, out_back, gates, members, slot)
    grad_tokens = collect(ids, here, grad_back, None, members, slot)
    return (mixed, grad_tokens, grad_w_gate, grad_w_up, grad_w_down)


def power_of_two(n):
    return n & (n - 1) == 0


def solution(mesh):
    members, parts = mesh.shape["expert"], mesh.shape["tensor"]

    def local(*args):
        unit = args[3].shape[2] // parts
        slot = 3 * args[0].shape[0] // (2 * members)
        fits = power_of_two(members) and power_of_two(parts) and parts >= 4
        fits = fits and unit % 128 == 0 and slot % 16 == 0 and args[0].shape[1] % 128 == 0
        fits = fits and args[2].shape[1] == 1
        return (hypercube if fits else general)(*args)

    in_specs = (
        P("expert", "tensor"),
        P("expert", None),
        P("expert", None),
        P("expert", "tensor", None),
        P("expert", "tensor", None),
        P("expert", None, "tensor"),
        P("expert", "tensor"),
    )
    out_specs = (
        P("expert", "tensor"),
        P("expert", "tensor"),
        P("expert", "tensor", None),
        P("expert", "tensor", None),
        P("expert", None, "tensor"),
    )
    return jax.shard_map(local, mesh=mesh, in_specs=in_specs, out_specs=out_specs, check_vma=False)
```

time: 192 us -> 124 us (0.65)
  blocking collectives: 63 us -> 0 us
  Pallas kernels: 0 us -> 34.1 us
  matrix products: 28.5 us -> 0 us
  waiting for transfers between devices: 71.9 us -> 50.8 us
  starting transfers between devices: 7.81 us -> 25.4 us
  between operations: 14.2 us -> 0.91 us
  local copies, waits for them, and re-layouts: 0.08 us -> 12.1 us
  other arithmetic: 6.05 us -> 0.69 us
    reduce_scatter x2 -> x0, waiting for transfers between devices: 69.2 us -> none  [spread_units(): lax.psum_scatter(function(jnp.int32(0), share * lax.axis_size('tensor')),...]
    ppermute x0 -> x24, waiting for transfers between devices: none -> 50.8 us  [the longest x8 40.4 us: step_swap(): return lax.ppermute(x, 'tensor', pairs(step))]
    all_gather x3 -> x0, blocking collectives: 47.4 us -> none  [the longest x1 16.3 us: local(): lax.all_gather(d_up_t, 'tensor', axis=0, tiled=True)]
    pallas_call x0 -> x12, Pallas kernels: none -> 34.1 us  [the longest x2 11.9 us: weight_grads(): pl.pallas_call(kernel, out_shape=[jax.ShapeDtypeStruct(shape, BF16)] * n,...]
    dot_general x13 -> x0, matrix products: 28.5 us -> none  [the longest x1 3.8 us: local(): lax.dot_general(hidden_full, weight_down, (((0,), (0,)), ((), ())), prefe...]
    ppermute x0 -> x24, starting transfers between devices: none -> 25.4 us  [the longest x12 15.2 us: expert_swap(): lax.ppermute(rows[m], 'expert', [(d, d ^ m) for d in range(members)])]
    all_to_all x1 -> x0, blocking collectives: 15.5 us -> none  [local(): lax.all_to_all(outgoing, 'expert', split_axis=0, concat_axis=0, tiled=True)]
    unnamed x10 -> x28, local copies, waits for them, and re-layouts: 0.03 us -> 12 us
  transfers between devices with their start and end apart: 4 -> 24, of which waited for: 3 -> 14; matrix products, arithmetic and copies ran while one was open for 10% -> 1% of each run, Pallas kernels for 0% -> 20%
where the time goes in v1:
time: 124 us
  waiting for transfers between devices  50.8 us (41%)
  Pallas kernels  34.1 us (28%)
  starting transfers between devices  25.4 us (20%)
  local copies, waits for them, and re-layouts  12.1 us (10%)
    ppermute x8, waiting for transfers between devices, step_swap(): return lax.ppermute(x, 'tensor', pairs(step))  40.4 us
    ppermute x12, starting transfers between devices, expert_swap(): lax.ppermute(rows[m], 'expert', [(d, d ^ m) for d in range(members)])  15.2 us
    unnamed x28, local copies, waits for them, and re-layouts  12 us
    pallas_call x2, Pallas kernels, weight_grads(): pl.pallas_call(kernel, out_shape=[jax.ShapeDtypeStruct(shape, BF16)] * n,...  11.9 us
    pallas_call x4, Pallas kernels, partial_units(): pl.pallas_call(kernel, out_shape=shapes, grid_spec=pltpu.PrefetchScalarGr...  10.7 us
    ppermute x8, starting transfers between devices, step_swap(): return lax.ppermute(x, 'tensor', pairs(step))  9.9 us
    ppermute x12, waiting for transfers between devices, expert_swap(): lax.ppermute(rows[m], 'expert', [(d, d ^ m) for d in range(members)])  8.75 us
    pallas_call x2, Pallas kernels, full_units(): pl.pallas_call(kernel, out_shape=[jax.ShapeDtypeStruct((slot, width), BF1...  8.58 us
  transfers between devices with their start and end apart: 24, of which 14 were waited for; matrix products, arithmetic and copies ran while one was open for 1% of the time, Pallas kernels for 20%

profile of v1, /device:TPU:0, one launch (start us, length us, event | category | flops | bytes accessed | tf_op | source)
XLA Modules:
  0.0 124.0 jit_solution(8573423348145753028)
XLA Ops:
  0.6 0.9 copy-done.9
  1.6 0.7 copy-done.11
  2.2 0.4 dispatch.2
  2.6 3.0 %collective-permute-start = (bf16[48,896]{1,0:T(8,128)(2,1)S(1)}, bf16[48,896]{1,0:T(8,128)(2,1)S(1)}, u32[]{:S(2)}, u32[]{:S(2)}) collective-permute-start(bf16[48,896]{1,0:T(8,128)(2,1)S(1)} %get-tuple-element.28), channel_id=1, source_target_pairs={{0,8},{8,0},{16,24},{24,16},{1,9},{9,1},{17,25},{25,17},{2,10},{10... | collective-permute-start | bytes 258056 | tf_op jit(solution)/shard_map/ppermute | solution.py:402
  5.6 1.5 %collective-permute-start.1 = (bf16[48,896]{1,0:T(8,128)(2,1)S(1)}, bf16[48,896]{1,0:T(8,128)(2,1)S(1)}, u32[]{:S(2)}, u32[]{:S(2)}) collective-permute-start(bf16[48,896]{1,0:T(8,128)(2,1)S(1)} %get-tuple-element.29), channel_id=1, source_target_pairs={{0,16},{8,24},{16,0},{24,8},{1,17},{9,25},{17,1},{25,9},{2,18},{10... | collective-permute-start | bytes 258056 | tf_op jit(solution)/shard_map/ppermute | solution.py:402
  7.2 0.0 collective-permute-start.2
  7.2 0.1 pad_add_fusion.1.order_ref
  7.3 1.2 collective-permute-done.refs_1_.refs_3_
  8.4 2.6 %collective-permute-done.1.refs_2_.refs_4_ = bf16[48,896]{1,0:T(8,128)(2,1)S(1)} collective-permute-done((bf16[48,896]{1,0:T(8,128)(2,1)S(1)}, bf16[48,896]{1,0:T(8,128)(2,1)S(1)}, u32[]{:S(2)}, u32[]{:S(2)}) %collective-permute-start.1) | collective-permute-done | bytes 86048 | tf_op jit(solution)/shard_map/ppermute | solution.py:402
  11.0 1.5 %collective-permute-done.2.refs_3_.refs_5_ = bf16[48,896]{1,0:T(8,128)(2,1)S(1)} collective-permute-done((bf16[48,896]{1,0:T(8,128)(2,1)S(1)}, bf16[48,896]{1,0:T(8,128)(2,1)S(1)}, u32[]{:S(2)}, u32[]{:S(2)}) %collective-permute-start.2) | collective-permute-done | bytes 86048 | tf_op jit(solution)/shard_map/ppermute | solution.py:402
  12.5 2.0 %copy-done.3 = bf16[1,896,2048]{2,1,0:T(8,128)(2,1)S(1)} copy-done((bf16[1,896,2048]{2,1,0:T(8,128)(2,1)S(1)}, bf16[1,896,2048]{2,1,0:T(8,128)(2,1)}, u32[]{:S(2)}) %copy-start.3) | copy-done | bytes 3670040
  14.6 2.0 %copy-done.6 = bf16[1,896,2048]{2,1,0:T(8,128)(2,1)S(1)} copy-done((bf16[1,896,2048]{2,1,0:T(8,128)(2,1)S(1)}, bf16[1,896,2048]{2,1,0:T(8,128)(2,1)}, u32[]{:S(2)}) %copy-start.6) | copy-done | bytes 3670040
  16.6 2.7 %partial_units.4 = bf16[4,2,192,256]{3,2,1,0:T(8,128)(2,1)S(1)} custom-call(s32[4]{0:T(128)S(1)} %pad_add_fusion.1.order_ref, bf16[48,896]{1,0:T(8,128)(2,1)S(1)} %get-tuple-element.27.refs_0_.refs_2_, bf16[48,896]{1,0:T(8,128)(2,1)S(1)} %collective-permute-done.refs_1_.refs_3_, bf16[48,896]{1,0:T(8,128)(2,1)S(1)} %collective-permute-done.1.refs_2_.refs_4_, ...), custom_call_target="tpu_custom_call" | custom-call | flops 704643072 | bytes 5242880 | tf_op jit(solution)/shard_map/partial_units/pallas_call | solution.py:209
  19.3 0.1 collective-permute-start.3
  19.5 0.4 dispatch.3
  19.8 0.6 collective-permute-start.12
  20.4 0.7 collective-permute-start.13
  21.1 2.2 %collective-permute-start.14 = (bf16[48,896]{1,0:T(8,128)(2,1)S(1)}, bf16[48,896]{1,0:T(8,128)(2,1)S(1)}, u32[]{:S(2)}, u32[]{:S(2)}) collective-permute-start(bf16[48,896]{1,0:T(8,128)(2,1)S(1)} %get-tuple-element.40), channel_id=1, source_target_pairs={{0,24},{8,16},{16,8},{24,0},{1,25},{9,17},{17,9},{25,1},{2,26},{10... | collective-permute-start | bytes 258056 | tf_op jit(solution)/shard_map/ppermute | solution.py:402
  23.4 0.1 pad_add_fusion.order_ref
  23.5 1.7 %collective-permute-done.12.refs_1_.refs_3_ = bf16[48,896]{1,0:T(8,128)(2,1)S(1)} collective-permute-done((bf16[48,896]{1,0:T(8,128)(2,1)S(1)}, bf16[48,896]{1,0:T(8,128)(2,1)S(1)}, u32[]{:S(2)}, u32[]{:S(2)}) %collective-permute-start.12) | collective-permute-done | bytes 86048 | tf_op jit(solution)/shard_map/ppermute | solution.py:402
  25.2 1.7 %collective-permute-done.13.refs_2_.refs_4_ = bf16[48,896]{1,0:T(8,128)(2,1)S(1)} collective-permute-done((bf16[48,896]{1,0:T(8,128)(2,1)S(1)}, bf16[48,896]{1,0:T(8,128)(2,1)S(1)}, u32[]{:S(2)}, u32[]{:S(2)}) %collective-permute-start.13) | collective-permute-done | bytes 86048 | tf_op jit(solution)/shard_map/ppermute | solution.py:402
  26.9 2.0 %copy-done = bf16[1,2048,896]{2,1,0:T(8,128)(2,1)S(1)} copy-done((bf16[1,2048,896]{2,1,0:T(8,128)(2,1)S(1)}, bf16[1,2048,896]{2,1,0:T(8,128)(2,1)}, u32[]{:S(2)}) %copy-start) | copy-done | bytes 3670040
  29.0 1.9 %partial_units.6 = bf16[4,1,192,256]{3,2,1,0:T(8,128)(2,1)S(1)} custom-call(s32[4]{0:T(128)S(1)} %pad_add_fusion.1.order_ref, bf16[48,896]{1,0:T(8,128)(2,1)S(1)} %get-tuple-element.37.refs_0_.refs_2_, bf16[48,896]{1,0:T(8,128)(2,1)S(1)} %collective-permute-done.12.refs_1_.refs_3_, bf16[48,896]{1,0:T(8,128)(2,1)S(1)} %collective-permute-done.13.refs_2_.refs_4_, ...), custom_call_target="tpu_custom_call" | custom-call | flops 352321536 | bytes 2621440 | tf_op jit(solution)/shard_map/partial_units/pallas_call | solution.py:209
  30.9 0.1 collective-permute-start.15
  31.0 2.2 %copy-done.7 = bf16[1,896,2048]{2,1,0:T(8,128)(2,1)S(1)} copy-done((bf16[1,896,2048]{2,1,0:T(8,128)(2,1)S(1)}, bf16[1,896,2048]{2,1,0:T(8,128)(2,1)}, u32[]{:S(2)}) %copy-start.7) | copy-done | bytes 3670040
  33.2 4.1 %partial_units.5 = (bf16[2,2,192,256]{3,2,1,0:T(8,128)(2,1)S(1)}, f32[2,2,192,256]{3,2,1,0:T(8,128)S(1)}) custom-call(s32[4]{0:T(128)S(1)} %pad_add_fusion.order_ref, bf16[48,896]{1,0:T(8,128)(2,1)S(1)} %get-tuple-element.27.refs_0_.refs_2_, bf16[48,896]{1,0:T(8,128)(2,1)S(1)} %collective-permute-done.refs_1_.refs_3_, ...), custom_call_target="tpu_custom_call" | custom-call | flops 704643072 | bytes 6815744 | tf_op jit(solution)/shard_map/partial_units/pallas_call | solution.py:224
  37.3 1.6 %collective-permute-start.4 = (bf16[2,2,192,256]{3,2,1,0:T(8,128)(2,1)S(1)}, bf16[2,2,192,256]{3,2,1,0:T(8,128)(2,1)S(1)}, u32[]{:S(2)}, u32[]{:S(2)}) collective-permute-start(bf16[2,2,192,256]{3,2,1,0:T(8,128)(2,1)S(1)} %get-tuple-element.32), channel_id=1, source_target_pairs={{0,2},{1,5},{2,0},{3,7},{4,6},{5,1},{6,4},{7,3},{8,10},{9,13},{10,... | collective-permute-start | bytes 1179656 | tf_op jit(solution)/shard_map/ppermute | solution.py:378
  38.9 2.0 %partial_units.7 = (bf16[2,1,192,256]{3,2,1,0:T(8,128)(2,1)S(1)}, f32[2,1,192,256]{3,2,1,0:T(8,128)S(1)}) custom-call(s32[4]{0:T(128)S(1)} %pad_add_fusion.order_ref, bf16[48,896]{1,0:T(8,128)(2,1)S(1)} %get-tuple-element.37.refs_0_.refs_2_, bf16[48,896]{1,0:T(8,128)(2,1)S(1)} %collective-permute-done.12.refs_1_.refs_3_, ...), custom_call_target="tpu_custom_call" | custom-call | flops 352321536 | bytes 3407872 | tf_op jit(solution)/shard_map/partial_units/pallas_call | solution.py:224
  41.0 0.5 collective-permute-start.16
  41.5 7.8 %collective-permute-done.4 = bf16[2,2,192,256]{3,2,1,0:T(8,128)(2,1)S(1)} collective-permute-done((bf16[2,2,192,256]{3,2,1,0:T(8,128)(2,1)S(1)}, bf16[2,2,192,256]{3,2,1,0:T(8,128)(2,1)S(1)}, u32[]{:S(2)}, u32[]{:S(2)}) %collective-permute-start.4) | collective-permute-done | bytes 393248 | tf_op jit(solution)/shard_map/ppermute | solution.py:378
  49.3 0.1 convert_add_fusion
  49.4 2.7 %collective-permute-start.5 = (bf16[1,2,192,256]{3,2,1,0:T(8,128)(2,1)S(1)}, bf16[1,2,192,256]{3,2,1,0:T(8,128)(2,1)S(1)}, u32[]{:S(2)}, u32[]{:S(2)}) collective-permute-start(bf16[1,2,192,256]{3,2,1,0:T(8,128)(2,1)S(1)} %slice.38), channel_id=1, source_target_pairs={{0,4},{1,3},{2,6},{3,1},{4,0},{5,7},{6,2},{7,5},{8,12},{9,11},{10,... | collective-permute-start | bytes 589832 | tf_op jit(solution)/shard_map/ppermute | solution.py:378
  52.1 3.8 %collective-permute-done.16 = bf16[2,1,192,256]{3,2,1,0:T(8,128)(2,1)S(1)} collective-permute-done((bf16[2,1,192,256]{3,2,1,0:T(8,128)(2,1)S(1)}, bf16[2,1,192,256]{3,2,1,0:T(8,128)(2,1)S(1)}, u32[]{:S(2)}, u32[]{:S(2)}) %collective-permute-start.16) | collective-permute-done | bytes 196640 | tf_op jit(solution)/shard_map/ppermute | solution.py:378
  56.0 0.1 collective-permute-start.17
  56.1 1.3 %collective-permute-done.5 = bf16[1,2,192,256]{3,2,1,0:T(8,128)(2,1)S(1)} collective-permute-done((bf16[1,2,192,256]{3,2,1,0:T(8,128)(2,1)S(1)}, bf16[1,2,192,256]{3,2,1,0:T(8,128)(2,1)S(1)}, u32[]{:S(2)}, u32[]{:S(2)}) %collective-permute-start.5) | collective-permute-done | bytes 196640 | tf_op jit(solution)/shard_map/ppermute | solution.py:378
  57.5 4.8 %collective-permute-done.17 = bf16[1,1,192,256]{3,2,1,0:T(8,128)(2,1)S(1)} collective-permute-done((bf16[1,1,192,256]{3,2,1,0:T(8,128)(2,1)S(1)}, bf16[1,1,192,256]{3,2,1,0:T(8,128)(2,1)S(1)}, u32[]{:S(2)}, u32[]{:S(2)}) %collective-permute-start.17) | collective-permute-done | bytes 98336 | tf_op jit(solution)/shard_map/ppermute | solution.py:378
  62.2 0.1 fusion.6
  62.4 0.2 collective-permute-start.18
  62.6 13.9 %collective-permute-done.18 = bf16[1,2,192,256]{3,2,1,0:T(8,128)(2,1)S(1)} collective-permute-done((bf16[1,2,192,256]{3,2,1,0:T(8,128)(2,1)S(1)}, bf16[1,2,192,256]{3,2,1,0:T(8,128)(2,1)S(1)}, u32[]{:S(2)}, u32[]{:S(2)}) %collective-permute-start.18) | collective-permute-done | bytes 196640 | tf_op jit(solution)/shard_map/ppermute | solution.py:378
  76.6 0.1 collective-permute-start.19
  76.6 0.1 multiply_convert_fusion
  76.7 2.3 %collective-permute-start.6 = (bf16[1,1,192,256]{3,2,1,0:T(8,128)(2,1)S(1)}, bf16[1,1,192,256]{3,2,1,0:T(8,128)(2,1)S(1)}, u32[]{:S(2)}, u32[]{:S(2)}) collective-permute-start(bf16[1,1,192,256]{3,2,1,0:T(8,128)(2,1)S(1)} %multiply_convert_fusion), channel_id=1, source_target_pairs={{0,4},{1,3},{2,6},{3,1},{4,0},{5,7},{6,2},{7,5},{8,12},{9,11},{10,... | collective-permute-start | bytes 294920 | tf_op jit(solution)/shard_map/ppermute | solution.py:378
  79.0 4.4 %collective-permute-done.6 = bf16[1,1,192,256]{3,2,1,0:T(8,128)(2,1)S(1)} collective-permute-done((bf16[1,1,192,256]{3,2,1,0:T(8,128)(2,1)S(1)}, bf16[1,1,192,256]{3,2,1,0:T(8,128)(2,1)S(1)}, u32[]{:S(2)}, u32[]{:S(2)}) %collective-permute-start.6) | collective-permute-done | bytes 98336 | tf_op jit(solution)/shard_map/ppermute | solution.py:378
  83.5 2.3 %collective-permute-start.7 = (bf16[2,1,192,256]{3,2,1,0:T(8,128)(2,1)S(1)}, bf16[2,1,192,256]{3,2,1,0:T(8,128)(2,1)S(1)}, u32[]{:S(2)}, u32[]{:S(2)}) collective-permute-start(bf16[2,1,192,256]{3,2,1,0:T(8,128)(2,1)S(1)} %pad_maximum_fusion.3), channel_id=1, source_target_pairs={{0,2},{1,5},{2,0},{3,7},{4,6},{5,1},{6,4},{7,3},{8,10},{9,13},{10,... | collective-permute-start | bytes 589832 | tf_op jit(solution)/shard_map/ppermute | solution.py:378
  85.8 2.4 %collective-permute-done.19 = bf16[2,2,192,256]{3,2,1,0:T(8,128)(2,1)S(1)} collective-permute-done((bf16[2,2,192,256]{3,2,1,0:T(8,128)(2,1)S(1)}, bf16[2,2,192,256]{3,2,1,0:T(8,128)(2,1)S(1)}, u32[]{:S(2)}, u32[]{:S(2)}) %collective-permute-start.19) | collective-permute-done | bytes 393248 | tf_op jit(solution)/shard_map/ppermute | solution.py:378
  88.2 0.1 pad_maximum_fusion.refs_0_
  88.3 0.1 collective-permute-start.20
  88.4 1.9 %collective-permute-done.7 = bf16[2,1,192,256]{3,2,1,0:T(8,128)(2,1)S(1)} collective-permute-done((bf16[2,1,192,256]{3,2,1,0:T(8,128)(2,1)S(1)}, bf16[2,1,192,256]{3,2,1,0:T(8,128)(2,1)S(1)}, u32[]{:S(2)}, u32[]{:S(2)}) %collective-permute-start.7) | collective-permute-done | bytes 196640 | tf_op jit(solution)/shard_map/ppermute | solution.py:378
  90.3 0.1 collective-permute-start.8
  90.4 0.1 concatenate.24.order_ref
  90.5 1.6 %collective-permute-done.8.refs_1_ = bf16[4,1,192,256]{3,2,1,0:T(8,128)(2,1)S(1)} collective-permute-done((bf16[4,1,192,256]{3,2,1,0:T(8,128)(2,1)S(1)}, bf16[4,1,192,256]{3,2,1,0:T(8,128)(2,1)S(1)}, u32[]{:S(2)}, u32[]{:S(2)}) %collective-permute-start.8) | collective-permute-done | bytes 393248 | tf_op jit(solution)/shard_map/ppermute | solution.py:381
  92.1 2.0 %copy-done.2 = bf16[1,2048,896]{2,1,0:T(8,128)(2,1)S(1)} copy-done((bf16[1,2048,896]{2,1,0:T(8,128)(2,1)S(1)}, bf16[1,2048,896]{2,1,0:T(8,128)(2,1)}, u32[]{:S(2)}) %copy-start.2) | copy-done | bytes 3670040
  94.2 3.0 %full_units.2 = (bf16[48,896]{1,0:T(8,128)(2,1)S(1)}, bf16[48,896]{1,0:T(8,128)(2,1)S(1)}, bf16[48,896]{1,0:T(8,128)(2,1)S(1)}, bf16[48,896]{1,0:T(8,128)(2,1)S(1)}) custom-call(s32[8]{0:T(128)S(1)} %concatenate.24.order_ref, bf16[4,1,192,256]{3,2,1,0:T(8,128)(2,1)S(1)} %pad_maximum_fusion.1.refs_0_, ...), custom_call_target="tpu_custom_call" | custom-call | flops 704643072 | bytes 4456448 | tf_op jit(solution)/shard_map/full_units/pallas_call | solution.py:276
  97.2 1.5 %collective-permute-start.9 = (bf16[48,896]{1,0:T(8,128)(2,1)S(1)}, bf16[48,896]{1,0:T(8,128)(2,1)S(1)}, u32[]{:S(2)}, u32[]{:S(2)}) collective-permute-start(bf16[48,896]{1,0:T(8,128)(2,1)S(1)} %get-tuple-element.34), channel_id=1, source_target_pairs={{0,8},{8,0},{16,24},{24,16},{1,9},{9,1},{17,25},{25,17},{2,10},{10... | collective-permute-start | bytes 258056 | tf_op jit(solution)/shard_map/ppermute | solution.py:402
  98.7 0.9 collective-permute-start.10
  99.7 1.1 collective-permute-start.11
  100.7 5.3 %weight_grads.3 = bf16[1,2048,896]{2,1,0:T(8,128)(2,1)} custom-call(s32[8]{0:T(128)S(1)} %concatenate.24.order_ref, bf16[4,1,192,256]{3,2,1,0:T(8,128)(2,1)S(1)} %pad_maximum_fusion.1.refs_0_, bf16[4,1,192,256]{3,2,1,0:T(8,128)(2,1)S(1)} %collective-permute-done.8.refs_1_, bf16[48,896]{1,0:T(8,128)(2,1)S(1)} %get-tuple-element.37.refs_0_.refs_2_, ...), custom_call_target="tpu_custom_call" | custom-call | flops 704643072 | bytes 4456448 | tf_op jit(solution)/shard_map/weight_grads/pallas_call | solution.py:336
  106.1 1.1 collect.2
  107.2 5.6 %full_units.3 = (bf16[48,896]{1,0:T(8,128)(2,1)S(1)}, bf16[48,896]{1,0:T(8,128)(2,1)S(1)}, bf16[48,896]{1,0:T(8,128)(2,1)S(1)}, bf16[48,896]{1,0:T(8,128)(2,1)S(1)}) custom-call(s32[8]{0:T(128)S(1)} %concatenate.24.order_ref, bf16[4,2,192,256]{3,2,1,0:T(8,128)(2,1)S(1)} %pad_maximum_fusion.refs_0_, ...), custom_call_target="tpu_custom_call" | custom-call | flops 1409286144 | bytes 8912896 | tf_op jit(solution)/shard_map/full_units/pallas_call | solution.py:276
  112.8 1.5 %collective-permute-start.21 = (bf16[48,896]{1,0:T(8,128)(2,1)S(1)}, bf16[48,896]{1,0:T(8,128)(2,1)S(1)}, u32[]{:S(2)}, u32[]{:S(2)}) collective-permute-start(bf16[48,896]{1,0:T(8,128)(2,1)S(1)} %get-tuple-element.44), channel_id=1, source_target_pairs={{0,8},{8,0},{16,24},{24,16},{1,9},{9,1},{17,25},{25,17},{2,10},{10... | collective-permute-start | bytes 258056 | tf_op jit(solution)/shard_map/ppermute | solution.py:402
  114.3 0.9 collective-permute-start.22
  115.2 1.1 collective-permute-start.23
  116.3 6.6 %weight_grads.2 = (bf16[1,896,2048]{2,1,0:T(8,128)(2,1)}, bf16[1,896,2048]{2,1,0:T(8,128)(2,1)}) custom-call(s32[8]{0:T(128)S(1)} %concatenate.24.order_ref, bf16[4,2,192,256]{3,2,1,0:T(8,128)(2,1)S(1)} %pad_maximum_fusion.refs_0_, bf16[4,2,192,256]{3,2,1,0:T(8,128)(2,1)S(1)} %collective-permute-done.20.refs_1_, ...), custom_call_target="tpu_custom_call" | custom-call | flops 1409286144 | bytes 8912896 | tf_op jit(solution)/shard_map/weight_grads/pallas_call | solution.py:336
  122.9 1.1 collect.3
  (39 shorter events, 0.3 us)
Async XLA Ops:
  0.6 0.9 copy-start.9
  1.6 0.7 copy-start.11
  2.6 5.8 %collective-permute-start = (bf16[48,896]{1,0:T(8,128)(2,1)S(1)}, bf16[48,896]{1,0:T(8,128)(2,1)S(1)}, u32[]{:S(2)}, u32[]{:S(2)}) collective-permute-start(bf16[48,896]{1,0:T(8,128)(2,1)S(1)} %get-tuple-element.28), channel_id=1, source_target_pairs={{0,8},{8,0},{16,24},{24,16},{1,9},{9,1},{17,25},{25,17},{2,10},{10... | collective-permute-start | bytes 258056 | tf_op jit(solution)/shard_map/ppermute | solution.py:402
  5.6 5.4 %collective-permute-start.1 = (bf16[48,896]{1,0:T(8,128)(2,1)S(1)}, bf16[48,896]{1,0:T(8,128)(2,1)S(1)}, u32[]{:S(2)}, u32[]{:S(2)}) collective-permute-start(bf16[48,896]{1,0:T(8,128)(2,1)S(1)} %get-tuple-element.29), channel_id=1, source_target_pairs={{0,16},{8,24},{16,0},{24,8},{1,17},{9,25},{17,1},{25,9},{2,18},{10... | collective-permute-start | bytes 258056 | tf_op jit(solution)/shard_map/ppermute | solution.py:402
  7.2 5.4 %collective-permute-start.2 = (bf16[48,896]{1,0:T(8,128)(2,1)S(1)}, bf16[48,896]{1,0:T(8,128)(2,1)S(1)}, u32[]{:S(2)}, u32[]{:S(2)}) collective-permute-start(bf16[48,896]{1,0:T(8,128)(2,1)S(1)} %get-tuple-element.30), channel_id=1, source_target_pairs={{0,24},{8,16},{16,8},{24,0},{1,25},{9,17},{17,9},{25,1},{2,26},{10... | collective-permute-start | bytes 258056 | tf_op jit(solution)/shard_map/ppermute | solution.py:402
  12.5 2.0 %copy-start.3 = (bf16[1,896,2048]{2,1,0:T(8,128)(2,1)S(1)}, bf16[1,896,2048]{2,1,0:T(8,128)(2,1)}, u32[]{:S(2)}) copy-start(bf16[1,896,2048]{2,1,0:T(8,128)(2,1)} %param.10) | copy-start | bytes 11010052
  14.6 2.0 %copy-start.6 = (bf16[1,896,2048]{2,1,0:T(8,128)(2,1)S(1)}, bf16[1,896,2048]{2,1,0:T(8,128)(2,1)}, u32[]{:S(2)}) copy-start(bf16[1,896,2048]{2,1,0:T(8,128)(2,1)} %param.11) | copy-start | bytes 11010052
  16.6 2.8 %copy-start.10 = (bf16[128,896]{1,0:T(8,128)(2,1)S(1)}, bf16[128,896]{1,0:T(8,128)(2,1)}, u32[]{:S(2)}) copy-start(bf16[128,896]{1,0:T(8,128)(2,1)} %refs_1_.1) | copy-start | bytes 688132
  16.6 2.8 %copy-start.12 = (s32[128,1]{0,1:T(1,128)S(1)}, s32[128,1]{0,1:T(1,128)}, u32[]{:S(2)}) copy-start(s32[128,1]{0,1:T(1,128)} %param.9) | copy-start | bytes 1540
  16.6 2.8 %copy-start.13 = (bf16[128,1]{0,1:T(2,128)(2,1)S(1)}, bf16[128,1]{0,1:T(2,128)(2,1)}, u32[]{:S(2)}) copy-start(bf16[128,1]{0,1:T(2,128)(2,1)} %param.8) | copy-start | bytes 772
  19.3 11.7 %collective-permute-start.3 = (bf16[4,2,192,256]{3,2,1,0:T(8,128)(2,1)S(1)}, bf16[4,2,192,256]{3,2,1,0:T(8,128)(2,1)S(1)}, u32[]{:S(2)}, u32[]{:S(2)}) collective-permute-start(bf16[4,2,192,256]{3,2,1,0:T(8,128)(2,1)S(1)} %partial_units.4), channel_id=1, source_target_pairs={{0,1},{1,0},{2,3},{3,2},{4,5},{5,4},{6,7},{7,6},{8,9},{9,8},{10,11... | collective-permute-start | bytes 2359304 | tf_op jit(solution)/shard_map/ppermute | solution.py:381
  19.8 5.4 %collective-permute-start.12 = (bf16[48,896]{1,0:T(8,128)(2,1)S(1)}, bf16[48,896]{1,0:T(8,128)(2,1)S(1)}, u32[]{:S(2)}, u32[]{:S(2)}) collective-permute-start(bf16[48,896]{1,0:T(8,128)(2,1)S(1)} %get-tuple-element.38), channel_id=1, source_target_pairs={{0,8},{8,0},{16,24},{24,16},{1,9},{9,1},{17,25},{25,17},{2,10},{10... | collective-permute-start | bytes 258056 | tf_op jit(solution)/shard_map/ppermute | solution.py:402
  20.4 6.5 %collective-permute-start.13 = (bf16[48,896]{1,0:T(8,128)(2,1)S(1)}, bf16[48,896]{1,0:T(8,128)(2,1)S(1)}, u32[]{:S(2)}, u32[]{:S(2)}) collective-permute-start(bf16[48,896]{1,0:T(8,128)(2,1)S(1)} %get-tuple-element.39), channel_id=1, source_target_pairs={{0,16},{8,24},{16,0},{24,8},{1,17},{9,25},{17,1},{25,9},{2,18},{10... | collective-permute-start | bytes 258056 | tf_op jit(solution)/shard_map/ppermute | solution.py:402
  21.1 5.8 %collective-permute-start.14 = (bf16[48,896]{1,0:T(8,128)(2,1)S(1)}, bf16[48,896]{1,0:T(8,128)(2,1)S(1)}, u32[]{:S(2)}, u32[]{:S(2)}) collective-permute-start(bf16[48,896]{1,0:T(8,128)(2,1)S(1)} %get-tuple-element.40), channel_id=1, source_target_pairs={{0,24},{8,16},{16,8},{24,0},{1,25},{9,17},{17,9},{25,1},{2,26},{10... | collective-permute-start | bytes 258056 | tf_op jit(solution)/shard_map/ppermute | solution.py:402
  26.9 2.0 %copy-start = (bf16[1,2048,896]{2,1,0:T(8,128)(2,1)S(1)}, bf16[1,2048,896]{2,1,0:T(8,128)(2,1)}, u32[]{:S(2)}) copy-start(bf16[1,2048,896]{2,1,0:T(8,128)(2,1)} %param.12) | copy-start | bytes 11010052
  29.0 2.0 %copy-start.4 = (bf16[1,896,2048]{2,1,0:T(8,128)(2,1)S(1)}, bf16[1,896,2048]{2,1,0:T(8,128)(2,1)}, u32[]{:S(2)}) copy-start(bf16[1,896,2048]{2,1,0:T(8,128)(2,1)} %param.10) | copy-start | bytes 11010052
  30.9 8.0 %copy-start.1 = (bf16[1,2048,896]{2,1,0:T(8,128)(2,1)S(1)}, bf16[1,2048,896]{2,1,0:T(8,128)(2,1)}, u32[]{:S(2)}) copy-start(bf16[1,2048,896]{2,1,0:T(8,128)(2,1)} %param.12) | copy-start | bytes 11010052
  30.9 8.0 %collective-permute-start.15 = (bf16[4,1,192,256]{3,2,1,0:T(8,128)(2,1)S(1)}, bf16[4,1,192,256]{3,2,1,0:T(8,128)(2,1)S(1)}, u32[]{:S(2)}, u32[]{:S(2)}) collective-permute-start(bf16[4,1,192,256]{3,2,1,0:T(8,128)(2,1)S(1)} %partial_units.6), channel_id=1, source_target_pairs={{0,1},{1,0},{2,3},{3,2},{4,5},{5,4},{6,7},{7,6},{8,9},{9,8},{10,11... | collective-permute-start | bytes 1179656 | tf_op jit(solution)/shard_map/ppermute | solution.py:381
  31.0 2.2 %copy-start.7 = (bf16[1,896,2048]{2,1,0:T(8,128)(2,1)S(1)}, bf16[1,896,2048]{2,1,0:T(8,128)(2,1)}, u32[]{:S(2)}) copy-start(bf16[1,896,2048]{2,1,0:T(8,128)(2,1)} %param.11) | copy-start | bytes 11010052
  37.3 12.0 %collective-permute-start.4 = (bf16[2,2,192,256]{3,2,1,0:T(8,128)(2,1)S(1)}, bf16[2,2,192,256]{3,2,1,0:T(8,128)(2,1)S(1)}, u32[]{:S(2)}, u32[]{:S(2)}) collective-permute-start(bf16[2,2,192,256]{3,2,1,0:T(8,128)(2,1)S(1)} %get-tuple-element.32), channel_id=1, source_target_pairs={{0,2},{1,5},{2,0},{3,7},{4,6},{5,1},{6,4},{7,3},{8,10},{9,13},{10,... | collective-permute-start | bytes 1179656 | tf_op jit(solution)/shard_map/ppermute | solution.py:378
  41.0 15.0 %collective-permute-start.16 = (bf16[2,1,192,256]{3,2,1,0:T(8,128)(2,1)S(1)}, bf16[2,1,192,256]{3,2,1,0:T(8,128)(2,1)S(1)}, u32[]{:S(2)}, u32[]{:S(2)}) collective-permute-start(bf16[2,1,192,256]{3,2,1,0:T(8,128)(2,1)S(1)} %get-tuple-element.42), channel_id=1, source_target_pairs={{0,2},{1,5},{2,0},{3,7},{4,6},{5,1},{6,4},{7,3},{8,10},{9,13},{10,... | collective-permute-start | bytes 589832 | tf_op jit(solution)/shard_map/ppermute | solution.py:378
  49.4 8.0 %collective-permute-start.5 = (bf16[1,2,192,256]{3,2,1,0:T(8,128)(2,1)S(1)}, bf16[1,2,192,256]{3,2,1,0:T(8,128)(2,1)S(1)}, u32[]{:S(2)}, u32[]{:S(2)}) collective-permute-start(bf16[1,2,192,256]{3,2,1,0:T(8,128)(2,1)S(1)} %slice.38), channel_id=1, source_target_pairs={{0,4},{1,3},{2,6},{3,1},{4,0},{5,7},{6,2},{7,5},{8,12},{9,11},{10,... | collective-permute-start | bytes 589832 | tf_op jit(solution)/shard_map/ppermute | solution.py:378
  56.0 6.2 %collective-permute-start.17 = (bf16[1,1,192,256]{3,2,1,0:T(8,128)(2,1)S(1)}, bf16[1,1,192,256]{3,2,1,0:T(8,128)(2,1)S(1)}, u32[]{:S(2)}, u32[]{:S(2)}) collective-permute-start(bf16[1,1,192,256]{3,2,1,0:T(8,128)(2,1)S(1)} %slice.39), channel_id=1, source_target_pairs={{0,4},{1,3},{2,6},{3,1},{4,0},{5,7},{6,2},{7,5},{8,12},{9,11},{10,... | collective-permute-start | bytes 294920 | tf_op jit(solution)/shard_map/ppermute | solution.py:378
  62.4 14.2 %collective-permute-start.18 = (bf16[1,2,192,256]{3,2,1,0:T(8,128)(2,1)S(1)}, bf16[1,2,192,256]{3,2,1,0:T(8,128)(2,1)S(1)}, u32[]{:S(2)}, u32[]{:S(2)}) collective-permute-start(bf16[1,2,192,256]{3,2,1,0:T(8,128)(2,1)S(1)} %maximum_bitcast_fusion), channel_id=1, source_target_pairs={{0,4},{1,3},{2,6},{3,1},{4,0},{5,7},{6,2},{7,5},{8,12},{9,11},{10,... | collective-permute-start | bytes 589832 | tf_op jit(solution)/shard_map/ppermute | solution.py:378
  76.6 11.6 %collective-permute-start.19 = (bf16[2,2,192,256]{3,2,1,0:T(8,128)(2,1)S(1)}, bf16[2,2,192,256]{3,2,1,0:T(8,128)(2,1)S(1)}, u32[]{:S(2)}, u32[]{:S(2)}) collective-permute-start(bf16[2,2,192,256]{3,2,1,0:T(8,128)(2,1)S(1)} %pad_maximum_fusion.2), channel_id=1, source_target_pairs={{0,2},{1,5},{2,0},{3,7},{4,6},{5,1},{6,4},{7,3},{8,10},{9,13},{10,... | collective-permute-start | bytes 1179656 | tf_op jit(solution)/shard_map/ppermute | solution.py:378
  76.7 6.7 %collective-permute-start.6 = (bf16[1,1,192,256]{3,2,1,0:T(8,128)(2,1)S(1)}, bf16[1,1,192,256]{3,2,1,0:T(8,128)(2,1)S(1)}, u32[]{:S(2)}, u32[]{:S(2)}) collective-permute-start(bf16[1,1,192,256]{3,2,1,0:T(8,128)(2,1)S(1)} %multiply_convert_fusion), channel_id=1, source_target_pairs={{0,4},{1,3},{2,6},{3,1},{4,0},{5,7},{6,2},{7,5},{8,12},{9,11},{10,... | collective-permute-start | bytes 294920 | tf_op jit(solution)/shard_map/ppermute | solution.py:378
  83.5 6.8 %collective-permute-start.7 = (bf16[2,1,192,256]{3,2,1,0:T(8,128)(2,1)S(1)}, bf16[2,1,192,256]{3,2,1,0:T(8,128)(2,1)S(1)}, u32[]{:S(2)}, u32[]{:S(2)}) collective-permute-start(bf16[2,1,192,256]{3,2,1,0:T(8,128)(2,1)S(1)} %pad_maximum_fusion.3), channel_id=1, source_target_pairs={{0,2},{1,5},{2,0},{3,7},{4,6},{5,1},{6,4},{7,3},{8,10},{9,13},{10,... | collective-permute-start | bytes 589832 | tf_op jit(solution)/shard_map/ppermute | solution.py:378
  88.3 18.9 %collective-permute-start.20 = (bf16[4,2,192,256]{3,2,1,0:T(8,128)(2,1)S(1)}, bf16[4,2,192,256]{3,2,1,0:T(8,128)(2,1)S(1)}, u32[]{:S(2)}, u32[]{:S(2)}) collective-permute-start(bf16[4,2,192,256]{3,2,1,0:T(8,128)(2,1)S(1)} %pad_maximum_fusion.refs_0_), channel_id=1, source_target_pairs={{0,1},{1,0},{2,3},{3,2},{4,5},{5,4},{6,7},{7,6},{8,9},{9,8},{10,11... | collective-permute-start | bytes 2359304 | tf_op jit(solution)/shard_map/ppermute | solution.py:381
  90.3 1.8 %collective-permute-start.8 = (bf16[4,1,192,256]{3,2,1,0:T(8,128)(2,1)S(1)}, bf16[4,1,192,256]{3,2,1,0:T(8,128)(2,1)S(1)}, u32[]{:S(2)}, u32[]{:S(2)}) collective-permute-start(bf16[4,1,192,256]{3,2,1,0:T(8,128)(2,1)S(1)} %pad_maximum_fusion.1.refs_0_), channel_id=1, source_target_pairs={{0,1},{1,0},{2,3},{3,2},{4,5},{5,4},{6,7},{7,6},{8,9},{9,8},{10,11... | collective-permute-start | bytes 1179656 | tf_op jit(solution)/shard_map/ppermute | solution.py:381
  92.1 2.0 %copy-start.2 = (bf16[1,2048,896]{2,1,0:T(8,128)(2,1)S(1)}, bf16[1,2048,896]{2,1,0:T(8,128)(2,1)}, u32[]{:S(2)}) copy-start(bf16[1,2048,896]{2,1,0:T(8,128)(2,1)} %param.12) | copy-start | bytes 11010052
  94.2 13.0 %copy-start.8 = (bf16[1,896,2048]{2,1,0:T(8,128)(2,1)S(1)}, bf16[1,896,2048]{2,1,0:T(8,128)(2,1)}, u32[]{:S(2)}) copy-start(bf16[1,896,2048]{2,1,0:T(8,128)(2,1)} %param.11) | copy-start | bytes 11010052
  97.2 10.0 %copy-start.5 = (bf16[1,896,2048]{2,1,0:T(8,128)(2,1)S(1)}, bf16[1,896,2048]{2,1,0:T(8,128)(2,1)}, u32[]{:S(2)}) copy-start(bf16[1,896,2048]{2,1,0:T(8,128)(2,1)} %param.10) | copy-start | bytes 11010052
  97.2 8.9 %collective-permute-start.9 = (bf16[48,896]{1,0:T(8,128)(2,1)S(1)}, bf16[48,896]{1,0:T(8,128)(2,1)S(1)}, u32[]{:S(2)}, u32[]{:S(2)}) collective-permute-start(bf16[48,896]{1,0:T(8,128)(2,1)S(1)} %get-tuple-element.34), channel_id=1, source_target_pairs={{0,8},{8,0},{16,24},{24,16},{1,9},{9,1},{17,25},{25,17},{2,10},{10... | collective-permute-start | bytes 258056 | tf_op jit(solution)/shard_map/ppermute | solution.py:402
  98.7 7.3 %collective-permute-start.10 = (bf16[48,896]{1,0:T(8,128)(2,1)S(1)}, bf16[48,896]{1,0:T(8,128)(2,1)S(1)}, u32[]{:S(2)}, u32[]{:S(2)}) collective-permute-start(bf16[48,896]{1,0:T(8,128)(2,1)S(1)} %get-tuple-element.35), channel_id=1, source_target_pairs={{0,16},{8,24},{16,0},{24,8},{1,17},{9,25},{17,1},{25,9},{2,18},{10... | collective-permute-start | bytes 258056 | tf_op jit(solution)/shard_map/ppermute | solution.py:402
  99.7 6.4 %collective-permute-start.11 = (bf16[48,896]{1,0:T(8,128)(2,1)S(1)}, bf16[48,896]{1,0:T(8,128)(2,1)S(1)}, u32[]{:S(2)}, u32[]{:S(2)}) collective-permute-start(bf16[48,896]{1,0:T(8,128)(2,1)S(1)} %get-tuple-element.36), channel_id=1, source_target_pairs={{0,24},{8,16},{16,8},{24,0},{1,25},{9,17},{17,9},{25,1},{2,26},{10... | collective-permute-start | bytes 258056 | tf_op jit(solution)/shard_map/ppermute | solution.py:402
  112.8 10.2 %collective-permute-start.21 = (bf16[48,896]{1,0:T(8,128)(2,1)S(1)}, bf16[48,896]{1,0:T(8,128)(2,1)S(1)}, u32[]{:S(2)}, u32[]{:S(2)}) collective-permute-start(bf16[48,896]{1,0:T(8,128)(2,1)S(1)} %get-tuple-element.44), channel_id=1, source_target_pairs={{0,8},{8,0},{16,24},{24,16},{1,9},{9,1},{17,25},{25,17},{2,10},{10... | collective-permute-start | bytes 258056 | tf_op jit(solution)/shard_map/ppermute | solution.py:402
  114.3 8.6 %collective-permute-start.22 = (bf16[48,896]{1,0:T(8,128)(2,1)S(1)}, bf16[48,896]{1,0:T(8,128)(2,1)S(1)}, u32[]{:S(2)}, u32[]{:S(2)}) collective-permute-start(bf16[48,896]{1,0:T(8,128)(2,1)S(1)} %get-tuple-element.45), channel_id=1, source_target_pairs={{0,16},{8,24},{16,0},{24,8},{1,17},{9,25},{17,1},{25,9},{2,18},{10... | collective-permute-start | bytes 258056 | tf_op jit(solution)/shard_map/ppermute | solution.py:402
  115.2 7.7 %collective-permute-start.23 = (bf16[48,896]{1,0:T(8,128)(2,1)S(1)}, bf16[48,896]{1,0:T(8,128)(2,1)S(1)}, u32[]{:S(2)}, u32[]{:S(2)}) collective-permute-start(bf16[48,896]{1,0:T(8,128)(2,1)S(1)} %get-tuple-element.46), channel_id=1, source_target_pairs={{0,24},{8,16},{16,8},{24,0},{1,25},{9,17},{17,9},{25,1},{2,26},{10... | collective-permute-start | bytes 258056 | tf_op jit(solution)/shard_map/ppermute | solution.py:402

commit v2 on v0

v2 whole, which is shorter than its diff:
```python
import functools

import jax
import jax.numpy as jnp
from jax import lax
from jax.experimental import pallas as pl
from jax.experimental.pallas import tpu as pltpu
from jax.sharding import PartitionSpec as P

F32 = jnp.float32
BF16 = jnp.bfloat16


def spread_units(function):
    return lax.psum_scatter(function(), "tensor", scatter_dimension=0, tiled=True)


def general(tokens, gate_weights, expert_ids, w_gate, w_up, w_down, grad_out):
    members = lax.axis_size("expert")
    tok_rows = tokens.shape[0]
    routes = expert_ids.shape[1]
    width = tokens.shape[1]
    slot = 3 * routes * tok_rows // (2 * members)
    total = members * slot
    flat_ids = expert_ids.reshape(-1)
    counted = (flat_ids[:, None] == jnp.arange(members, dtype=jnp.int32)[None, :]).astype(jnp.int32)
    ranks = jnp.cumsum(counted, axis=0) - 1
    position = jnp.sum(counted * ranks, axis=1)
    target = (flat_ids * slot + position).reshape(tok_rows, routes)
    matched = target[None, :, :] == jnp.arange(total, dtype=jnp.int32)[:, None, None]
    place = jnp.sum(matched.astype(F32), axis=2).astype(BF16)
    weighted = jnp.sum(jnp.where(matched, gate_weights.astype(F32)[None], 0.0), axis=2).astype(BF16)
    x_slots = jnp.dot(place, tokens, preferred_element_type=F32).astype(BF16)
    dy_slots = jnp.dot(weighted, grad_out, preferred_element_type=F32).astype(BF16)
    outgoing = jnp.stack(
        [x_slots.reshape(members, slot, width), dy_slots.reshape(members, slot, width)], axis=1
    )
    arrived = lax.all_to_all(outgoing, "expert", split_axis=0, concat_axis=0, tiled=True)
    x_rows = arrived[:, 0].reshape(total, width)
    dy_rows = arrived[:, 1].reshape(total, width)
    weight_gate, weight_up, weight_down = w_gate[0], w_up[0], w_down[0]
    dot = functools.partial(lax.dot_general, preferred_element_type=F32)

    def gate_terms():
        return jnp.concatenate(
            [dot(w, x_rows, (((0,), (1,)), ((), ()))) for w in (weight_gate, weight_up)], axis=1
        )

    summed = spread_units(gate_terms)
    gate_t, up_t = summed[:, :total], summed[:, total:]
    sigma = jax.nn.sigmoid(gate_t)
    active = gate_t * sigma
    hidden_t = (active * up_t).astype(BF16)
    hidden = lax.all_gather(hidden_t, "tensor", axis=0, tiled=True)
    out_rows = dot(hidden, weight_down, (((0,), (0,)), ((), ()))).astype(BF16)
    swap = functools.partial(
        lax.all_to_all, axis_name="expert", split_axis=0, concat_axis=0, tiled=True
    )
    out_back = swap(out_rows.reshape(members, slot, width))
    d_hidden = spread_units(lambda: dot(weight_down, dy_rows, (((1,), (1,)), ((), ()))))
    d_gate_t = (d_hidden * up_t * sigma * (1.0 + gate_t * (1.0 - sigma))).astype(BF16)
    d_up_t = (d_hidden * active).astype(BF16)
    d_gate = lax.all_gather(d_gate_t, "tensor", axis=0, tiled=True)
    d_up = lax.all_gather(d_up_t, "tensor", axis=0, tiled=True)
    back_rows = (
        dot(d_gate, weight_gate, (((0,), (1,)), ((), ())))
        + dot(d_up, weight_up, (((0,), (1,)), ((), ())))
    ).astype(BF16)
    grad_w_gate = dot(x_rows, d_gate, (((0,), (1,)), ((), ()))).astype(BF16)[None]
    grad_w_up = dot(x_rows, d_up, (((0,), (1,)), ((), ()))).astype(BF16)[None]
    grad_w_down = dot(hidden, dy_rows, (((1,), (0,)), ((), ()))).astype(BF16)[None]
    grad_back = swap(back_rows.reshape(members, slot, width))
    mixed = dot(weighted, out_back.reshape(total, width), (((0,), (0,)), ((), ()))).astype(BF16)
    grad_tokens = dot(place, grad_back.reshape(total, width), (((0,), (0,)), ((), ()))).astype(BF16)
    return (mixed, grad_tokens, grad_w_gate, grad_w_up, grad_w_down)


NT = (((1,), (1,)), ((), ()))
TN = (((0,), (0,)), ((), ()))
NN = (((1,), (0,)), ((), ()))
VMEM = pl.BlockSpec(memory_space=pltpu.VMEM)
SMEM = pl.BlockSpec(memory_space=pltpu.SMEM)
ANY = pl.BlockSpec(memory_space=pl.ANY)


def mm(a, b, dims=NN):
    return lax.dot_general(a, b, dims, preferred_element_type=F32)


def spec(shape, dtype=BF16):
    return jax.ShapeDtypeStruct(shape, dtype)


def call(name, kernel, outs, out_specs, ins, in_specs, scratch=(), after=(), flops=0, mib=16):
    late = len(after)

    def body(*refs):
        kernel(*refs[: len(ins)], *refs[len(ins) + late :])

    moved = sum(x.size * x.dtype.itemsize for x in (*ins, *outs))
    return pl.pallas_call(
        body,
        out_shape=list(outs),
        in_specs=list(in_specs) + [ANY] * late,
        out_specs=list(out_specs),
        scratch_shapes=list(scratch),
        compiler_params=pltpu.CompilerParams(vmem_limit_bytes=mib * 2**20),
        cost_estimate=pl.CostEstimate(flops=int(flops), bytes_accessed=int(moved), transcendentals=0),
        name=name,
    )(*ins, *after)


def placement(ids, here, members, slot, total):
    count = ids.shape[1]
    lanes = lax.broadcasted_iota(jnp.int32, (max(members, 8), count), 0)
    chosen = (lanes == ids).astype(F32)
    before = lax.broadcasted_iota(jnp.int32, (count, count), 0) < lax.broadcasted_iota(
        jnp.int32, (count, count), 1
    )
    ranks = mm(chosen.astype(BF16), before.astype(F32).astype(BF16))
    rank = jnp.sum(chosen * ranks, axis=0, keepdims=True).astype(jnp.int32)
    target = (ids ^ here) * slot + rank
    return lax.broadcasted_iota(jnp.int32, (total, count), 0) == target


def dispatch(ids, here, data, gates, members, slot, after=()):
    total, width, count = members * slot, data.shape[1], data.shape[0]
    gated = gates is not None
    small = [ids] + ([gates] if gated else [])

    def kernel(here_ref, *refs):
        sources = refs[: len(small) + 1]
        out_refs = refs[len(small) + 1 :][:members]
        held, sems = refs[len(small) + 1 + members : -1], refs[-1]
        copies = [
            pltpu.make_async_copy(s, h, sems.at[i]) for i, (s, h) in enumerate(zip(sources, held))
        ]
        for copy in copies:
            copy.start()
        for copy in copies[:-1]:
            copy.wait()
        mask = placement(held[0][...], here_ref[0], members, slot, total)
        value = held[1][...].astype(F32) if gated else 1.0
        pick = jnp.where(mask, value, 0.0).astype(BF16)
        copies[-1].wait()
        rows = mm(pick, held[-1][...]).astype(BF16)
        for m, ref in enumerate(out_refs):
            ref[...] = rows[m * slot : (m + 1) * slot]

    ins = [*small, data]
    return call(
        "dispatch",
        kernel,
        [spec((slot, width))] * members,
        [VMEM] * members,
        [here, *ins],
        [SMEM] + [ANY] * len(ins),
        [pltpu.VMEM(x.shape, x.dtype) for x in ins] + [pltpu.SemaphoreType.DMA((len(ins),))],
        after,
        2 * total * count * width,
    )


def collect(ids, here, rows, gates, members, slot, after=()):
    total, width, count = members * slot, rows[0].shape[1], ids.shape[1]
    gated = gates is not None
    small = [ids] + ([gates] if gated else [])

    def kernel(here_ref, *refs):
        row_refs = refs[len(small) : len(small) + members]
        out_ref, joined = refs[-2], refs[-1]
        for m, ref in enumerate(row_refs):
            joined[m * slot : (m + 1) * slot, :] = ref[...]
        mask = placement(refs[0][...], here_ref[0], members, slot, total)
        value = refs[1][...].astype(F32) if gated else 1.0
        pick = jnp.where(mask, value, 0.0).astype(BF16)
        out_ref[...] = mm(pick, joined[...], TN).astype(BF16)

    return call(
        "collect",
        kernel,
        [spec((count, width))],
        [VMEM],
        [here, *small, *rows],
        [SMEM] + [VMEM] * (len(small) + members),
        [pltpu.VMEM((total, width), BF16)],
        after,
        2 * count * total * width,
    )[0]


def load(arrays, after=()):
    def kernel(*refs):
        n = len(arrays)
        copies = [
            pltpu.make_async_copy(refs[i], refs[n + i], refs[-1].at[i]) for i in range(n)
        ]
        for copy in copies:
            copy.start()
        for copy in copies:
            copy.wait()

    return call(
        "load",
        kernel,
        [spec(x.shape, x.dtype) for x in arrays],
        [VMEM] * len(arrays),
        arrays,
        [ANY] * len(arrays),
        [pltpu.SemaphoreType.DMA((len(arrays),))],
        after,
    )


def block_of(ref, index, unit, axis):
    at = pl.ds(pl.multiple_of(index * unit, unit), unit)
    return ref[at, :] if axis == 0 else ref[:, at]


def away_terms(ids, rows, weights, unit, down, after=()):
    members, (slot, width) = len(rows), rows[0].shape
    total, n, blocks = members * slot, len(weights), ids.shape[0]

    def kernel(ids_ref, *refs):
        row_refs, w_refs = refs[:members], refs[members : members + n]
        out_ref, joined = refs[-2:]
        for m, ref in enumerate(row_refs):
            joined[m * slot : (m + 1) * slot, :] = ref[...]
        x = joined[...]
        for j in range(blocks):
            for i, w_ref in enumerate(w_refs):
                w = block_of(w_ref, ids_ref[j], unit, 0 if down else 1)
                out_ref[j, i] = mm(x, w, NT if down else NN).astype(BF16)

    return call(
        "away_terms",
        kernel,
        [spec((blocks, n, total, unit)), spec((total, width))],
        [VMEM] * 2,
        [ids, *rows, *weights],
        [SMEM] + [VMEM] * (members + n),
        (),
        after,
        2 * n * blocks * total * width * unit,
    )


def kept_terms(ids, joined, weights, arrived, unit, down, after=()):
    (total, width), n, blocks = joined.shape, len(weights), ids.shape[0]
    first = blocks // 2

    def kernel(ids_ref, x_ref, *refs):
        w_refs, (got, send, keep) = refs[:n], refs[n:]
        x = x_ref[...]
        for j in (*range(first, blocks), *range(first)):
            for i, w_ref in enumerate(w_refs):
                w = block_of(w_ref, ids_ref[j], unit, 0 if down else 1)
                term = mm(x, w, NT if down else NN) + got[j, i].astype(F32)
                if j >= first:
                    send[j - first, i] = term.astype(BF16)
                else:
                    keep[j, i] = term

    return call(
        "kept_terms",
        kernel,
        [spec((blocks - first, n, total, unit)), spec((first, n, total, unit), F32)],
        [VMEM] * 2,
        [ids, joined, *weights, arrived],
        [SMEM] + [VMEM] * (2 + n),
        (),
        after,
        2 * n * blocks * total * width * unit,
    )


def unit_rows(pieces, weights, unit, down, before=None, split=None, after=()):
    ids = [p[0] for p in pieces]
    units = [p[1] for p in pieces]
    n, total = units[0].shape[1], units[0].shape[2]
    width = weights[0].shape[1] if down else weights[0].shape[0]
    blocks = sum(u.shape[0] for u in units)
    started = [] if before is None else [before]
    k = len(pieces)

    def kernel(*refs):
        id_refs, u_refs, w_refs = refs[:k], refs[k : 2 * k], refs[2 * k : 2 * k + n]
        acc = refs[-1]
        start_refs = refs[2 * k + n : 2 * k + n + len(started)]
        out_refs = refs[2 * k + n + len(started) : -1]
        acc[...] = start_refs[0][...] if started else jnp.zeros_like(acc)
        for id_ref, u_ref in zip(id_refs, u_refs):
            for j in range(u_ref.shape[0]):
                term = None
                for i, w_ref in enumerate(w_refs):
                    w = block_of(w_ref, id_ref[j], unit, 0 if down else 1)
                    more = mm(u_ref[j, i], w, NN if down else NT)
                    term = more if term is None else term + more
                acc[...] += term
        if split is None:
            out_refs[0][...] = acc[...]
        else:
            for m, ref in enumerate(out_refs):
                ref[...] = acc[m * split : (m + 1) * split, :].astype(BF16)

    if split is None:
        outs = [spec((total, width), F32)]
    else:
        outs = [spec((split, width))] * (total // split)
    return call(
        "unit_rows",
        kernel,
        outs,
        [VMEM] * len(outs),
        [*ids, *units, *weights, *started],
        [SMEM] * k + [VMEM] * (k + n + len(started)),
        [pltpu.VMEM((total, width), F32)],
        after,
        2 * n * blocks * total * width * unit,
    )


def weight_grads(pieces, joined, unit, down, after=()):
    (total, width), k = joined.shape, len(pieces)
    ids = [p[0] for p in pieces]
    parts = len(pieces[0][1])
    units = [u for p in pieces for u in p[1]]
    n = units[0].shape[1]
    blocks = sum(p[1][0].shape[0] for p in pieces)
    shape = (1, blocks * unit, width) if down else (1, width, blocks * unit)

    def kernel(*refs):
        id_refs, u_refs, x_ref = refs[:k], refs[k : k + k * parts], refs[k + k * parts]
        out_refs = refs[k + k * parts + 1 :][:n]
        turned, rows, held, sems = refs[-4:]
        if not down:
            turned[...] = x_ref[...].T
        waits, step = [None, None], 0
        for p in range(k):
            for j in range(pieces[p][1][0].shape[0]):
                at = pl.ds(pl.multiple_of(id_refs[p][j] * unit, unit), unit)
                for i in range(n):
                    slot = step % 2
                    step += 1
                    if parts == 1:
                        u = u_refs[p][j, i]
                    else:
                        top = 0
                        for ref in u_refs[p * parts : (p + 1) * parts]:
                            rows[top : top + ref.shape[2], :] = ref[j, i]
                            top += ref.shape[2]
                        u = rows[...]
                    if waits[slot] is not None:
                        waits[slot].wait()
                    if down:
                        held[slot] = mm(u, x_ref[...], TN).astype(BF16)
                        target = out_refs[i].at[0, at, :]
                    else:
                        held[slot] = mm(turned[...], u).astype(BF16)
                        target = out_refs[i].at[0, :, at]
                    waits[slot] = pltpu.make_async_copy(held.at[slot], target, sems.at[slot])
                    waits[slot].start()
        for wait in waits:
            wait.wait()

    return call(
        "weight_grads",
        kernel,
        [spec(shape)] * n,
        [ANY] * n,
        [*ids, *units, joined],
        [SMEM] * k + [VMEM] * (k * parts + 1),
        [
            pltpu.VMEM((width, total), BF16),
            pltpu.VMEM((total, unit), BF16),
            pltpu.VMEM((2, unit, width) if down else (2, width, unit), BF16),
            pltpu.SemaphoreType.DMA((2,)),
        ],
        after,
        2 * n * blocks * total * width * unit,
    )


def hypercube(tokens, gate_weights, expert_ids, w_gate, w_up, w_down, grad_out):
    members = lax.axis_size("expert")
    parts = lax.axis_size("tensor")
    bits = (parts // 2).bit_length() - 1
    count = tokens.shape[0]
    slot = 3 * count // (2 * members)
    unit = w_gate.shape[2] // parts
    half = parts // 2

    here = lax.axis_index("expert").reshape(1)
    ids = expert_ids.reshape(1, count)
    gates = gate_weights.reshape(1, count)

    t = lax.axis_index("tensor")
    core, chip = t & 1, t >> 1
    orders = (tuple(range(bits)), tuple(reversed(range(bits))))

    def pairs(step):
        return [(d, d ^ (2 << orders[d % 2][step])) for d in range(parts)]

    def step_swap(x, step):
        return lax.ppermute(x, "tensor", pairs(step))

    def core_swap(x):
        return lax.ppermute(x, "tensor", [(d, d ^ 1) for d in range(parts)])

    def block_ids(c):
        rel = jnp.arange(half, dtype=jnp.int32)
        place = [jnp.zeros_like(rel), jnp.zeros_like(rel)]
        for k in range(2):
            for step in range(bits):
                bit = (chip >> orders[k][step]) & 1
                flip = (rel >> (bits - 1 - step)) & 1
                place[k] = place[k] * 2 + (bit ^ flip)
        return half * c + jnp.where(c == 0, place[0], place[1])

    mine, other = block_ids(core), block_ids(1 - core)

    def expert_swap(rows, skipped=1):
        return [
            lax.ppermute(rows[m - skipped], "expert", [(d, d ^ m) for d in range(members)])
            for m in range(1, members)
        ]

    def halve(send, keep):
        size = send.shape[0]
        for step in range(bits):
            got = step_swap(send, step)
            total = keep + got.astype(F32)
            size //= 2
            if step < bits - 1:
                send, keep = total[size:].astype(BF16), total[:size]
        return total[0]

    def gather_units(x):
        firsts = []
        for step in reversed(range(bits)):
            got = step_swap(x, step)
            firsts.append(got)
            x = jnp.concatenate([x, got], axis=0)
        return x, core_swap(x), firsts[0]

    def later(x, *others):
        return lax.optimization_barrier((x, *others))[0]

    x_slots = dispatch(ids, here, tokens, None, members, slot)
    x_rows = [x_slots[0]] + expert_swap(x_slots, 0)
    weight_gate, weight_up = load((w_gate[0], w_up[0]), (x_slots[1],))
    dy_slots = dispatch(ids, here, grad_out, gates, members, slot, (weight_gate,))
    dy_rows = [dy_slots[0]] + expert_swap(dy_slots, 0)

    away, x_all = away_terms(other, x_rows, (weight_gate, weight_up), unit, False, (dy_slots[1],))
    (weight_down,) = load((w_down[0],), (away,))
    send, keep = kept_terms(
        mine, x_all, (weight_gate, weight_up), core_swap(away), unit, False, (weight_down,)
    )
    away, dy_all = away_terms(other, dy_rows, (weight_down,), unit, True, (send,))
    gate, up = halve(send, keep)
    send, keep = kept_terms(mine, dy_all, (weight_down,), core_swap(away), unit, True)
    (d_hidden,) = halve(send, keep)

    sigma = jax.nn.sigmoid(gate)
    active = gate * sigma
    hidden = (active * up).astype(BF16)
    d_gate = (d_hidden * up * sigma * (1.0 + gate * (1.0 - sigma))).astype(BF16)
    d_up = (d_hidden * active).astype(BF16)
    d_far = jnp.stack([d_gate[slot:], d_up[slot:]])[None]
    d_own = jnp.stack([d_gate[:slot], d_up[:slot]])[None]

    hidden_mine, hidden_other, _ = gather_units(hidden[None, None])
    far_mine, far_other, first = gather_units(d_far)
    own_mine, own_other, _ = gather_units(later(d_own, first))

    hidden_pieces = ((mine, hidden_mine), (other, hidden_other))
    out = unit_rows(hidden_pieces, (weight_down,), unit, True, split=slot)
    out_back = expert_swap(out, 0)
    (grad_w_down,) = weight_grads(
        [(i, (u,)) for i, u in hidden_pieces], dy_all, unit, True, (out[0],)
    )

    gate_up = (weight_gate, weight_up)
    (back,) = unit_rows(((mine, far_mine),), gate_up, unit, False, after=(grad_w_down,))
    far = unit_rows(((other, far_other),), gate_up, unit, False, back, slot)
    grad_back = expert_swap(far, 1)
    (own,) = unit_rows(
        ((mine, own_mine), (other, own_other)), gate_up, unit, False, None, slot, (far[0],)
    )
    grad_w_gate, grad_w_up = weight_grads(
        ((mine, (own_mine, far_mine)), (other, (own_other, far_other))), x_all, unit, False, (own,)
    )

    mixed = collect(ids, here, [out[0]] + out_back, gates, members, slot)
    grad_tokens = collect(ids, here, [own] + grad_back, None, members, slot)
    return (mixed, grad_tokens, grad_w_gate, grad_w_up, grad_w_down)


def power_of_two(n):
    return n & (n - 1) == 0


def solution(mesh):
    members, parts = mesh.shape["expert"], mesh.shape["tensor"]

    def local(*args):
        unit = args[3].shape[2] // parts
        slot = 3 * args[0].shape[0] // (2 * members)
        fits = power_of_two(members) and power_of_two(parts) and parts >= 4
        fits = fits and unit % 128 == 0 and slot % 16 == 0 and args[0].shape[1] % 128 == 0
        fits = fits and args[2].shape[1] == 1
        return (hypercube if fits else general)(*args)

    in_specs = (
        P("expert", "tensor"),
        P("expert", None),
        P("expert", None),
        P("expert", "tensor", None),
        P("expert", "tensor", None),
        P("expert", None, "tensor"),
        P("expert", "tensor"),
    )
    out_specs = (
        P("expert", "tensor"),
        P("expert", "tensor"),
        P("expert", "tensor", None),
        P("expert", "tensor", None),
        P("expert", None, "tensor"),
    )
    return jax.shard_map(local, mesh=mesh, in_specs=in_specs, out_specs=out_specs, check_vma=False)
```

time: 192 us -> 115 us (0.60)
  blocking collectives: 63 us -> 0 us
  waiting for transfers between devices: 71.9 us -> 27.9 us
  Pallas kernels: 0 us -> 33.3 us
  starting transfers between devices: 7.81 us -> 38.2 us
  matrix products: 28.5 us -> 0 us
  local copies, waits for them, and re-layouts: 0.08 us -> 13.4 us
  between operations: 14.2 us -> 1.07 us
  other arithmetic: 6.05 us -> 0.58 us
    reduce_scatter x2 -> x0, waiting for transfers between devices: 69.2 us -> none  [spread_units(): lax.psum_scatter(function(jnp.int32(0), share * lax.axis_size('tensor')),...]
    all_gather x3 -> x0, blocking collectives: 47.4 us -> none  [the longest x1 16.3 us: local(): lax.all_gather(d_up_t, 'tensor', axis=0, tiled=True)]
    ppermute x0 -> x27, starting transfers between devices: none -> 38.2 us  [the longest x10 22.2 us: step_swap(): return lax.ppermute(x, 'tensor', pairs(step))]
    pallas_call x0 -> x16, Pallas kernels: none -> 33.3 us  [call(): pl.pallas_call(body, out_shape=list(outs), in_specs=list(in_specs) + [ANY...]
    dot_general x13 -> x0, matrix products: 28.5 us -> none  [the longest x1 3.8 us: local(): lax.dot_general(hidden_full, weight_down, (((0,), (0,)), ((), ())), prefe...]
    ppermute x0 -> x27, waiting for transfers between devices: none -> 27.9 us  [the longest x10 27.9 us: step_swap(): return lax.ppermute(x, 'tensor', pairs(step))]
    all_to_all x1 -> x0, blocking collectives: 15.5 us -> none  [local(): lax.all_to_all(outgoing, 'expert', split_axis=0, concat_axis=0, tiled=True)]
    unnamed x10 -> x28, local copies, waits for them, and re-layouts: 0.03 us -> 13.3 us
  transfers between devices with their start and end apart: 4 -> 27, of which waited for: 3 -> 7; matrix products, arithmetic and copies ran while one was open for 10% -> 1% of each run, Pallas kernels for 0% -> 25%
where the time goes in v2:
time: 115 us
  starting transfers between devices  38.2 us (33%)
  Pallas kernels  33.3 us (29%)
  waiting for transfers between devices  27.9 us (24%)
  local copies, waits for them, and re-layouts  13.4 us (12%)
    pallas_call x16, Pallas kernels, call(): pl.pallas_call(body, out_shape=list(outs), in_specs=list(in_specs) + [ANY...  33.3 us
    ppermute x10, waiting for transfers between devices, step_swap(): return lax.ppermute(x, 'tensor', pairs(step))  27.9 us
    ppermute x10, starting transfers between devices, step_swap(): return lax.ppermute(x, 'tensor', pairs(step))  22.2 us
    ppermute x12, starting transfers between devices, expert_swap(): lax.ppermute(rows[m - skipped], 'expert', [(d, d ^ m) for d in range(memb...  15.7 us
    unnamed x28, local copies, waits for them, and re-layouts  13.3 us
  transfers between devices with their start and end apart: 27, of which 7 were waited for; matrix products, arithmetic and copies ran while one was open for 1% of the time, Pallas kernels for 25%

profile of v2, /device:TPU:0, one launch (start us, length us, event | category | flops | bytes accessed | tf_op | source)
XLA Modules:
  0.0 114.5 jit_solution(16947457718246713823)
XLA Ops:
  0.6 0.9 copy-done.8
  1.6 0.7 copy-done.10
  2.2 0.7 dispatch.2
  2.9 3.1 %collective-permute-start.1 = (bf16[48,896]{1,0:T(8,128)(2,1)S(1)}, bf16[48,896]{1,0:T(8,128)(2,1)S(1)}, u32[]{:S(2)}, u32[]{:S(2)}) collective-permute-start(bf16[48,896]{1,0:T(8,128)(2,1)S(1)} %get-tuple-element.35), channel_id=1, source_target_pairs={{0,16},{8,24},{16,0},{24,8},{1,17},{9,25},{17,1},{25,9},{2,18},{10... | collective-permute-start | bytes 258056 | tf_op jit(solution)/shard_map/ppermute | solution.py:424
  6.0 1.4 %collective-permute-start.2 = (bf16[48,896]{1,0:T(8,128)(2,1)S(1)}, bf16[48,896]{1,0:T(8,128)(2,1)S(1)}, u32[]{:S(2)}, u32[]{:S(2)}) collective-permute-start(bf16[48,896]{1,0:T(8,128)(2,1)S(1)} %get-tuple-element.36), channel_id=1, source_target_pairs={{0,24},{8,16},{16,8},{24,0},{1,25},{9,17},{17,9},{25,1},{2,26},{10... | collective-permute-start | bytes 258056 | tf_op jit(solution)/shard_map/ppermute | solution.py:424
  7.4 0.1 collective-permute-start
  7.5 2.0 %copy-done.5 = bf16[1,896,2048]{2,1,0:T(8,128)(2,1)S(1)} copy-done((bf16[1,896,2048]{2,1,0:T(8,128)(2,1)S(1)}, bf16[1,896,2048]{2,1,0:T(8,128)(2,1)}, u32[]{:S(2)}) %copy-start.5) | copy-done | bytes 3670040
  9.6 2.0 %copy-done.6 = bf16[1,896,2048]{2,1,0:T(8,128)(2,1)S(1)} copy-done((bf16[1,896,2048]{2,1,0:T(8,128)(2,1)S(1)}, bf16[1,896,2048]{2,1,0:T(8,128)(2,1)}, u32[]{:S(2)}) %copy-start.6) | copy-done | bytes 3670040
  11.6 0.5 load.2
  12.2 0.4 copy-done.9
  12.6 0.7 dispatch.3
  13.3 1.6 %away_terms.2 = (bf16[4,2,192,256]{3,2,1,0:T(8,128)(2,1)S(1)}, bf16[192,896]{1,0:T(8,128)(2,1)S(1)}) custom-call(s32[4]{0:T(128)S(1)} %fusion.11.refs_0_.refs_1_, bf16[48,896]{1,0:T(8,128)(2,1)S(1)} %get-tuple-element.33.refs_1_, bf16[48,896]{1,0:T(8,128)(2,1)S(1)} %collective-permute-done.refs_2_, bf16[48,896]{1,0:T(8,128)(2,1)S(1)} %collective-permute-done.1.refs_3_, ...), custom_call_target="tpu_custom_call" | custom-call | flops 704643072 | bytes 8814608 | tf_op jit(solution)/shard_map/away_terms/pallas_call | solution.py:101
  14.9 0.3 copy-done.2
  15.2 1.9 %collective-permute-start.12 = (bf16[48,896]{1,0:T(8,128)(2,1)S(1)}, bf16[48,896]{1,0:T(8,128)(2,1)S(1)}, u32[]{:S(2)}, u32[]{:S(2)}) collective-permute-start(bf16[48,896]{1,0:T(8,128)(2,1)S(1)} %get-tuple-element.39.refs_7_), channel_id=1, source_target_pairs={{0,8},{8,0},{16,24},{24,16},{1,9},{9,1},{17,25},{25,17},{2,10},{10... | collective-permute-start | bytes 258056 | tf_op jit(solution)/shard_map/ppermute | solution.py:424
  17.1 1.5 %collective-permute-start.13 = (bf16[48,896]{1,0:T(8,128)(2,1)S(1)}, bf16[48,896]{1,0:T(8,128)(2,1)S(1)}, u32[]{:S(2)}, u32[]{:S(2)}) collective-permute-start(bf16[48,896]{1,0:T(8,128)(2,1)S(1)} %get-tuple-element.49), channel_id=1, source_target_pairs={{0,16},{8,24},{16,0},{24,8},{1,17},{9,25},{17,1},{25,9},{2,18},{10... | collective-permute-start | bytes 258056 | tf_op jit(solution)/shard_map/ppermute | solution.py:424
  18.6 0.1 collective-permute-start.14
  18.7 2.0 %copy-done.7 = bf16[1,2048,896]{2,1,0:T(8,128)(2,1)S(1)} copy-done((bf16[1,2048,896]{2,1,0:T(8,128)(2,1)S(1)}, bf16[1,2048,896]{2,1,0:T(8,128)(2,1)}, u32[]{:S(2)}) %copy-start.7) | copy-done | bytes 3670040
  20.7 0.3 load.3.refs_5_.refs_4_.refs_2_
  21.0 1.8 %copy-done.1 = bf16[896,2048]{1,0:T(8,128)(2,1)S(1)} copy-done((bf16[896,2048]{1,0:T(8,128)(2,1)S(1)}, bf16[896,2048]{1,0:T(8,128)(2,1)}, u32[]{:S(2)}) %copy-start.1) | copy-done | bytes 3670040
  22.8 1.1 copy-done.3
  23.9 1.6 %kept_terms.2 = (bf16[2,2,192,256]{3,2,1,0:T(8,128)(2,1)S(1)}, f32[2,2,192,256]{3,2,1,0:T(8,128)S(1)}) custom-call(s32[4]{0:T(128)S(1)} %fusion.10.refs_0_, bf16[192,896]{1,0:T(8,128)(2,1)S(1)} %get-tuple-element.40.refs_1_.refs_6_, bf16[896,2048]{1,0:T(8,128)(2,1)S(1)} %copy-done.1, bf16[896,2048]{1,0:T(8,128)(2,1)S(1)} %copy-done.3, ...), custom_call_target="tpu_custom_call" | custom-call | flops 704643072 | bytes 9650192 | tf_op jit(solution)/shard_map/kept_terms/pallas_call | solution.py:101
  25.5 1.3 %away_terms.3 = (bf16[4,1,192,256]{3,2,1,0:T(8,128)(2,1)S(1)}, bf16[192,896]{1,0:T(8,128)(2,1)S(1)}) custom-call(s32[4]{0:T(128)S(1)} %fusion.11.refs_0_.refs_1_, bf16[48,896]{1,0:T(8,128)(2,1)S(1)} %get-tuple-element.48.refs_1_, bf16[48,896]{1,0:T(8,128)(2,1)S(1)} %collective-permute-done.12.refs_2_, bf16[48,896]{1,0:T(8,128)(2,1)S(1)} %collective-permute-done.13.refs_3_, ...), custom_call_target="tpu_custom_call" | custom-call | flops 352321536 | bytes 4751376 | tf_op jit(solution)/shard_map/away_terms/pallas_call | solution.py:101
  26.8 0.1 collective-permute-start.15
  26.9 2.1 %collective-permute-start.4 = (bf16[2,2,192,256]{3,2,1,0:T(8,128)(2,1)S(1)}, bf16[2,2,192,256]{3,2,1,0:T(8,128)(2,1)S(1)}, u32[]{:S(2)}, u32[]{:S(2)}) collective-permute-start(bf16[2,2,192,256]{3,2,1,0:T(8,128)(2,1)S(1)} %get-tuple-element.43.refs_6_), channel_id=1, source_target_pairs={{0,2},{1,5},{2,0},{3,7},{4,6},{5,1},{6,4},{7,3},{8,10},{9,13},{10,... | collective-permute-start | bytes 1179656 | tf_op jit(solution)/shard_map/ppermute | solution.py:405
  29.0 1.3 %kept_terms.3 = (bf16[2,1,192,256]{3,2,1,0:T(8,128)(2,1)S(1)}, f32[2,1,192,256]{3,2,1,0:T(8,128)S(1)}) custom-call(s32[4]{0:T(128)S(1)} %fusion.10.refs_0_, bf16[192,896]{1,0:T(8,128)(2,1)S(1)} %get-tuple-element.51.refs_1_.refs_4_, bf16[2048,896]{1,0:T(8,128)(2,1)S(1)} %load.3.refs_5_.refs_4_.refs_2_, ...), custom_call_target="tpu_custom_call" | custom-call | flops 352321536 | bytes 4997136 | tf_op jit(solution)/shard_map/kept_terms/pallas_call | solution.py:101
  30.3 1.7 %collective-permute-start.16 = (bf16[2,1,192,256]{3,2,1,0:T(8,128)(2,1)S(1)}, bf16[2,1,192,256]{3,2,1,0:T(8,128)(2,1)S(1)}, u32[]{:S(2)}, u32[]{:S(2)}) collective-permute-start(bf16[2,1,192,256]{3,2,1,0:T(8,128)(2,1)S(1)} %get-tuple-element.54), channel_id=1, source_target_pairs={{0,2},{1,5},{2,0},{3,7},{4,6},{5,1},{6,4},{7,3},{8,10},{9,13},{10,... | collective-permute-start | bytes 589832 | tf_op jit(solution)/shard_map/ppermute | solution.py:405
  32.0 6.5 %collective-permute-done.4 = bf16[2,2,192,256]{3,2,1,0:T(8,128)(2,1)S(1)} collective-permute-done((bf16[2,2,192,256]{3,2,1,0:T(8,128)(2,1)S(1)}, bf16[2,2,192,256]{3,2,1,0:T(8,128)(2,1)S(1)}, u32[]{:S(2)}, u32[]{:S(2)}) %collective-permute-start.4) | collective-permute-done | bytes 393248 | tf_op jit(solution)/shard_map/ppermute | solution.py:405
  38.5 0.1 convert_add_fusion
  38.6 3.5 %collective-permute-start.5 = (bf16[1,2,192,256]{3,2,1,0:T(8,128)(2,1)S(1)}, bf16[1,2,192,256]{3,2,1,0:T(8,128)(2,1)S(1)}, u32[]{:S(2)}, u32[]{:S(2)}) collective-permute-start(bf16[1,2,192,256]{3,2,1,0:T(8,128)(2,1)S(1)} %slice.58), channel_id=1, source_target_pairs={{0,4},{1,3},{2,6},{3,1},{4,0},{5,7},{6,2},{7,5},{8,12},{9,11},{10,... | collective-permute-start | bytes 589832 | tf_op jit(solution)/shard_map/ppermute | solution.py:405
  42.2 1.3 %collective-permute-done.16 = bf16[2,1,192,256]{3,2,1,0:T(8,128)(2,1)S(1)} collective-permute-done((bf16[2,1,192,256]{3,2,1,0:T(8,128)(2,1)S(1)}, bf16[2,1,192,256]{3,2,1,0:T(8,128)(2,1)S(1)}, u32[]{:S(2)}, u32[]{:S(2)}) %collective-permute-start.16) | collective-permute-done | bytes 196640 | tf_op jit(solution)/shard_map/ppermute | solution.py:405
  43.5 2.7 %collective-permute-start.17 = (bf16[1,1,192,256]{3,2,1,0:T(8,128)(2,1)S(1)}, bf16[1,1,192,256]{3,2,1,0:T(8,128)(2,1)S(1)}, u32[]{:S(2)}, u32[]{:S(2)}) collective-permute-start(bf16[1,1,192,256]{3,2,1,0:T(8,128)(2,1)S(1)} %slice.59), channel_id=1, source_target_pairs={{0,4},{1,3},{2,6},{3,1},{4,0},{5,7},{6,2},{7,5},{8,12},{9,11},{10,... | collective-permute-start | bytes 294920 | tf_op jit(solution)/shard_map/ppermute | solution.py:405
  46.2 1.2 %collective-permute-done.5 = bf16[1,2,192,256]{3,2,1,0:T(8,128)(2,1)S(1)} collective-permute-done((bf16[1,2,192,256]{3,2,1,0:T(8,128)(2,1)S(1)}, bf16[1,2,192,256]{3,2,1,0:T(8,128)(2,1)S(1)}, u32[]{:S(2)}, u32[]{:S(2)}) %collective-permute-start.5) | collective-permute-done | bytes 196640 | tf_op jit(solution)/shard_map/ppermute | solution.py:405
  47.5 0.1 multiply_convert_fusion
  47.6 3.4 %collective-permute-start.6 = (bf16[1,1,192,256]{3,2,1,0:T(8,128)(2,1)S(1)}, bf16[1,1,192,256]{3,2,1,0:T(8,128)(2,1)S(1)}, u32[]{:S(2)}, u32[]{:S(2)}) collective-permute-start(bf16[1,1,192,256]{3,2,1,0:T(8,128)(2,1)S(1)} %multiply_convert_fusion), channel_id=1, source_target_pairs={{0,4},{1,3},{2,6},{3,1},{4,0},{5,7},{6,2},{7,5},{8,12},{9,11},{10,... | collective-permute-start | bytes 294920 | tf_op jit(solution)/shard_map/ppermute | solution.py:405
  51.0 0.1 fusion.6
  51.2 1.5 %collective-permute-start.18 = (bf16[1,2,144,256]{3,2,1,0:T(8,128)(2,1)S(1)}, bf16[1,2,144,256]{3,2,1,0:T(8,128)(2,1)S(1)}, u32[]{:S(2)}, u32[]{:S(2)}) collective-permute-start(bf16[1,2,144,256]{3,2,1,0:T(8,128)(2,1)S(1)} %maximum_bitcast_fusion), channel_id=1, source_target_pairs={{0,4},{1,3},{2,6},{3,1},{4,0},{5,7},{6,2},{7,5},{8,12},{9,11},{10,... | collective-permute-start | bytes 442376 | tf_op jit(solution)/shard_map/ppermute | solution.py:405
  52.7 1.3 %collective-permute-done.6 = bf16[1,1,192,256]{3,2,1,0:T(8,128)(2,1)S(1)} collective-permute-done((bf16[1,1,192,256]{3,2,1,0:T(8,128)(2,1)S(1)}, bf16[1,1,192,256]{3,2,1,0:T(8,128)(2,1)S(1)}, u32[]{:S(2)}, u32[]{:S(2)}) %collective-permute-start.6) | collective-permute-done | bytes 98336 | tf_op jit(solution)/shard_map/ppermute | solution.py:405
  54.0 2.7 %collective-permute-start.7 = (bf16[2,1,192,256]{3,2,1,0:T(8,128)(2,1)S(1)}, bf16[2,1,192,256]{3,2,1,0:T(8,128)(2,1)S(1)}, u32[]{:S(2)}, u32[]{:S(2)}) collective-permute-start(bf16[2,1,192,256]{3,2,1,0:T(8,128)(2,1)S(1)} %pad_maximum_fusion.3), channel_id=1, source_target_pairs={{0,2},{1,5},{2,0},{3,7},{4,6},{5,1},{6,4},{7,3},{8,10},{9,13},{10,... | collective-permute-start | bytes 589832 | tf_op jit(solution)/shard_map/ppermute | solution.py:405
  56.8 9.2 %collective-permute-done.18 = bf16[1,2,144,256]{3,2,1,0:T(8,128)(2,1)S(1)} collective-permute-done((bf16[1,2,144,256]{3,2,1,0:T(8,128)(2,1)S(1)}, bf16[1,2,144,256]{3,2,1,0:T(8,128)(2,1)S(1)}, u32[]{:S(2)}, u32[]{:S(2)}) %collective-permute-start.18) | collective-permute-done | bytes 147488 | tf_op jit(solution)/shard_map/ppermute | solution.py:405
  65.9 0.1 collective-permute-start.22
  66.0 3.3 %collective-permute-start.19 = (bf16[1,2,48,256]{3,2,1,0:T(8,128)(2,1)S(1)}, bf16[1,2,48,256]{3,2,1,0:T(8,128)(2,1)S(1)}, u32[]{:S(2)}, u32[]{:S(2)}) collective-permute-start(bf16[1,2,48,256]{3,2,1,0:T(8,128)(2,1)S(1)} %maximum_bitcast_fusion.1), channel_id=1, source_target_pairs={{0,4},{1,3},{2,6},{3,1},{4,0},{5,7},{6,2},{7,5},{8,12},{9,11},{10,... | collective-permute-start | bytes 147464 | tf_op jit(solution)/shard_map/ppermute | solution.py:405
  69.4 0.1 collective-permute-start.8
  69.4 3.8 %collective-permute-done.22 = bf16[2,2,144,256]{3,2,1,0:T(8,128)(2,1)S(1)} collective-permute-done((bf16[2,2,144,256]{3,2,1,0:T(8,128)(2,1)S(1)}, bf16[2,2,144,256]{3,2,1,0:T(8,128)(2,1)S(1)}, u32[]{:S(2)}, u32[]{:S(2)}) %collective-permute-start.22) | collective-permute-done | bytes 294944 | tf_op jit(solution)/shard_map/ppermute | solution.py:405
  73.3 0.1 pad_maximum_fusion.refs_1_.refs_3_
  73.3 0.1 collective-permute-start.23
  73.4 1.1 collective-permute-start.20
  74.6 4.6 %collective-permute-done.20 = bf16[2,2,48,256]{3,2,1,0:T(8,128)(2,1)S(1)} collective-permute-done((bf16[2,2,48,256]{3,2,1,0:T(8,128)(2,1)S(1)}, bf16[2,2,48,256]{3,2,1,0:T(8,128)(2,1)S(1)}, u32[]{:S(2)}, u32[]{:S(2)}) %collective-permute-start.20) | collective-permute-done | bytes 98336 | tf_op jit(solution)/shard_map/ppermute | solution.py:405
  79.2 0.1 collective-permute-start.21
  79.3 1.5 %unit_rows.4 = (bf16[48,896]{1,0:T(8,128)(2,1)S(1)}, bf16[48,896]{1,0:T(8,128)(2,1)S(1)}, bf16[48,896]{1,0:T(8,128)(2,1)S(1)}, bf16[48,896]{1,0:T(8,128)(2,1)S(1)}) custom-call(s32[4]{0:T(128)S(1)} %fusion.10.refs_0_, s32[4]{0:T(128)S(1)} %fusion.11.refs_0_.refs_1_, bf16[4,1,192,256]{3,2,1,0:T(8,128)(2,1)S(1)} %pad_maximum_fusion.1.refs_2_, ...), custom_call_target="tpu_custom_call" | custom-call | flops 704643072 | bytes 4800544 | tf_op jit(solution)/shard_map/unit_rows/pallas_call | solution.py:101
  80.8 2.5 %collective-permute-start.9 = (bf16[48,896]{1,0:T(8,128)(2,1)S(1)}, bf16[48,896]{1,0:T(8,128)(2,1)S(1)}, u32[]{:S(2)}, u32[]{:S(2)}) collective-permute-start(bf16[48,896]{1,0:T(8,128)(2,1)S(1)} %get-tuple-element.45), channel_id=1, source_target_pairs={{0,8},{8,0},{16,24},{24,16},{1,9},{9,1},{17,25},{25,17},{2,10},{10... | collective-permute-start | bytes 258056 | tf_op jit(solution)/shard_map/ppermute | solution.py:424
  83.3 1.5 %collective-permute-start.10 = (bf16[48,896]{1,0:T(8,128)(2,1)S(1)}, bf16[48,896]{1,0:T(8,128)(2,1)S(1)}, u32[]{:S(2)}, u32[]{:S(2)}) collective-permute-start(bf16[48,896]{1,0:T(8,128)(2,1)S(1)} %get-tuple-element.46), channel_id=1, source_target_pairs={{0,16},{8,24},{16,0},{24,8},{1,17},{9,25},{17,1},{25,9},{2,18},{10... | collective-permute-start | bytes 258056 | tf_op jit(solution)/shard_map/ppermute | solution.py:424
  84.8 0.0 collective-permute-start.11
  84.9 5.2 %weight_grads.2.refs_4_ = bf16[1,2048,896]{2,1,0:T(8,128)(2,1)} custom-call(s32[4]{0:T(128)S(1)} %fusion.10.refs_0_, s32[4]{0:T(128)S(1)} %fusion.11.refs_0_.refs_1_, bf16[4,1,192,256]{3,2,1,0:T(8,128)(2,1)S(1)} %pad_maximum_fusion.1.refs_2_, bf16[4,1,192,256]{3,2,1,0:T(8,128)(2,1)S(1)} %collective-permute-done.8.refs_3_, ...), custom_call_target="tpu_custom_call" | custom-call | flops 704643072 | bytes 4800544 | tf_op jit(solution)/shard_map/weight_grads/pallas_call | solution.py:101
  90.1 0.0 copy-start.4
  90.1 2.0 %copy-done.4 = bf16[1,2048,896]{2,1,0:T(8,128)(2,1)S(1)} copy-done((bf16[1,2048,896]{2,1,0:T(8,128)(2,1)S(1)}, bf16[1,2048,896]{2,1,0:T(8,128)(2,1)}, u32[]{:S(2)}) %copy-start.4) | copy-done | bytes 3670040
  92.1 1.8 %unit_rows.5.refs_4_ = f32[144,896]{1,0:T(8,128)S(1)} custom-call(s32[4]{0:T(128)S(1)} %fusion.10.refs_0_, bf16[4,2,144,256]{3,2,1,0:T(8,128)(2,1)S(1)} %pad_maximum_fusion.refs_1_.refs_3_, bf16[896,2048]{1,0:T(8,128)(2,1)S(1)} %copy-done.1, bf16[896,2048]{1,0:T(8,128)(2,1)S(1)} %copy-done.3, bf16[1,2048,896]{2,1,0:T(8,128)(2,1)S(1)} %copy-done.4), custom_call_target="tpu_custom_call" | custom-call | flops 528482304 | bytes 8445968 | tf_op jit(solution)/shard_map/unit_rows/pallas_call | solution.py:101
  94.0 1.1 collect.2
  95.1 1.8 %unit_rows.6 = (bf16[48,896]{1,0:T(8,128)(2,1)S(1)}, bf16[48,896]{1,0:T(8,128)(2,1)S(1)}, bf16[48,896]{1,0:T(8,128)(2,1)S(1)}) custom-call(s32[4]{0:T(128)S(1)} %fusion.11.refs_0_.refs_1_, bf16[4,2,144,256]{3,2,1,0:T(8,128)(2,1)S(1)} %collective-permute-done.23.refs_1_.refs_5_, bf16[896,2048]{1,0:T(8,128)(2,1)S(1)} %copy-done.1, ...), custom_call_target="tpu_custom_call" | custom-call | flops 528482304 | bytes 8704016 | tf_op jit(solution)/shard_map/unit_rows/pallas_call | solution.py:101
  96.9 2.1 %collective-permute-start.25 = (bf16[48,896]{1,0:T(8,128)(2,1)S(1)}, bf16[48,896]{1,0:T(8,128)(2,1)S(1)}, u32[]{:S(2)}, u32[]{:S(2)}) collective-permute-start(bf16[48,896]{1,0:T(8,128)(2,1)S(1)} %get-tuple-element.57), channel_id=1, source_target_pairs={{0,16},{8,24},{16,0},{24,8},{1,17},{9,25},{17,1},{25,9},{2,18},{10... | collective-permute-start | bytes 258056 | tf_op jit(solution)/shard_map/ppermute | solution.py:424
  98.9 1.4 %collective-permute-start.26 = (bf16[48,896]{1,0:T(8,128)(2,1)S(1)}, bf16[48,896]{1,0:T(8,128)(2,1)S(1)}, u32[]{:S(2)}, u32[]{:S(2)}) collective-permute-start(bf16[48,896]{1,0:T(8,128)(2,1)S(1)} %get-tuple-element.58), channel_id=1, source_target_pairs={{0,24},{8,16},{16,8},{24,0},{1,25},{9,17},{17,9},{25,1},{2,26},{10... | collective-permute-start | bytes 258056 | tf_op jit(solution)/shard_map/ppermute | solution.py:424
  100.3 0.1 collective-permute-start.24
  100.5 2.7 %unit_rows.7.refs_2_.refs_7_ = bf16[48,896]{1,0:T(8,128)(2,1)S(1)} custom-call(s32[4]{0:T(128)S(1)} %fusion.10.refs_0_, s32[4]{0:T(128)S(1)} %fusion.11.refs_0_.refs_1_, bf16[4,2,48,256]{3,2,1,0:T(8,128)(2,1)S(1)} %constant_dynamic-update-slice_fusion.refs_2_, bf16[4,2,48,256]{3,2,1,0:T(8,128)(2,1)S(1)} %collective-permute-done.21.refs_3_.refs_4_, ...), custom_call_target="tpu_custom_call" | custom-call | flops 352321536 | bytes 7819296 | tf_op jit(solution)/shard_map/unit_rows/pallas_call | solution.py:101
  103.2 10.2 %weight_grads.3 = (bf16[1,896,2048]{2,1,0:T(8,128)(2,1)}, bf16[1,896,2048]{2,1,0:T(8,128)(2,1)}) custom-call(s32[4]{0:T(128)S(1)} %fusion.10.refs_0_, s32[4]{0:T(128)S(1)} %fusion.11.refs_0_.refs_1_, bf16[4,2,48,256]{3,2,1,0:T(8,128)(2,1)S(1)} %constant_dynamic-update-slice_fusion.refs_2_, bf16[4,2,144,256]{3,2,1,0:T(8,128)(2,1)S(1)} %pad_maximum_fusion.refs_1_.refs_3_, ...), custom_call_target="tpu_custom_call" | custom-call | flops 1409286144 | bytes 9256992 | tf_op jit(solution)/shard_map/weight_grads/pallas_call | solution.py:101
  113.4 1.1 collect.3
  (53 shorter events, 0.4 us)
Async XLA Ops:
  0.6 0.9 copy-start.8
  1.6 0.7 copy-start.10
  2.9 10.4 %collective-permute-start.1 = (bf16[48,896]{1,0:T(8,128)(2,1)S(1)}, bf16[48,896]{1,0:T(8,128)(2,1)S(1)}, u32[]{:S(2)}, u32[]{:S(2)}) collective-permute-start(bf16[48,896]{1,0:T(8,128)(2,1)S(1)} %get-tuple-element.35), channel_id=1, source_target_pairs={{0,16},{8,24},{16,0},{24,8},{1,17},{9,25},{17,1},{25,9},{2,18},{10... | collective-permute-start | bytes 258056 | tf_op jit(solution)/shard_map/ppermute | solution.py:424
  6.0 7.3 %collective-permute-start.2 = (bf16[48,896]{1,0:T(8,128)(2,1)S(1)}, bf16[48,896]{1,0:T(8,128)(2,1)S(1)}, u32[]{:S(2)}, u32[]{:S(2)}) collective-permute-start(bf16[48,896]{1,0:T(8,128)(2,1)S(1)} %get-tuple-element.36), channel_id=1, source_target_pairs={{0,24},{8,16},{16,8},{24,0},{1,25},{9,17},{17,9},{25,1},{2,26},{10... | collective-permute-start | bytes 258056 | tf_op jit(solution)/shard_map/ppermute | solution.py:424
  7.4 5.9 %collective-permute-start = (bf16[48,896]{1,0:T(8,128)(2,1)S(1)}, bf16[48,896]{1,0:T(8,128)(2,1)S(1)}, u32[]{:S(2)}, u32[]{:S(2)}) collective-permute-start(bf16[48,896]{1,0:T(8,128)(2,1)S(1)} %get-tuple-element.34.refs_2_), channel_id=1, source_target_pairs={{0,8},{8,0},{16,24},{24,16},{1,9},{9,1},{17,25},{25,17},{2,10},{10... | collective-permute-start | bytes 258056 | tf_op jit(solution)/shard_map/ppermute | solution.py:424
  7.5 2.0 %copy-start.5 = (bf16[1,896,2048]{2,1,0:T(8,128)(2,1)S(1)}, bf16[1,896,2048]{2,1,0:T(8,128)(2,1)}, u32[]{:S(2)}) copy-start(bf16[1,896,2048]{2,1,0:T(8,128)(2,1)} %param.10) | copy-start | bytes 11010052
  9.6 2.0 %copy-start.6 = (bf16[1,896,2048]{2,1,0:T(8,128)(2,1)S(1)}, bf16[1,896,2048]{2,1,0:T(8,128)(2,1)}, u32[]{:S(2)}) copy-start(bf16[1,896,2048]{2,1,0:T(8,128)(2,1)} %param.11) | copy-start | bytes 11010052
  11.6 0.9 copy-start.9
  11.6 0.9 copy-start.11
  11.6 0.9 copy-start.12
  12.1 2.8 %copy-start = (bf16[896,2048]{1,0:T(8,128)(2,1)}, bf16[896,2048]{1,0:T(8,128)(2,1)S(1)}, u32[]{:S(2)}) copy-start(bf16[896,2048]{1,0:T(8,128)(2,1)S(1)} %get-tuple-element.37.refs_4_.refs_5_.refs_2_) | copy-start | bytes 11010052
  12.1 3.0 %copy-start.2 = (bf16[896,2048]{1,0:T(8,128)(2,1)}, bf16[896,2048]{1,0:T(8,128)(2,1)S(1)}, u32[]{:S(2)}) copy-start(bf16[896,2048]{1,0:T(8,128)(2,1)S(1)} %get-tuple-element.38.refs_6_.refs_3_.refs_5_) | copy-start | bytes 11010052
  15.2 5.8 %collective-permute-start.3 = (bf16[4,2,192,256]{3,2,1,0:T(8,128)(2,1)S(1)}, bf16[4,2,192,256]{3,2,1,0:T(8,128)(2,1)S(1)}, u32[]{:S(2)}, u32[]{:S(2)}) collective-permute-start(bf16[4,2,192,256]{3,2,1,0:T(8,128)(2,1)S(1)} %get-tuple-element.41.refs_1_), channel_id=1, source_target_pairs={{0,1},{1,0},{2,3},{3,2},{4,5},{5,4},{6,7},{7,6},{8,9},{9,8},{10,11... | collective-permute-start | bytes 2359304 | tf_op jit(solution)/shard_map/ppermute | solution.py:408
  15.2 10.3 %collective-permute-start.12 = (bf16[48,896]{1,0:T(8,128)(2,1)S(1)}, bf16[48,896]{1,0:T(8,128)(2,1)S(1)}, u32[]{:S(2)}, u32[]{:S(2)}) collective-permute-start(bf16[48,896]{1,0:T(8,128)(2,1)S(1)} %get-tuple-element.39.refs_7_), channel_id=1, source_target_pairs={{0,8},{8,0},{16,24},{24,16},{1,9},{9,1},{17,25},{25,17},{2,10},{10... | collective-permute-start | bytes 258056 | tf_op jit(solution)/shard_map/ppermute | solution.py:424
  17.1 8.3 %collective-permute-start.13 = (bf16[48,896]{1,0:T(8,128)(2,1)S(1)}, bf16[48,896]{1,0:T(8,128)(2,1)S(1)}, u32[]{:S(2)}, u32[]{:S(2)}) collective-permute-start(bf16[48,896]{1,0:T(8,128)(2,1)S(1)} %get-tuple-element.49), channel_id=1, source_target_pairs={{0,16},{8,24},{16,0},{24,8},{1,17},{9,25},{17,1},{25,9},{2,18},{10... | collective-permute-start | bytes 258056 | tf_op jit(solution)/shard_map/ppermute | solution.py:424
  18.6 6.8 %collective-permute-start.14 = (bf16[48,896]{1,0:T(8,128)(2,1)S(1)}, bf16[48,896]{1,0:T(8,128)(2,1)S(1)}, u32[]{:S(2)}, u32[]{:S(2)}) collective-permute-start(bf16[48,896]{1,0:T(8,128)(2,1)S(1)} %get-tuple-element.50), channel_id=1, source_target_pairs={{0,24},{8,16},{16,8},{24,0},{1,25},{9,17},{17,9},{25,1},{2,26},{10... | collective-permute-start | bytes 258056 | tf_op jit(solution)/shard_map/ppermute | solution.py:424
  18.7 2.0 %copy-start.7 = (bf16[1,2048,896]{2,1,0:T(8,128)(2,1)S(1)}, bf16[1,2048,896]{2,1,0:T(8,128)(2,1)}, u32[]{:S(2)}) copy-start(bf16[1,2048,896]{2,1,0:T(8,128)(2,1)} %param.12) | copy-start | bytes 11010052
  20.7 2.0 %copy-start.1 = (bf16[896,2048]{1,0:T(8,128)(2,1)S(1)}, bf16[896,2048]{1,0:T(8,128)(2,1)}, u32[]{:S(2)}) copy-start(bf16[896,2048]{1,0:T(8,128)(2,1)} %copy-done) | copy-start | bytes 11010052
  20.7 3.2 %copy-start.3 = (bf16[896,2048]{1,0:T(8,128)(2,1)S(1)}, bf16[896,2048]{1,0:T(8,128)(2,1)}, u32[]{:S(2)}) copy-start(bf16[896,2048]{1,0:T(8,128)(2,1)} %copy-done.2) | copy-start | bytes 11010052
  26.8 2.2 %collective-permute-start.15 = (bf16[4,1,192,256]{3,2,1,0:T(8,128)(2,1)S(1)}, bf16[4,1,192,256]{3,2,1,0:T(8,128)(2,1)S(1)}, u32[]{:S(2)}, u32[]{:S(2)}) collective-permute-start(bf16[4,1,192,256]{3,2,1,0:T(8,128)(2,1)S(1)} %get-tuple-element.52), channel_id=1, source_target_pairs={{0,1},{1,0},{2,3},{3,2},{4,5},{5,4},{6,7},{7,6},{8,9},{9,8},{10,11... | collective-permute-start | bytes 1179656 | tf_op jit(solution)/shard_map/ppermute | solution.py:408
  26.9 11.6 %collective-permute-start.4 = (bf16[2,2,192,256]{3,2,1,0:T(8,128)(2,1)S(1)}, bf16[2,2,192,256]{3,2,1,0:T(8,128)(2,1)S(1)}, u32[]{:S(2)}, u32[]{:S(2)}) collective-permute-start(bf16[2,2,192,256]{3,2,1,0:T(8,128)(2,1)S(1)} %get-tuple-element.43.refs_6_), channel_id=1, source_target_pairs={{0,2},{1,5},{2,0},{3,7},{4,6},{5,1},{6,4},{7,3},{8,10},{9,13},{10,... | collective-permute-start | bytes 1179656 | tf_op jit(solution)/shard_map/ppermute | solution.py:405
  30.3 13.2 %collective-permute-start.16 = (bf16[2,1,192,256]{3,2,1,0:T(8,128)(2,1)S(1)}, bf16[2,1,192,256]{3,2,1,0:T(8,128)(2,1)S(1)}, u32[]{:S(2)}, u32[]{:S(2)}) collective-permute-start(bf16[2,1,192,256]{3,2,1,0:T(8,128)(2,1)S(1)} %get-tuple-element.54), channel_id=1, source_target_pairs={{0,2},{1,5},{2,0},{3,7},{4,6},{5,1},{6,4},{7,3},{8,10},{9,13},{10,... | collective-permute-start | bytes 589832 | tf_op jit(solution)/shard_map/ppermute | solution.py:405
  38.6 8.8 %collective-permute-start.5 = (bf16[1,2,192,256]{3,2,1,0:T(8,128)(2,1)S(1)}, bf16[1,2,192,256]{3,2,1,0:T(8,128)(2,1)S(1)}, u32[]{:S(2)}, u32[]{:S(2)}) collective-permute-start(bf16[1,2,192,256]{3,2,1,0:T(8,128)(2,1)S(1)} %slice.58), channel_id=1, source_target_pairs={{0,4},{1,3},{2,6},{3,1},{4,0},{5,7},{6,2},{7,5},{8,12},{9,11},{10,... | collective-permute-start | bytes 589832 | tf_op jit(solution)/shard_map/ppermute | solution.py:405
  43.5 7.5 %collective-permute-start.17 = (bf16[1,1,192,256]{3,2,1,0:T(8,128)(2,1)S(1)}, bf16[1,1,192,256]{3,2,1,0:T(8,128)(2,1)S(1)}, u32[]{:S(2)}, u32[]{:S(2)}) collective-permute-start(bf16[1,1,192,256]{3,2,1,0:T(8,128)(2,1)S(1)} %slice.59), channel_id=1, source_target_pairs={{0,4},{1,3},{2,6},{3,1},{4,0},{5,7},{6,2},{7,5},{8,12},{9,11},{10,... | collective-permute-start | bytes 294920 | tf_op jit(solution)/shard_map/ppermute | solution.py:405
  47.6 6.4 %collective-permute-start.6 = (bf16[1,1,192,256]{3,2,1,0:T(8,128)(2,1)S(1)}, bf16[1,1,192,256]{3,2,1,0:T(8,128)(2,1)S(1)}, u32[]{:S(2)}, u32[]{:S(2)}) collective-permute-start(bf16[1,1,192,256]{3,2,1,0:T(8,128)(2,1)S(1)} %multiply_convert_fusion), channel_id=1, source_target_pairs={{0,4},{1,3},{2,6},{3,1},{4,0},{5,7},{6,2},{7,5},{8,12},{9,11},{10,... | collective-permute-start | bytes 294920 | tf_op jit(solution)/shard_map/ppermute | solution.py:405
  51.2 14.7 %collective-permute-start.18 = (bf16[1,2,144,256]{3,2,1,0:T(8,128)(2,1)S(1)}, bf16[1,2,144,256]{3,2,1,0:T(8,128)(2,1)S(1)}, u32[]{:S(2)}, u32[]{:S(2)}) collective-permute-start(bf16[1,2,144,256]{3,2,1,0:T(8,128)(2,1)S(1)} %maximum_bitcast_fusion), channel_id=1, source_target_pairs={{0,4},{1,3},{2,6},{3,1},{4,0},{5,7},{6,2},{7,5},{8,12},{9,11},{10,... | collective-permute-start | bytes 442376 | tf_op jit(solution)/shard_map/ppermute | solution.py:405
  54.0 15.3 %collective-permute-start.7 = (bf16[2,1,192,256]{3,2,1,0:T(8,128)(2,1)S(1)}, bf16[2,1,192,256]{3,2,1,0:T(8,128)(2,1)S(1)}, u32[]{:S(2)}, u32[]{:S(2)}) collective-permute-start(bf16[2,1,192,256]{3,2,1,0:T(8,128)(2,1)S(1)} %pad_maximum_fusion.3), channel_id=1, source_target_pairs={{0,2},{1,5},{2,0},{3,7},{4,6},{5,1},{6,4},{7,3},{8,10},{9,13},{10,... | collective-permute-start | bytes 589832 | tf_op jit(solution)/shard_map/ppermute | solution.py:405
  65.9 7.3 %collective-permute-start.22 = (bf16[2,2,144,256]{3,2,1,0:T(8,128)(2,1)S(1)}, bf16[2,2,144,256]{3,2,1,0:T(8,128)(2,1)S(1)}, u32[]{:S(2)}, u32[]{:S(2)}) collective-permute-start(bf16[2,2,144,256]{3,2,1,0:T(8,128)(2,1)S(1)} %pad_maximum_fusion.2), channel_id=1, source_target_pairs={{0,2},{1,5},{2,0},{3,7},{4,6},{5,1},{6,4},{7,3},{8,10},{9,13},{10,... | collective-permute-start | bytes 884744 | tf_op jit(solution)/shard_map/ppermute | solution.py:405
  66.0 7.4 %collective-permute-start.19 = (bf16[1,2,48,256]{3,2,1,0:T(8,128)(2,1)S(1)}, bf16[1,2,48,256]{3,2,1,0:T(8,128)(2,1)S(1)}, u32[]{:S(2)}, u32[]{:S(2)}) collective-permute-start(bf16[1,2,48,256]{3,2,1,0:T(8,128)(2,1)S(1)} %maximum_bitcast_fusion.1), channel_id=1, source_target_pairs={{0,4},{1,3},{2,6},{3,1},{4,0},{5,7},{6,2},{7,5},{8,12},{9,11},{10,... | collective-permute-start | bytes 147464 | tf_op jit(solution)/shard_map/ppermute | solution.py:405
  69.4 9.9 %collective-permute-start.8 = (bf16[4,1,192,256]{3,2,1,0:T(8,128)(2,1)S(1)}, bf16[4,1,192,256]{3,2,1,0:T(8,128)(2,1)S(1)}, u32[]{:S(2)}, u32[]{:S(2)}) collective-permute-start(bf16[4,1,192,256]{3,2,1,0:T(8,128)(2,1)S(1)} %pad_maximum_fusion.1.refs_2_), channel_id=1, source_target_pairs={{0,1},{1,0},{2,3},{3,2},{4,5},{5,4},{6,7},{7,6},{8,9},{9,8},{10,11... | collective-permute-start | bytes 1179656 | tf_op jit(solution)/shard_map/ppermute | solution.py:408
  73.3 21.7 %collective-permute-start.23 = (bf16[4,2,144,256]{3,2,1,0:T(8,128)(2,1)S(1)}, bf16[4,2,144,256]{3,2,1,0:T(8,128)(2,1)S(1)}, u32[]{:S(2)}, u32[]{:S(2)}) collective-permute-start(bf16[4,2,144,256]{3,2,1,0:T(8,128)(2,1)S(1)} %pad_maximum_fusion.refs_1_.refs_3_), channel_id=1, source_target_pairs={{0,1},{1,0},{2,3},{3,2},{4,5},{5,4},{6,7},{7,6},{8,9},{9,8},{10,11... | collective-permute-start | bytes 1769480 | tf_op jit(solution)/shard_map/ppermute | solution.py:408
  73.4 5.7 %collective-permute-start.20 = (bf16[2,2,48,256]{3,2,1,0:T(8,128)(2,1)S(1)}, bf16[2,2,48,256]{3,2,1,0:T(8,128)(2,1)S(1)}, u32[]{:S(2)}, u32[]{:S(2)}) collective-permute-start(bf16[2,2,48,256]{3,2,1,0:T(8,128)(2,1)S(1)} %pad_maximum_fusion.4), channel_id=1, source_target_pairs={{0,2},{1,5},{2,0},{3,7},{4,6},{5,1},{6,4},{7,3},{8,10},{9,13},{10,... | collective-permute-start | bytes 294920 | tf_op jit(solution)/shard_map/ppermute | solution.py:405
  79.2 21.3 %collective-permute-start.21 = (bf16[4,2,48,256]{3,2,1,0:T(8,128)(2,1)S(1)}, bf16[4,2,48,256]{3,2,1,0:T(8,128)(2,1)S(1)}, u32[]{:S(2)}, u32[]{:S(2)}) collective-permute-start(bf16[4,2,48,256]{3,2,1,0:T(8,128)(2,1)S(1)} %constant_dynamic-update-slice_fusion.refs_2_), channel_id=1, source_target_pairs={{0,1},{1,0},{2,3},{3,2},{4,5},{5,4},{6,7},{7,6},{8,9},{9,8},{10,11... | collective-permute-start | bytes 589832 | tf_op jit(solution)/shard_map/ppermute | solution.py:408
  80.8 13.1 %collective-permute-start.9 = (bf16[48,896]{1,0:T(8,128)(2,1)S(1)}, bf16[48,896]{1,0:T(8,128)(2,1)S(1)}, u32[]{:S(2)}, u32[]{:S(2)}) collective-permute-start(bf16[48,896]{1,0:T(8,128)(2,1)S(1)} %get-tuple-element.45), channel_id=1, source_target_pairs={{0,8},{8,0},{16,24},{24,16},{1,9},{9,1},{17,25},{25,17},{2,10},{10... | collective-permute-start | bytes 258056 | tf_op jit(solution)/shard_map/ppermute | solution.py:424
  83.3 10.6 %collective-permute-start.10 = (bf16[48,896]{1,0:T(8,128)(2,1)S(1)}, bf16[48,896]{1,0:T(8,128)(2,1)S(1)}, u32[]{:S(2)}, u32[]{:S(2)}) collective-permute-start(bf16[48,896]{1,0:T(8,128)(2,1)S(1)} %get-tuple-element.46), channel_id=1, source_target_pairs={{0,16},{8,24},{16,0},{24,8},{1,17},{9,25},{17,1},{25,9},{2,18},{10... | collective-permute-start | bytes 258056 | tf_op jit(solution)/shard_map/ppermute | solution.py:424
  84.8 9.1 %collective-permute-start.11 = (bf16[48,896]{1,0:T(8,128)(2,1)S(1)}, bf16[48,896]{1,0:T(8,128)(2,1)S(1)}, u32[]{:S(2)}, u32[]{:S(2)}) collective-permute-start(bf16[48,896]{1,0:T(8,128)(2,1)S(1)} %get-tuple-element.47), channel_id=1, source_target_pairs={{0,24},{8,16},{16,8},{24,0},{1,25},{9,17},{17,9},{25,1},{2,26},{10... | collective-permute-start | bytes 258056 | tf_op jit(solution)/shard_map/ppermute | solution.py:424
  90.1 2.0 %copy-start.4 = (bf16[1,2048,896]{2,1,0:T(8,128)(2,1)S(1)}, bf16[1,2048,896]{2,1,0:T(8,128)(2,1)}, u32[]{:S(2)}) copy-start(bf16[1,2048,896]{2,1,0:T(8,128)(2,1)} %weight_grads.2.refs_4_) | copy-start | bytes 11010052
  96.9 16.5 %collective-permute-start.25 = (bf16[48,896]{1,0:T(8,128)(2,1)S(1)}, bf16[48,896]{1,0:T(8,128)(2,1)S(1)}, u32[]{:S(2)}, u32[]{:S(2)}) collective-permute-start(bf16[48,896]{1,0:T(8,128)(2,1)S(1)} %get-tuple-element.57), channel_id=1, source_target_pairs={{0,16},{8,24},{16,0},{24,8},{1,17},{9,25},{17,1},{25,9},{2,18},{10... | collective-permute-start | bytes 258056 | tf_op jit(solution)/shard_map/ppermute | solution.py:424
  98.9 14.5 %collective-permute-start.26 = (bf16[48,896]{1,0:T(8,128)(2,1)S(1)}, bf16[48,896]{1,0:T(8,128)(2,1)S(1)}, u32[]{:S(2)}, u32[]{:S(2)}) collective-permute-start(bf16[48,896]{1,0:T(8,128)(2,1)S(1)} %get-tuple-element.58), channel_id=1, source_target_pairs={{0,24},{8,16},{16,8},{24,0},{1,25},{9,17},{17,9},{25,1},{2,26},{10... | collective-permute-start | bytes 258056 | tf_op jit(solution)/shard_map/ppermute | solution.py:424
  100.3 13.1 %collective-permute-start.24 = (bf16[48,896]{1,0:T(8,128)(2,1)S(1)}, bf16[48,896]{1,0:T(8,128)(2,1)S(1)}, u32[]{:S(2)}, u32[]{:S(2)}) collective-permute-start(bf16[48,896]{1,0:T(8,128)(2,1)S(1)} %get-tuple-element.56.refs_6_), channel_id=1, source_target_pairs={{0,8},{8,0},{16,24},{24,16},{1,9},{9,1},{17,25},{25,17},{2,10},{10... | collective-permute-start | bytes 258056 | tf_op jit(solution)/shard_map/ppermute | solution.py:424

commit v3 on v2

--- a/solution.py
+++ b/solution.py
@@ -87,11 +87,15 @@
     return lax.dot_general(a, b, dims, preferred_element_type=F32)
 
 
+def in_hbm(x):
+    return pltpu.with_memory_space_constraint(x, pltpu.HBM)
+
+
 def spec(shape, dtype=BF16):
     return jax.ShapeDtypeStruct(shape, dtype)
 
 
-def call(name, kernel, outs, out_specs, ins, in_specs, scratch=(), after=(), flops=0, mib=16):
+def call(kernel, outs, out_specs, ins, in_specs, scratch=(), after=(), flops=0, mib=16):
     late = len(after)
 
     def body(*refs):
@@ -106,7 +110,6 @@
         scratch_shapes=list(scratch),
         compiler_params=pltpu.CompilerParams(vmem_limit_bytes=mib * 2**20),
         cost_estimate=pl.CostEstimate(flops=int(flops), bytes_accessed=int(moved), transcendentals=0),
-        name=name,
     )(*ins, *after)
 
 
@@ -123,42 +126,40 @@
     return lax.broadcasted_iota(jnp.int32, (total, count), 0) == target
 
 
-def dispatch(ids, here, data, gates, members, slot, after=()):
-    total, width, count = members * slot, data.shape[1], data.shape[0]
-    gated = gates is not None
-    small = [ids] + ([gates] if gated else [])
+def dispatch(ids, here, gates, tokens, cotangents, members, slot):
+    (count, width), total = tokens.shape, members * slot
+    ins = [ids, gates, tokens, cotangents]
 
     def kernel(here_ref, *refs):
-        sources = refs[: len(small) + 1]
-        out_refs = refs[len(small) + 1 :][:members]
-        held, sems = refs[len(small) + 1 + members : -1], refs[-1]
+        sources, out_refs = refs[:4], refs[4 : 4 + 2 * members]
+        held, sems = refs[4 + 2 * members : -1], refs[-1]
         copies = [
             pltpu.make_async_copy(s, h, sems.at[i]) for i, (s, h) in enumerate(zip(sources, held))
         ]
         for copy in copies:
             copy.start()
-        for copy in copies[:-1]:
-            copy.wait()
+        copies[0].wait()
+        copies[1].wait()
         mask = placement(held[0][...], here_ref[0], members, slot, total)
-        value = held[1][...].astype(F32) if gated else 1.0
-        pick = jnp.where(mask, value, 0.0).astype(BF16)
-        copies[-1].wait()
-        rows = mm(pick, held[-1][...]).astype(BF16)
-        for m, ref in enumerate(out_refs):
-            ref[...] = rows[m * slot : (m + 1) * slot]
-
-    ins = [*small, data]
-    return call(
-        "dispatch",
-        kernel,
-        [spec((slot, width))] * members,
-        [VMEM] * members,
-        [here, *ins],
-        [SMEM] + [ANY] * len(ins),
-        [pltpu.VMEM(x.shape, x.dtype) for x in ins] + [pltpu.SemaphoreType.DMA((len(ins),))],
-        after,
-        2 * total * count * width,
-    )
+        gate = held[1][...].astype(F32)
+        for i, value in enumerate((1.0, gate)):
+            pick = jnp.where(mask, value, 0.0).astype(BF16)
+            copies[2 + i].wait()
+            rows = mm(pick, held[2 + i][...]).astype(BF16)
+            for m in range(members):
+                out_refs[members * i + m][...] = rows[m * slot : (m + 1) * slot]
+
+    out = call(
+        kernel,
+        [spec((slot, width))] * (2 * members),
+        [VMEM] * (2 * members),
+        [here, *map(in_hbm, ins)],
+        [SMEM] + [ANY] * 4,
+        [pltpu.VMEM(x.shape, x.dtype) for x in ins] + [pltpu.SemaphoreType.DMA((4,))],
+        (),
+        4 * total * count * width,
+    )
+    return out[:members], out[members:]
 
 
 def collect(ids, here, rows, gates, members, slot, after=()):
@@ -177,7 +178,6 @@
         out_ref[...] = mm(pick, joined[...], TN).astype(BF16)
 
     return call(
-        "collect",
         kernel,
         [spec((count, width))],
         [VMEM],
@@ -201,11 +201,10 @@
             copy.wait()
 
     return call(
-        "load",
         kernel,
         [spec(x.shape, x.dtype) for x in arrays],
         [VMEM] * len(arrays),
-        arrays,
+        [in_hbm(x) for x in arrays],
         [ANY] * len(arrays),
         [pltpu.SemaphoreType.DMA((len(arrays),))],
         after,
@@ -233,7 +232,6 @@
                 out_ref[j, i] = mm(x, w, NT if down else NN).astype(BF16)
 
     return call(
-        "away_terms",
         kernel,
         [spec((blocks, n, total, unit)), spec((total, width))],
         [VMEM] * 2,
@@ -262,7 +260,6 @@
                     keep[j, i] = term
 
     return call(
-        "kept_terms",
         kernel,
         [spec((blocks - first, n, total, unit)), spec((first, n, total, unit), F32)],
         [VMEM] * 2,
@@ -308,7 +305,6 @@
     else:
         outs = [spec((split, width))] * (total // split)
     return call(
-        "unit_rows",
         kernel,
         outs,
         [VMEM] * len(outs),
@@ -335,13 +331,12 @@
         turned, rows, held, sems = refs[-4:]
         if not down:
             turned[...] = x_ref[...].T
-        waits, step = [None, None], 0
+        waits = []
         for p in range(k):
             for j in range(pieces[p][1][0].shape[0]):
                 at = pl.ds(pl.multiple_of(id_refs[p][j] * unit, unit), unit)
                 for i in range(n):
-                    slot = step % 2
-                    step += 1
+                    slot = len(waits)
                     if parts == 1:
                         u = u_refs[p][j, i]
                     else:
@@ -350,21 +345,18 @@
                             rows[top : top + ref.shape[2], :] = ref[j, i]
                             top += ref.shape[2]
                         u = rows[...]
-                    if waits[slot] is not None:
-                        waits[slot].wait()
                     if down:
                         held[slot] = mm(u, x_ref[...], TN).astype(BF16)
                         target = out_refs[i].at[0, at, :]
                     else:
                         held[slot] = mm(turned[...], u).astype(BF16)
                         target = out_refs[i].at[0, :, at]
-                    waits[slot] = pltpu.make_async_copy(held.at[slot], target, sems.at[slot])
+                    waits.append(pltpu.make_async_copy(held.at[slot], target, sems.at[slot]))
                     waits[slot].start()
         for wait in waits:
             wait.wait()
 
     return call(
-        "weight_grads",
         kernel,
         [spec(shape)] * n,
         [ANY] * n,
@@ -373,8 +365,8 @@
         [
             pltpu.VMEM((width, total), BF16),
             pltpu.VMEM((total, unit), BF16),
-            pltpu.VMEM((2, unit, width) if down else (2, width, unit), BF16),
-            pltpu.SemaphoreType.DMA((2,)),
+            pltpu.VMEM((n * blocks, unit, width) if down else (n * blocks, width, unit), BF16),
+            pltpu.SemaphoreType.DMA((n * blocks,)),
         ],
         after,
         2 * n * blocks * total * width * unit,
@@ -396,39 +388,45 @@
 
     t = lax.axis_index("tensor")
     core, chip = t & 1, t >> 1
-    orders = (tuple(range(bits)), tuple(reversed(range(bits))))
-
-    def pairs(step):
-        return [(d, d ^ (2 << orders[d % 2][step])) for d in range(parts)]
-
-    def step_swap(x, step):
-        return lax.ppermute(x, "tensor", pairs(step))
+    forward = tuple(range(bits))
+    halving = (forward, forward[::-1])
+    doubling = (forward[::-1], forward[::-1])
+
+    def step_swap(x, orders, step):
+        pairs = [(d, d ^ (2 << orders[d % 2][step])) for d in range(parts)]
+        return lax.ppermute(x, "tensor", pairs)
 
     def core_swap(x):
         return lax.ppermute(x, "tensor", [(d, d ^ 1) for d in range(parts)])
 
-    def block_ids(c):
+    def block_ids(c, orders):
         rel = jnp.arange(half, dtype=jnp.int32)
-        place = [jnp.zeros_like(rel), jnp.zeros_like(rel)]
+        place = []
         for k in range(2):
-            for step in range(bits):
-                bit = (chip >> orders[k][step]) & 1
-                flip = (rel >> (bits - 1 - step)) & 1
-                place[k] = place[k] * 2 + (bit ^ flip)
+            at = jnp.broadcast_to(chip, rel.shape)
+            for step, bit in enumerate(orders[k]):
+                at = at ^ (((rel >> (bits - 1 - step)) & 1) << bit)
+            block = jnp.zeros_like(rel)
+            for bit in halving[k]:
+                block = block * 2 + ((at >> bit) & 1)
+            place.append(block)
         return half * c + jnp.where(c == 0, place[0], place[1])
 
-    mine, other = block_ids(core), block_ids(1 - core)
-
-    def expert_swap(rows, skipped=1):
-        return [
-            lax.ppermute(rows[m - skipped], "expert", [(d, d ^ m) for d in range(members)])
-            for m in range(1, members)
-        ]
+    here_ids, there_ids = block_ids(core, halving), block_ids(1 - core, halving)
+    turned = tuple(order[::-1] for order in doubling)
+    mine, other = block_ids(core, turned), block_ids(1 - core, turned)
+
+    def expert_swap(rows, skipped=0):
+        out = []
+        for m in range(1, members):
+            pairs = [(d, d ^ m) for d in range(members)]
+            out.append(lax.ppermute(rows[m - skipped], "expert", pairs))
+        return out
 
     def halve(send, keep):
         size = send.shape[0]
         for step in range(bits):
-            got = step_swap(send, step)
+            got = step_swap(send, halving, step)
             total = keep + got.astype(F32)
             size //= 2
             if step < bits - 1:
@@ -436,30 +434,24 @@
         return total[0]
 
     def gather_units(x):
-        firsts = []
-        for step in reversed(range(bits)):
-            got = step_swap(x, step)
-            firsts.append(got)
+        for step in range(bits):
+            got = step_swap(x, doubling, step)
             x = jnp.concatenate([x, got], axis=0)
-        return x, core_swap(x), firsts[0]
-
-    def later(x, *others):
-        return lax.optimization_barrier((x, *others))[0]
-
-    x_slots = dispatch(ids, here, tokens, None, members, slot)
-    x_rows = [x_slots[0]] + expert_swap(x_slots, 0)
-    weight_gate, weight_up = load((w_gate[0], w_up[0]), (x_slots[1],))
-    dy_slots = dispatch(ids, here, grad_out, gates, members, slot, (weight_gate,))
-    dy_rows = [dy_slots[0]] + expert_swap(dy_slots, 0)
-
-    away, x_all = away_terms(other, x_rows, (weight_gate, weight_up), unit, False, (dy_slots[1],))
-    (weight_down,) = load((w_down[0],), (away,))
-    send, keep = kept_terms(
-        mine, x_all, (weight_gate, weight_up), core_swap(away), unit, False, (weight_down,)
-    )
-    away, dy_all = away_terms(other, dy_rows, (weight_down,), unit, True, (send,))
+        return x, core_swap(x)
+
+    x_slots, dy_slots = dispatch(ids, here, gates, tokens, grad_out, members, slot)
+    x_rows = [x_slots[0]] + expert_swap(x_slots)
+    weight_gate, weight_up, weight_down = load(
+        (w_gate[0], w_up[0], w_down[0]), (x_slots[1], here_ids, there_ids, mine, other)
+    )
+    gate_up = (weight_gate, weight_up)
+    dy_rows = [dy_slots[0]] + expert_swap(dy_slots)
+
+    away, x_all = away_terms(there_ids, x_rows, gate_up, unit, False)
+    send, keep = kept_terms(here_ids, x_all, gate_up, core_swap(away), unit, False)
+    away, dy_all = away_terms(there_ids, dy_rows, (weight_down,), unit, True, (send,))
     gate, up = halve(send, keep)
-    send, keep = kept_terms(mine, dy_all, (weight_down,), core_swap(away), unit, True)
+    send, keep = kept_terms(here_ids, dy_all, (weight_down,), core_swap(away), unit, True)
     (d_hidden,) = halve(send, keep)
 
     sigma = jax.nn.sigmoid(gate)
@@ -470,29 +462,28 @@
     d_far = jnp.stack([d_gate[slot:], d_up[slot:]])[None]
     d_own = jnp.stack([d_gate[:slot], d_up[:slot]])[None]
 
-    hidden_mine, hidden_other, _ = gather_units(hidden[None, None])
-    far_mine, far_other, first = gather_units(d_far)
-    own_mine, own_other, _ = gather_units(later(d_own, first))
+    hidden_mine, hidden_other = gather_units(hidden[None, None])
+    far_mine, far_other = gather_units(d_far)
+    own_mine, own_other = gather_units(d_own)
 
     hidden_pieces = ((mine, hidden_mine), (other, hidden_other))
     out = unit_rows(hidden_pieces, (weight_down,), unit, True, split=slot)
-    out_back = expert_swap(out, 0)
+    out_back = expert_swap(out)
     (grad_w_down,) = weight_grads(
         [(i, (u,)) for i, u in hidden_pieces], dy_all, unit, True, (out[0],)
     )
 
-    gate_up = (weight_gate, weight_up)
-    (back,) = unit_rows(((mine, far_mine),), gate_up, unit, False, after=(grad_w_down,))
+    (back,) = unit_rows(((mine, far_mine),), gate_up, unit, False, after=(out[0],))
     far = unit_rows(((other, far_other),), gate_up, unit, False, back, slot)
     grad_back = expert_swap(far, 1)
+    mixed = collect(ids, here, [out[0]] + out_back, gates, members, slot, (in_hbm(grad_w_down),))
     (own,) = unit_rows(
-        ((mine, own_mine), (other, own_other)), gate_up, unit, False, None, slot, (far[0],)
+        ((mine, own_mine), (other, own_other)), gate_up, unit, False, None, slot, (mixed,)
     )
     grad_w_gate, grad_w_up = weight_grads(
         ((mine, (own_mine, far_mine)), (other, (own_other, far_other))), x_all, unit, False, (own,)
     )
 
-    mixed = collect(ids, here, [out[0]] + out_back, gates, members, slot)
     grad_tokens = collect(ids, here, [own] + grad_back, None, members, slot)
     return (mixed, grad_tokens, grad_w_gate, grad_w_up, grad_w_down)
 

time: 115 us -> 101 us (0.88)
  waiting for transfers between devices: 27.9 us -> 40.9 us
  local copies, waits for them, and re-layouts: 13.4 us -> 1.01 us
  starting transfers between devices: 38.2 us -> 28.5 us
  Pallas kernels: 33.3 us -> 28.4 us
    ppermute x22, waiting for transfers between devices: 27.9 us -> 40.8 us  [the longest x10 37.1 us: step_swap(): return lax.ppermute(x, 'tensor', pairs)]
    unnamed x28 -> x6, local copies, waits for them, and re-layouts: 13.3 us -> 0.95 us
    ppermute x22, starting transfers between devices: 37.9 us -> 28.2 us  [the longest x12 15.3 us: expert_swap(): out.append(lax.ppermute(rows[m - skipped], 'expert', pairs))]
    pallas_call x16 -> x14, Pallas kernels: 33.3 us -> 28.4 us  [call(): pl.pallas_call(body, out_shape=list(outs), in_specs=list(in_specs) + [ANY...]
  transfers between devices with their start and end apart: 27 -> 27, of which waited for: 7 -> 13; matrix products, arithmetic and copies ran while one was open for 1% -> 1% of each run, Pallas kernels for 25% -> 21%
where the time goes in v3:
time: 101 us
  waiting for transfers between devices  40.9 us (40%)
  starting transfers between devices  28.5 us (28%)
  Pallas kernels  28.4 us (28%)
  between operations  1.04 us (1%)
  local copies, waits for them, and re-layouts  1.01 us (1%)
    ppermute x10, waiting for transfers between devices, step_swap(): return lax.ppermute(x, 'tensor', pairs)  37.1 us
    pallas_call x14, Pallas kernels, call(): pl.pallas_call(body, out_shape=list(outs), in_specs=list(in_specs) + [ANY...  28.4 us
    ppermute x12, starting transfers between devices, expert_swap(): out.append(lax.ppermute(rows[m - skipped], 'expert', pairs))  15.3 us
    ppermute x10, starting transfers between devices, step_swap(): return lax.ppermute(x, 'tensor', pairs)  12.9 us
    ppermute x12, waiting for transfers between devices, expert_swap(): out.append(lax.ppermute(rows[m - skipped], 'expert', pairs))  3.78 us
  transfers between devices with their start and end apart: 27, of which 13 were waited for; matrix products, arithmetic and copies ran while one was open for 1% of the time, Pallas kernels for 21%

profile of v3, /device:TPU:0, one launch (start us, length us, event | category | flops | bytes accessed | tf_op | source)
XLA Modules:
  0.0 100.5 jit_solution(5399844910082390033)
XLA Ops:
  0.6 1.5 %shard_map.110 = (bf16[48,896]{1,0:T(8,128)(2,1)S(1)}, bf16[48,896]{1,0:T(8,128)(2,1)S(1)}, bf16[48,896]{1,0:T(8,128)(2,1)S(1)}, bf16[48,896]{1,0:T(8,128)(2,1)S...) custom-call(s32[1]{0:T(128)} %bitcast.refs_0_, ...), custom_call_target="tpu_custom_call" | custom-call | flops 88080384 | bytes 1147652 | tf_op jit(solution)/shard_map/pallas_call | solution.py:105
  2.2 3.1 %collective-permute-start.1 = (bf16[48,896]{1,0:T(8,128)(2,1)S(1)}, bf16[48,896]{1,0:T(8,128)(2,1)S(1)}, u32[]{:S(2)}, u32[]{:S(2)}) collective-permute-start(bf16[48,896]{1,0:T(8,128)(2,1)S(1)} %get-tuple-element.35), channel_id=1, source_target_pairs={{0,16},{8,24},{16,0},{24,8},{1,17},{9,25},{17,1},{25,9},{2,18},{10... | collective-permute-start | bytes 258056 | tf_op jit(solution)/shard_map/ppermute | solution.py:423
  5.2 1.4 %collective-permute-start.2 = (bf16[48,896]{1,0:T(8,128)(2,1)S(1)}, bf16[48,896]{1,0:T(8,128)(2,1)S(1)}, u32[]{:S(2)}, u32[]{:S(2)}) collective-permute-start(bf16[48,896]{1,0:T(8,128)(2,1)S(1)} %get-tuple-element.36), channel_id=1, source_target_pairs={{0,24},{8,16},{16,8},{24,0},{1,25},{9,17},{17,9},{25,1},{2,26},{10... | collective-permute-start | bytes 258056 | tf_op jit(solution)/shard_map/ppermute | solution.py:423
  6.6 0.1 collective-permute-start
  6.8 4.2 %shard_map.111 = (bf16[896,2048]{1,0:T(8,128)(2,1)S(1)}, bf16[896,2048]{1,0:T(8,128)(2,1)S(1)}, bf16[2048,896]{1,0:T(8,128)(2,1)S(1)}) custom-call(bf16[896,2048]{1,0:T(8,128)(2,1)} %bitcast.59, bf16[896,2048]{1,0:T(8,128)(2,1)} %bitcast.60, bf16[2048,896]{1,0:T(8,128)(2,1)} %bitcast.61, bf16[48,896]{1,0:T(8,128)(2,1)S(1)} %get-tuple-element.34.refs_3_, ...), custom_call_target="tpu_custom_call" | custom-call | bytes 22020096 | tf_op jit(solution)/shard_map/pallas_call | solution.py:105
  11.0 0.0 collective-permute-done.1.refs_3_
  11.0 0.3 collective-permute-done.2.refs_4_
  11.3 0.0 collective-permute-done.refs_2_
  11.3 1.6 %shard_map.112 = (bf16[4,2,192,256]{3,2,1,0:T(8,128)(2,1)S(1)}, bf16[192,896]{1,0:T(8,128)(2,1)S(1)}) custom-call(s32[4]{0:T(128)S(1)} %get-tuple-element.66.refs_5_.refs_0_, bf16[48,896]{1,0:T(8,128)(2,1)S(1)} %get-tuple-element.33.refs_1_, bf16[48,896]{1,0:T(8,128)(2,1)S(1)} %collective-permute-done.refs_2_, ...), custom_call_target="tpu_custom_call" | custom-call | flops 704643072 | bytes 8814608 | tf_op jit(solution)/shard_map/pallas_call | solution.py:105
  12.9 0.1 collective-permute-start.3
  13.0 1.7 %collective-permute-start.12 = (bf16[48,896]{1,0:T(8,128)(2,1)S(1)}, bf16[48,896]{1,0:T(8,128)(2,1)S(1)}, u32[]{:S(2)}, u32[]{:S(2)}) collective-permute-start(bf16[48,896]{1,0:T(8,128)(2,1)S(1)} %get-tuple-element.49), channel_id=1, source_target_pairs={{0,8},{8,0},{16,24},{24,16},{1,9},{9,1},{17,25},{25,17},{2,10},{10... | collective-permute-start | bytes 258056 | tf_op jit(solution)/shard_map/ppermute | solution.py:423
  14.7 1.5 %collective-permute-start.13 = (bf16[48,896]{1,0:T(8,128)(2,1)S(1)}, bf16[48,896]{1,0:T(8,128)(2,1)S(1)}, u32[]{:S(2)}, u32[]{:S(2)}) collective-permute-start(bf16[48,896]{1,0:T(8,128)(2,1)S(1)} %get-tuple-element.50), channel_id=1, source_target_pairs={{0,16},{8,24},{16,0},{24,8},{1,17},{9,25},{17,1},{25,9},{2,18},{10... | collective-permute-start | bytes 258056 | tf_op jit(solution)/shard_map/ppermute | solution.py:423
  16.2 0.3 collective-permute-start.14
  16.5 0.0 collective-permute-done.3.refs_4_
  16.5 1.6 %shard_map.113 = (bf16[2,2,192,256]{3,2,1,0:T(8,128)(2,1)S(1)}, f32[2,2,192,256]{3,2,1,0:T(8,128)S(1)}) custom-call(s32[4]{0:T(128)S(1)} %get-tuple-element.65.refs_4_.refs_0_, bf16[192,896]{1,0:T(8,128)(2,1)S(1)} %get-tuple-element.39.refs_1_.refs_6_, bf16[896,2048]{1,0:T(8,128)(2,1)S(1)} %get-tuple-element.37.refs_5_.refs_2_.refs_4_, ...), custom_call_target="tpu_custom_call" | custom-call | flops 704643072 | bytes 9650192 | tf_op jit(solution)/shard_map/pallas_call | solution.py:105
  18.1 2.1 %collective-permute-done.13.refs_3_ = bf16[48,896]{1,0:T(8,128)(2,1)S(1)} collective-permute-done((bf16[48,896]{1,0:T(8,128)(2,1)S(1)}, bf16[48,896]{1,0:T(8,128)(2,1)S(1)}, u32[]{:S(2)}, u32[]{:S(2)}) %collective-permute-start.13) | collective-permute-done | bytes 86048 | tf_op jit(solution)/shard_map/ppermute | solution.py:423
  20.2 1.4 %collective-permute-done.14.refs_4_ = bf16[48,896]{1,0:T(8,128)(2,1)S(1)} collective-permute-done((bf16[48,896]{1,0:T(8,128)(2,1)S(1)}, bf16[48,896]{1,0:T(8,128)(2,1)S(1)}, u32[]{:S(2)}, u32[]{:S(2)}) %collective-permute-start.14) | collective-permute-done | bytes 86048 | tf_op jit(solution)/shard_map/ppermute | solution.py:423
  21.6 1.3 %shard_map.115 = (bf16[4,1,192,256]{3,2,1,0:T(8,128)(2,1)S(1)}, bf16[192,896]{1,0:T(8,128)(2,1)S(1)}) custom-call(s32[4]{0:T(128)S(1)} %get-tuple-element.66.refs_5_.refs_0_, bf16[48,896]{1,0:T(8,128)(2,1)S(1)} %get-tuple-element.48.refs_1_, bf16[48,896]{1,0:T(8,128)(2,1)S(1)} %collective-permute-done.12.refs_2_, ...), custom_call_target="tpu_custom_call" | custom-call | flops 352321536 | bytes 4751376 | tf_op jit(solution)/shard_map/pallas_call | solution.py:105
  22.9 0.1 collective-permute-start.15
  23.0 1.7 %collective-permute-start.4 = (bf16[2,2,192,256]{3,2,1,0:T(8,128)(2,1)S(1)}, bf16[2,2,192,256]{3,2,1,0:T(8,128)(2,1)S(1)}, u32[]{:S(2)}, u32[]{:S(2)}) collective-permute-start(bf16[2,2,192,256]{3,2,1,0:T(8,128)(2,1)S(1)} %get-tuple-element.42.refs_6_), channel_id=1, source_target_pairs={{0,2},{1,5},{2,0},{3,7},{4,6},{5,1},{6,4},{7,3},{8,10},{9,13},{10,... | collective-permute-start | bytes 1179656 | tf_op jit(solution)/shard_map/ppermute | solution.py:397
  24.6 0.1 collective-permute-done.15.refs_3_
  24.7 1.3 %shard_map.118 = (bf16[2,1,192,256]{3,2,1,0:T(8,128)(2,1)S(1)}, f32[2,1,192,256]{3,2,1,0:T(8,128)S(1)}) custom-call(s32[4]{0:T(128)S(1)} %get-tuple-element.65.refs_4_.refs_0_, bf16[192,896]{1,0:T(8,128)(2,1)S(1)} %get-tuple-element.52.refs_4_.refs_1_, bf16[2048,896]{1,0:T(8,128)(2,1)S(1)} %get-tuple-element.43.refs_4_.refs_5_.refs_2_, ...), custom_call_target="tpu_custom_call" | custom-call | flops 352321536 | bytes 4997136 | tf_op jit(solution)/shard_map/pallas_call | solution.py:105
  26.0 1.7 %collective-permute-start.16 = (bf16[2,1,192,256]{3,2,1,0:T(8,128)(2,1)S(1)}, bf16[2,1,192,256]{3,2,1,0:T(8,128)(2,1)S(1)}, u32[]{:S(2)}, u32[]{:S(2)}) collective-permute-start(bf16[2,1,192,256]{3,2,1,0:T(8,128)(2,1)S(1)} %get-tuple-element.55), channel_id=1, source_target_pairs={{0,2},{1,5},{2,0},{3,7},{4,6},{5,1},{6,4},{7,3},{8,10},{9,13},{10,... | collective-permute-start | bytes 589832 | tf_op jit(solution)/shard_map/ppermute | solution.py:397
  27.7 7.3 %collective-permute-done.4 = bf16[2,2,192,256]{3,2,1,0:T(8,128)(2,1)S(1)} collective-permute-done((bf16[2,2,192,256]{3,2,1,0:T(8,128)(2,1)S(1)}, bf16[2,2,192,256]{3,2,1,0:T(8,128)(2,1)S(1)}, u32[]{:S(2)}, u32[]{:S(2)}) %collective-permute-start.4) | collective-permute-done | bytes 393248 | tf_op jit(solution)/shard_map/ppermute | solution.py:397
  35.0 0.1 convert_add_fusion
  35.1 2.7 %collective-permute-start.5 = (bf16[1,2,192,256]{3,2,1,0:T(8,128)(2,1)S(1)}, bf16[1,2,192,256]{3,2,1,0:T(8,128)(2,1)S(1)}, u32[]{:S(2)}, u32[]{:S(2)}) collective-permute-start(bf16[1,2,192,256]{3,2,1,0:T(8,128)(2,1)S(1)} %slice.58), channel_id=1, source_target_pairs={{0,4},{1,3},{2,6},{3,1},{4,0},{5,7},{6,2},{7,5},{8,12},{9,11},{10,... | collective-permute-start | bytes 589832 | tf_op jit(solution)/shard_map/ppermute | solution.py:397
  37.8 3.7 %collective-permute-done.16 = bf16[2,1,192,256]{3,2,1,0:T(8,128)(2,1)S(1)} collective-permute-done((bf16[2,1,192,256]{3,2,1,0:T(8,128)(2,1)S(1)}, bf16[2,1,192,256]{3,2,1,0:T(8,128)(2,1)S(1)}, u32[]{:S(2)}, u32[]{:S(2)}) %collective-permute-start.16) | collective-permute-done | bytes 196640 | tf_op jit(solution)/shard_map/ppermute | solution.py:397
  41.6 0.4 collective-permute-start.17
  41.9 1.2 %collective-permute-done.5 = bf16[1,2,192,256]{3,2,1,0:T(8,128)(2,1)S(1)} collective-permute-done((bf16[1,2,192,256]{3,2,1,0:T(8,128)(2,1)S(1)}, bf16[1,2,192,256]{3,2,1,0:T(8,128)(2,1)S(1)}, u32[]{:S(2)}, u32[]{:S(2)}) %collective-permute-start.5) | collective-permute-done | bytes 196640 | tf_op jit(solution)/shard_map/ppermute | solution.py:397
  43.2 0.1 multiply_convert_fusion
  43.2 3.4 %collective-permute-start.6 = (bf16[1,1,192,256]{3,2,1,0:T(8,128)(2,1)S(1)}, bf16[1,1,192,256]{3,2,1,0:T(8,128)(2,1)S(1)}, u32[]{:S(2)}, u32[]{:S(2)}) collective-permute-start(bf16[1,1,192,256]{3,2,1,0:T(8,128)(2,1)S(1)} %multiply_convert_fusion), channel_id=1, source_target_pairs={{0,4},{1,5},{2,6},{3,7},{4,0},{5,1},{6,2},{7,3},{8,12},{9,13},{10,... | collective-permute-start | bytes 294920 | tf_op jit(solution)/shard_map/ppermute | solution.py:397
  46.7 2.8 %collective-permute-done.17 = bf16[1,1,192,256]{3,2,1,0:T(8,128)(2,1)S(1)} collective-permute-done((bf16[1,1,192,256]{3,2,1,0:T(8,128)(2,1)S(1)}, bf16[1,1,192,256]{3,2,1,0:T(8,128)(2,1)S(1)}, u32[]{:S(2)}, u32[]{:S(2)}) %collective-permute-start.17) | collective-permute-done | bytes 98336 | tf_op jit(solution)/shard_map/ppermute | solution.py:397
  49.4 0.1 fusion.6
  49.6 0.1 collective-permute-start.21
  49.7 6.1 %collective-permute-done.6 = bf16[1,1,192,256]{3,2,1,0:T(8,128)(2,1)S(1)} collective-permute-done((bf16[1,1,192,256]{3,2,1,0:T(8,128)(2,1)S(1)}, bf16[1,1,192,256]{3,2,1,0:T(8,128)(2,1)S(1)}, u32[]{:S(2)}, u32[]{:S(2)}) %collective-permute-start.6) | collective-permute-done | bytes 98336 | tf_op jit(solution)/shard_map/ppermute | solution.py:397
  55.8 0.1 collective-permute-start.7
  55.9 2.5 %collective-permute-done.21 = bf16[1,2,144,256]{3,2,1,0:T(8,128)(2,1)S(1)} collective-permute-done((bf16[1,2,144,256]{3,2,1,0:T(8,128)(2,1)S(1)}, bf16[1,2,144,256]{3,2,1,0:T(8,128)(2,1)S(1)}, u32[]{:S(2)}, u32[]{:S(2)}) %collective-permute-start.21) | collective-permute-done | bytes 147488 | tf_op jit(solution)/shard_map/ppermute | solution.py:397
  58.4 0.1 collective-permute-start.22
  58.5 2.7 %collective-permute-start.18 = (bf16[1,2,48,256]{3,2,1,0:T(8,128)(2,1)S(1)}, bf16[1,2,48,256]{3,2,1,0:T(8,128)(2,1)S(1)}, u32[]{:S(2)}, u32[]{:S(2)}) collective-permute-start(bf16[1,2,48,256]{3,2,1,0:T(8,128)(2,1)S(1)} %maximum_bitcast_fusion.1), channel_id=1, source_target_pairs={{0,4},{1,5},{2,6},{3,7},{4,0},{5,1},{6,2},{7,3},{8,12},{9,13},{10,... | collective-permute-start | bytes 147464 | tf_op jit(solution)/shard_map/ppermute | solution.py:397
  61.2 3.4 %collective-permute-done.7 = bf16[2,1,192,256]{3,2,1,0:T(8,128)(2,1)S(1)} collective-permute-done((bf16[2,1,192,256]{3,2,1,0:T(8,128)(2,1)S(1)}, bf16[2,1,192,256]{3,2,1,0:T(8,128)(2,1)S(1)}, u32[]{:S(2)}, u32[]{:S(2)}) %collective-permute-start.7) | collective-permute-done | bytes 196640 | tf_op jit(solution)/shard_map/ppermute | solution.py:397
  64.7 0.1 collective-permute-start.8
  64.8 5.0 %collective-permute-done.22 = bf16[2,2,144,256]{3,2,1,0:T(8,128)(2,1)S(1)} collective-permute-done((bf16[2,2,144,256]{3,2,1,0:T(8,128)(2,1)S(1)}, bf16[2,2,144,256]{3,2,1,0:T(8,128)(2,1)S(1)}, u32[]{:S(2)}, u32[]{:S(2)}) %collective-permute-start.22) | collective-permute-done | bytes 294944 | tf_op jit(solution)/shard_map/ppermute | solution.py:397
  69.9 0.1 pad_maximum_fusion.refs_1_.refs_3_
  69.9 0.1 collective-permute-start.23
  70.0 0.1 collective-permute-start.19
  70.2 5.1 %collective-permute-done.19 = bf16[2,2,48,256]{3,2,1,0:T(8,128)(2,1)S(1)} collective-permute-done((bf16[2,2,48,256]{3,2,1,0:T(8,128)(2,1)S(1)}, bf16[2,2,48,256]{3,2,1,0:T(8,128)(2,1)S(1)}, u32[]{:S(2)}, u32[]{:S(2)}) %collective-permute-start.19) | collective-permute-done | bytes 98336 | tf_op jit(solution)/shard_map/ppermute | solution.py:397
  75.3 0.1 collective-permute-start.20
  75.4 1.6 %shard_map.114 = (bf16[48,896]{1,0:T(8,128)(2,1)S(1)}, bf16[48,896]{1,0:T(8,128)(2,1)S(1)}, bf16[48,896]{1,0:T(8,128)(2,1)S(1)}, bf16[48,896]{1,0:T(8,128)(2,1)S(1)}) custom-call(s32[4]{0:T(128)S(1)} %get-tuple-element.63.refs_6_.refs_0_, s32[4]{0:T(128)S(1)} %get-tuple-element.64.refs_7_.refs_1_.refs_0_, ...), custom_call_target="tpu_custom_call" | custom-call | flops 704643072 | bytes 4800544 | tf_op jit(solution)/shard_map/pallas_call | solution.py:105
  77.0 0.8 collective-permute-start.9
  77.8 0.8 collective-permute-start.10
  78.6 1.9 %collective-permute-start.11 = (bf16[48,896]{1,0:T(8,128)(2,1)S(1)}, bf16[48,896]{1,0:T(8,128)(2,1)S(1)}, u32[]{:S(2)}, u32[]{:S(2)}) collective-permute-start(bf16[48,896]{1,0:T(8,128)(2,1)S(1)} %get-tuple-element.47), channel_id=1, source_target_pairs={{0,24},{8,16},{16,8},{24,0},{1,25},{9,17},{17,9},{25,1},{2,26},{10... | collective-permute-start | bytes 258056 | tf_op jit(solution)/shard_map/ppermute | solution.py:423
  80.5 1.8 %shard_map.120.refs_4_ = f32[144,896]{1,0:T(8,128)S(1)} custom-call(s32[4]{0:T(128)S(1)} %get-tuple-element.63.refs_6_.refs_0_, bf16[4,2,144,256]{3,2,1,0:T(8,128)(2,1)S(1)} %pad_maximum_fusion.refs_1_.refs_3_, bf16[896,2048]{1,0:T(8,128)(2,1)S(1)} %get-tuple-element.37.refs_5_.refs_2_.refs_4_, ...), custom_call_target="tpu_custom_call" | custom-call | flops 528482304 | bytes 8445968 | tf_op jit(solution)/shard_map/pallas_call | solution.py:105
  82.3 0.0 copy-start.1
  82.3 0.0 copy-start.2
  82.3 2.8 %shard_map.116.refs_7_ = bf16[1,2048,896]{2,1,0:T(8,128)(2,1)} custom-call(s32[4]{0:T(128)S(1)} %get-tuple-element.63.refs_6_.refs_0_, s32[4]{0:T(128)S(1)} %get-tuple-element.64.refs_7_.refs_1_.refs_0_, bf16[4,1,192,256]{3,2,1,0:T(8,128)(2,1)S(1)} %pad_maximum_fusion.1.refs_2_, bf16[4,1,192,256]{3,2,1,0:T(8,128)(2,1)S(1)} %collective-permute-done.8.refs_3_, ...), custom_call_target="tpu_custom_call" | custom-call | flops 704643072 | bytes 4800544 | tf_op jit(solution)/shard_map/pallas_call | solution.py:105
  85.1 1.1 %shard_map.117.refs_6_ = bf16[128,896]{1,0:T(8,128)(2,1)} custom-call(s32[1]{0:T(128)} %bitcast.refs_0_, s32[1,128]{1,0:T(1,128)S(1)} %bitcast.55, bf16[1,128]{1,0:T(2,128)(2,1)S(1)} %bitcast.58, bf16[48,896]{1,0:T(8,128)(2,1)S(1)} %get-tuple-element.44.refs_5_.refs_3_.refs_4_, bf16[48,896]{1,0:T(8,128)(2,1)S(1)} %collective-permute-done.9.refs_4_, ...), custom_call_target="tpu_custom_call" | custom-call | flops 44040192 | bytes 574212 | tf_op jit(solution)/shard_map/pallas_call | solution.py:105
  86.2 0.9 copy-done
  87.2 2.7 %shard_map.119.refs_2_.refs_7_ = bf16[48,896]{1,0:T(8,128)(2,1)S(1)} custom-call(s32[4]{0:T(128)S(1)} %get-tuple-element.63.refs_6_.refs_0_, s32[4]{0:T(128)S(1)} %get-tuple-element.64.refs_7_.refs_1_.refs_0_, bf16[4,2,48,256]{3,2,1,0:T(8,128)(2,1)S(1)} %pad_maximum_fusion.4.refs_2_, bf16[4,2,48,256]{3,2,1,0:T(8,128)(2,1)S(1)} %collective-permute-done.20.refs_3_.refs_4_, ...), custom_call_target="tpu_custom_call" | custom-call | flops 352321536 | bytes 7819296 | tf_op jit(solution)/shard_map/pallas_call | solution.py:105
  89.9 1.8 %shard_map.121 = (bf16[48,896]{1,0:T(8,128)(2,1)S(1)}, bf16[48,896]{1,0:T(8,128)(2,1)S(1)}, bf16[48,896]{1,0:T(8,128)(2,1)S(1)}) custom-call(s32[4]{0:T(128)S(1)} %get-tuple-element.64.refs_7_.refs_1_.refs_0_, bf16[4,2,144,256]{3,2,1,0:T(8,128)(2,1)S(1)} %collective-permute-done.23.refs_1_.refs_5_, ...), custom_call_target="tpu_custom_call" | custom-call | flops 528482304 | bytes 8704016 | tf_op jit(solution)/shard_map/pallas_call | solution.py:105
  91.7 0.8 collective-permute-start.24
  92.6 0.8 collective-permute-start.25
  93.4 1.9 %collective-permute-start.26 = (bf16[48,896]{1,0:T(8,128)(2,1)S(1)}, bf16[48,896]{1,0:T(8,128)(2,1)S(1)}, u32[]{:S(2)}, u32[]{:S(2)}) collective-permute-start(bf16[48,896]{1,0:T(8,128)(2,1)S(1)} %get-tuple-element.58), channel_id=1, source_target_pairs={{0,24},{8,16},{16,8},{24,0},{1,25},{9,17},{17,9},{25,1},{2,26},{10... | collective-permute-start | bytes 258056 | tf_op jit(solution)/shard_map/ppermute | solution.py:423
  95.3 4.1 %shard_map.123 = (bf16[1,896,2048]{2,1,0:T(8,128)(2,1)}, bf16[1,896,2048]{2,1,0:T(8,128)(2,1)}) custom-call(s32[4]{0:T(128)S(1)} %get-tuple-element.63.refs_6_.refs_0_, s32[4]{0:T(128)S(1)} %get-tuple-element.64.refs_7_.refs_1_.refs_0_, bf16[4,2,48,256]{3,2,1,0:T(8,128)(2,1)S(1)} %pad_maximum_fusion.4.refs_2_, ...), custom_call_target="tpu_custom_call" | custom-call | flops 1409286144 | bytes 9256992 | tf_op jit(solution)/shard_map/pallas_call | solution.py:105
  99.4 1.1 %shard_map.122 = bf16[128,896]{1,0:T(8,128)(2,1)} custom-call(s32[1]{0:T(128)} %bitcast.refs_0_, s32[1,128]{1,0:T(1,128)S(1)} %bitcast.56, bf16[48,896]{1,0:T(8,128)(2,1)S(1)} %shard_map.119.refs_2_.refs_7_, bf16[48,896]{1,0:T(8,128)(2,1)S(1)} %collective-permute-done.24.refs_3_, bf16[48,896]{1,0:T(8,128)(2,1)S(1)} %collective-permute-done.25.refs_4_, ...), custom_call_target="tpu_custom_call" | custom-call | flops 44040192 | bytes 573956 | tf_op jit(solution)/shard_map/pallas_call | solution.py:105
  (31 shorter events, 0.3 us)
Async XLA Ops:
  2.2 8.9 %collective-permute-start.1 = (bf16[48,896]{1,0:T(8,128)(2,1)S(1)}, bf16[48,896]{1,0:T(8,128)(2,1)S(1)}, u32[]{:S(2)}, u32[]{:S(2)}) collective-permute-start(bf16[48,896]{1,0:T(8,128)(2,1)S(1)} %get-tuple-element.35), channel_id=1, source_target_pairs={{0,16},{8,24},{16,0},{24,8},{1,17},{9,25},{17,1},{25,9},{2,18},{10... | collective-permute-start | bytes 258056 | tf_op jit(solution)/shard_map/ppermute | solution.py:423
  5.2 6.1 %collective-permute-start.2 = (bf16[48,896]{1,0:T(8,128)(2,1)S(1)}, bf16[48,896]{1,0:T(8,128)(2,1)S(1)}, u32[]{:S(2)}, u32[]{:S(2)}) collective-permute-start(bf16[48,896]{1,0:T(8,128)(2,1)S(1)} %get-tuple-element.36), channel_id=1, source_target_pairs={{0,24},{8,16},{16,8},{24,0},{1,25},{9,17},{17,9},{25,1},{2,26},{10... | collective-permute-start | bytes 258056 | tf_op jit(solution)/shard_map/ppermute | solution.py:423
  6.6 4.7 %collective-permute-start = (bf16[48,896]{1,0:T(8,128)(2,1)S(1)}, bf16[48,896]{1,0:T(8,128)(2,1)S(1)}, u32[]{:S(2)}, u32[]{:S(2)}) collective-permute-start(bf16[48,896]{1,0:T(8,128)(2,1)S(1)} %get-tuple-element.34.refs_3_), channel_id=1, source_target_pairs={{0,8},{8,0},{16,24},{24,16},{1,9},{9,1},{17,25},{25,17},{2,10},{10... | collective-permute-start | bytes 258056 | tf_op jit(solution)/shard_map/ppermute | solution.py:423
  12.9 3.6 %collective-permute-start.3 = (bf16[4,2,192,256]{3,2,1,0:T(8,128)(2,1)S(1)}, bf16[4,2,192,256]{3,2,1,0:T(8,128)(2,1)S(1)}, u32[]{:S(2)}, u32[]{:S(2)}) collective-permute-start(bf16[4,2,192,256]{3,2,1,0:T(8,128)(2,1)S(1)} %get-tuple-element.40), channel_id=1, source_target_pairs={{0,1},{1,0},{2,3},{3,2},{4,5},{5,4},{6,7},{7,6},{8,9},{9,8},{10,11... | collective-permute-start | bytes 2359304 | tf_op jit(solution)/shard_map/ppermute | solution.py:400
  13.0 5.1 %collective-permute-start.12 = (bf16[48,896]{1,0:T(8,128)(2,1)S(1)}, bf16[48,896]{1,0:T(8,128)(2,1)S(1)}, u32[]{:S(2)}, u32[]{:S(2)}) collective-permute-start(bf16[48,896]{1,0:T(8,128)(2,1)S(1)} %get-tuple-element.49), channel_id=1, source_target_pairs={{0,8},{8,0},{16,24},{24,16},{1,9},{9,1},{17,25},{25,17},{2,10},{10... | collective-permute-start | bytes 258056 | tf_op jit(solution)/shard_map/ppermute | solution.py:423
  14.7 5.5 %collective-permute-start.13 = (bf16[48,896]{1,0:T(8,128)(2,1)S(1)}, bf16[48,896]{1,0:T(8,128)(2,1)S(1)}, u32[]{:S(2)}, u32[]{:S(2)}) collective-permute-start(bf16[48,896]{1,0:T(8,128)(2,1)S(1)} %get-tuple-element.50), channel_id=1, source_target_pairs={{0,16},{8,24},{16,0},{24,8},{1,17},{9,25},{17,1},{25,9},{2,18},{10... | collective-permute-start | bytes 258056 | tf_op jit(solution)/shard_map/ppermute | solution.py:423
  16.2 5.4 %collective-permute-start.14 = (bf16[48,896]{1,0:T(8,128)(2,1)S(1)}, bf16[48,896]{1,0:T(8,128)(2,1)S(1)}, u32[]{:S(2)}, u32[]{:S(2)}) collective-permute-start(bf16[48,896]{1,0:T(8,128)(2,1)S(1)} %get-tuple-element.51), channel_id=1, source_target_pairs={{0,24},{8,16},{16,8},{24,0},{1,25},{9,17},{17,9},{25,1},{2,26},{10... | collective-permute-start | bytes 258056 | tf_op jit(solution)/shard_map/ppermute | solution.py:423
  22.9 1.8 %collective-permute-start.15 = (bf16[4,1,192,256]{3,2,1,0:T(8,128)(2,1)S(1)}, bf16[4,1,192,256]{3,2,1,0:T(8,128)(2,1)S(1)}, u32[]{:S(2)}, u32[]{:S(2)}) collective-permute-start(bf16[4,1,192,256]{3,2,1,0:T(8,128)(2,1)S(1)} %get-tuple-element.53), channel_id=1, source_target_pairs={{0,1},{1,0},{2,3},{3,2},{4,5},{5,4},{6,7},{7,6},{8,9},{9,8},{10,11... | collective-permute-start | bytes 1179656 | tf_op jit(solution)/shard_map/ppermute | solution.py:400
  23.0 12.0 %collective-permute-start.4 = (bf16[2,2,192,256]{3,2,1,0:T(8,128)(2,1)S(1)}, bf16[2,2,192,256]{3,2,1,0:T(8,128)(2,1)S(1)}, u32[]{:S(2)}, u32[]{:S(2)}) collective-permute-start(bf16[2,2,192,256]{3,2,1,0:T(8,128)(2,1)S(1)} %get-tuple-element.42.refs_6_), channel_id=1, source_target_pairs={{0,2},{1,5},{2,0},{3,7},{4,6},{5,1},{6,4},{7,3},{8,10},{9,13},{10,... | collective-permute-start | bytes 1179656 | tf_op jit(solution)/shard_map/ppermute | solution.py:397
  26.0 15.5 %collective-permute-start.16 = (bf16[2,1,192,256]{3,2,1,0:T(8,128)(2,1)S(1)}, bf16[2,1,192,256]{3,2,1,0:T(8,128)(2,1)S(1)}, u32[]{:S(2)}, u32[]{:S(2)}) collective-permute-start(bf16[2,1,192,256]{3,2,1,0:T(8,128)(2,1)S(1)} %get-tuple-element.55), channel_id=1, source_target_pairs={{0,2},{1,5},{2,0},{3,7},{4,6},{5,1},{6,4},{7,3},{8,10},{9,13},{10,... | collective-permute-start | bytes 589832 | tf_op jit(solution)/shard_map/ppermute | solution.py:397
  35.1 8.0 %collective-permute-start.5 = (bf16[1,2,192,256]{3,2,1,0:T(8,128)(2,1)S(1)}, bf16[1,2,192,256]{3,2,1,0:T(8,128)(2,1)S(1)}, u32[]{:S(2)}, u32[]{:S(2)}) collective-permute-start(bf16[1,2,192,256]{3,2,1,0:T(8,128)(2,1)S(1)} %slice.58), channel_id=1, source_target_pairs={{0,4},{1,3},{2,6},{3,1},{4,0},{5,7},{6,2},{7,5},{8,12},{9,11},{10,... | collective-permute-start | bytes 589832 | tf_op jit(solution)/shard_map/ppermute | solution.py:397
  41.6 7.9 %collective-permute-start.17 = (bf16[1,1,192,256]{3,2,1,0:T(8,128)(2,1)S(1)}, bf16[1,1,192,256]{3,2,1,0:T(8,128)(2,1)S(1)}, u32[]{:S(2)}, u32[]{:S(2)}) collective-permute-start(bf16[1,1,192,256]{3,2,1,0:T(8,128)(2,1)S(1)} %slice.59), channel_id=1, source_target_pairs={{0,4},{1,3},{2,6},{3,1},{4,0},{5,7},{6,2},{7,5},{8,12},{9,11},{10,... | collective-permute-start | bytes 294920 | tf_op jit(solution)/shard_map/ppermute | solution.py:397
  43.2 12.5 %collective-permute-start.6 = (bf16[1,1,192,256]{3,2,1,0:T(8,128)(2,1)S(1)}, bf16[1,1,192,256]{3,2,1,0:T(8,128)(2,1)S(1)}, u32[]{:S(2)}, u32[]{:S(2)}) collective-permute-start(bf16[1,1,192,256]{3,2,1,0:T(8,128)(2,1)S(1)} %multiply_convert_fusion), channel_id=1, source_target_pairs={{0,4},{1,5},{2,6},{3,7},{4,0},{5,1},{6,2},{7,3},{8,12},{9,13},{10,... | collective-permute-start | bytes 294920 | tf_op jit(solution)/shard_map/ppermute | solution.py:397
  49.6 8.7 %collective-permute-start.21 = (bf16[1,2,144,256]{3,2,1,0:T(8,128)(2,1)S(1)}, bf16[1,2,144,256]{3,2,1,0:T(8,128)(2,1)S(1)}, u32[]{:S(2)}, u32[]{:S(2)}) collective-permute-start(bf16[1,2,144,256]{3,2,1,0:T(8,128)(2,1)S(1)} %maximum_bitcast_fusion), channel_id=1, source_target_pairs={{0,4},{1,5},{2,6},{3,7},{4,0},{5,1},{6,2},{7,3},{8,12},{9,13},{10,... | collective-permute-start | bytes 442376 | tf_op jit(solution)/shard_map/ppermute | solution.py:397
  55.8 8.9 %collective-permute-start.7 = (bf16[2,1,192,256]{3,2,1,0:T(8,128)(2,1)S(1)}, bf16[2,1,192,256]{3,2,1,0:T(8,128)(2,1)S(1)}, u32[]{:S(2)}, u32[]{:S(2)}) collective-permute-start(bf16[2,1,192,256]{3,2,1,0:T(8,128)(2,1)S(1)} %pad_maximum_fusion.3), channel_id=1, source_target_pairs={{0,2},{1,3},{2,0},{3,1},{4,6},{5,7},{6,4},{7,5},{8,10},{9,11},{10,... | collective-permute-start | bytes 589832 | tf_op jit(solution)/shard_map/ppermute | solution.py:397
  58.4 11.5 %collective-permute-start.22 = (bf16[2,2,144,256]{3,2,1,0:T(8,128)(2,1)S(1)}, bf16[2,2,144,256]{3,2,1,0:T(8,128)(2,1)S(1)}, u32[]{:S(2)}, u32[]{:S(2)}) collective-permute-start(bf16[2,2,144,256]{3,2,1,0:T(8,128)(2,1)S(1)} %pad_maximum_fusion.2), channel_id=1, source_target_pairs={{0,2},{1,3},{2,0},{3,1},{4,6},{5,7},{6,4},{7,5},{8,10},{9,11},{10,... | collective-permute-start | bytes 884744 | tf_op jit(solution)/shard_map/ppermute | solution.py:397
  58.5 11.5 %collective-permute-start.18 = (bf16[1,2,48,256]{3,2,1,0:T(8,128)(2,1)S(1)}, bf16[1,2,48,256]{3,2,1,0:T(8,128)(2,1)S(1)}, u32[]{:S(2)}, u32[]{:S(2)}) collective-permute-start(bf16[1,2,48,256]{3,2,1,0:T(8,128)(2,1)S(1)} %maximum_bitcast_fusion.1), channel_id=1, source_target_pairs={{0,4},{1,5},{2,6},{3,7},{4,0},{5,1},{6,2},{7,3},{8,12},{9,13},{10,... | collective-permute-start | bytes 147464 | tf_op jit(solution)/shard_map/ppermute | solution.py:397
  64.7 10.6 %collective-permute-start.8 = (bf16[4,1,192,256]{3,2,1,0:T(8,128)(2,1)S(1)}, bf16[4,1,192,256]{3,2,1,0:T(8,128)(2,1)S(1)}, u32[]{:S(2)}, u32[]{:S(2)}) collective-permute-start(bf16[4,1,192,256]{3,2,1,0:T(8,128)(2,1)S(1)} %pad_maximum_fusion.1.refs_2_), channel_id=1, source_target_pairs={{0,1},{1,0},{2,3},{3,2},{4,5},{5,4},{6,7},{7,6},{8,9},{9,8},{10,11... | collective-permute-start | bytes 1179656 | tf_op jit(solution)/shard_map/ppermute | solution.py:400
  69.9 20.0 %collective-permute-start.23 = (bf16[4,2,144,256]{3,2,1,0:T(8,128)(2,1)S(1)}, bf16[4,2,144,256]{3,2,1,0:T(8,128)(2,1)S(1)}, u32[]{:S(2)}, u32[]{:S(2)}) collective-permute-start(bf16[4,2,144,256]{3,2,1,0:T(8,128)(2,1)S(1)} %pad_maximum_fusion.refs_1_.refs_3_), channel_id=1, source_target_pairs={{0,1},{1,0},{2,3},{3,2},{4,5},{5,4},{6,7},{7,6},{8,9},{9,8},{10,11... | collective-permute-start | bytes 1769480 | tf_op jit(solution)/shard_map/ppermute | solution.py:400
  70.0 5.2 %collective-permute-start.19 = (bf16[2,2,48,256]{3,2,1,0:T(8,128)(2,1)S(1)}, bf16[2,2,48,256]{3,2,1,0:T(8,128)(2,1)S(1)}, u32[]{:S(2)}, u32[]{:S(2)}) collective-permute-start(bf16[2,2,48,256]{3,2,1,0:T(8,128)(2,1)S(1)} %pad_maximum_fusion.5), channel_id=1, source_target_pairs={{0,2},{1,3},{2,0},{3,1},{4,6},{5,7},{6,4},{7,5},{8,10},{9,11},{10,... | collective-permute-start | bytes 294920 | tf_op jit(solution)/shard_map/ppermute | solution.py:397
  75.3 10.9 %collective-permute-start.20 = (bf16[4,2,48,256]{3,2,1,0:T(8,128)(2,1)S(1)}, bf16[4,2,48,256]{3,2,1,0:T(8,128)(2,1)S(1)}, u32[]{:S(2)}, u32[]{:S(2)}) collective-permute-start(bf16[4,2,48,256]{3,2,1,0:T(8,128)(2,1)S(1)} %pad_maximum_fusion.4.refs_2_), channel_id=1, source_target_pairs={{0,1},{1,0},{2,3},{3,2},{4,5},{5,4},{6,7},{7,6},{8,9},{9,8},{10,11... | collective-permute-start | bytes 589832 | tf_op jit(solution)/shard_map/ppermute | solution.py:400
  77.0 8.1 %collective-permute-start.9 = (bf16[48,896]{1,0:T(8,128)(2,1)S(1)}, bf16[48,896]{1,0:T(8,128)(2,1)S(1)}, u32[]{:S(2)}, u32[]{:S(2)}) collective-permute-start(bf16[48,896]{1,0:T(8,128)(2,1)S(1)} %get-tuple-element.45), channel_id=1, source_target_pairs={{0,8},{8,0},{16,24},{24,16},{1,9},{9,1},{17,25},{25,17},{2,10},{10... | collective-permute-start | bytes 258056 | tf_op jit(solution)/shard_map/ppermute | solution.py:423
  77.8 7.3 %collective-permute-start.10 = (bf16[48,896]{1,0:T(8,128)(2,1)S(1)}, bf16[48,896]{1,0:T(8,128)(2,1)S(1)}, u32[]{:S(2)}, u32[]{:S(2)}) collective-permute-start(bf16[48,896]{1,0:T(8,128)(2,1)S(1)} %get-tuple-element.46), channel_id=1, source_target_pairs={{0,16},{8,24},{16,0},{24,8},{1,17},{9,25},{17,1},{25,9},{2,18},{10... | collective-permute-start | bytes 258056 | tf_op jit(solution)/shard_map/ppermute | solution.py:423
  78.6 6.5 %collective-permute-start.11 = (bf16[48,896]{1,0:T(8,128)(2,1)S(1)}, bf16[48,896]{1,0:T(8,128)(2,1)S(1)}, u32[]{:S(2)}, u32[]{:S(2)}) collective-permute-start(bf16[48,896]{1,0:T(8,128)(2,1)S(1)} %get-tuple-element.47), channel_id=1, source_target_pairs={{0,24},{8,16},{16,8},{24,0},{1,25},{9,17},{17,9},{25,1},{2,26},{10... | collective-permute-start | bytes 258056 | tf_op jit(solution)/shard_map/ppermute | solution.py:423
  82.3 2.8 %copy-start.1 = (s32[128,1]{0,1:T(1,128)S(1)}, s32[128,1]{0,1:T(1,128)}, u32[]{:S(2)}) copy-start(s32[128,1]{0,1:T(1,128)} %param.9) | copy-start | bytes 1540
  82.3 2.8 %copy-start.2 = (bf16[128,1]{0,1:T(2,128)(2,1)S(1)}, bf16[128,1]{0,1:T(2,128)(2,1)}, u32[]{:S(2)}) copy-start(bf16[128,1]{0,1:T(2,128)(2,1)} %param.8) | copy-start | bytes 772
  86.2 0.9 copy-start
  91.7 7.7 %collective-permute-start.24 = (bf16[48,896]{1,0:T(8,128)(2,1)S(1)}, bf16[48,896]{1,0:T(8,128)(2,1)S(1)}, u32[]{:S(2)}, u32[]{:S(2)}) collective-permute-start(bf16[48,896]{1,0:T(8,128)(2,1)S(1)} %get-tuple-element.56), channel_id=1, source_target_pairs={{0,8},{8,0},{16,24},{24,16},{1,9},{9,1},{17,25},{25,17},{2,10},{10... | collective-permute-start | bytes 258056 | tf_op jit(solution)/shard_map/ppermute | solution.py:423
  92.6 6.9 %collective-permute-start.25 = (bf16[48,896]{1,0:T(8,128)(2,1)S(1)}, bf16[48,896]{1,0:T(8,128)(2,1)S(1)}, u32[]{:S(2)}, u32[]{:S(2)}) collective-permute-start(bf16[48,896]{1,0:T(8,128)(2,1)S(1)} %get-tuple-element.57), channel_id=1, source_target_pairs={{0,16},{8,24},{16,0},{24,8},{1,17},{9,25},{17,1},{25,9},{2,18},{10... | collective-permute-start | bytes 258056 | tf_op jit(solution)/shard_map/ppermute | solution.py:423
  93.4 6.0 %collective-permute-start.26 = (bf16[48,896]{1,0:T(8,128)(2,1)S(1)}, bf16[48,896]{1,0:T(8,128)(2,1)S(1)}, u32[]{:S(2)}, u32[]{:S(2)}) collective-permute-start(bf16[48,896]{1,0:T(8,128)(2,1)S(1)} %get-tuple-element.58), channel_id=1, source_target_pairs={{0,24},{8,16},{16,8},{24,0},{1,25},{9,17},{17,9},{25,1},{2,26},{10... | collective-permute-start | bytes 258056 | tf_op jit(solution)/shard_map/ppermute | solution.py:423

commit v4 on v3

v4 whole, which is shorter than its diff:
```python
import functools

import jax
import jax.numpy as jnp
from jax import lax
from jax.experimental import pallas as pl
from jax.experimental.pallas import tpu as pltpu
from jax.sharding import PartitionSpec as P


F32 = jnp.float32
BF16 = jnp.bfloat16


def spread_units(function):
    return lax.psum_scatter(function(), "tensor", scatter_dimension=0, tiled=True)


def general(tokens, gate_weights, expert_ids, w_gate, w_up, w_down, grad_out):
    members = lax.axis_size("expert")
    tok_rows = tokens.shape[0]
    routes = expert_ids.shape[1]
    width = tokens.shape[1]
    slot = 3 * routes * tok_rows // (2 * members)
    total = members * slot
    flat_ids = expert_ids.reshape(-1)
    counted = (flat_ids[:, None] == jnp.arange(members, dtype=jnp.int32)[None, :]).astype(jnp.int32)
    ranks = jnp.cumsum(counted, axis=0) - 1
    position = jnp.sum(counted * ranks, axis=1)
    target = (flat_ids * slot + position).reshape(tok_rows, routes)
    matched = target[None, :, :] == jnp.arange(total, dtype=jnp.int32)[:, None, None]
    place = jnp.sum(matched.astype(F32), axis=2).astype(BF16)
    weighted = jnp.sum(jnp.where(matched, gate_weights.astype(F32)[None], 0.0), axis=2).astype(BF16)
    x_slots = jnp.dot(place, tokens, preferred_element_type=F32).astype(BF16)
    dy_slots = jnp.dot(weighted, grad_out, preferred_element_type=F32).astype(BF16)
    outgoing = jnp.stack(
        [x_slots.reshape(members, slot, width), dy_slots.reshape(members, slot, width)], axis=1
    )
    arrived = lax.all_to_all(outgoing, "expert", split_axis=0, concat_axis=0, tiled=True)
    x_rows = arrived[:, 0].reshape(total, width)
    dy_rows = arrived[:, 1].reshape(total, width)
    weight_gate, weight_up, weight_down = w_gate[0], w_up[0], w_down[0]
    dot = functools.partial(lax.dot_general, preferred_element_type=F32)

    def gate_terms():
        return jnp.concatenate(
            [dot(w, x_rows, (((0,), (1,)), ((), ()))) for w in (weight_gate, weight_up)], axis=1
        )

    summed = spread_units(gate_terms)
    gate_t, up_t = summed[:, :total], summed[:, total:]
    sigma = jax.nn.sigmoid(gate_t)
    active = gate_t * sigma
    hidden_t = (active * up_t).astype(BF16)
    hidden = lax.all_gather(hidden_t, "tensor", axis=0, tiled=True)
    out_rows = dot(hidden, weight_down, (((0,), (0,)), ((), ()))).astype(BF16)
    swap = functools.partial(
        lax.all_to_all, axis_name="expert", split_axis=0, concat_axis=0, tiled=True
    )
    out_back = swap(out_rows.reshape(members, slot, width))
    d_hidden = spread_units(lambda: dot(weight_down, dy_rows, (((1,), (1,)), ((), ()))))
    d_gate_t = (d_hidden * up_t * sigma * (1.0 + gate_t * (1.0 - sigma))).astype(BF16)
    d_up_t = (d_hidden * active).astype(BF16)
    d_gate = lax.all_gather(d_gate_t, "tensor", axis=0, tiled=True)
    d_up = lax.all_gather(d_up_t, "tensor", axis=0, tiled=True)
    back_rows = (
        dot(d_gate, weight_gate, (((0,), (1,)), ((), ())))
        + dot(d_up, weight_up, (((0,), (1,)), ((), ())))
    ).astype(BF16)
    grad_w_gate = dot(x_rows, d_gate, (((0,), (1,)), ((), ()))).astype(BF16)[None]
    grad_w_up = dot(x_rows, d_up, (((0,), (1,)), ((), ()))).astype(BF16)[None]
    grad_w_down = dot(hidden, dy_rows, (((1,), (0,)), ((), ()))).astype(BF16)[None]
    grad_back = swap(back_rows.reshape(members, slot, width))
    mixed = dot(weighted, out_back.reshape(total, width), (((0,), (0,)), ((), ()))).astype(BF16)
    grad_tokens = dot(place, grad_back.reshape(total, width), (((0,), (0,)), ((), ()))).astype(BF16)
    return (mixed, grad_tokens, grad_w_gate, grad_w_up, grad_w_down)


NT = (((1,), (1,)), ((), ()))
TN = (((0,), (0,)), ((), ()))
NN = (((1,), (0,)), ((), ()))
VMEM = pl.BlockSpec(memory_space=pltpu.VMEM)
ANY = pl.BlockSpec(memory_space=pl.ANY)


def mm(a, b, dims=NN):
    return lax.dot_general(a, b, dims, preferred_element_type=F32)


def in_hbm(x):
    return pltpu.with_memory_space_constraint(x, pltpu.HBM)


def spec(shape, dtype=BF16):
    return jax.ShapeDtypeStruct(shape, dtype)


def call(kernel, outs, out_specs, ins, in_specs, scratch=(), after=(), flops=0, mib=16):
    late = len(after)

    def body(*refs):
        kernel(*refs[: len(ins)], *refs[len(ins) + late :])

    moved = sum(x.size * x.dtype.itemsize for x in (*ins, *outs))
    return pl.pallas_call(
        body,
        out_shape=list(outs),
        in_specs=list(in_specs) + [ANY] * late,
        out_specs=list(out_specs),
        scratch_shapes=list(scratch),
        compiler_params=pltpu.CompilerParams(vmem_limit_bytes=mib * 2**20),
        cost_estimate=pl.CostEstimate(flops=int(flops), bytes_accessed=int(moved), transcendentals=0),
    )(*ins, *after)


def placement(ids, members, slot, total):
    count = ids.shape[1]
    lanes = lax.broadcasted_iota(jnp.int32, (max(members, 8), count), 0)
    chosen = (lanes == ids).astype(F32)
    before = lax.broadcasted_iota(jnp.int32, (count, count), 0) < lax.broadcasted_iota(
        jnp.int32, (count, count), 1
    )
    ranks = mm(chosen.astype(BF16), before.astype(F32).astype(BF16))
    rank = jnp.sum(chosen * ranks, axis=0, keepdims=True).astype(jnp.int32)
    target = (ids ^ lax.axis_index("expert")) * slot + rank
    return lax.broadcasted_iota(jnp.int32, (total, count), 0) == target


def dispatch(ids, gates, tokens, cotangents, members, slot):
    (count, width), total = tokens.shape, members * slot
    ins = [ids, gates, tokens, cotangents]

    def kernel(*refs):
        sources, out_refs = refs[:4], refs[4 : 4 + 2 * members]
        held, sems = refs[4 + 2 * members : -1], refs[-1]
        copies = [
            pltpu.make_async_copy(s, h, sems.at[i]) for i, (s, h) in enumerate(zip(sources, held))
        ]
        for copy in copies:
            copy.start()
        copies[0].wait()
        copies[1].wait()
        mask = placement(held[0][...], members, slot, total)
        gate = held[1][...].astype(F32)
        for i, value in enumerate((1.0, gate)):
            pick = jnp.where(mask, value, 0.0).astype(BF16)
            copies[2 + i].wait()
            rows = mm(pick, held[2 + i][...]).astype(BF16)
            for m in range(members):
                out_refs[members * i + m][...] = rows[m * slot : (m + 1) * slot]

    out = call(
        kernel,
        [spec((slot, width))] * (2 * members),
        [VMEM] * (2 * members),
        [*map(in_hbm, ins)],
        [ANY] * 4,
        [pltpu.VMEM(x.shape, x.dtype) for x in ins] + [pltpu.SemaphoreType.DMA((4,))],
        (),
        4 * total * count * width,
    )
    return out[:members], out[members:]


def plan(ids, gates, members, slot, after=()):
    count, total = ids.shape[1], members * slot

    def kernel(ids_ref, gates_ref, plain, gated):
        mask = placement(ids_ref[...], members, slot, total)
        plain[...] = jnp.where(mask, 1.0, 0.0).T.astype(BF16)
        gated[...] = jnp.where(mask, gates_ref[...].astype(F32), 0.0).T.astype(BF16)

    return call(
        kernel, [spec((count, total))] * 2, [VMEM] * 2, [ids, gates], [VMEM, VMEM], (), after
    )


def collect(picks, rows, after=()):
    (count, total), (slot, width) = picks.shape, rows[0].shape

    def kernel(picks_ref, *refs):
        row_refs, out_ref, joined = refs[:-2], refs[-2], refs[-1]
        for m, ref in enumerate(row_refs):
            joined[m * slot : (m + 1) * slot, :] = ref[...]
        out_ref[...] = mm(picks_ref[...], joined[...]).astype(BF16)

    return call(
        kernel,
        [spec((count, width))],
        [VMEM],
        [picks, *rows],
        [VMEM] * (1 + len(rows)),
        [pltpu.VMEM((total, width), BF16)],
        after,
        2 * count * total * width,
    )[0]


def load(arrays, after=()):
    def kernel(*refs):
        n = len(arrays)
        copies = [
            pltpu.make_async_copy(refs[i], refs[n + i], refs[-1].at[i]) for i in range(n)
        ]
        for copy in copies:
            copy.start()
        for copy in copies:
            copy.wait()

    return call(
        kernel,
        [spec(x.shape, x.dtype) for x in arrays],
        [VMEM] * len(arrays),
        [in_hbm(x) for x in arrays],
        [ANY] * len(arrays),
        [pltpu.SemaphoreType.DMA((len(arrays),))],
        after,
    )


def block_of(ref, index, unit, axis):
    at = pl.ds(pl.multiple_of(index * unit, unit), unit)
    return ref[at, :] if axis == 0 else ref[:, at]


def away_terms(block, rows, weights, blocks, unit, down, after=()):
    members, (slot, width) = len(rows), rows[0].shape
    total, n = members * slot, len(weights)

    def kernel(*refs):
        row_refs, w_refs = refs[:members], refs[members : members + n]
        out_ref, joined = refs[-2:]
        for m, ref in enumerate(row_refs):
            joined[m * slot : (m + 1) * slot, :] = ref[...]
        x = joined[...]
        for j in range(blocks):
            for i, w_ref in enumerate(w_refs):
                w = block_of(w_ref, block(j), unit, 0 if down else 1)
                out_ref[j, i] = mm(x, w, NT if down else NN).astype(BF16)

    return call(
        kernel,
        [spec((blocks, n, total, unit)), spec((total, width))],
        [VMEM] * 2,
        [*rows, *weights],
        [VMEM] * (members + n),
        (),
        after,
        2 * n * blocks * total * width * unit,
    )


def kept_terms(block, joined, weights, arrived, unit, down, after=()):
    (total, width), n, blocks = joined.shape, len(weights), arrived.shape[0]
    first = blocks // 2

    def kernel(x_ref, *refs):
        w_refs, (got, send, keep) = refs[:n], refs[n:]
        x = x_ref[...]
        for j in (*range(first, blocks), *range(first)):
            for i, w_ref in enumerate(w_refs):
                w = block_of(w_ref, block(j), unit, 0 if down else 1)
                term = mm(x, w, NT if down else NN) + got[j, i].astype(F32)
                if j >= first:
                    send[j - first, i] = term.astype(BF16)
                else:
                    keep[j, i] = term

    return call(
        kernel,
        [spec((blocks - first, n, total, unit)), spec((first, n, total, unit), F32)],
        [VMEM] * 2,
        [joined, *weights, arrived],
        [VMEM] * (2 + n),
        (),
        after,
        2 * n * blocks * total * width * unit,
    )


def unit_rows(terms, unit, down, before=None, split=None, after=()):
    weights = [w for w, _ in terms]
    pieces = [(i, *piece) for i, (_, group) in enumerate(terms) for piece in group]
    units = [u for _, _, _, u in pieces]
    total = units[0].shape[2]
    width = weights[0].shape[1] if down else weights[0].shape[0]
    started = [] if before is None else [before]
    k, n = len(pieces), len(weights)

    def kernel(*refs):
        u_refs, w_refs, rest = refs[:k], refs[k : k + n], refs[k + n :]
        out_refs = rest[len(started) :]
        held, blocks = [], []
        for (i, block, first, _), u_ref in zip(pieces, u_refs):
            for j in range(u_ref.shape[0]):
                held.append(u_ref[j, 0])
                blocks.append(block_of(w_refs[i], block(first + j), unit, 0 if down else 1))
        acc = mm(
            jnp.concatenate(held, axis=1),
            jnp.concatenate(blocks, axis=0 if down else 1),
            NN if down else NT,
        )
        if started:
            acc = acc + rest[0][...]
        if split is None:
            out_refs[0][...] = acc
        else:
            for m, ref in enumerate(out_refs):
                ref[...] = acc[m * split : (m + 1) * split, :].astype(BF16)

    if split is None:
        outs = [spec((total, width), F32)]
    else:
        outs = [spec((split, width))] * (total // split)
    return call(
        kernel,
        outs,
        [VMEM] * len(outs),
        [*units, *weights, *started],
        [VMEM] * (k + n + len(started)),
        (),
        after,
        2 * sum(u.shape[0] for u in units) * total * width * unit,
    )


def weight_grads(groups, joined, unit, down, after=()):
    total, width = joined.shape
    pieces = [(i, *piece) for i, group in enumerate(groups) for piece in group]
    units = [u for _, _, _, u in pieces]
    k, n = len(pieces), len(groups)
    steps = sum(u.shape[0] for u in units)
    blocks = steps // n
    shape = (1, blocks * unit, width) if down else (1, width, blocks * unit)

    def kernel(*refs):
        u_refs, x_ref, out_refs = refs[:k], refs[k], refs[k + 1 :][:n]
        turned, held, sems = refs[-3:]
        if not down:
            turned[...] = x_ref[...].T
        waits = []
        for (i, block, first, _), u_ref in zip(pieces, u_refs):
            for j in range(u_ref.shape[0]):
                at = pl.ds(pl.multiple_of(block(first + j) * unit, unit), unit)
                slot = len(waits)
                if down:
                    held[slot] = mm(u_ref[j, 0], x_ref[...], TN).astype(BF16)
                    target = out_refs[i].at[0, at, :]
                else:
                    held[slot] = mm(turned[...], u_ref[j, 0]).astype(BF16)
                    target = out_refs[i].at[0, :, at]
                waits.append(pltpu.make_async_copy(held.at[slot], target, sems.at[slot]))
                waits[slot].start()
        for wait in waits:
            wait.wait()

    return call(
        kernel,
        [spec(shape)] * n,
        [ANY] * n,
        [*units, joined],
        [VMEM] * (k + 1),
        [
            pltpu.VMEM((8, 128) if down else (width, total), BF16),
            pltpu.VMEM((steps, unit, width) if down else (steps, width, unit), BF16),
            pltpu.SemaphoreType.DMA((steps,)),
        ],
        after,
        2 * steps * total * width * unit,
    )


def hypercube(tokens, gate_weights, expert_ids, w_gate, w_up, w_down, grad_out):
    members = lax.axis_size("expert")
    parts = lax.axis_size("tensor")
    bits = (parts // 2).bit_length() - 1
    count = tokens.shape[0]
    slot = 3 * count // (2 * members)
    unit = w_gate.shape[2] // parts
    half = parts // 2

    ids = expert_ids.reshape(1, count)
    gates = gate_weights.reshape(1, count)

    forward = tuple(range(bits))
    halving = (forward, forward[::-1])
    doubling = (forward[::-1], forward[::-1])

    def step_swap(x, orders, step):
        pairs = [(d, d ^ (2 << orders[d % 2][step])) for d in range(parts)]
        return lax.ppermute(x, "tensor", pairs)

    def core_swap(x):
        return lax.ppermute(x, "tensor", [(d, d ^ 1) for d in range(parts)])

    def blocks_by(orders, other):
        def block(rel):
            t = lax.axis_index("tensor")
            core, chip = (t & 1) ^ other, t >> 1
            found = []
            for k in range(2):
                at = chip
                for step, bit in enumerate(orders[k]):
                    at = at ^ (((rel >> (bits - 1 - step)) & 1) << bit)
                index = jnp.int32(0)
                for bit in halving[k]:
                    index = index * 2 + ((at >> bit) & 1)
                found.append(index)
            return half * core + jnp.where(core == 0, found[0], found[1])

        return block

    here_ids, there_ids = blocks_by(halving, 0), blocks_by(halving, 1)
    turned = tuple(order[::-1] for order in doubling)
    mine, other = blocks_by(turned, 0), blocks_by(turned, 1)

    def expert_swap(rows, skipped=0):
        out = []
        for m in range(1, members):
            pairs = [(d, d ^ m) for d in range(members)]
            out.append(lax.ppermute(rows[m - skipped], "expert", pairs))
        return out

    def halve(send, keep):
        size = send.shape[0]
        for step in range(bits):
            got = step_swap(send, halving, step)
            total = keep + got.astype(F32)
            size //= 2
            if step < bits - 1:
                send, keep = total[size:].astype(BF16), total[:size]
        return total[0]

    def gather_units(x):
        for step in range(bits - 1):
            x = jnp.concatenate([x, step_swap(x, doubling, step)], axis=0)
        got = step_swap(x, doubling, bits - 1)
        size = x.shape[0]
        early = ((mine, 0, x), (other, 0, core_swap(x)))
        late = ((mine, size, got), (other, size, core_swap(got)))
        return early, late

    x_slots, dy_slots = dispatch(ids, gates, tokens, grad_out, members, slot)
    x_rows = [x_slots[0]] + expert_swap(x_slots)
    weight_gate, weight_up, weight_down = load(
        (w_gate[0], w_up[0], w_down[0]), (x_slots[1],)
    )
    plain, gated = plan(ids, gates, members, slot, (weight_gate,))
    gate_up = (weight_gate, weight_up)
    dy_rows = [dy_slots[0]] + expert_swap(dy_slots)

    away, x_all = away_terms(there_ids, x_rows, gate_up, half, unit, False, (plain,))
    send, keep = kept_terms(here_ids, x_all, gate_up, core_swap(away), unit, False)
    away, dy_all = away_terms(there_ids, dy_rows, (weight_down,), half, unit, True, (send,))
    gate, up = halve(send, keep)
    send, keep = kept_terms(here_ids, dy_all, (weight_down,), core_swap(away), unit, True)
    (d_hidden,) = halve(send, keep)

    hidden = (gate * jax.nn.sigmoid(gate) * up).astype(BF16)
    hidden, gate, up = lax.optimization_barrier((hidden, gate, up))
    sigma = jax.nn.sigmoid(gate)
    active = gate * sigma
    d_gate = (d_hidden * up * sigma * (1.0 + gate * (1.0 - sigma))).astype(BF16)
    d_up = (d_hidden * active).astype(BF16)

    hidden_early, hidden_late = gather_units(hidden[None, None])
    up_early, up_late = gather_units(d_up[None, None])
    gate_early, gate_late = gather_units(d_gate[None, None])
    hidden_all, up_all, gate_all = (
        hidden_early + hidden_late,
        up_early + up_late,
        gate_early + gate_late,
    )

    out = unit_rows(((weight_down, hidden_all),), unit, True, split=slot)
    out_back = expert_swap(out)
    (grad_w_down,) = weight_grads((hidden_all,), dy_all, unit, True, (out[0],))

    (part,) = unit_rows(
        ((weight_up, up_all), (weight_gate, gate_early)), unit, False, after=(in_hbm(grad_w_down),)
    )
    back = unit_rows(((weight_gate, gate_late),), unit, False, part, slot)
    grad_back = expert_swap(back)
    grad_w_gate, grad_w_up = weight_grads((gate_all, up_all), x_all, unit, False, (back[0],))
    mixed = collect(gated, [out[0]] + out_back, (in_hbm(grad_w_gate),))
    grad_tokens = collect(plain, [back[0]] + grad_back)
    return (mixed, grad_tokens, grad_w_gate, grad_w_up, grad_w_down)


def power_of_two(n):
    return n & (n - 1) == 0


def solution(mesh):
    members, parts = mesh.shape["expert"], mesh.shape["tensor"]

    def local(*args):
        unit = args[3].shape[2] // parts
        slot = 3 * args[0].shape[0] // (2 * members)
        fits = power_of_two(members) and power_of_two(parts) and parts >= 4
        fits = fits and unit % 128 == 0 and slot % 16 == 0 and args[0].shape[1] % 128 == 0
        fits = fits and args[2].shape[1] == 1
        return (hypercube if fits else general)(*args)

    in_specs = (
        P("expert", "tensor"),
        P("expert", None),
        P("expert", None),
        P("expert", "tensor", None),
        P("expert", "tensor", None),
        P("expert", None, "tensor"),
        P("expert", "tensor"),
    )
    out_specs = (
        P("expert", "tensor"),
        P("expert", "tensor"),
        P("expert", "tensor", None),
        P("expert", "tensor", None),
        P("expert", None, "tensor"),
    )
    return jax.shard_map(local, mesh=mesh, in_specs=in_specs, out_specs=out_specs, check_vma=False)
```

time: 101 us -> 89 us (0.88)
  Pallas kernels: 28.4 us -> 20.9 us
  waiting for transfers between devices: 40.9 us -> 35.9 us
  starting transfers between devices: 28.5 us -> 30.6 us
    pallas_call x14, Pallas kernels: 28.4 us -> 20.9 us  [call(): pl.pallas_call(body, out_shape=list(outs), in_specs=list(in_specs) + [ANY...]
    ppermute x10, waiting for transfers between devices: 37.1 us -> 31.5 us  [step_swap(): return lax.ppermute(x, 'tensor', pairs)]
    ppermute x10, starting transfers between devices: 12.9 us -> 14.6 us  [step_swap(): return lax.ppermute(x, 'tensor', pairs)]
  transfers between devices with their start and end apart: 27 -> 30, of which waited for: 13 -> 12; matrix products, arithmetic and copies ran while one was open for 1% -> 1% of each run, Pallas kernels for 21% -> 19%
where the time goes in v4:
time: 89 us; the launch traced here: 88.8 us
  waiting for transfers between devices  35.9 us (40%)
  starting transfers between devices  30.6 us (34%)
  Pallas kernels  20.9 us (23%)
  between operations  0.9 us (1%)
    ppermute x10, waiting for transfers between devices, step_swap(): return lax.ppermute(x, 'tensor', pairs)  31.5 us
    pallas_call x14, Pallas kernels, call(): pl.pallas_call(body, out_shape=list(outs), in_specs=list(in_specs) + [ANY...  20.9 us
    ppermute x12, starting transfers between devices, expert_swap(): out.append(lax.ppermute(rows[m - skipped], 'expert', pairs))  15.3 us
    ppermute x10, starting transfers between devices, step_swap(): return lax.ppermute(x, 'tensor', pairs)  14.6 us
    ppermute x12, waiting for transfers between devices, expert_swap(): out.append(lax.ppermute(rows[m - skipped], 'expert', pairs))  4.35 us
  transfers between devices with their start and end apart: 30, of which 12 were waited for; matrix products, arithmetic and copies ran while one was open for 1% of the time, Pallas kernels for 19%

profile of v4, /device:TPU:0, one launch (start us, length us, event | category | flops | bytes accessed | tf_op | source)
XLA Modules:
  0.0 88.8 jit_solution(12600437726178352805)
XLA Ops:
  0.6 1.5 %shard_map.110 = (bf16[48,896]{1,0:T(8,128)(2,1)S(1)}, bf16[48,896]{1,0:T(8,128)(2,1)S(1)}, bf16[48,896]{1,0:T(8,128)(2,1)S(1)}, bf16[48,896]{1,0:T(8,128)(2,1)S...) custom-call(s32[1,128]{1,0:T(1,128)} %bitcast.28, ...), custom_call_target="tpu_custom_call" | custom-call | flops 88080384 | bytes 1147648 | tf_op jit(solution)/shard_map/pallas_call | solution.py:105
  2.2 3.1 %collective-permute-start.1 = (bf16[48,896]{1,0:T(8,128)(2,1)S(1)}, bf16[48,896]{1,0:T(8,128)(2,1)S(1)}, u32[]{:S(2)}, u32[]{:S(2)}) collective-permute-start(bf16[48,896]{1,0:T(8,128)(2,1)S(1)} %get-tuple-element.43), channel_id=1, source_target_pairs={{0,16},{8,24},{16,0},{24,8},{1,17},{9,25},{17,1},{25,9},{2,18},{10... | collective-permute-start | bytes 258056 | tf_op jit(solution)/shard_map/ppermute | solution.py:421
  5.2 1.4 %collective-permute-start.2 = (bf16[48,896]{1,0:T(8,128)(2,1)S(1)}, bf16[48,896]{1,0:T(8,128)(2,1)S(1)}, u32[]{:S(2)}, u32[]{:S(2)}) collective-permute-start(bf16[48,896]{1,0:T(8,128)(2,1)S(1)} %get-tuple-element.44), channel_id=1, source_target_pairs={{0,24},{8,16},{16,8},{24,0},{1,25},{9,17},{17,9},{25,1},{2,26},{10... | collective-permute-start | bytes 258056 | tf_op jit(solution)/shard_map/ppermute | solution.py:421
  6.6 0.1 collective-permute-start
  6.8 4.2 %shard_map.111 = (bf16[896,2048]{1,0:T(8,128)(2,1)S(1)}, bf16[896,2048]{1,0:T(8,128)(2,1)S(1)}, bf16[2048,896]{1,0:T(8,128)(2,1)S(1)}) custom-call(bf16[896,2048]{1,0:T(8,128)(2,1)} %bitcast.32, bf16[896,2048]{1,0:T(8,128)(2,1)} %bitcast.33, bf16[2048,896]{1,0:T(8,128)(2,1)} %bitcast.34, bf16[48,896]{1,0:T(8,128)(2,1)S(1)} %get-tuple-element.39.refs_3_), custom_call_target="tpu_custom_call" | custom-call | bytes 22020096 | tf_op jit(solution)/shard_map/pallas_call | solution.py:105
  11.0 0.2 shard_map.112
  11.3 0.0 collective-permute-done.1.refs_2_
  11.3 0.0 collective-permute-done.2.refs_3_
  11.3 0.0 collective-permute-done.refs_1_
  11.3 1.0 %shard_map.113 = (bf16[4,2,192,256]{3,2,1,0:T(8,128)(2,1)S(1)}, bf16[192,896]{1,0:T(8,128)(2,1)S(1)}) custom-call(bf16[48,896]{1,0:T(8,128)(2,1)S(1)} %get-tuple-element.42.refs_0_, bf16[48,896]{1,0:T(8,128)(2,1)S(1)} %collective-permute-done.refs_1_, bf16[48,896]{1,0:T(8,128)(2,1)S(1)} %collective-permute-done.1.refs_2_, ...), custom_call_target="tpu_custom_call" | custom-call | flops 704643072 | bytes 8814592 | tf_op jit(solution)/shard_map/pallas_call | solution.py:105
  12.3 0.1 collective-permute-start.3
  12.4 2.0 %collective-permute-start.13 = (bf16[48,896]{1,0:T(8,128)(2,1)S(1)}, bf16[48,896]{1,0:T(8,128)(2,1)S(1)}, u32[]{:S(2)}, u32[]{:S(2)}) collective-permute-start(bf16[48,896]{1,0:T(8,128)(2,1)S(1)} %get-tuple-element.58), channel_id=1, source_target_pairs={{0,8},{8,0},{16,24},{24,16},{1,9},{9,1},{17,25},{25,17},{2,10},{10... | collective-permute-start | bytes 258056 | tf_op jit(solution)/shard_map/ppermute | solution.py:421
  14.4 1.5 %collective-permute-start.14 = (bf16[48,896]{1,0:T(8,128)(2,1)S(1)}, bf16[48,896]{1,0:T(8,128)(2,1)S(1)}, u32[]{:S(2)}, u32[]{:S(2)}) collective-permute-start(bf16[48,896]{1,0:T(8,128)(2,1)S(1)} %get-tuple-element.59), channel_id=1, source_target_pairs={{0,16},{8,24},{16,0},{24,8},{1,17},{9,25},{17,1},{25,9},{2,18},{10... | collective-permute-start | bytes 258056 | tf_op jit(solution)/shard_map/ppermute | solution.py:421
  15.9 0.0 collective-permute-start.15
  16.0 0.0 collective-permute-done.3.refs_3_
  16.0 1.0 %shard_map.114 = (bf16[2,2,192,256]{3,2,1,0:T(8,128)(2,1)S(1)}, f32[2,2,192,256]{3,2,1,0:T(8,128)S(1)}) custom-call(bf16[192,896]{1,0:T(8,128)(2,1)S(1)} %get-tuple-element.47.refs_0_.refs_8_, bf16[896,2048]{1,0:T(8,128)(2,1)S(1)} %get-tuple-element.40.refs_2_.refs_4_.refs_1_.refs_7_, bf16[896,2048]{1,0:T(8,128)(2,1)S(1)} %get-tuple-element.45.refs_5_.refs_2_.refs_6_, ...), custom_call_target="tpu_custom_call" | custom-call | flops 704643072 | bytes 9650176 | tf_op jit(solution)/shard_map/pallas_call | solution.py:105
  17.0 0.5 collective-permute-done.13.refs_1_
  17.5 2.4 %collective-permute-done.14.refs_2_ = bf16[48,896]{1,0:T(8,128)(2,1)S(1)} collective-permute-done((bf16[48,896]{1,0:T(8,128)(2,1)S(1)}, bf16[48,896]{1,0:T(8,128)(2,1)S(1)}, u32[]{:S(2)}, u32[]{:S(2)}) %collective-permute-start.14) | collective-permute-done | bytes 86048 | tf_op jit(solution)/shard_map/ppermute | solution.py:421
  19.9 1.4 %collective-permute-done.15.refs_3_ = bf16[48,896]{1,0:T(8,128)(2,1)S(1)} collective-permute-done((bf16[48,896]{1,0:T(8,128)(2,1)S(1)}, bf16[48,896]{1,0:T(8,128)(2,1)S(1)}, u32[]{:S(2)}, u32[]{:S(2)}) %collective-permute-start.15) | collective-permute-done | bytes 86048 | tf_op jit(solution)/shard_map/ppermute | solution.py:421
  21.3 0.8 shard_map.116
  22.1 0.1 collective-permute-start.16
  22.2 1.6 %collective-permute-start.4 = (bf16[2,2,192,256]{3,2,1,0:T(8,128)(2,1)S(1)}, bf16[2,2,192,256]{3,2,1,0:T(8,128)(2,1)S(1)}, u32[]{:S(2)}, u32[]{:S(2)}) collective-permute-start(bf16[2,2,192,256]{3,2,1,0:T(8,128)(2,1)S(1)} %get-tuple-element.50.refs_5_), channel_id=1, source_target_pairs={{0,2},{1,5},{2,0},{3,7},{4,6},{5,1},{6,4},{7,3},{8,10},{9,13},{10,... | collective-permute-start | bytes 1179656 | tf_op jit(solution)/shard_map/ppermute | solution.py:391
  23.8 0.1 collective-permute-done.16.refs_2_
  23.9 0.8 shard_map.117
  24.6 1.6 %collective-permute-start.17 = (bf16[2,1,192,256]{3,2,1,0:T(8,128)(2,1)S(1)}, bf16[2,1,192,256]{3,2,1,0:T(8,128)(2,1)S(1)}, u32[]{:S(2)}, u32[]{:S(2)}) collective-permute-start(bf16[2,1,192,256]{3,2,1,0:T(8,128)(2,1)S(1)} %get-tuple-element.64), channel_id=1, source_target_pairs={{0,2},{1,5},{2,0},{3,7},{4,6},{5,1},{6,4},{7,3},{8,10},{9,13},{10,... | collective-permute-start | bytes 589832 | tf_op jit(solution)/shard_map/ppermute | solution.py:391
  26.3 7.9 %collective-permute-done.4 = bf16[2,2,192,256]{3,2,1,0:T(8,128)(2,1)S(1)} collective-permute-done((bf16[2,2,192,256]{3,2,1,0:T(8,128)(2,1)S(1)}, bf16[2,2,192,256]{3,2,1,0:T(8,128)(2,1)S(1)}, u32[]{:S(2)}, u32[]{:S(2)}) %collective-permute-start.4) | collective-permute-done | bytes 393248 | tf_op jit(solution)/shard_map/ppermute | solution.py:391
  34.1 0.1 convert_add_fusion
  34.2 2.7 %collective-permute-start.5 = (bf16[1,2,192,256]{3,2,1,0:T(8,128)(2,1)S(1)}, bf16[1,2,192,256]{3,2,1,0:T(8,128)(2,1)S(1)}, u32[]{:S(2)}, u32[]{:S(2)}) collective-permute-start(bf16[1,2,192,256]{3,2,1,0:T(8,128)(2,1)S(1)} %slice.38), channel_id=1, source_target_pairs={{0,4},{1,3},{2,6},{3,1},{4,0},{5,7},{6,2},{7,5},{8,12},{9,11},{10,... | collective-permute-start | bytes 589832 | tf_op jit(solution)/shard_map/ppermute | solution.py:391
  37.0 3.7 %collective-permute-done.17 = bf16[2,1,192,256]{3,2,1,0:T(8,128)(2,1)S(1)} collective-permute-done((bf16[2,1,192,256]{3,2,1,0:T(8,128)(2,1)S(1)}, bf16[2,1,192,256]{3,2,1,0:T(8,128)(2,1)S(1)}, u32[]{:S(2)}, u32[]{:S(2)}) %collective-permute-start.17) | collective-permute-done | bytes 196640 | tf_op jit(solution)/shard_map/ppermute | solution.py:391
  40.7 0.4 collective-permute-start.18
  41.1 1.2 %collective-permute-done.5 = bf16[1,2,192,256]{3,2,1,0:T(8,128)(2,1)S(1)} collective-permute-done((bf16[1,2,192,256]{3,2,1,0:T(8,128)(2,1)S(1)}, bf16[1,2,192,256]{3,2,1,0:T(8,128)(2,1)S(1)}, u32[]{:S(2)}, u32[]{:S(2)}) %collective-permute-start.5) | collective-permute-done | bytes 196640 | tf_op jit(solution)/shard_map/ppermute | solution.py:391
  42.3 0.1 multiply_convert_fusion.2
  42.4 3.4 %collective-permute-start.6 = (bf16[1,1,192,256]{3,2,1,0:T(8,128)(2,1)S(1)}, bf16[1,1,192,256]{3,2,1,0:T(8,128)(2,1)S(1)}, u32[]{:S(2)}, u32[]{:S(2)}) collective-permute-start(bf16[1,1,192,256]{3,2,1,0:T(8,128)(2,1)S(1)} %bitcast.35), channel_id=1, source_target_pairs={{0,4},{1,5},{2,6},{3,7},{4,0},{5,1},{6,2},{7,3},{8,12},{9,13},{10,... | collective-permute-start | bytes 294920 | tf_op jit(solution)/shard_map/ppermute | solution.py:391
  45.9 2.7 %collective-permute-done.18 = bf16[1,1,192,256]{3,2,1,0:T(8,128)(2,1)S(1)} collective-permute-done((bf16[1,1,192,256]{3,2,1,0:T(8,128)(2,1)S(1)}, bf16[1,1,192,256]{3,2,1,0:T(8,128)(2,1)S(1)}, u32[]{:S(2)}, u32[]{:S(2)}) %collective-permute-start.18) | collective-permute-done | bytes 98336 | tf_op jit(solution)/shard_map/ppermute | solution.py:391
  48.6 0.1 fusion.1
  48.7 0.1 collective-permute-start.23
  48.8 5.1 %collective-permute-done.6 = bf16[1,1,192,256]{3,2,1,0:T(8,128)(2,1)S(1)} collective-permute-done((bf16[1,1,192,256]{3,2,1,0:T(8,128)(2,1)S(1)}, bf16[1,1,192,256]{3,2,1,0:T(8,128)(2,1)S(1)}, u32[]{:S(2)}, u32[]{:S(2)}) %collective-permute-start.6) | collective-permute-done | bytes 98336 | tf_op jit(solution)/shard_map/ppermute | solution.py:391
  53.9 0.1 collective-permute-start.8
  54.0 0.1 collective-permute-start.7
  54.1 3.1 %collective-permute-start.19 = (bf16[1,1,192,256]{3,2,1,0:T(8,128)(2,1)S(1)}, bf16[1,1,192,256]{3,2,1,0:T(8,128)(2,1)S(1)}, u32[]{:S(2)}, u32[]{:S(2)}) collective-permute-start(bf16[1,1,192,256]{3,2,1,0:T(8,128)(2,1)S(1)} %get-tuple-element.74), channel_id=1, source_target_pairs={{0,4},{1,5},{2,6},{3,7},{4,0},{5,1},{6,2},{7,3},{8,12},{9,13},{10,... | collective-permute-start | bytes 294920 | tf_op jit(solution)/shard_map/ppermute | solution.py:391
  57.1 0.0 collective-permute-done.23
  57.1 0.2 collective-permute-start.25
  57.4 5.0 %collective-permute-done.19 = bf16[1,1,192,256]{3,2,1,0:T(8,128)(2,1)S(1)} collective-permute-done((bf16[1,1,192,256]{3,2,1,0:T(8,128)(2,1)S(1)}, bf16[1,1,192,256]{3,2,1,0:T(8,128)(2,1)S(1)}, u32[]{:S(2)}, u32[]{:S(2)}) %collective-permute-start.19) | collective-permute-done | bytes 98336 | tf_op jit(solution)/shard_map/ppermute | solution.py:391
  62.4 1.4 %collective-permute-start.21 = (bf16[2,1,192,256]{3,2,1,0:T(8,128)(2,1)S(1)}, bf16[2,1,192,256]{3,2,1,0:T(8,128)(2,1)S(1)}, u32[]{:S(2)}, u32[]{:S(2)}) collective-permute-start(bf16[2,1,192,256]{3,2,1,0:T(8,128)(2,1)S(1)} %pad_maximum_fusion.1.refs_4_.refs_0_), channel_id=1, source_target_pairs={{0,2},{1,3},{2,0},{3,1},{4,6},{5,7},{6,4},{7,5},{8,10},{9,11},{10,... | collective-permute-start | bytes 589832 | tf_op jit(solution)/shard_map/ppermute | solution.py:391
  63.7 0.0 collective-permute-done.8.refs_2_
  63.7 0.0 collective-permute-start.9
  63.7 0.5 collective-permute-start.20
  64.2 0.0 collective-permute-done.7.refs_1_
  64.2 0.0 collective-permute-start.24
  64.2 2.6 %collective-permute-done.25.refs_2_.refs_6_ = bf16[2,1,192,256]{3,2,1,0:T(8,128)(2,1)S(1)} collective-permute-done((bf16[2,1,192,256]{3,2,1,0:T(8,128)(2,1)S(1)}, bf16[2,1,192,256]{3,2,1,0:T(8,128)(2,1)S(1)}, u32[]{:S(2)}, u32[]{:S(2)}) %collective-permute-start.25) | collective-permute-done | bytes 196640 | tf_op jit(solution)/shard_map/ppermute | solution.py:391
  66.8 3.4 %collective-permute-done.21.refs_0_.refs_2_ = bf16[2,1,192,256]{3,2,1,0:T(8,128)(2,1)S(1)} collective-permute-done((bf16[2,1,192,256]{3,2,1,0:T(8,128)(2,1)S(1)}, bf16[2,1,192,256]{3,2,1,0:T(8,128)(2,1)S(1)}, u32[]{:S(2)}, u32[]{:S(2)}) %collective-permute-start.21) | collective-permute-done | bytes 196640 | tf_op jit(solution)/shard_map/ppermute | solution.py:391
  70.2 1.0 %shard_map.115 = (bf16[48,896]{1,0:T(8,128)(2,1)S(1)}, bf16[48,896]{1,0:T(8,128)(2,1)S(1)}, bf16[48,896]{1,0:T(8,128)(2,1)S(1)}, bf16[48,896]{1,0:T(8,128)(2,1)S(1)}) custom-call(bf16[2,1,192,256]{3,2,1,0:T(8,128)(2,1)S(1)} %pad_maximum_fusion.refs_0_, bf16[2,1,192,256]{3,2,1,0:T(8,128)(2,1)S(1)} %collective-permute-done.7.refs_1_, ...), custom_call_target="tpu_custom_call" | custom-call | flops 704643072 | bytes 4800512 | tf_op jit(solution)/shard_map/pallas_call | solution.py:105
  71.2 0.8 collective-permute-start.10
  72.0 2.2 %shard_map.118.refs_8_ = bf16[1,2048,896]{2,1,0:T(8,128)(2,1)} custom-call(bf16[2,1,192,256]{3,2,1,0:T(8,128)(2,1)S(1)} %pad_maximum_fusion.refs_0_, bf16[2,1,192,256]{3,2,1,0:T(8,128)(2,1)S(1)} %collective-permute-done.7.refs_1_, bf16[2,1,192,256]{3,2,1,0:T(8,128)(2,1)S(1)} %collective-permute-done.8.refs_2_, ...), custom_call_target="tpu_custom_call" | custom-call | flops 704643072 | bytes 4800512 | tf_op jit(solution)/shard_map/pallas_call | solution.py:105
  74.2 0.9 %collective-permute-start.11 = (bf16[48,896]{1,0:T(8,128)(2,1)S(1)}, bf16[48,896]{1,0:T(8,128)(2,1)S(1)}, u32[]{:S(2)}, u32[]{:S(2)}) collective-permute-start(bf16[48,896]{1,0:T(8,128)(2,1)S(1)} %get-tuple-element.55), channel_id=1, source_target_pairs={{0,16},{8,24},{16,0},{24,8},{1,17},{9,25},{17,1},{25,9},{2,18},{10... | collective-permute-start | bytes 258056 | tf_op jit(solution)/shard_map/ppermute | solution.py:421
  75.1 1.9 %collective-permute-start.12 = (bf16[48,896]{1,0:T(8,128)(2,1)S(1)}, bf16[48,896]{1,0:T(8,128)(2,1)S(1)}, u32[]{:S(2)}, u32[]{:S(2)}) collective-permute-start(bf16[48,896]{1,0:T(8,128)(2,1)S(1)} %get-tuple-element.56), channel_id=1, source_target_pairs={{0,24},{8,16},{16,8},{24,0},{1,25},{9,17},{17,9},{25,1},{2,26},{10... | collective-permute-start | bytes 258056 | tf_op jit(solution)/shard_map/ppermute | solution.py:421
  77.0 1.9 %shard_map.119.refs_3_ = f32[192,896]{1,0:T(8,128)S(1)} custom-call(bf16[2,1,192,256]{3,2,1,0:T(8,128)(2,1)S(1)} %pad_maximum_fusion.2.refs_0_.refs_4_, bf16[2,1,192,256]{3,2,1,0:T(8,128)(2,1)S(1)} %collective-permute-done.24.refs_1_.refs_5_, bf16[2,1,192,256]{3,2,1,0:T(8,128)(2,1)S(1)} %collective-permute-done.25.refs_2_.refs_6_, ...), custom_call_target="tpu_custom_call" | custom-call | flops 1056964608 | bytes 9207808 | tf_op jit(solution)/shard_map/pallas_call | solution.py:105
  79.0 0.8 shard_map.120
  79.8 0.8 collective-permute-start.27
  80.6 0.8 collective-permute-start.28
  81.5 1.9 %collective-permute-start.29 = (bf16[48,896]{1,0:T(8,128)(2,1)S(1)}, bf16[48,896]{1,0:T(8,128)(2,1)S(1)}, u32[]{:S(2)}, u32[]{:S(2)}) collective-permute-start(bf16[48,896]{1,0:T(8,128)(2,1)S(1)} %get-tuple-element.71), channel_id=1, source_target_pairs={{0,24},{8,16},{16,8},{24,0},{1,25},{9,17},{17,9},{25,1},{2,26},{10... | collective-permute-start | bytes 258056 | tf_op jit(solution)/shard_map/ppermute | solution.py:421
  83.4 3.6 %shard_map.121 = (bf16[1,896,2048]{2,1,0:T(8,128)(2,1)}, bf16[1,896,2048]{2,1,0:T(8,128)(2,1)}) custom-call(bf16[2,1,192,256]{3,2,1,0:T(8,128)(2,1)S(1)} %pad_maximum_fusion.1.refs_4_.refs_0_, bf16[2,1,192,256]{3,2,1,0:T(8,128)(2,1)S(1)} %collective-permute-done.20.refs_5_.refs_1_, bf16[2,1,192,256]{3,2,1,0:T(8,128)(2,1)S(1)} %collective-permute-done.21.refs_0_.refs_2_, ...), custom_call_target="tpu_custom_call" | custom-call | flops 1409286144 | bytes 9256960 | tf_op jit(solution)/shard_map/pallas_call | solution.py:105
  87.0 0.9 %shard_map.122 = bf16[128,896]{1,0:T(8,128)(2,1)} custom-call(bf16[128,192]{1,0:T(8,128)(2,1)S(1)} %get-tuple-element.41.refs_0_, bf16[48,896]{1,0:T(8,128)(2,1)S(1)} %get-tuple-element.53.refs_5_.refs_1_, bf16[48,896]{1,0:T(8,128)(2,1)S(1)} %collective-permute-done.10.refs_2_, bf16[48,896]{1,0:T(8,128)(2,1)S(1)} %collective-permute-done.11.refs_3_, ...), custom_call_target="tpu_custom_call" | custom-call | flops 44040192 | bytes 622592 | tf_op jit(solution)/shard_map/pallas_call | solution.py:105
  87.9 0.9 %shard_map.123 = bf16[128,896]{1,0:T(8,128)(2,1)} custom-call(bf16[128,192]{1,0:T(8,128)(2,1)S(1)} %get-tuple-element.46.refs_6_.refs_0_, bf16[48,896]{1,0:T(8,128)(2,1)S(1)} %get-tuple-element.67.refs_9_.refs_1_, bf16[48,896]{1,0:T(8,128)(2,1)S(1)} %collective-permute-done.27.refs_2_, bf16[48,896]{1,0:T(8,128)(2,1)S(1)} %collective-permute-done.28.refs_3_, ...), custom_call_target="tpu_custom_call" | custom-call | flops 44040192 | bytes 622592 | tf_op jit(solution)/shard_map/pallas_call | solution.py:105
  (25 shorter events, 0.2 us)
Async XLA Ops:
  2.2 9.1 %collective-permute-start.1 = (bf16[48,896]{1,0:T(8,128)(2,1)S(1)}, bf16[48,896]{1,0:T(8,128)(2,1)S(1)}, u32[]{:S(2)}, u32[]{:S(2)}) collective-permute-start(bf16[48,896]{1,0:T(8,128)(2,1)S(1)} %get-tuple-element.43), channel_id=1, source_target_pairs={{0,16},{8,24},{16,0},{24,8},{1,17},{9,25},{17,1},{25,9},{2,18},{10... | collective-permute-start | bytes 258056 | tf_op jit(solution)/shard_map/ppermute | solution.py:421
  5.2 6.1 %collective-permute-start.2 = (bf16[48,896]{1,0:T(8,128)(2,1)S(1)}, bf16[48,896]{1,0:T(8,128)(2,1)S(1)}, u32[]{:S(2)}, u32[]{:S(2)}) collective-permute-start(bf16[48,896]{1,0:T(8,128)(2,1)S(1)} %get-tuple-element.44), channel_id=1, source_target_pairs={{0,24},{8,16},{16,8},{24,0},{1,25},{9,17},{17,9},{25,1},{2,26},{10... | collective-permute-start | bytes 258056 | tf_op jit(solution)/shard_map/ppermute | solution.py:421
  6.6 4.7 %collective-permute-start = (bf16[48,896]{1,0:T(8,128)(2,1)S(1)}, bf16[48,896]{1,0:T(8,128)(2,1)S(1)}, u32[]{:S(2)}, u32[]{:S(2)}) collective-permute-start(bf16[48,896]{1,0:T(8,128)(2,1)S(1)} %get-tuple-element.39.refs_3_), channel_id=1, source_target_pairs={{0,8},{8,0},{16,24},{24,16},{1,9},{9,1},{17,25},{25,17},{2,10},{10... | collective-permute-start | bytes 258056 | tf_op jit(solution)/shard_map/ppermute | solution.py:421
  6.8 4.3 %copy-start = (s32[128,1]{0,1:T(1,128)S(1)}, s32[128,1]{0,1:T(1,128)}, u32[]{:S(2)}) copy-start(s32[128,1]{0,1:T(1,128)} %param.9) | copy-start | bytes 1540
  6.8 4.3 %copy-start.1 = (bf16[128,1]{0,1:T(2,128)(2,1)S(1)}, bf16[128,1]{0,1:T(2,128)(2,1)}, u32[]{:S(2)}) copy-start(bf16[128,1]{0,1:T(2,128)(2,1)} %param.8) | copy-start | bytes 772
  12.3 3.6 %collective-permute-start.3 = (bf16[4,2,192,256]{3,2,1,0:T(8,128)(2,1)S(1)}, bf16[4,2,192,256]{3,2,1,0:T(8,128)(2,1)S(1)}, u32[]{:S(2)}, u32[]{:S(2)}) collective-permute-start(bf16[4,2,192,256]{3,2,1,0:T(8,128)(2,1)S(1)} %get-tuple-element.48), channel_id=1, source_target_pairs={{0,1},{1,0},{2,3},{3,2},{4,5},{5,4},{6,7},{7,6},{8,9},{9,8},{10,11... | collective-permute-start | bytes 2359304 | tf_op jit(solution)/shard_map/ppermute | solution.py:394
  12.4 5.1 %collective-permute-start.13 = (bf16[48,896]{1,0:T(8,128)(2,1)S(1)}, bf16[48,896]{1,0:T(8,128)(2,1)S(1)}, u32[]{:S(2)}, u32[]{:S(2)}) collective-permute-start(bf16[48,896]{1,0:T(8,128)(2,1)S(1)} %get-tuple-element.58), channel_id=1, source_target_pairs={{0,8},{8,0},{16,24},{24,16},{1,9},{9,1},{17,25},{25,17},{2,10},{10... | collective-permute-start | bytes 258056 | tf_op jit(solution)/shard_map/ppermute | solution.py:421
  14.4 5.5 %collective-permute-start.14 = (bf16[48,896]{1,0:T(8,128)(2,1)S(1)}, bf16[48,896]{1,0:T(8,128)(2,1)S(1)}, u32[]{:S(2)}, u32[]{:S(2)}) collective-permute-start(bf16[48,896]{1,0:T(8,128)(2,1)S(1)} %get-tuple-element.59), channel_id=1, source_target_pairs={{0,16},{8,24},{16,0},{24,8},{1,17},{9,25},{17,1},{25,9},{2,18},{10... | collective-permute-start | bytes 258056 | tf_op jit(solution)/shard_map/ppermute | solution.py:421
  15.9 5.4 %collective-permute-start.15 = (bf16[48,896]{1,0:T(8,128)(2,1)S(1)}, bf16[48,896]{1,0:T(8,128)(2,1)S(1)}, u32[]{:S(2)}, u32[]{:S(2)}) collective-permute-start(bf16[48,896]{1,0:T(8,128)(2,1)S(1)} %get-tuple-element.60), channel_id=1, source_target_pairs={{0,24},{8,16},{16,8},{24,0},{1,25},{9,17},{17,9},{25,1},{2,26},{10... | collective-permute-start | bytes 258056 | tf_op jit(solution)/shard_map/ppermute | solution.py:421
  22.1 1.8 %collective-permute-start.16 = (bf16[4,1,192,256]{3,2,1,0:T(8,128)(2,1)S(1)}, bf16[4,1,192,256]{3,2,1,0:T(8,128)(2,1)S(1)}, u32[]{:S(2)}, u32[]{:S(2)}) collective-permute-start(bf16[4,1,192,256]{3,2,1,0:T(8,128)(2,1)S(1)} %get-tuple-element.62), channel_id=1, source_target_pairs={{0,1},{1,0},{2,3},{3,2},{4,5},{5,4},{6,7},{7,6},{8,9},{9,8},{10,11... | collective-permute-start | bytes 1179656 | tf_op jit(solution)/shard_map/ppermute | solution.py:394
  22.2 12.0 %collective-permute-start.4 = (bf16[2,2,192,256]{3,2,1,0:T(8,128)(2,1)S(1)}, bf16[2,2,192,256]{3,2,1,0:T(8,128)(2,1)S(1)}, u32[]{:S(2)}, u32[]{:S(2)}) collective-permute-start(bf16[2,2,192,256]{3,2,1,0:T(8,128)(2,1)S(1)} %get-tuple-element.50.refs_5_), channel_id=1, source_target_pairs={{0,2},{1,5},{2,0},{3,7},{4,6},{5,1},{6,4},{7,3},{8,10},{9,13},{10,... | collective-permute-start | bytes 1179656 | tf_op jit(solution)/shard_map/ppermute | solution.py:391
  24.6 16.0 %collective-permute-start.17 = (bf16[2,1,192,256]{3,2,1,0:T(8,128)(2,1)S(1)}, bf16[2,1,192,256]{3,2,1,0:T(8,128)(2,1)S(1)}, u32[]{:S(2)}, u32[]{:S(2)}) collective-permute-start(bf16[2,1,192,256]{3,2,1,0:T(8,128)(2,1)S(1)} %get-tuple-element.64), channel_id=1, source_target_pairs={{0,2},{1,5},{2,0},{3,7},{4,6},{5,1},{6,4},{7,3},{8,10},{9,13},{10,... | collective-permute-start | bytes 589832 | tf_op jit(solution)/shard_map/ppermute | solution.py:391
  34.2 8.0 %collective-permute-start.5 = (bf16[1,2,192,256]{3,2,1,0:T(8,128)(2,1)S(1)}, bf16[1,2,192,256]{3,2,1,0:T(8,128)(2,1)S(1)}, u32[]{:S(2)}, u32[]{:S(2)}) collective-permute-start(bf16[1,2,192,256]{3,2,1,0:T(8,128)(2,1)S(1)} %slice.38), channel_id=1, source_target_pairs={{0,4},{1,3},{2,6},{3,1},{4,0},{5,7},{6,2},{7,5},{8,12},{9,11},{10,... | collective-permute-start | bytes 589832 | tf_op jit(solution)/shard_map/ppermute | solution.py:391
  40.7 7.9 %collective-permute-start.18 = (bf16[1,1,192,256]{3,2,1,0:T(8,128)(2,1)S(1)}, bf16[1,1,192,256]{3,2,1,0:T(8,128)(2,1)S(1)}, u32[]{:S(2)}, u32[]{:S(2)}) collective-permute-start(bf16[1,1,192,256]{3,2,1,0:T(8,128)(2,1)S(1)} %slice.39), channel_id=1, source_target_pairs={{0,4},{1,3},{2,6},{3,1},{4,0},{5,7},{6,2},{7,5},{8,12},{9,11},{10,... | collective-permute-start | bytes 294920 | tf_op jit(solution)/shard_map/ppermute | solution.py:391
  42.4 11.5 %collective-permute-start.6 = (bf16[1,1,192,256]{3,2,1,0:T(8,128)(2,1)S(1)}, bf16[1,1,192,256]{3,2,1,0:T(8,128)(2,1)S(1)}, u32[]{:S(2)}, u32[]{:S(2)}) collective-permute-start(bf16[1,1,192,256]{3,2,1,0:T(8,128)(2,1)S(1)} %bitcast.35), channel_id=1, source_target_pairs={{0,4},{1,5},{2,6},{3,7},{4,0},{5,1},{6,2},{7,3},{8,12},{9,13},{10,... | collective-permute-start | bytes 294920 | tf_op jit(solution)/shard_map/ppermute | solution.py:391
  48.7 8.4 %collective-permute-start.23 = (bf16[1,1,192,256]{3,2,1,0:T(8,128)(2,1)S(1)}, bf16[1,1,192,256]{3,2,1,0:T(8,128)(2,1)S(1)}, u32[]{:S(2)}, u32[]{:S(2)}) collective-permute-start(bf16[1,1,192,256]{3,2,1,0:T(8,128)(2,1)S(1)} %get-tuple-element.73), channel_id=1, source_target_pairs={{0,4},{1,5},{2,6},{3,7},{4,0},{5,1},{6,2},{7,3},{8,12},{9,13},{10,... | collective-permute-start | bytes 294920 | tf_op jit(solution)/shard_map/ppermute | solution.py:391
  53.9 9.8 %collective-permute-start.8 = (bf16[2,1,192,256]{3,2,1,0:T(8,128)(2,1)S(1)}, bf16[2,1,192,256]{3,2,1,0:T(8,128)(2,1)S(1)}, u32[]{:S(2)}, u32[]{:S(2)}) collective-permute-start(bf16[2,1,192,256]{3,2,1,0:T(8,128)(2,1)S(1)} %pad_maximum_fusion.refs_0_), channel_id=1, source_target_pairs={{0,2},{1,3},{2,0},{3,1},{4,6},{5,7},{6,4},{7,5},{8,10},{9,11},{10,... | collective-permute-start | bytes 589832 | tf_op jit(solution)/shard_map/ppermute | solution.py:391
  54.0 10.3 %collective-permute-start.7 = (bf16[2,1,192,256]{3,2,1,0:T(8,128)(2,1)S(1)}, bf16[2,1,192,256]{3,2,1,0:T(8,128)(2,1)S(1)}, u32[]{:S(2)}, u32[]{:S(2)}) collective-permute-start(bf16[2,1,192,256]{3,2,1,0:T(8,128)(2,1)S(1)} %pad_maximum_fusion.refs_0_), channel_id=1, source_target_pairs={{0,1},{1,0},{2,3},{3,2},{4,5},{5,4},{6,7},{7,6},{8,9},{9,8},{10,11... | collective-permute-start | bytes 589832 | tf_op jit(solution)/shard_map/ppermute | solution.py:394
  54.1 8.3 %collective-permute-start.19 = (bf16[1,1,192,256]{3,2,1,0:T(8,128)(2,1)S(1)}, bf16[1,1,192,256]{3,2,1,0:T(8,128)(2,1)S(1)}, u32[]{:S(2)}, u32[]{:S(2)}) collective-permute-start(bf16[1,1,192,256]{3,2,1,0:T(8,128)(2,1)S(1)} %get-tuple-element.74), channel_id=1, source_target_pairs={{0,4},{1,5},{2,6},{3,7},{4,0},{5,1},{6,2},{7,3},{8,12},{9,13},{10,... | collective-permute-start | bytes 294920 | tf_op jit(solution)/shard_map/ppermute | solution.py:391
  57.1 9.7 %collective-permute-start.25 = (bf16[2,1,192,256]{3,2,1,0:T(8,128)(2,1)S(1)}, bf16[2,1,192,256]{3,2,1,0:T(8,128)(2,1)S(1)}, u32[]{:S(2)}, u32[]{:S(2)}) collective-permute-start(bf16[2,1,192,256]{3,2,1,0:T(8,128)(2,1)S(1)} %pad_maximum_fusion.2.refs_0_.refs_4_), channel_id=1, source_target_pairs={{0,2},{1,3},{2,0},{3,1},{4,6},{5,7},{6,4},{7,5},{8,10},{9,11},{10,... | collective-permute-start | bytes 589832 | tf_op jit(solution)/shard_map/ppermute | solution.py:391
  62.4 7.8 %collective-permute-start.21 = (bf16[2,1,192,256]{3,2,1,0:T(8,128)(2,1)S(1)}, bf16[2,1,192,256]{3,2,1,0:T(8,128)(2,1)S(1)}, u32[]{:S(2)}, u32[]{:S(2)}) collective-permute-start(bf16[2,1,192,256]{3,2,1,0:T(8,128)(2,1)S(1)} %pad_maximum_fusion.1.refs_4_.refs_0_), channel_id=1, source_target_pairs={{0,2},{1,3},{2,0},{3,1},{4,6},{5,7},{6,4},{7,5},{8,10},{9,11},{10,... | collective-permute-start | bytes 589832 | tf_op jit(solution)/shard_map/ppermute | solution.py:391
  63.7 6.5 %collective-permute-start.9 = (bf16[2,1,192,256]{3,2,1,0:T(8,128)(2,1)S(1)}, bf16[2,1,192,256]{3,2,1,0:T(8,128)(2,1)S(1)}, u32[]{:S(2)}, u32[]{:S(2)}) collective-permute-start(bf16[2,1,192,256]{3,2,1,0:T(8,128)(2,1)S(1)} %collective-permute-done.8.refs_2_), channel_id=1, source_target_pairs={{0,1},{1,0},{2,3},{3,2},{4,5},{5,4},{6,7},{7,6},{8,9},{9,8},{10,11... | collective-permute-start | bytes 589832 | tf_op jit(solution)/shard_map/ppermute | solution.py:394
  63.7 10.5 %collective-permute-start.20 = (bf16[2,1,192,256]{3,2,1,0:T(8,128)(2,1)S(1)}, bf16[2,1,192,256]{3,2,1,0:T(8,128)(2,1)S(1)}, u32[]{:S(2)}, u32[]{:S(2)}) collective-permute-start(bf16[2,1,192,256]{3,2,1,0:T(8,128)(2,1)S(1)} %pad_maximum_fusion.1.refs_4_.refs_0_), channel_id=1, source_target_pairs={{0,1},{1,0},{2,3},{3,2},{4,5},{5,4},{6,7},{7,6},{8,9},{9,8},{10,11... | collective-permute-start | bytes 589832 | tf_op jit(solution)/shard_map/ppermute | solution.py:394
  64.2 10.9 %collective-permute-start.24 = (bf16[2,1,192,256]{3,2,1,0:T(8,128)(2,1)S(1)}, bf16[2,1,192,256]{3,2,1,0:T(8,128)(2,1)S(1)}, u32[]{:S(2)}, u32[]{:S(2)}) collective-permute-start(bf16[2,1,192,256]{3,2,1,0:T(8,128)(2,1)S(1)} %pad_maximum_fusion.2.refs_0_.refs_4_), channel_id=1, source_target_pairs={{0,1},{1,0},{2,3},{3,2},{4,5},{5,4},{6,7},{7,6},{8,9},{9,8},{10,11... | collective-permute-start | bytes 589832 | tf_op jit(solution)/shard_map/ppermute | solution.py:394
  66.8 10.3 %collective-permute-start.26 = (bf16[2,1,192,256]{3,2,1,0:T(8,128)(2,1)S(1)}, bf16[2,1,192,256]{3,2,1,0:T(8,128)(2,1)S(1)}, u32[]{:S(2)}, u32[]{:S(2)}) collective-permute-start(bf16[2,1,192,256]{3,2,1,0:T(8,128)(2,1)S(1)} %collective-permute-done.25.refs_2_.refs_6_), channel_id=1, source_target_pairs={{0,1},{1,0},{2,3},{3,2},{4,5},{5,4},{6,7},{7,6},{8,9},{9,8},{10,11... | collective-permute-start | bytes 589832 | tf_op jit(solution)/shard_map/ppermute | solution.py:394
  70.2 8.8 %collective-permute-start.22 = (bf16[2,1,192,256]{3,2,1,0:T(8,128)(2,1)S(1)}, bf16[2,1,192,256]{3,2,1,0:T(8,128)(2,1)S(1)}, u32[]{:S(2)}, u32[]{:S(2)}) collective-permute-start(bf16[2,1,192,256]{3,2,1,0:T(8,128)(2,1)S(1)} %collective-permute-done.21.refs_0_.refs_2_), channel_id=1, source_target_pairs={{0,1},{1,0},{2,3},{3,2},{4,5},{5,4},{6,7},{7,6},{8,9},{9,8},{10,11... | collective-permute-start | bytes 589832 | tf_op jit(solution)/shard_map/ppermute | solution.py:394
  71.2 10.3 %collective-permute-start.10 = (bf16[48,896]{1,0:T(8,128)(2,1)S(1)}, bf16[48,896]{1,0:T(8,128)(2,1)S(1)}, u32[]{:S(2)}, u32[]{:S(2)}) collective-permute-start(bf16[48,896]{1,0:T(8,128)(2,1)S(1)} %get-tuple-element.54), channel_id=1, source_target_pairs={{0,8},{8,0},{16,24},{24,16},{1,9},{9,1},{17,25},{25,17},{2,10},{10... | collective-permute-start | bytes 258056 | tf_op jit(solution)/shard_map/ppermute | solution.py:421
  74.2 12.7 %collective-permute-start.11 = (bf16[48,896]{1,0:T(8,128)(2,1)S(1)}, bf16[48,896]{1,0:T(8,128)(2,1)S(1)}, u32[]{:S(2)}, u32[]{:S(2)}) collective-permute-start(bf16[48,896]{1,0:T(8,128)(2,1)S(1)} %get-tuple-element.55), channel_id=1, source_target_pairs={{0,16},{8,24},{16,0},{24,8},{1,17},{9,25},{17,1},{25,9},{2,18},{10... | collective-permute-start | bytes 258056 | tf_op jit(solution)/shard_map/ppermute | solution.py:421
  75.1 11.8 %collective-permute-start.12 = (bf16[48,896]{1,0:T(8,128)(2,1)S(1)}, bf16[48,896]{1,0:T(8,128)(2,1)S(1)}, u32[]{:S(2)}, u32[]{:S(2)}) collective-permute-start(bf16[48,896]{1,0:T(8,128)(2,1)S(1)} %get-tuple-element.56), channel_id=1, source_target_pairs={{0,24},{8,16},{16,8},{24,0},{1,25},{9,17},{17,9},{25,1},{2,26},{10... | collective-permute-start | bytes 258056 | tf_op jit(solution)/shard_map/ppermute | solution.py:421
  79.8 8.1 %collective-permute-start.27 = (bf16[48,896]{1,0:T(8,128)(2,1)S(1)}, bf16[48,896]{1,0:T(8,128)(2,1)S(1)}, u32[]{:S(2)}, u32[]{:S(2)}) collective-permute-start(bf16[48,896]{1,0:T(8,128)(2,1)S(1)} %get-tuple-element.69), channel_id=1, source_target_pairs={{0,8},{8,0},{16,24},{24,16},{1,9},{9,1},{17,25},{25,17},{2,10},{10... | collective-permute-start | bytes 258056 | tf_op jit(solution)/shard_map/ppermute | solution.py:421
  80.6 7.3 %collective-permute-start.28 = (bf16[48,896]{1,0:T(8,128)(2,1)S(1)}, bf16[48,896]{1,0:T(8,128)(2,1)S(1)}, u32[]{:S(2)}, u32[]{:S(2)}) collective-permute-start(bf16[48,896]{1,0:T(8,128)(2,1)S(1)} %get-tuple-element.70), channel_id=1, source_target_pairs={{0,16},{8,24},{16,0},{24,8},{1,17},{9,25},{17,1},{25,9},{2,18},{10... | collective-permute-start | bytes 258056 | tf_op jit(solution)/shard_map/ppermute | solution.py:421
  81.5 6.5 %collective-permute-start.29 = (bf16[48,896]{1,0:T(8,128)(2,1)S(1)}, bf16[48,896]{1,0:T(8,128)(2,1)S(1)}, u32[]{:S(2)}, u32[]{:S(2)}) collective-permute-start(bf16[48,896]{1,0:T(8,128)(2,1)S(1)} %get-tuple-element.71), channel_id=1, source_target_pairs={{0,24},{8,16},{16,8},{24,0},{1,25},{9,17},{17,9},{25,1},{2,26},{10... | collective-permute-start | bytes 258056 | tf_op jit(solution)/shard_map/ppermute | solution.py:421

commit v5 on v4

--- a/solution.py
+++ b/solution.py
@@ -175,25 +175,28 @@
     )
 
 
-def collect(picks, rows, after=()):
-    (count, total), (slot, width) = picks.shape, rows[0].shape
-
-    def kernel(picks_ref, *refs):
-        row_refs, out_ref, joined = refs[:-2], refs[-2], refs[-1]
-        for m, ref in enumerate(row_refs):
-            joined[m * slot : (m + 1) * slot, :] = ref[...]
-        out_ref[...] = mm(picks_ref[...], joined[...]).astype(BF16)
-
-    return call(
-        kernel,
-        [spec((count, width))],
-        [VMEM],
-        [picks, *rows],
-        [VMEM] * (1 + len(rows)),
-        [pltpu.VMEM((total, width), BF16)],
-        after,
-        2 * count * total * width,
-    )[0]
+def collect(picks, rows):
+    (count, total), (slot, width) = picks[0].shape, rows[0][0].shape
+    n, members = len(picks), len(rows[0])
+
+    def kernel(*refs):
+        pick_refs, row_refs, out_refs = refs[:n], refs[n : n + n * members], refs[-n - 1 : -1]
+        joined = refs[-1]
+        for i in range(n):
+            for m in range(members):
+                joined[i, m * slot : (m + 1) * slot, :] = row_refs[i * members + m][...]
+            out_refs[i][...] = mm(pick_refs[i][...], joined[i]).astype(BF16)
+
+    return call(
+        kernel,
+        [spec((count, width))] * n,
+        [VMEM] * n,
+        [*picks, *(r for group in rows for r in group)],
+        [VMEM] * (n + n * members),
+        [pltpu.VMEM((n, total, width), BF16)],
+        (),
+        2 * n * count * total * width,
+    )
 
 
 def load(arrays, after=()):
@@ -370,6 +373,10 @@
     )
 
 
+def hop_orders(up, down):
+    return (up, down), (up, down), (down, down), (down, down), (down, up)
+
+
 def hypercube(tokens, gate_weights, expert_ids, w_gate, w_up, w_down, grad_out):
     members = lax.axis_size("expert")
     parts = lax.axis_size("tensor")
@@ -383,36 +390,39 @@
     gates = gate_weights.reshape(1, count)
 
     forward = tuple(range(bits))
-    halving = (forward, forward[::-1])
-    doubling = (forward[::-1], forward[::-1])
-
-    def step_swap(x, orders, step):
-        pairs = [(d, d ^ (2 << orders[d % 2][step])) for d in range(parts)]
+    backward = forward[::-1]
+    orders = dict(zip(("gu", "d", "h", "u", "g"), hop_orders(forward, backward)))
+
+    def step_swap(x, step, name):
+        pairs = [(d, d ^ (2 << orders[name][d % 2][step])) for d in range(parts)]
         return lax.ppermute(x, "tensor", pairs)
 
     def core_swap(x):
         return lax.ppermute(x, "tensor", [(d, d ^ 1) for d in range(parts)])
 
-    def blocks_by(orders, other):
+    def blocks_by(hops, other):
         def block(rel):
             t = lax.axis_index("tensor")
             core, chip = (t & 1) ^ other, t >> 1
             found = []
             for k in range(2):
                 at = chip
-                for step, bit in enumerate(orders[k]):
+                for step, bit in enumerate(hops[k]):
                     at = at ^ (((rel >> (bits - 1 - step)) & 1) << bit)
                 index = jnp.int32(0)
-                for bit in halving[k]:
+                for bit in forward:
                     index = index * 2 + ((at >> bit) & 1)
                 found.append(index)
             return half * core + jnp.where(core == 0, found[0], found[1])
 
         return block
 
-    here_ids, there_ids = blocks_by(halving, 0), blocks_by(halving, 1)
-    turned = tuple(order[::-1] for order in doubling)
-    mine, other = blocks_by(turned, 0), blocks_by(turned, 1)
+    def halved(name):
+        return blocks_by(orders[name], 0), blocks_by(orders[name], 1)
+
+    def gathered(name):
+        back = tuple(order[::-1] for order in orders[name])
+        return blocks_by(back, 0), blocks_by(back, 1)
 
     def expert_swap(rows, skipped=0):
         out = []
@@ -421,20 +431,21 @@
             out.append(lax.ppermute(rows[m - skipped], "expert", pairs))
         return out
 
-    def halve(send, keep):
+    def halve(send, keep, name):
         size = send.shape[0]
         for step in range(bits):
-            got = step_swap(send, halving, step)
+            got = step_swap(send, step, name)
             total = keep + got.astype(F32)
             size //= 2
             if step < bits - 1:
                 send, keep = total[size:].astype(BF16), total[:size]
         return total[0]
 
-    def gather_units(x):
+    def gather_units(x, name):
         for step in range(bits - 1):
-            x = jnp.concatenate([x, step_swap(x, doubling, step)], axis=0)
-        got = step_swap(x, doubling, bits - 1)
+            x = jnp.concatenate([x, step_swap(x, step, name)], axis=0)
+        got = step_swap(x, bits - 1, name)
+        mine, other = gathered(name)
         size = x.shape[0]
         early = ((mine, 0, x), (other, 0, core_swap(x)))
         late = ((mine, size, got), (other, size, core_swap(got)))
@@ -449,12 +460,14 @@
     gate_up = (weight_gate, weight_up)
     dy_rows = [dy_slots[0]] + expert_swap(dy_slots)
 
-    away, x_all = away_terms(there_ids, x_rows, gate_up, half, unit, False, (plain,))
-    send, keep = kept_terms(here_ids, x_all, gate_up, core_swap(away), unit, False)
-    away, dy_all = away_terms(there_ids, dy_rows, (weight_down,), half, unit, True, (send,))
-    gate, up = halve(send, keep)
-    send, keep = kept_terms(here_ids, dy_all, (weight_down,), core_swap(away), unit, True)
-    (d_hidden,) = halve(send, keep)
+    mine, other = halved("gu")
+    away, x_all = away_terms(other, x_rows, gate_up, half, unit, False, (plain,))
+    send, keep = kept_terms(mine, x_all, gate_up, core_swap(away), unit, False)
+    mine, other = halved("d")
+    away, dy_all = away_terms(other, dy_rows, (weight_down,), half, unit, True, (send,))
+    gate, up = halve(send, keep, "gu")
+    send, keep = kept_terms(mine, dy_all, (weight_down,), core_swap(away), unit, True)
+    (d_hidden,) = halve(send, keep, "d")
 
     hidden = (gate * jax.nn.sigmoid(gate) * up).astype(BF16)
     hidden, gate, up = lax.optimization_barrier((hidden, gate, up))
@@ -463,9 +476,9 @@
     d_gate = (d_hidden * up * sigma * (1.0 + gate * (1.0 - sigma))).astype(BF16)
     d_up = (d_hidden * active).astype(BF16)
 
-    hidden_early, hidden_late = gather_units(hidden[None, None])
-    up_early, up_late = gather_units(d_up[None, None])
-    gate_early, gate_late = gather_units(d_gate[None, None])
+    hidden_early, hidden_late = gather_units(hidden[None, None], "h")
+    up_early, up_late = gather_units(d_up[None, None], "u")
+    gate_early, gate_late = gather_units(d_gate[None, None], "g")
     hidden_all, up_all, gate_all = (
         hidden_early + hidden_late,
         up_early + up_late,
@@ -476,14 +489,13 @@
     out_back = expert_swap(out)
     (grad_w_down,) = weight_grads((hidden_all,), dy_all, unit, True, (out[0],))
 
-    (part,) = unit_rows(
-        ((weight_up, up_all), (weight_gate, gate_early)), unit, False, after=(in_hbm(grad_w_down),)
-    )
+    (part,) = unit_rows(((weight_up, up_all), (weight_gate, gate_early)), unit, False)
     back = unit_rows(((weight_gate, gate_late),), unit, False, part, slot)
     grad_back = expert_swap(back)
     grad_w_gate, grad_w_up = weight_grads((gate_all, up_all), x_all, unit, False, (back[0],))
-    mixed = collect(gated, [out[0]] + out_back, (in_hbm(grad_w_gate),))
-    grad_tokens = collect(plain, [back[0]] + grad_back)
+    mixed, grad_tokens = collect(
+        (gated, plain), ([out[0]] + out_back, [back[0]] + grad_back)
+    )
     return (mixed, grad_tokens, grad_w_gate, grad_w_up, grad_w_down)
 
 

time: 89 us -> 88.1 us (0.990)
  waiting for transfers between devices: 35.9 us -> 34 us
  starting transfers between devices: 30.6 us -> 32.4 us
    ppermute x10, waiting for transfers between devices: 31.5 us -> 29.5 us  [step_swap(): return lax.ppermute(x, 'tensor', pairs)]
    ppermute x10, starting transfers between devices: 14.6 us -> 16.4 us  [step_swap(): return lax.ppermute(x, 'tensor', pairs)]
    pallas_call x14 -> x13, Pallas kernels: 20.9 us -> 20.1 us  [call(): pl.pallas_call(body, out_shape=list(outs), in_specs=list(in_specs) + [ANY...]
  transfers between devices with their start and end apart: 30 -> 30, of which waited for: 12 -> 12; matrix products, arithmetic and copies ran while one was open for 1% -> 1% of each run, Pallas kernels for 19% -> 18%
where the time goes in v5:
time: 88.1 us; the launch traced here: 87.9 us
  waiting for transfers between devices  34 us (39%)
  starting transfers between devices  32.4 us (37%)
  Pallas kernels  20.1 us (23%)
  between operations  0.92 us (1%)
    ppermute x10, waiting for transfers between devices, step_swap(): return lax.ppermute(x, 'tensor', pairs)  29.5 us
    pallas_call x13, Pallas kernels, call(): pl.pallas_call(body, out_shape=list(outs), in_specs=list(in_specs) + [ANY...  20.1 us
    ppermute x10, starting transfers between devices, step_swap(): return lax.ppermute(x, 'tensor', pairs)  16.4 us
    ppermute x12, starting transfers between devices, expert_swap(): out.append(lax.ppermute(rows[m - skipped], 'expert', pairs))  15.3 us
    ppermute x12, waiting for transfers between devices, expert_swap(): out.append(lax.ppermute(rows[m - skipped], 'expert', pairs))  4.35 us
  transfers between devices with their start and end apart: 30, of which 12 were waited for; matrix products, arithmetic and copies ran while one was open for 1% of the time, Pallas kernels for 18%

profile of v5, /device:TPU:0, one launch (start us, length us, event | category | flops | bytes accessed | tf_op | source)
XLA Modules:
  0.0 87.9 jit_solution(6977545143309107425)
XLA Ops:
  0.6 1.5 %shard_map.110 = (bf16[48,896]{1,0:T(8,128)(2,1)S(1)}, bf16[48,896]{1,0:T(8,128)(2,1)S(1)}, bf16[48,896]{1,0:T(8,128)(2,1)S(1)}, bf16[48,896]{1,0:T(8,128)(2,1)S...) custom-call(s32[1,128]{1,0:T(1,128)} %bitcast.28, ...), custom_call_target="tpu_custom_call" | custom-call | flops 88080384 | bytes 1147648 | tf_op jit(solution)/shard_map/pallas_call | solution.py:105
  2.2 3.1 %collective-permute-start.1 = (bf16[48,896]{1,0:T(8,128)(2,1)S(1)}, bf16[48,896]{1,0:T(8,128)(2,1)S(1)}, u32[]{:S(2)}, u32[]{:S(2)}) collective-permute-start(bf16[48,896]{1,0:T(8,128)(2,1)S(1)} %get-tuple-element.46), channel_id=1, source_target_pairs={{0,16},{8,24},{16,0},{24,8},{1,17},{9,25},{17,1},{25,9},{2,18},{10... | collective-permute-start | bytes 258056 | tf_op jit(solution)/shard_map/ppermute | solution.py:431
  5.2 1.4 %collective-permute-start.2 = (bf16[48,896]{1,0:T(8,128)(2,1)S(1)}, bf16[48,896]{1,0:T(8,128)(2,1)S(1)}, u32[]{:S(2)}, u32[]{:S(2)}) collective-permute-start(bf16[48,896]{1,0:T(8,128)(2,1)S(1)} %get-tuple-element.47), channel_id=1, source_target_pairs={{0,24},{8,16},{16,8},{24,0},{1,25},{9,17},{17,9},{25,1},{2,26},{10... | collective-permute-start | bytes 258056 | tf_op jit(solution)/shard_map/ppermute | solution.py:431
  6.6 0.1 collective-permute-start
  6.8 4.2 %shard_map.111 = (bf16[896,2048]{1,0:T(8,128)(2,1)S(1)}, bf16[896,2048]{1,0:T(8,128)(2,1)S(1)}, bf16[2048,896]{1,0:T(8,128)(2,1)S(1)}) custom-call(bf16[896,2048]{1,0:T(8,128)(2,1)} %bitcast.32, bf16[896,2048]{1,0:T(8,128)(2,1)} %bitcast.33, bf16[2048,896]{1,0:T(8,128)(2,1)} %bitcast.34, bf16[48,896]{1,0:T(8,128)(2,1)S(1)} %get-tuple-element.41.refs_3_), custom_call_target="tpu_custom_call" | custom-call | bytes 22020096 | tf_op jit(solution)/shard_map/pallas_call | solution.py:105
  11.0 0.2 shard_map.112
  11.3 0.0 collective-permute-done.1.refs_2_
  11.3 0.0 collective-permute-done.2.refs_3_
  11.3 0.0 collective-permute-done.refs_1_
  11.3 1.0 %shard_map.113 = (bf16[4,2,192,256]{3,2,1,0:T(8,128)(2,1)S(1)}, bf16[192,896]{1,0:T(8,128)(2,1)S(1)}) custom-call(bf16[48,896]{1,0:T(8,128)(2,1)S(1)} %get-tuple-element.45.refs_0_, bf16[48,896]{1,0:T(8,128)(2,1)S(1)} %collective-permute-done.refs_1_, bf16[48,896]{1,0:T(8,128)(2,1)S(1)} %collective-permute-done.1.refs_2_, ...), custom_call_target="tpu_custom_call" | custom-call | flops 704643072 | bytes 8814592 | tf_op jit(solution)/shard_map/pallas_call | solution.py:105
  12.3 0.1 collective-permute-start.3
  12.4 2.0 %collective-permute-start.13 = (bf16[48,896]{1,0:T(8,128)(2,1)S(1)}, bf16[48,896]{1,0:T(8,128)(2,1)S(1)}, u32[]{:S(2)}, u32[]{:S(2)}) collective-permute-start(bf16[48,896]{1,0:T(8,128)(2,1)S(1)} %get-tuple-element.60), channel_id=1, source_target_pairs={{0,8},{8,0},{16,24},{24,16},{1,9},{9,1},{17,25},{25,17},{2,10},{10... | collective-permute-start | bytes 258056 | tf_op jit(solution)/shard_map/ppermute | solution.py:431
  14.4 1.5 %collective-permute-start.14 = (bf16[48,896]{1,0:T(8,128)(2,1)S(1)}, bf16[48,896]{1,0:T(8,128)(2,1)S(1)}, u32[]{:S(2)}, u32[]{:S(2)}) collective-permute-start(bf16[48,896]{1,0:T(8,128)(2,1)S(1)} %get-tuple-element.61), channel_id=1, source_target_pairs={{0,16},{8,24},{16,0},{24,8},{1,17},{9,25},{17,1},{25,9},{2,18},{10... | collective-permute-start | bytes 258056 | tf_op jit(solution)/shard_map/ppermute | solution.py:431
  15.9 0.0 collective-permute-start.15
  16.0 0.0 collective-permute-done.3.refs_3_
  16.0 1.0 %shard_map.114 = (bf16[2,2,192,256]{3,2,1,0:T(8,128)(2,1)S(1)}, f32[2,2,192,256]{3,2,1,0:T(8,128)S(1)}) custom-call(bf16[192,896]{1,0:T(8,128)(2,1)S(1)} %get-tuple-element.49.refs_0_.refs_8_, bf16[896,2048]{1,0:T(8,128)(2,1)S(1)} %get-tuple-element.42.refs_2_.refs_4_.refs_1_.refs_7_, bf16[896,2048]{1,0:T(8,128)(2,1)S(1)} %get-tuple-element.48.refs_5_.refs_2_.refs_6_, ...), custom_call_target="tpu_custom_call" | custom-call | flops 704643072 | bytes 9650176 | tf_op jit(solution)/shard_map/pallas_call | solution.py:105
  17.0 0.5 collective-permute-done.13.refs_1_
  17.5 2.4 %collective-permute-done.14.refs_2_ = bf16[48,896]{1,0:T(8,128)(2,1)S(1)} collective-permute-done((bf16[48,896]{1,0:T(8,128)(2,1)S(1)}, bf16[48,896]{1,0:T(8,128)(2,1)S(1)}, u32[]{:S(2)}, u32[]{:S(2)}) %collective-permute-start.14) | collective-permute-done | bytes 86048 | tf_op jit(solution)/shard_map/ppermute | solution.py:431
  19.9 1.4 %collective-permute-done.15.refs_3_ = bf16[48,896]{1,0:T(8,128)(2,1)S(1)} collective-permute-done((bf16[48,896]{1,0:T(8,128)(2,1)S(1)}, bf16[48,896]{1,0:T(8,128)(2,1)S(1)}, u32[]{:S(2)}, u32[]{:S(2)}) %collective-permute-start.15) | collective-permute-done | bytes 86048 | tf_op jit(solution)/shard_map/ppermute | solution.py:431
  21.3 0.8 shard_map.116
  22.1 0.1 collective-permute-start.16
  22.2 1.6 %collective-permute-start.4 = (bf16[2,2,192,256]{3,2,1,0:T(8,128)(2,1)S(1)}, bf16[2,2,192,256]{3,2,1,0:T(8,128)(2,1)S(1)}, u32[]{:S(2)}, u32[]{:S(2)}) collective-permute-start(bf16[2,2,192,256]{3,2,1,0:T(8,128)(2,1)S(1)} %get-tuple-element.52.refs_5_), channel_id=1, source_target_pairs={{0,2},{1,5},{2,0},{3,7},{4,6},{5,1},{6,4},{7,3},{8,10},{9,13},{10,... | collective-permute-start | bytes 1179656 | tf_op jit(solution)/shard_map/ppermute | solution.py:398
  23.8 0.1 collective-permute-done.16.refs_2_
  23.9 0.8 shard_map.117
  24.7 1.6 %collective-permute-start.17 = (bf16[2,1,192,256]{3,2,1,0:T(8,128)(2,1)S(1)}, bf16[2,1,192,256]{3,2,1,0:T(8,128)(2,1)S(1)}, u32[]{:S(2)}, u32[]{:S(2)}) collective-permute-start(bf16[2,1,192,256]{3,2,1,0:T(8,128)(2,1)S(1)} %get-tuple-element.66), channel_id=1, source_target_pairs={{0,2},{1,5},{2,0},{3,7},{4,6},{5,1},{6,4},{7,3},{8,10},{9,13},{10,... | collective-permute-start | bytes 589832 | tf_op jit(solution)/shard_map/ppermute | solution.py:398
  26.3 7.8 %collective-permute-done.4 = bf16[2,2,192,256]{3,2,1,0:T(8,128)(2,1)S(1)} collective-permute-done((bf16[2,2,192,256]{3,2,1,0:T(8,128)(2,1)S(1)}, bf16[2,2,192,256]{3,2,1,0:T(8,128)(2,1)S(1)}, u32[]{:S(2)}, u32[]{:S(2)}) %collective-permute-start.4) | collective-permute-done | bytes 393248 | tf_op jit(solution)/shard_map/ppermute | solution.py:398
  34.1 0.1 convert_add_fusion
  34.3 2.7 %collective-permute-start.5 = (bf16[1,2,192,256]{3,2,1,0:T(8,128)(2,1)S(1)}, bf16[1,2,192,256]{3,2,1,0:T(8,128)(2,1)S(1)}, u32[]{:S(2)}, u32[]{:S(2)}) collective-permute-start(bf16[1,2,192,256]{3,2,1,0:T(8,128)(2,1)S(1)} %slice.38), channel_id=1, source_target_pairs={{0,4},{1,3},{2,6},{3,1},{4,0},{5,7},{6,2},{7,5},{8,12},{9,11},{10,... | collective-permute-start | bytes 589832 | tf_op jit(solution)/shard_map/ppermute | solution.py:398
  37.0 3.7 %collective-permute-done.17 = bf16[2,1,192,256]{3,2,1,0:T(8,128)(2,1)S(1)} collective-permute-done((bf16[2,1,192,256]{3,2,1,0:T(8,128)(2,1)S(1)}, bf16[2,1,192,256]{3,2,1,0:T(8,128)(2,1)S(1)}, u32[]{:S(2)}, u32[]{:S(2)}) %collective-permute-start.17) | collective-permute-done | bytes 196640 | tf_op jit(solution)/shard_map/ppermute | solution.py:398
  40.8 0.3 collective-permute-start.18
  41.1 1.2 %collective-permute-done.5 = bf16[1,2,192,256]{3,2,1,0:T(8,128)(2,1)S(1)} collective-permute-done((bf16[1,2,192,256]{3,2,1,0:T(8,128)(2,1)S(1)}, bf16[1,2,192,256]{3,2,1,0:T(8,128)(2,1)S(1)}, u32[]{:S(2)}, u32[]{:S(2)}) %collective-permute-start.5) | collective-permute-done | bytes 196640 | tf_op jit(solution)/shard_map/ppermute | solution.py:398
  42.4 0.1 multiply_convert_fusion.2
  42.4 3.4 %collective-permute-start.6 = (bf16[1,1,192,256]{3,2,1,0:T(8,128)(2,1)S(1)}, bf16[1,1,192,256]{3,2,1,0:T(8,128)(2,1)S(1)}, u32[]{:S(2)}, u32[]{:S(2)}) collective-permute-start(bf16[1,1,192,256]{3,2,1,0:T(8,128)(2,1)S(1)} %bitcast.35), channel_id=1, source_target_pairs={{0,4},{1,5},{2,6},{3,7},{4,0},{5,1},{6,2},{7,3},{8,12},{9,13},{10,... | collective-permute-start | bytes 294920 | tf_op jit(solution)/shard_map/ppermute | solution.py:398
  45.9 2.7 %collective-permute-done.18 = bf16[1,1,192,256]{3,2,1,0:T(8,128)(2,1)S(1)} collective-permute-done((bf16[1,1,192,256]{3,2,1,0:T(8,128)(2,1)S(1)}, bf16[1,1,192,256]{3,2,1,0:T(8,128)(2,1)S(1)}, u32[]{:S(2)}, u32[]{:S(2)}) %collective-permute-start.18) | collective-permute-done | bytes 98336 | tf_op jit(solution)/shard_map/ppermute | solution.py:398
  48.6 0.1 fusion.1
  48.7 0.1 collective-permute-start.22
  48.8 5.1 %collective-permute-done.6 = bf16[1,1,192,256]{3,2,1,0:T(8,128)(2,1)S(1)} collective-permute-done((bf16[1,1,192,256]{3,2,1,0:T(8,128)(2,1)S(1)}, bf16[1,1,192,256]{3,2,1,0:T(8,128)(2,1)S(1)}, u32[]{:S(2)}, u32[]{:S(2)}) %collective-permute-start.6) | collective-permute-done | bytes 98336 | tf_op jit(solution)/shard_map/ppermute | solution.py:398
  53.9 0.1 collective-permute-start.8
  54.0 0.1 collective-permute-start.7
  54.1 3.1 %collective-permute-start.19 = (bf16[1,1,192,256]{3,2,1,0:T(8,128)(2,1)S(1)}, bf16[1,1,192,256]{3,2,1,0:T(8,128)(2,1)S(1)}, u32[]{:S(2)}, u32[]{:S(2)}) collective-permute-start(bf16[1,1,192,256]{3,2,1,0:T(8,128)(2,1)S(1)} %get-tuple-element.78), channel_id=1, source_target_pairs={{0,4},{1,3},{2,6},{3,1},{4,0},{5,7},{6,2},{7,5},{8,12},{9,11},{10,... | collective-permute-start | bytes 294920 | tf_op jit(solution)/shard_map/ppermute | solution.py:398
  57.2 0.2 collective-permute-start.24
  57.4 2.9 %collective-permute-done.19 = bf16[1,1,192,256]{3,2,1,0:T(8,128)(2,1)S(1)} collective-permute-done((bf16[1,1,192,256]{3,2,1,0:T(8,128)(2,1)S(1)}, bf16[1,1,192,256]{3,2,1,0:T(8,128)(2,1)S(1)}, u32[]{:S(2)}, u32[]{:S(2)}) %collective-permute-start.19) | collective-permute-done | bytes 98336 | tf_op jit(solution)/shard_map/ppermute | solution.py:398
  60.3 3.2 %collective-permute-start.20 = (bf16[2,1,192,256]{3,2,1,0:T(8,128)(2,1)S(1)}, bf16[2,1,192,256]{3,2,1,0:T(8,128)(2,1)S(1)}, u32[]{:S(2)}, u32[]{:S(2)}) collective-permute-start(bf16[2,1,192,256]{3,2,1,0:T(8,128)(2,1)S(1)} %pad_maximum_fusion.1.refs_4_.refs_0_), channel_id=1, source_target_pairs={{0,2},{1,5},{2,0},{3,7},{4,6},{5,1},{6,4},{7,3},{8,10},{9,13},{10,... | collective-permute-start | bytes 589832 | tf_op jit(solution)/shard_map/ppermute | solution.py:398
  63.5 0.0 collective-permute-done.8.refs_2_
  63.5 0.0 collective-permute-start.9
  63.5 0.5 collective-permute-start.26
  64.0 0.0 collective-permute-done.7.refs_1_
  64.0 0.0 collective-permute-start.23
  64.0 3.9 %collective-permute-done.24.refs_2_.refs_6_ = bf16[2,1,192,256]{3,2,1,0:T(8,128)(2,1)S(1)} collective-permute-done((bf16[2,1,192,256]{3,2,1,0:T(8,128)(2,1)S(1)}, bf16[2,1,192,256]{3,2,1,0:T(8,128)(2,1)S(1)}, u32[]{:S(2)}, u32[]{:S(2)}) %collective-permute-start.24) | collective-permute-done | bytes 196640 | tf_op jit(solution)/shard_map/ppermute | solution.py:398
  68.0 2.1 %collective-permute-done.20.refs_0_.refs_2_ = bf16[2,1,192,256]{3,2,1,0:T(8,128)(2,1)S(1)} collective-permute-done((bf16[2,1,192,256]{3,2,1,0:T(8,128)(2,1)S(1)}, bf16[2,1,192,256]{3,2,1,0:T(8,128)(2,1)S(1)}, u32[]{:S(2)}, u32[]{:S(2)}) %collective-permute-start.20) | collective-permute-done | bytes 196640 | tf_op jit(solution)/shard_map/ppermute | solution.py:398
  70.1 1.0 %shard_map.115 = (bf16[48,896]{1,0:T(8,128)(2,1)S(1)}, bf16[48,896]{1,0:T(8,128)(2,1)S(1)}, bf16[48,896]{1,0:T(8,128)(2,1)S(1)}, bf16[48,896]{1,0:T(8,128)(2,1)S(1)}) custom-call(bf16[2,1,192,256]{3,2,1,0:T(8,128)(2,1)S(1)} %pad_maximum_fusion.refs_0_, bf16[2,1,192,256]{3,2,1,0:T(8,128)(2,1)S(1)} %collective-permute-done.7.refs_1_, ...), custom_call_target="tpu_custom_call" | custom-call | flops 704643072 | bytes 4800512 | tf_op jit(solution)/shard_map/pallas_call | solution.py:105
  71.1 0.8 collective-permute-start.10
  71.9 2.2 %shard_map.122 = bf16[1,2048,896]{2,1,0:T(8,128)(2,1)} custom-call(bf16[2,1,192,256]{3,2,1,0:T(8,128)(2,1)S(1)} %pad_maximum_fusion.refs_0_, bf16[2,1,192,256]{3,2,1,0:T(8,128)(2,1)S(1)} %collective-permute-done.7.refs_1_, bf16[2,1,192,256]{3,2,1,0:T(8,128)(2,1)S(1)} %collective-permute-done.8.refs_2_, ...), custom_call_target="tpu_custom_call" | custom-call | flops 704643072 | bytes 4800512 | tf_op jit(solution)/shard_map/pallas_call | solution.py:105
  74.2 0.9 %collective-permute-start.11 = (bf16[48,896]{1,0:T(8,128)(2,1)S(1)}, bf16[48,896]{1,0:T(8,128)(2,1)S(1)}, u32[]{:S(2)}, u32[]{:S(2)}) collective-permute-start(bf16[48,896]{1,0:T(8,128)(2,1)S(1)} %get-tuple-element.57), channel_id=1, source_target_pairs={{0,16},{8,24},{16,0},{24,8},{1,17},{9,25},{17,1},{25,9},{2,18},{10... | collective-permute-start | bytes 258056 | tf_op jit(solution)/shard_map/ppermute | solution.py:431
  75.1 1.9 %collective-permute-start.12 = (bf16[48,896]{1,0:T(8,128)(2,1)S(1)}, bf16[48,896]{1,0:T(8,128)(2,1)S(1)}, u32[]{:S(2)}, u32[]{:S(2)}) collective-permute-start(bf16[48,896]{1,0:T(8,128)(2,1)S(1)} %get-tuple-element.58), channel_id=1, source_target_pairs={{0,24},{8,16},{16,8},{24,0},{1,25},{9,17},{17,9},{25,1},{2,26},{10... | collective-permute-start | bytes 258056 | tf_op jit(solution)/shard_map/ppermute | solution.py:431
  77.0 0.0 collective-permute-done.25.refs_3_.refs_7_
  77.0 1.9 %shard_map.118.refs_3_ = f32[192,896]{1,0:T(8,128)S(1)} custom-call(bf16[2,1,192,256]{3,2,1,0:T(8,128)(2,1)S(1)} %pad_maximum_fusion.2.refs_0_.refs_4_, bf16[2,1,192,256]{3,2,1,0:T(8,128)(2,1)S(1)} %collective-permute-done.23.refs_1_.refs_5_, bf16[2,1,192,256]{3,2,1,0:T(8,128)(2,1)S(1)} %collective-permute-done.24.refs_2_.refs_6_, ...), custom_call_target="tpu_custom_call" | custom-call | flops 1056964608 | bytes 9207808 | tf_op jit(solution)/shard_map/pallas_call | solution.py:105
  78.9 0.0 collective-permute-done.21.refs_1_.refs_3_
  78.9 0.8 shard_map.119
  79.7 0.8 collective-permute-start.27
  80.5 0.8 collective-permute-start.28
  81.4 1.9 %collective-permute-start.29 = (bf16[48,896]{1,0:T(8,128)(2,1)S(1)}, bf16[48,896]{1,0:T(8,128)(2,1)S(1)}, u32[]{:S(2)}, u32[]{:S(2)}) collective-permute-start(bf16[48,896]{1,0:T(8,128)(2,1)S(1)} %get-tuple-element.72), channel_id=1, source_target_pairs={{0,24},{8,16},{16,8},{24,0},{1,25},{9,17},{17,9},{25,1},{2,26},{10... | collective-permute-start | bytes 258056 | tf_op jit(solution)/shard_map/ppermute | solution.py:431
  83.3 3.6 %shard_map.121 = (bf16[1,896,2048]{2,1,0:T(8,128)(2,1)}, bf16[1,896,2048]{2,1,0:T(8,128)(2,1)}) custom-call(bf16[2,1,192,256]{3,2,1,0:T(8,128)(2,1)S(1)} %pad_maximum_fusion.1.refs_4_.refs_0_, bf16[2,1,192,256]{3,2,1,0:T(8,128)(2,1)S(1)} %collective-permute-done.26.refs_5_.refs_1_, bf16[2,1,192,256]{3,2,1,0:T(8,128)(2,1)S(1)} %collective-permute-done.20.refs_0_.refs_2_, ...), custom_call_target="tpu_custom_call" | custom-call | flops 1409286144 | bytes 9256960 | tf_op jit(solution)/shard_map/pallas_call | solution.py:105
  86.9 1.0 %shard_map.120 = (bf16[128,896]{1,0:T(8,128)(2,1)}, bf16[128,896]{1,0:T(8,128)(2,1)}) custom-call(bf16[128,192]{1,0:T(8,128)(2,1)S(1)} %get-tuple-element.43.refs_0_, bf16[128,192]{1,0:T(8,128)(2,1)S(1)} %get-tuple-element.44.refs_6_.refs_1_, bf16[48,896]{1,0:T(8,128)(2,1)S(1)} %get-tuple-element.55.refs_2_.refs_5_, ...), custom_call_target="tpu_custom_call" | custom-call | flops 88080384 | bytes 1245184 | tf_op jit(solution)/shard_map/pallas_call | solution.py:105
  (24 shorter events, 0.2 us)
Async XLA Ops:
  2.2 9.1 %collective-permute-start.1 = (bf16[48,896]{1,0:T(8,128)(2,1)S(1)}, bf16[48,896]{1,0:T(8,128)(2,1)S(1)}, u32[]{:S(2)}, u32[]{:S(2)}) collective-permute-start(bf16[48,896]{1,0:T(8,128)(2,1)S(1)} %get-tuple-element.46), channel_id=1, source_target_pairs={{0,16},{8,24},{16,0},{24,8},{1,17},{9,25},{17,1},{25,9},{2,18},{10... | collective-permute-start | bytes 258056 | tf_op jit(solution)/shard_map/ppermute | solution.py:431
  5.2 6.1 %collective-permute-start.2 = (bf16[48,896]{1,0:T(8,128)(2,1)S(1)}, bf16[48,896]{1,0:T(8,128)(2,1)S(1)}, u32[]{:S(2)}, u32[]{:S(2)}) collective-permute-start(bf16[48,896]{1,0:T(8,128)(2,1)S(1)} %get-tuple-element.47), channel_id=1, source_target_pairs={{0,24},{8,16},{16,8},{24,0},{1,25},{9,17},{17,9},{25,1},{2,26},{10... | collective-permute-start | bytes 258056 | tf_op jit(solution)/shard_map/ppermute | solution.py:431
  6.6 4.7 %collective-permute-start = (bf16[48,896]{1,0:T(8,128)(2,1)S(1)}, bf16[48,896]{1,0:T(8,128)(2,1)S(1)}, u32[]{:S(2)}, u32[]{:S(2)}) collective-permute-start(bf16[48,896]{1,0:T(8,128)(2,1)S(1)} %get-tuple-element.41.refs_3_), channel_id=1, source_target_pairs={{0,8},{8,0},{16,24},{24,16},{1,9},{9,1},{17,25},{25,17},{2,10},{10... | collective-permute-start | bytes 258056 | tf_op jit(solution)/shard_map/ppermute | solution.py:431
  6.8 4.3 %copy-start = (s32[128,1]{0,1:T(1,128)S(1)}, s32[128,1]{0,1:T(1,128)}, u32[]{:S(2)}) copy-start(s32[128,1]{0,1:T(1,128)} %param.9) | copy-start | bytes 1540
  6.8 4.3 %copy-start.1 = (bf16[128,1]{0,1:T(2,128)(2,1)S(1)}, bf16[128,1]{0,1:T(2,128)(2,1)}, u32[]{:S(2)}) copy-start(bf16[128,1]{0,1:T(2,128)(2,1)} %param.8) | copy-start | bytes 772
  12.3 3.6 %collective-permute-start.3 = (bf16[4,2,192,256]{3,2,1,0:T(8,128)(2,1)S(1)}, bf16[4,2,192,256]{3,2,1,0:T(8,128)(2,1)S(1)}, u32[]{:S(2)}, u32[]{:S(2)}) collective-permute-start(bf16[4,2,192,256]{3,2,1,0:T(8,128)(2,1)S(1)} %get-tuple-element.50), channel_id=1, source_target_pairs={{0,1},{1,0},{2,3},{3,2},{4,5},{5,4},{6,7},{7,6},{8,9},{9,8},{10,11... | collective-permute-start | bytes 2359304 | tf_op jit(solution)/shard_map/ppermute | solution.py:401
  12.4 5.1 %collective-permute-start.13 = (bf16[48,896]{1,0:T(8,128)(2,1)S(1)}, bf16[48,896]{1,0:T(8,128)(2,1)S(1)}, u32[]{:S(2)}, u32[]{:S(2)}) collective-permute-start(bf16[48,896]{1,0:T(8,128)(2,1)S(1)} %get-tuple-element.60), channel_id=1, source_target_pairs={{0,8},{8,0},{16,24},{24,16},{1,9},{9,1},{17,25},{25,17},{2,10},{10... | collective-permute-start | bytes 258056 | tf_op jit(solution)/shard_map/ppermute | solution.py:431
  14.4 5.5 %collective-permute-start.14 = (bf16[48,896]{1,0:T(8,128)(2,1)S(1)}, bf16[48,896]{1,0:T(8,128)(2,1)S(1)}, u32[]{:S(2)}, u32[]{:S(2)}) collective-permute-start(bf16[48,896]{1,0:T(8,128)(2,1)S(1)} %get-tuple-element.61), channel_id=1, source_target_pairs={{0,16},{8,24},{16,0},{24,8},{1,17},{9,25},{17,1},{25,9},{2,18},{10... | collective-permute-start | bytes 258056 | tf_op jit(solution)/shard_map/ppermute | solution.py:431
  15.9 5.4 %collective-permute-start.15 = (bf16[48,896]{1,0:T(8,128)(2,1)S(1)}, bf16[48,896]{1,0:T(8,128)(2,1)S(1)}, u32[]{:S(2)}, u32[]{:S(2)}) collective-permute-start(bf16[48,896]{1,0:T(8,128)(2,1)S(1)} %get-tuple-element.62), channel_id=1, source_target_pairs={{0,24},{8,16},{16,8},{24,0},{1,25},{9,17},{17,9},{25,1},{2,26},{10... | collective-permute-start | bytes 258056 | tf_op jit(solution)/shard_map/ppermute | solution.py:431
  22.1 1.8 %collective-permute-start.16 = (bf16[4,1,192,256]{3,2,1,0:T(8,128)(2,1)S(1)}, bf16[4,1,192,256]{3,2,1,0:T(8,128)(2,1)S(1)}, u32[]{:S(2)}, u32[]{:S(2)}) collective-permute-start(bf16[4,1,192,256]{3,2,1,0:T(8,128)(2,1)S(1)} %get-tuple-element.64), channel_id=1, source_target_pairs={{0,1},{1,0},{2,3},{3,2},{4,5},{5,4},{6,7},{7,6},{8,9},{9,8},{10,11... | collective-permute-start | bytes 1179656 | tf_op jit(solution)/shard_map/ppermute | solution.py:401
  22.2 12.0 %collective-permute-start.4 = (bf16[2,2,192,256]{3,2,1,0:T(8,128)(2,1)S(1)}, bf16[2,2,192,256]{3,2,1,0:T(8,128)(2,1)S(1)}, u32[]{:S(2)}, u32[]{:S(2)}) collective-permute-start(bf16[2,2,192,256]{3,2,1,0:T(8,128)(2,1)S(1)} %get-tuple-element.52.refs_5_), channel_id=1, source_target_pairs={{0,2},{1,5},{2,0},{3,7},{4,6},{5,1},{6,4},{7,3},{8,10},{9,13},{10,... | collective-permute-start | bytes 1179656 | tf_op jit(solution)/shard_map/ppermute | solution.py:398
  24.7 16.0 %collective-permute-start.17 = (bf16[2,1,192,256]{3,2,1,0:T(8,128)(2,1)S(1)}, bf16[2,1,192,256]{3,2,1,0:T(8,128)(2,1)S(1)}, u32[]{:S(2)}, u32[]{:S(2)}) collective-permute-start(bf16[2,1,192,256]{3,2,1,0:T(8,128)(2,1)S(1)} %get-tuple-element.66), channel_id=1, source_target_pairs={{0,2},{1,5},{2,0},{3,7},{4,6},{5,1},{6,4},{7,3},{8,10},{9,13},{10,... | collective-permute-start | bytes 589832 | tf_op jit(solution)/shard_map/ppermute | solution.py:398
  34.3 8.0 %collective-permute-start.5 = (bf16[1,2,192,256]{3,2,1,0:T(8,128)(2,1)S(1)}, bf16[1,2,192,256]{3,2,1,0:T(8,128)(2,1)S(1)}, u32[]{:S(2)}, u32[]{:S(2)}) collective-permute-start(bf16[1,2,192,256]{3,2,1,0:T(8,128)(2,1)S(1)} %slice.38), channel_id=1, source_target_pairs={{0,4},{1,3},{2,6},{3,1},{4,0},{5,7},{6,2},{7,5},{8,12},{9,11},{10,... | collective-permute-start | bytes 589832 | tf_op jit(solution)/shard_map/ppermute | solution.py:398
  40.8 7.9 %collective-permute-start.18 = (bf16[1,1,192,256]{3,2,1,0:T(8,128)(2,1)S(1)}, bf16[1,1,192,256]{3,2,1,0:T(8,128)(2,1)S(1)}, u32[]{:S(2)}, u32[]{:S(2)}) collective-permute-start(bf16[1,1,192,256]{3,2,1,0:T(8,128)(2,1)S(1)} %slice.39), channel_id=1, source_target_pairs={{0,4},{1,3},{2,6},{3,1},{4,0},{5,7},{6,2},{7,5},{8,12},{9,11},{10,... | collective-permute-start | bytes 294920 | tf_op jit(solution)/shard_map/ppermute | solution.py:398
  42.4 11.5 %collective-permute-start.6 = (bf16[1,1,192,256]{3,2,1,0:T(8,128)(2,1)S(1)}, bf16[1,1,192,256]{3,2,1,0:T(8,128)(2,1)S(1)}, u32[]{:S(2)}, u32[]{:S(2)}) collective-permute-start(bf16[1,1,192,256]{3,2,1,0:T(8,128)(2,1)S(1)} %bitcast.35), channel_id=1, source_target_pairs={{0,4},{1,5},{2,6},{3,7},{4,0},{5,1},{6,2},{7,3},{8,12},{9,13},{10,... | collective-permute-start | bytes 294920 | tf_op jit(solution)/shard_map/ppermute | solution.py:398
  48.7 8.4 %collective-permute-start.22 = (bf16[1,1,192,256]{3,2,1,0:T(8,128)(2,1)S(1)}, bf16[1,1,192,256]{3,2,1,0:T(8,128)(2,1)S(1)}, u32[]{:S(2)}, u32[]{:S(2)}) collective-permute-start(bf16[1,1,192,256]{3,2,1,0:T(8,128)(2,1)S(1)} %get-tuple-element.77), channel_id=1, source_target_pairs={{0,4},{1,5},{2,6},{3,7},{4,0},{5,1},{6,2},{7,3},{8,12},{9,13},{10,... | collective-permute-start | bytes 294920 | tf_op jit(solution)/shard_map/ppermute | solution.py:398
  53.9 9.6 %collective-permute-start.8 = (bf16[2,1,192,256]{3,2,1,0:T(8,128)(2,1)S(1)}, bf16[2,1,192,256]{3,2,1,0:T(8,128)(2,1)S(1)}, u32[]{:S(2)}, u32[]{:S(2)}) collective-permute-start(bf16[2,1,192,256]{3,2,1,0:T(8,128)(2,1)S(1)} %pad_maximum_fusion.refs_0_), channel_id=1, source_target_pairs={{0,2},{1,3},{2,0},{3,1},{4,6},{5,7},{6,4},{7,5},{8,10},{9,11},{10,... | collective-permute-start | bytes 589832 | tf_op jit(solution)/shard_map/ppermute | solution.py:398
  54.0 10.0 %collective-permute-start.7 = (bf16[2,1,192,256]{3,2,1,0:T(8,128)(2,1)S(1)}, bf16[2,1,192,256]{3,2,1,0:T(8,128)(2,1)S(1)}, u32[]{:S(2)}, u32[]{:S(2)}) collective-permute-start(bf16[2,1,192,256]{3,2,1,0:T(8,128)(2,1)S(1)} %pad_maximum_fusion.refs_0_), channel_id=1, source_target_pairs={{0,1},{1,0},{2,3},{3,2},{4,5},{5,4},{6,7},{7,6},{8,9},{9,8},{10,11... | collective-permute-start | bytes 589832 | tf_op jit(solution)/shard_map/ppermute | solution.py:401
  54.1 6.2 %collective-permute-start.19 = (bf16[1,1,192,256]{3,2,1,0:T(8,128)(2,1)S(1)}, bf16[1,1,192,256]{3,2,1,0:T(8,128)(2,1)S(1)}, u32[]{:S(2)}, u32[]{:S(2)}) collective-permute-start(bf16[1,1,192,256]{3,2,1,0:T(8,128)(2,1)S(1)} %get-tuple-element.78), channel_id=1, source_target_pairs={{0,4},{1,3},{2,6},{3,1},{4,0},{5,7},{6,2},{7,5},{8,12},{9,11},{10,... | collective-permute-start | bytes 294920 | tf_op jit(solution)/shard_map/ppermute | solution.py:398
  57.2 10.8 %collective-permute-start.24 = (bf16[2,1,192,256]{3,2,1,0:T(8,128)(2,1)S(1)}, bf16[2,1,192,256]{3,2,1,0:T(8,128)(2,1)S(1)}, u32[]{:S(2)}, u32[]{:S(2)}) collective-permute-start(bf16[2,1,192,256]{3,2,1,0:T(8,128)(2,1)S(1)} %pad_maximum_fusion.2.refs_0_.refs_4_), channel_id=1, source_target_pairs={{0,2},{1,3},{2,0},{3,1},{4,6},{5,7},{6,4},{7,5},{8,10},{9,11},{10,... | collective-permute-start | bytes 589832 | tf_op jit(solution)/shard_map/ppermute | solution.py:398
  60.3 9.7 %collective-permute-start.20 = (bf16[2,1,192,256]{3,2,1,0:T(8,128)(2,1)S(1)}, bf16[2,1,192,256]{3,2,1,0:T(8,128)(2,1)S(1)}, u32[]{:S(2)}, u32[]{:S(2)}) collective-permute-start(bf16[2,1,192,256]{3,2,1,0:T(8,128)(2,1)S(1)} %pad_maximum_fusion.1.refs_4_.refs_0_), channel_id=1, source_target_pairs={{0,2},{1,5},{2,0},{3,7},{4,6},{5,1},{6,4},{7,3},{8,10},{9,13},{10,... | collective-permute-start | bytes 589832 | tf_op jit(solution)/shard_map/ppermute | solution.py:398
  63.5 6.6 %collective-permute-start.9 = (bf16[2,1,192,256]{3,2,1,0:T(8,128)(2,1)S(1)}, bf16[2,1,192,256]{3,2,1,0:T(8,128)(2,1)S(1)}, u32[]{:S(2)}, u32[]{:S(2)}) collective-permute-start(bf16[2,1,192,256]{3,2,1,0:T(8,128)(2,1)S(1)} %collective-permute-done.8.refs_2_), channel_id=1, source_target_pairs={{0,1},{1,0},{2,3},{3,2},{4,5},{5,4},{6,7},{7,6},{8,9},{9,8},{10,11... | collective-permute-start | bytes 589832 | tf_op jit(solution)/shard_map/ppermute | solution.py:401
  63.5 10.6 %collective-permute-start.26 = (bf16[2,1,192,256]{3,2,1,0:T(8,128)(2,1)S(1)}, bf16[2,1,192,256]{3,2,1,0:T(8,128)(2,1)S(1)}, u32[]{:S(2)}, u32[]{:S(2)}) collective-permute-start(bf16[2,1,192,256]{3,2,1,0:T(8,128)(2,1)S(1)} %pad_maximum_fusion.1.refs_4_.refs_0_), channel_id=1, source_target_pairs={{0,1},{1,0},{2,3},{3,2},{4,5},{5,4},{6,7},{7,6},{8,9},{9,8},{10,11... | collective-permute-start | bytes 589832 | tf_op jit(solution)/shard_map/ppermute | solution.py:401
  64.0 11.0 %collective-permute-start.23 = (bf16[2,1,192,256]{3,2,1,0:T(8,128)(2,1)S(1)}, bf16[2,1,192,256]{3,2,1,0:T(8,128)(2,1)S(1)}, u32[]{:S(2)}, u32[]{:S(2)}) collective-permute-start(bf16[2,1,192,256]{3,2,1,0:T(8,128)(2,1)S(1)} %pad_maximum_fusion.2.refs_0_.refs_4_), channel_id=1, source_target_pairs={{0,1},{1,0},{2,3},{3,2},{4,5},{5,4},{6,7},{7,6},{8,9},{9,8},{10,11... | collective-permute-start | bytes 589832 | tf_op jit(solution)/shard_map/ppermute | solution.py:401
  68.0 9.0 %collective-permute-start.25 = (bf16[2,1,192,256]{3,2,1,0:T(8,128)(2,1)S(1)}, bf16[2,1,192,256]{3,2,1,0:T(8,128)(2,1)S(1)}, u32[]{:S(2)}, u32[]{:S(2)}) collective-permute-start(bf16[2,1,192,256]{3,2,1,0:T(8,128)(2,1)S(1)} %collective-permute-done.24.refs_2_.refs_6_), channel_id=1, source_target_pairs={{0,1},{1,0},{2,3},{3,2},{4,5},{5,4},{6,7},{7,6},{8,9},{9,8},{10,11... | collective-permute-start | bytes 589832 | tf_op jit(solution)/shard_map/ppermute | solution.py:401
  70.1 8.8 %collective-permute-start.21 = (bf16[2,1,192,256]{3,2,1,0:T(8,128)(2,1)S(1)}, bf16[2,1,192,256]{3,2,1,0:T(8,128)(2,1)S(1)}, u32[]{:S(2)}, u32[]{:S(2)}) collective-permute-start(bf16[2,1,192,256]{3,2,1,0:T(8,128)(2,1)S(1)} %collective-permute-done.20.refs_0_.refs_2_), channel_id=1, source_target_pairs={{0,1},{1,0},{2,3},{3,2},{4,5},{5,4},{6,7},{7,6},{8,9},{9,8},{10,11... | collective-permute-start | bytes 589832 | tf_op jit(solution)/shard_map/ppermute | solution.py:401
  71.1 10.3 %collective-permute-start.10 = (bf16[48,896]{1,0:T(8,128)(2,1)S(1)}, bf16[48,896]{1,0:T(8,128)(2,1)S(1)}, u32[]{:S(2)}, u32[]{:S(2)}) collective-permute-start(bf16[48,896]{1,0:T(8,128)(2,1)S(1)} %get-tuple-element.56), channel_id=1, source_target_pairs={{0,8},{8,0},{16,24},{24,16},{1,9},{9,1},{17,25},{25,17},{2,10},{10... | collective-permute-start | bytes 258056 | tf_op jit(solution)/shard_map/ppermute | solution.py:431
  74.2 12.7 %collective-permute-start.11 = (bf16[48,896]{1,0:T(8,128)(2,1)S(1)}, bf16[48,896]{1,0:T(8,128)(2,1)S(1)}, u32[]{:S(2)}, u32[]{:S(2)}) collective-permute-start(bf16[48,896]{1,0:T(8,128)(2,1)S(1)} %get-tuple-element.57), channel_id=1, source_target_pairs={{0,16},{8,24},{16,0},{24,8},{1,17},{9,25},{17,1},{25,9},{2,18},{10... | collective-permute-start | bytes 258056 | tf_op jit(solution)/shard_map/ppermute | solution.py:431
  75.1 11.8 %collective-permute-start.12 = (bf16[48,896]{1,0:T(8,128)(2,1)S(1)}, bf16[48,896]{1,0:T(8,128)(2,1)S(1)}, u32[]{:S(2)}, u32[]{:S(2)}) collective-permute-start(bf16[48,896]{1,0:T(8,128)(2,1)S(1)} %get-tuple-element.58), channel_id=1, source_target_pairs={{0,24},{8,16},{16,8},{24,0},{1,25},{9,17},{17,9},{25,1},{2,26},{10... | collective-permute-start | bytes 258056 | tf_op jit(solution)/shard_map/ppermute | solution.py:431
  79.7 7.2 %collective-permute-start.27 = (bf16[48,896]{1,0:T(8,128)(2,1)S(1)}, bf16[48,896]{1,0:T(8,128)(2,1)S(1)}, u32[]{:S(2)}, u32[]{:S(2)}) collective-permute-start(bf16[48,896]{1,0:T(8,128)(2,1)S(1)} %get-tuple-element.70), channel_id=1, source_target_pairs={{0,8},{8,0},{16,24},{24,16},{1,9},{9,1},{17,25},{25,17},{2,10},{10... | collective-permute-start | bytes 258056 | tf_op jit(solution)/shard_map/ppermute | solution.py:431
  80.5 6.4 %collective-permute-start.28 = (bf16[48,896]{1,0:T(8,128)(2,1)S(1)}, bf16[48,896]{1,0:T(8,128)(2,1)S(1)}, u32[]{:S(2)}, u32[]{:S(2)}) collective-permute-start(bf16[48,896]{1,0:T(8,128)(2,1)S(1)} %get-tuple-element.71), channel_id=1, source_target_pairs={{0,16},{8,24},{16,0},{24,8},{1,17},{9,25},{17,1},{25,9},{2,18},{10... | collective-permute-start | bytes 258056 | tf_op jit(solution)/shard_map/ppermute | solution.py:431
  81.4 5.5 %collective-permute-start.29 = (bf16[48,896]{1,0:T(8,128)(2,1)S(1)}, bf16[48,896]{1,0:T(8,128)(2,1)S(1)}, u32[]{:S(2)}, u32[]{:S(2)}) collective-permute-start(bf16[48,896]{1,0:T(8,128)(2,1)S(1)} %get-tuple-element.72), channel_id=1, source_target_pairs={{0,24},{8,16},{16,8},{24,0},{1,25},{9,17},{17,9},{25,1},{2,26},{10... | collective-permute-start | bytes 258056 | tf_op jit(solution)/shard_map/ppermute | solution.py:431

commit v6 on v5

--- a/solution.py
+++ b/solution.py
@@ -95,7 +95,9 @@
     return jax.ShapeDtypeStruct(shape, dtype)
 
 
-def call(kernel, outs, out_specs, ins, in_specs, scratch=(), after=(), flops=0, mib=16):
+def call(
+    kernel, outs, out_specs, ins, in_specs, scratch=(), after=(), flops=0, aliases=None, mib=16
+):
     late = len(after)
 
     def body(*refs):
@@ -108,6 +110,7 @@
         in_specs=list(in_specs) + [ANY] * late,
         out_specs=list(out_specs),
         scratch_shapes=list(scratch),
+        input_output_aliases=aliases or {},
         compiler_params=pltpu.CompilerParams(vmem_limit_bytes=mib * 2**20),
         cost_estimate=pl.CostEstimate(flops=int(flops), bytes_accessed=int(moved), transcendentals=0),
     )(*ins, *after)
@@ -327,17 +330,17 @@
     )
 
 
-def weight_grads(groups, joined, unit, down, after=()):
+def weight_grads(groups, joined, unit, count, down, onto=(), after=()):
     total, width = joined.shape
     pieces = [(i, *piece) for i, group in enumerate(groups) for piece in group]
     units = [u for _, _, _, u in pieces]
     k, n = len(pieces), len(groups)
     steps = sum(u.shape[0] for u in units)
-    blocks = steps // n
-    shape = (1, blocks * unit, width) if down else (1, width, blocks * unit)
+    shape = (1, count * unit, width) if down else (1, width, count * unit)
 
     def kernel(*refs):
-        u_refs, x_ref, out_refs = refs[:k], refs[k], refs[k + 1 :][:n]
+        u_refs, x_ref = refs[:k], refs[k]
+        out_refs = refs[k + 1 + len(onto) :][:n]
         turned, held, sems = refs[-3:]
         if not down:
             turned[...] = x_ref[...].T
@@ -361,8 +364,8 @@
         kernel,
         [spec(shape)] * n,
         [ANY] * n,
-        [*units, joined],
-        [VMEM] * (k + 1),
+        [*units, joined, *onto],
+        [VMEM] * (k + 1) + [ANY] * len(onto),
         [
             pltpu.VMEM((8, 128) if down else (width, total), BF16),
             pltpu.VMEM((steps, unit, width) if down else (steps, width, unit), BF16),
@@ -370,11 +373,12 @@
         ],
         after,
         2 * steps * total * width * unit,
+        {k + 1 + i: n - len(onto) + i for i in range(len(onto))},
     )
 
 
 def hop_orders(up, down):
-    return (up, down), (up, down), (down, down), (down, down), (down, up)
+    return (up, down), (up, down), (down, down), (down, up), (down, down)
 
 
 def hypercube(tokens, gate_weights, expert_ids, w_gate, w_up, w_down, grad_out):
@@ -461,7 +465,7 @@
     dy_rows = [dy_slots[0]] + expert_swap(dy_slots)
 
     mine, other = halved("gu")
-    away, x_all = away_terms(other, x_rows, gate_up, half, unit, False, (plain,))
+    away, x_all = away_terms(other, x_rows, gate_up, half, unit, False)
     send, keep = kept_terms(mine, x_all, gate_up, core_swap(away), unit, False)
     mine, other = halved("d")
     away, dy_all = away_terms(other, dy_rows, (weight_down,), half, unit, True, (send,))
@@ -479,20 +483,20 @@
     hidden_early, hidden_late = gather_units(hidden[None, None], "h")
     up_early, up_late = gather_units(d_up[None, None], "u")
     gate_early, gate_late = gather_units(d_gate[None, None], "g")
-    hidden_all, up_all, gate_all = (
-        hidden_early + hidden_late,
-        up_early + up_late,
-        gate_early + gate_late,
-    )
-
-    out = unit_rows(((weight_down, hidden_all),), unit, True, split=slot)
+    gate_all = gate_early + gate_late
+
+    (part,) = unit_rows(((weight_down, hidden_early),), unit, True)
+    out = unit_rows(((weight_down, hidden_late),), unit, True, part, slot)
     out_back = expert_swap(out)
-    (grad_w_down,) = weight_grads((hidden_all,), dy_all, unit, True, (out[0],))
-
-    (part,) = unit_rows(((weight_up, up_all), (weight_gate, gate_early)), unit, False)
+    grad_w_down = weight_grads((hidden_early,), dy_all, unit, parts, True)
+    (grad_w_down,) = weight_grads((hidden_late,), dy_all, unit, parts, True, grad_w_down)
+
+    (part,) = unit_rows(((weight_up, up_early),), unit, False)
+    (part,) = unit_rows(((weight_up, up_late), (weight_gate, gate_early)), unit, False, part)
     back = unit_rows(((weight_gate, gate_late),), unit, False, part, slot)
     grad_back = expert_swap(back)
-    grad_w_gate, grad_w_up = weight_grads((gate_all, up_all), x_all, unit, False, (back[0],))
+    grad_w_up = weight_grads((up_early,), x_all, unit, parts, False)
+    grad_w_gate, grad_w_up = weight_grads((gate_all, up_late), x_all, unit, parts, False, grad_w_up)
     mixed, grad_tokens = collect(
         (gated, plain), ([out[0]] + out_back, [back[0]] + grad_back)
     )

time: 88.1 us -> 90.3 us (1.025)
  Pallas kernels: 20.1 us -> 22.5 us
  waiting for transfers between devices: 34 us -> 33 us
    ppermute x10, waiting for transfers between devices: 29.5 us -> 23.7 us  [step_swap(): return lax.ppermute(x, 'tensor', pairs)]
    ppermute x12, waiting for transfers between devices: 4.35 us -> 6.95 us  [expert_swap(): out.append(lax.ppermute(rows[m - skipped], 'expert', pairs))]
    pallas_call x13 -> x17, Pallas kernels: 20.1 us -> 22.5 us  [call(): pl.pallas_call(body, out_shape=list(outs), in_specs=list(in_specs) + [ANY...]
    ppermute x8, waiting for transfers between devices: 0.09 us -> 2.29 us  [core_swap(): return lax.ppermute(x, 'tensor', [(d, d ^ 1) for d in range(parts)])]
  transfers between devices with their start and end apart: 30 -> 30, of which waited for: 12 -> 12; matrix products, arithmetic and copies ran while one was open for 1% -> 0% of each run, Pallas kernels for 18% -> 20%
where the time goes in v6:
time: 90.3 us; the launch traced here: 90.1 us
  starting transfers between devices  33.1 us (37%)
  waiting for transfers between devices  33 us (37%)
  Pallas kernels  22.5 us (25%)
  between operations  0.97 us (1%)
    ppermute x10, waiting for transfers between devices, step_swap(): return lax.ppermute(x, 'tensor', pairs)  23.7 us
    pallas_call x17, Pallas kernels, call(): pl.pallas_call(body, out_shape=list(outs), in_specs=list(in_specs) + [ANY...  22.5 us
    ppermute x10, starting transfers between devices, step_swap(): return lax.ppermute(x, 'tensor', pairs)  16.5 us
    ppermute x12, starting transfers between devices, expert_swap(): out.append(lax.ppermute(rows[m - skipped], 'expert', pairs))  15.2 us
    ppermute x12, waiting for transfers between devices, expert_swap(): out.append(lax.ppermute(rows[m - skipped], 'expert', pairs))  6.95 us
    ppermute x8, waiting for transfers between devices, core_swap(): return lax.ppermute(x, 'tensor', [(d, d ^ 1) for d in range(parts)])  2.29 us
  transfers between devices with their start and end apart: 30, of which 12 were waited for; matrix products, arithmetic and copies ran while one was open for 0% of the time, Pallas kernels for 20%

profile of v6, /device:TPU:0, one launch (start us, length us, event | category | flops | bytes accessed | tf_op | source)
XLA Modules:
  0.0 90.1 jit_solution(9160692684041243698)
XLA Ops:
  0.6 1.5 %shard_map.110 = (bf16[48,896]{1,0:T(8,128)(2,1)S(1)}, bf16[48,896]{1,0:T(8,128)(2,1)S(1)}, bf16[48,896]{1,0:T(8,128)(2,1)S(1)}, bf16[48,896]{1,0:T(8,128)(2,1)S...) custom-call(s32[1,128]{1,0:T(1,128)} %bitcast.28, ...), custom_call_target="tpu_custom_call" | custom-call | flops 88080384 | bytes 1147648 | tf_op jit(solution)/shard_map/pallas_call | solution.py:107
  2.2 3.0 %collective-permute-start = (bf16[48,896]{1,0:T(8,128)(2,1)S(1)}, bf16[48,896]{1,0:T(8,128)(2,1)S(1)}, u32[]{:S(2)}, u32[]{:S(2)}) collective-permute-start(bf16[48,896]{1,0:T(8,128)(2,1)S(1)} %get-tuple-element.41.refs_3_), channel_id=1, source_target_pairs={{0,8},{8,0},{16,24},{24,16},{1,9},{9,1},{17,25},{25,17},{2,10},{10... | collective-permute-start | bytes 258056 | tf_op jit(solution)/shard_map/ppermute | solution.py:435
  5.2 1.5 %collective-permute-start.1 = (bf16[48,896]{1,0:T(8,128)(2,1)S(1)}, bf16[48,896]{1,0:T(8,128)(2,1)S(1)}, u32[]{:S(2)}, u32[]{:S(2)}) collective-permute-start(bf16[48,896]{1,0:T(8,128)(2,1)S(1)} %get-tuple-element.46), channel_id=1, source_target_pairs={{0,16},{8,24},{16,0},{24,8},{1,17},{9,25},{17,1},{25,9},{2,18},{10... | collective-permute-start | bytes 258056 | tf_op jit(solution)/shard_map/ppermute | solution.py:435
  6.7 0.0 collective-permute-start.2
  6.7 4.2 %shard_map.111 = (bf16[896,2048]{1,0:T(8,128)(2,1)S(1)}, bf16[896,2048]{1,0:T(8,128)(2,1)S(1)}, bf16[2048,896]{1,0:T(8,128)(2,1)S(1)}) custom-call(bf16[896,2048]{1,0:T(8,128)(2,1)} %bitcast.32, bf16[896,2048]{1,0:T(8,128)(2,1)} %bitcast.33, bf16[2048,896]{1,0:T(8,128)(2,1)} %bitcast.34, bf16[48,896]{1,0:T(8,128)(2,1)S(1)} %get-tuple-element.41.refs_3_), custom_call_target="tpu_custom_call" | custom-call | bytes 22020096 | tf_op jit(solution)/shard_map/pallas_call | solution.py:107
  11.0 0.0 collective-permute-done.refs_1_
  11.0 1.1 %collective-permute-done.2.refs_3_ = bf16[48,896]{1,0:T(8,128)(2,1)S(1)} collective-permute-done((bf16[48,896]{1,0:T(8,128)(2,1)S(1)}, bf16[48,896]{1,0:T(8,128)(2,1)S(1)}, u32[]{:S(2)}, u32[]{:S(2)}) %collective-permute-start.2) | collective-permute-done | bytes 86048 | tf_op jit(solution)/shard_map/ppermute | solution.py:435
  12.1 1.0 %shard_map.113 = (bf16[4,2,192,256]{3,2,1,0:T(8,128)(2,1)S(1)}, bf16[192,896]{1,0:T(8,128)(2,1)S(1)}) custom-call(bf16[48,896]{1,0:T(8,128)(2,1)S(1)} %get-tuple-element.45.refs_0_, bf16[48,896]{1,0:T(8,128)(2,1)S(1)} %collective-permute-done.refs_1_, bf16[48,896]{1,0:T(8,128)(2,1)S(1)} %collective-permute-done.1.refs_2_, ...), custom_call_target="tpu_custom_call" | custom-call | flops 704643072 | bytes 8814592 | tf_op jit(solution)/shard_map/pallas_call | solution.py:107
  13.1 0.1 collective-permute-start.3
  13.2 2.3 %collective-permute-done.3.refs_3_ = bf16[4,2,192,256]{3,2,1,0:T(8,128)(2,1)S(1)} collective-permute-done((bf16[4,2,192,256]{3,2,1,0:T(8,128)(2,1)S(1)}, bf16[4,2,192,256]{3,2,1,0:T(8,128)(2,1)S(1)}, u32[]{:S(2)}, u32[]{:S(2)}) %collective-permute-start.3) | collective-permute-done | bytes 786464 | tf_op jit(solution)/shard_map/ppermute | solution.py:405
  15.5 1.0 %shard_map.114 = (bf16[2,2,192,256]{3,2,1,0:T(8,128)(2,1)S(1)}, f32[2,2,192,256]{3,2,1,0:T(8,128)S(1)}) custom-call(bf16[192,896]{1,0:T(8,128)(2,1)S(1)} %get-tuple-element.49.refs_0_.refs_2_.refs_6_, bf16[896,2048]{1,0:T(8,128)(2,1)S(1)} %get-tuple-element.42.refs_2_.refs_4_.refs_1_.refs_5_, ...), custom_call_target="tpu_custom_call" | custom-call | flops 704643072 | bytes 9650176 | tf_op jit(solution)/shard_map/pallas_call | solution.py:107
  16.5 1.7 %collective-permute-start.4 = (bf16[2,2,192,256]{3,2,1,0:T(8,128)(2,1)S(1)}, bf16[2,2,192,256]{3,2,1,0:T(8,128)(2,1)S(1)}, u32[]{:S(2)}, u32[]{:S(2)}) collective-permute-start(bf16[2,2,192,256]{3,2,1,0:T(8,128)(2,1)S(1)} %get-tuple-element.52.refs_5_), channel_id=1, source_target_pairs={{0,2},{1,5},{2,0},{3,7},{4,6},{5,1},{6,4},{7,3},{8,10},{9,13},{10,... | collective-permute-start | bytes 1179656 | tf_op jit(solution)/shard_map/ppermute | solution.py:402
  18.1 0.9 collective-permute-start.13
  19.0 1.5 %collective-permute-start.14 = (bf16[48,896]{1,0:T(8,128)(2,1)S(1)}, bf16[48,896]{1,0:T(8,128)(2,1)S(1)}, u32[]{:S(2)}, u32[]{:S(2)}) collective-permute-start(bf16[48,896]{1,0:T(8,128)(2,1)S(1)} %get-tuple-element.61), channel_id=1, source_target_pairs={{0,16},{8,24},{16,0},{24,8},{1,17},{9,25},{17,1},{25,9},{2,18},{10... | collective-permute-start | bytes 258056 | tf_op jit(solution)/shard_map/ppermute | solution.py:435
  20.5 1.1 %collective-permute-start.15 = (bf16[48,896]{1,0:T(8,128)(2,1)S(1)}, bf16[48,896]{1,0:T(8,128)(2,1)S(1)}, u32[]{:S(2)}, u32[]{:S(2)}) collective-permute-start(bf16[48,896]{1,0:T(8,128)(2,1)S(1)} %get-tuple-element.62), channel_id=1, source_target_pairs={{0,24},{8,16},{16,8},{24,0},{1,25},{9,17},{17,9},{25,1},{2,26},{10... | collective-permute-start | bytes 258056 | tf_op jit(solution)/shard_map/ppermute | solution.py:435
  21.6 1.9 %collective-permute-done.13.refs_1_ = bf16[48,896]{1,0:T(8,128)(2,1)S(1)} collective-permute-done((bf16[48,896]{1,0:T(8,128)(2,1)S(1)}, bf16[48,896]{1,0:T(8,128)(2,1)S(1)}, u32[]{:S(2)}, u32[]{:S(2)}) %collective-permute-start.13) | collective-permute-done | bytes 86048 | tf_op jit(solution)/shard_map/ppermute | solution.py:435
  23.5 1.4 %collective-permute-done.14.refs_2_ = bf16[48,896]{1,0:T(8,128)(2,1)S(1)} collective-permute-done((bf16[48,896]{1,0:T(8,128)(2,1)S(1)}, bf16[48,896]{1,0:T(8,128)(2,1)S(1)}, u32[]{:S(2)}, u32[]{:S(2)}) %collective-permute-start.14) | collective-permute-done | bytes 86048 | tf_op jit(solution)/shard_map/ppermute | solution.py:435
  24.9 1.2 %collective-permute-done.15.refs_3_ = bf16[48,896]{1,0:T(8,128)(2,1)S(1)} collective-permute-done((bf16[48,896]{1,0:T(8,128)(2,1)S(1)}, bf16[48,896]{1,0:T(8,128)(2,1)S(1)}, u32[]{:S(2)}, u32[]{:S(2)}) %collective-permute-start.15) | collective-permute-done | bytes 86048 | tf_op jit(solution)/shard_map/ppermute | solution.py:435
  26.2 0.8 shard_map.117
  26.9 0.1 collective-permute-start.16
  27.0 1.5 %collective-permute-done.4 = bf16[2,2,192,256]{3,2,1,0:T(8,128)(2,1)S(1)} collective-permute-done((bf16[2,2,192,256]{3,2,1,0:T(8,128)(2,1)S(1)}, bf16[2,2,192,256]{3,2,1,0:T(8,128)(2,1)S(1)}, u32[]{:S(2)}, u32[]{:S(2)}) %collective-permute-start.4) | collective-permute-done | bytes 393248 | tf_op jit(solution)/shard_map/ppermute | solution.py:402
  28.5 0.1 convert_add_fusion
  28.6 1.8 %collective-permute-start.5 = (bf16[1,2,192,256]{3,2,1,0:T(8,128)(2,1)S(1)}, bf16[1,2,192,256]{3,2,1,0:T(8,128)(2,1)S(1)}, u32[]{:S(2)}, u32[]{:S(2)}) collective-permute-start(bf16[1,2,192,256]{3,2,1,0:T(8,128)(2,1)S(1)} %slice.38), channel_id=1, source_target_pairs={{0,4},{1,3},{2,6},{3,1},{4,0},{5,7},{6,2},{7,5},{8,12},{9,11},{10,... | collective-permute-start | bytes 589832 | tf_op jit(solution)/shard_map/ppermute | solution.py:402
  30.4 0.0 collective-permute-done.16.refs_2_
  30.4 0.8 shard_map.118
  31.2 0.0 copy-start
  31.2 0.0 copy-start.1
  31.2 2.4 %collective-permute-start.17 = (bf16[2,1,192,256]{3,2,1,0:T(8,128)(2,1)S(1)}, bf16[2,1,192,256]{3,2,1,0:T(8,128)(2,1)S(1)}, u32[]{:S(2)}, u32[]{:S(2)}) collective-permute-start(bf16[2,1,192,256]{3,2,1,0:T(8,128)(2,1)S(1)} %get-tuple-element.66), channel_id=1, source_target_pairs={{0,2},{1,5},{2,0},{3,7},{4,6},{5,1},{6,4},{7,3},{8,10},{9,13},{10,... | collective-permute-start | bytes 589832 | tf_op jit(solution)/shard_map/ppermute | solution.py:402
  33.6 6.7 %collective-permute-done.5 = bf16[1,2,192,256]{3,2,1,0:T(8,128)(2,1)S(1)} collective-permute-done((bf16[1,2,192,256]{3,2,1,0:T(8,128)(2,1)S(1)}, bf16[1,2,192,256]{3,2,1,0:T(8,128)(2,1)S(1)}, u32[]{:S(2)}, u32[]{:S(2)}) %collective-permute-start.5) | collective-permute-done | bytes 196640 | tf_op jit(solution)/shard_map/ppermute | solution.py:402
  40.5 1.8 %collective-permute-start.18 = (bf16[1,1,192,256]{3,2,1,0:T(8,128)(2,1)S(1)}, bf16[1,1,192,256]{3,2,1,0:T(8,128)(2,1)S(1)}, u32[]{:S(2)}, u32[]{:S(2)}) collective-permute-start(bf16[1,1,192,256]{3,2,1,0:T(8,128)(2,1)S(1)} %slice.39), channel_id=1, source_target_pairs={{0,4},{1,3},{2,6},{3,1},{4,0},{5,7},{6,2},{7,5},{8,12},{9,11},{10,... | collective-permute-start | bytes 294920 | tf_op jit(solution)/shard_map/ppermute | solution.py:402
  42.3 0.1 multiply_convert_fusion.2
  42.4 1.3 %collective-permute-start.6 = (bf16[1,1,192,256]{3,2,1,0:T(8,128)(2,1)S(1)}, bf16[1,1,192,256]{3,2,1,0:T(8,128)(2,1)S(1)}, u32[]{:S(2)}, u32[]{:S(2)}) collective-permute-start(bf16[1,1,192,256]{3,2,1,0:T(8,128)(2,1)S(1)} %bitcast.35), channel_id=1, source_target_pairs={{0,4},{1,5},{2,6},{3,7},{4,0},{5,1},{6,2},{7,3},{8,12},{9,13},{10,... | collective-permute-start | bytes 294920 | tf_op jit(solution)/shard_map/ppermute | solution.py:402
  43.7 2.9 %collective-permute-done.18 = bf16[1,1,192,256]{3,2,1,0:T(8,128)(2,1)S(1)} collective-permute-done((bf16[1,1,192,256]{3,2,1,0:T(8,128)(2,1)S(1)}, bf16[1,1,192,256]{3,2,1,0:T(8,128)(2,1)S(1)}, u32[]{:S(2)}, u32[]{:S(2)}) %collective-permute-start.18) | collective-permute-done | bytes 98336 | tf_op jit(solution)/shard_map/ppermute | solution.py:402
  46.5 0.1 fusion.1
  46.6 1.4 %collective-permute-start.22 = (bf16[1,1,192,256]{3,2,1,0:T(8,128)(2,1)S(1)}, bf16[1,1,192,256]{3,2,1,0:T(8,128)(2,1)S(1)}, u32[]{:S(2)}, u32[]{:S(2)}) collective-permute-start(bf16[1,1,192,256]{3,2,1,0:T(8,128)(2,1)S(1)} %get-tuple-element.77), channel_id=1, source_target_pairs={{0,4},{1,3},{2,6},{3,1},{4,0},{5,7},{6,2},{7,5},{8,12},{9,11},{10,... | collective-permute-start | bytes 294920 | tf_op jit(solution)/shard_map/ppermute | solution.py:402
  48.0 3.4 %collective-permute-done.6 = bf16[1,1,192,256]{3,2,1,0:T(8,128)(2,1)S(1)} collective-permute-done((bf16[1,1,192,256]{3,2,1,0:T(8,128)(2,1)S(1)}, bf16[1,1,192,256]{3,2,1,0:T(8,128)(2,1)S(1)}, u32[]{:S(2)}, u32[]{:S(2)}) %collective-permute-start.6) | collective-permute-done | bytes 98336 | tf_op jit(solution)/shard_map/ppermute | solution.py:402
  51.4 2.4 %collective-permute-start.7 = (bf16[2,1,192,256]{3,2,1,0:T(8,128)(2,1)S(1)}, bf16[2,1,192,256]{3,2,1,0:T(8,128)(2,1)S(1)}, u32[]{:S(2)}, u32[]{:S(2)}) collective-permute-start(bf16[2,1,192,256]{3,2,1,0:T(8,128)(2,1)S(1)} %pad_maximum_fusion.refs_0_), channel_id=1, source_target_pairs={{0,2},{1,3},{2,0},{3,1},{4,6},{5,7},{6,4},{7,5},{8,10},{9,11},{10,... | collective-permute-start | bytes 589832 | tf_op jit(solution)/shard_map/ppermute | solution.py:402
  53.9 1.9 %collective-permute-start.19 = (bf16[1,1,192,256]{3,2,1,0:T(8,128)(2,1)S(1)}, bf16[1,1,192,256]{3,2,1,0:T(8,128)(2,1)S(1)}, u32[]{:S(2)}, u32[]{:S(2)}) collective-permute-start(bf16[1,1,192,256]{3,2,1,0:T(8,128)(2,1)S(1)} %get-tuple-element.78), channel_id=1, source_target_pairs={{0,4},{1,5},{2,6},{3,7},{4,0},{5,1},{6,2},{7,3},{8,12},{9,13},{10,... | collective-permute-start | bytes 294920 | tf_op jit(solution)/shard_map/ppermute | solution.py:402
  55.7 1.8 %collective-permute-start.23 = (bf16[2,1,192,256]{3,2,1,0:T(8,128)(2,1)S(1)}, bf16[2,1,192,256]{3,2,1,0:T(8,128)(2,1)S(1)}, u32[]{:S(2)}, u32[]{:S(2)}) collective-permute-start(bf16[2,1,192,256]{3,2,1,0:T(8,128)(2,1)S(1)} %pad_maximum_fusion.2.refs_0_), channel_id=1, source_target_pairs={{0,2},{1,5},{2,0},{3,7},{4,6},{5,1},{6,4},{7,3},{8,10},{9,13},{10,... | collective-permute-start | bytes 589832 | tf_op jit(solution)/shard_map/ppermute | solution.py:402
  57.5 6.7 %collective-permute-done.19 = bf16[1,1,192,256]{3,2,1,0:T(8,128)(2,1)S(1)} collective-permute-done((bf16[1,1,192,256]{3,2,1,0:T(8,128)(2,1)S(1)}, bf16[1,1,192,256]{3,2,1,0:T(8,128)(2,1)S(1)}, u32[]{:S(2)}, u32[]{:S(2)}) %collective-permute-start.19) | collective-permute-done | bytes 98336 | tf_op jit(solution)/shard_map/ppermute | solution.py:402
  64.2 0.1 collective-permute-start.20
  64.3 0.1 collective-permute-start.26
  64.4 0.5 collective-permute-start.8
  64.8 0.2 shard_map.112
  65.1 0.2 collective-permute-start.25
  65.3 0.6 collective-permute-start.24
  65.9 0.6 shard_map.115.refs_3_
  66.5 1.6 %shard_map.125.refs_3_ = bf16[1,2048,896]{2,1,0:T(8,128)(2,1)} custom-call(bf16[2,1,192,256]{3,2,1,0:T(8,128)(2,1)S(1)} %pad_maximum_fusion.refs_0_, bf16[2,1,192,256]{3,2,1,0:T(8,128)(2,1)S(1)} %collective-permute-done.9.refs_1_, bf16[192,896]{1,0:T(8,128)(2,1)S(1)} %get-tuple-element.63.refs_0_.refs_2_), custom_call_target="tpu_custom_call" | custom-call | flops 352321536 | bytes 4407296 | tf_op jit(solution)/shard_map/pallas_call | solution.py:107
  68.0 2.6 %collective-permute-done.20.refs_0_.refs_2_ = bf16[2,1,192,256]{3,2,1,0:T(8,128)(2,1)S(1)} collective-permute-done((bf16[2,1,192,256]{3,2,1,0:T(8,128)(2,1)S(1)}, bf16[2,1,192,256]{3,2,1,0:T(8,128)(2,1)S(1)}, u32[]{:S(2)}, u32[]{:S(2)}) %collective-permute-start.20) | collective-permute-done | bytes 196640 | tf_op jit(solution)/shard_map/ppermute | solution.py:402
  70.7 0.8 shard_map.119.refs_6_
  71.5 1.7 %shard_map.123.refs_7_ = bf16[1,896,2048]{2,1,0:T(8,128)(2,1)} custom-call(bf16[2,1,192,256]{3,2,1,0:T(8,128)(2,1)S(1)} %pad_maximum_fusion.2.refs_0_, bf16[2,1,192,256]{3,2,1,0:T(8,128)(2,1)S(1)} %collective-permute-done.26.refs_1_, bf16[192,896]{1,0:T(8,128)(2,1)S(1)} %get-tuple-element.49.refs_0_.refs_2_.refs_6_), custom_call_target="tpu_custom_call" | custom-call | flops 352321536 | bytes 4407296 | tf_op jit(solution)/shard_map/pallas_call | solution.py:107
  73.2 0.6 shard_map.116
  73.8 0.9 %collective-permute-start.10 = (bf16[48,896]{1,0:T(8,128)(2,1)S(1)}, bf16[48,896]{1,0:T(8,128)(2,1)S(1)}, u32[]{:S(2)}, u32[]{:S(2)}) collective-permute-start(bf16[48,896]{1,0:T(8,128)(2,1)S(1)} %get-tuple-element.56), channel_id=1, source_target_pairs={{0,8},{8,0},{16,24},{24,16},{1,9},{9,1},{17,25},{25,17},{2,10},{10... | collective-permute-start | bytes 258056 | tf_op jit(solution)/shard_map/ppermute | solution.py:435
  74.7 1.6 %collective-permute-start.11 = (bf16[48,896]{1,0:T(8,128)(2,1)S(1)}, bf16[48,896]{1,0:T(8,128)(2,1)S(1)}, u32[]{:S(2)}, u32[]{:S(2)}) collective-permute-start(bf16[48,896]{1,0:T(8,128)(2,1)S(1)} %get-tuple-element.57), channel_id=1, source_target_pairs={{0,16},{8,24},{16,0},{24,8},{1,17},{9,25},{17,1},{25,9},{2,18},{10... | collective-permute-start | bytes 258056 | tf_op jit(solution)/shard_map/ppermute | solution.py:435
  76.3 1.6 %shard_map.126 = bf16[1,2048,896]{2,1,0:T(8,128)(2,1)} custom-call(bf16[2,1,192,256]{3,2,1,0:T(8,128)(2,1)S(1)} %collective-permute-done.7.refs_0_, bf16[2,1,192,256]{3,2,1,0:T(8,128)(2,1)S(1)} %collective-permute-done.8.refs_1_, bf16[192,896]{1,0:T(8,128)(2,1)S(1)} %get-tuple-element.63.refs_0_.refs_2_, ...), custom_call_target="tpu_custom_call", output_to_operand_aliasing={{}: (3, {})} | custom-call | flops 352321536 | bytes 8077312 | tf_op jit(solution)/shard_map/pallas_call | solution.py:107
  77.9 1.1 %collective-permute-start.12 = (bf16[48,896]{1,0:T(8,128)(2,1)S(1)}, bf16[48,896]{1,0:T(8,128)(2,1)S(1)}, u32[]{:S(2)}, u32[]{:S(2)}) collective-permute-start(bf16[48,896]{1,0:T(8,128)(2,1)S(1)} %get-tuple-element.58), channel_id=1, source_target_pairs={{0,24},{8,16},{16,8},{24,0},{1,25},{9,17},{17,9},{25,1},{2,26},{10... | collective-permute-start | bytes 258056 | tf_op jit(solution)/shard_map/ppermute | solution.py:435
  79.0 1.4 %shard_map.120.refs_3_ = f32[192,896]{1,0:T(8,128)S(1)} custom-call(bf16[2,1,192,256]{3,2,1,0:T(8,128)(2,1)S(1)} %collective-permute-done.23.refs_0_.refs_4_, bf16[2,1,192,256]{3,2,1,0:T(8,128)(2,1)S(1)} %collective-permute-done.24.refs_1_.refs_5_, bf16[2,1,192,256]{3,2,1,0:T(8,128)(2,1)S(1)} %pad_maximum_fusion.1.refs_2_.refs_0_, ...), custom_call_target="tpu_custom_call" | custom-call | flops 704643072 | bytes 9502720 | tf_op jit(solution)/shard_map/pallas_call | solution.py:107
  80.4 0.8 shard_map.121
  81.2 0.9 %collective-permute-start.27 = (bf16[48,896]{1,0:T(8,128)(2,1)S(1)}, bf16[48,896]{1,0:T(8,128)(2,1)S(1)}, u32[]{:S(2)}, u32[]{:S(2)}) collective-permute-start(bf16[48,896]{1,0:T(8,128)(2,1)S(1)} %get-tuple-element.70), channel_id=1, source_target_pairs={{0,8},{8,0},{16,24},{24,16},{1,9},{9,1},{17,25},{25,17},{2,10},{10... | collective-permute-start | bytes 258056 | tf_op jit(solution)/shard_map/ppermute | solution.py:435
  82.2 1.6 %collective-permute-start.28 = (bf16[48,896]{1,0:T(8,128)(2,1)S(1)}, bf16[48,896]{1,0:T(8,128)(2,1)S(1)}, u32[]{:S(2)}, u32[]{:S(2)}) collective-permute-start(bf16[48,896]{1,0:T(8,128)(2,1)S(1)} %get-tuple-element.71), channel_id=1, source_target_pairs={{0,16},{8,24},{16,0},{24,8},{1,17},{9,25},{17,1},{25,9},{2,18},{10... | collective-permute-start | bytes 258056 | tf_op jit(solution)/shard_map/ppermute | solution.py:435
  83.7 1.1 %collective-permute-start.29 = (bf16[48,896]{1,0:T(8,128)(2,1)S(1)}, bf16[48,896]{1,0:T(8,128)(2,1)S(1)}, u32[]{:S(2)}, u32[]{:S(2)}) collective-permute-start(bf16[48,896]{1,0:T(8,128)(2,1)S(1)} %get-tuple-element.72), channel_id=1, source_target_pairs={{0,24},{8,16},{16,8},{24,0},{1,25},{9,17},{17,9},{25,1},{2,26},{10... | collective-permute-start | bytes 258056 | tf_op jit(solution)/shard_map/ppermute | solution.py:435
  84.8 3.0 %shard_map.124 = (bf16[1,896,2048]{2,1,0:T(8,128)(2,1)}, bf16[1,896,2048]{2,1,0:T(8,128)(2,1)}) custom-call(bf16[2,1,192,256]{3,2,1,0:T(8,128)(2,1)S(1)} %pad_maximum_fusion.1.refs_2_.refs_0_, bf16[2,1,192,256]{3,2,1,0:T(8,128)(2,1)S(1)} %collective-permute-done.25.refs_3_.refs_1_, ...), custom_call_target="tpu_custom_call", output_to_operand_aliasing={{1}: (7, {})} | custom-call | flops 1056964608 | bytes 12533760 | tf_op jit(solution)/shard_map/pallas_call | solution.py:107
  87.8 1.3 %collective-permute-done.29.refs_9_ = bf16[48,896]{1,0:T(8,128)(2,1)S(1)} collective-permute-done((bf16[48,896]{1,0:T(8,128)(2,1)S(1)}, bf16[48,896]{1,0:T(8,128)(2,1)S(1)}, u32[]{:S(2)}, u32[]{:S(2)}) %collective-permute-start.29) | collective-permute-done | bytes 86048 | tf_op jit(solution)/shard_map/ppermute | solution.py:435
  89.1 1.0 %shard_map.122 = (bf16[128,896]{1,0:T(8,128)(2,1)}, bf16[128,896]{1,0:T(8,128)(2,1)}) custom-call(bf16[128,192]{1,0:T(8,128)(2,1)S(1)} %get-tuple-element.43.refs_0_, bf16[128,192]{1,0:T(8,128)(2,1)S(1)} %get-tuple-element.44.refs_1_, bf16[48,896]{1,0:T(8,128)(2,1)S(1)} %get-tuple-element.55.refs_2_, bf16[48,896]{1,0:T(8,128)(2,1)S(1)} %collective-permute-done.10.refs_3_, ...), custom_call_target="tpu_custom_call" | custom-call | flops 88080384 | bytes 1245184 | tf_op jit(solution)/shard_map/pallas_call | solution.py:107
  (28 shorter events, 0.2 us)
Async XLA Ops:
  2.2 8.8 %collective-permute-start = (bf16[48,896]{1,0:T(8,128)(2,1)S(1)}, bf16[48,896]{1,0:T(8,128)(2,1)S(1)}, u32[]{:S(2)}, u32[]{:S(2)}) collective-permute-start(bf16[48,896]{1,0:T(8,128)(2,1)S(1)} %get-tuple-element.41.refs_3_), channel_id=1, source_target_pairs={{0,8},{8,0},{16,24},{24,16},{1,9},{9,1},{17,25},{25,17},{2,10},{10... | collective-permute-start | bytes 258056 | tf_op jit(solution)/shard_map/ppermute | solution.py:435
  5.2 5.8 %collective-permute-start.1 = (bf16[48,896]{1,0:T(8,128)(2,1)S(1)}, bf16[48,896]{1,0:T(8,128)(2,1)S(1)}, u32[]{:S(2)}, u32[]{:S(2)}) collective-permute-start(bf16[48,896]{1,0:T(8,128)(2,1)S(1)} %get-tuple-element.46), channel_id=1, source_target_pairs={{0,16},{8,24},{16,0},{24,8},{1,17},{9,25},{17,1},{25,9},{2,18},{10... | collective-permute-start | bytes 258056 | tf_op jit(solution)/shard_map/ppermute | solution.py:435
  6.7 5.4 %collective-permute-start.2 = (bf16[48,896]{1,0:T(8,128)(2,1)S(1)}, bf16[48,896]{1,0:T(8,128)(2,1)S(1)}, u32[]{:S(2)}, u32[]{:S(2)}) collective-permute-start(bf16[48,896]{1,0:T(8,128)(2,1)S(1)} %get-tuple-element.47), channel_id=1, source_target_pairs={{0,24},{8,16},{16,8},{24,0},{1,25},{9,17},{17,9},{25,1},{2,26},{10... | collective-permute-start | bytes 258056 | tf_op jit(solution)/shard_map/ppermute | solution.py:435
  13.1 2.4 %collective-permute-start.3 = (bf16[4,2,192,256]{3,2,1,0:T(8,128)(2,1)S(1)}, bf16[4,2,192,256]{3,2,1,0:T(8,128)(2,1)S(1)}, u32[]{:S(2)}, u32[]{:S(2)}) collective-permute-start(bf16[4,2,192,256]{3,2,1,0:T(8,128)(2,1)S(1)} %get-tuple-element.50), channel_id=1, source_target_pairs={{0,1},{1,0},{2,3},{3,2},{4,5},{5,4},{6,7},{7,6},{8,9},{9,8},{10,11... | collective-permute-start | bytes 2359304 | tf_op jit(solution)/shard_map/ppermute | solution.py:405
  16.5 12.0 %collective-permute-start.4 = (bf16[2,2,192,256]{3,2,1,0:T(8,128)(2,1)S(1)}, bf16[2,2,192,256]{3,2,1,0:T(8,128)(2,1)S(1)}, u32[]{:S(2)}, u32[]{:S(2)}) collective-permute-start(bf16[2,2,192,256]{3,2,1,0:T(8,128)(2,1)S(1)} %get-tuple-element.52.refs_5_), channel_id=1, source_target_pairs={{0,2},{1,5},{2,0},{3,7},{4,6},{5,1},{6,4},{7,3},{8,10},{9,13},{10,... | collective-permute-start | bytes 1179656 | tf_op jit(solution)/shard_map/ppermute | solution.py:402
  18.1 5.4 %collective-permute-start.13 = (bf16[48,896]{1,0:T(8,128)(2,1)S(1)}, bf16[48,896]{1,0:T(8,128)(2,1)S(1)}, u32[]{:S(2)}, u32[]{:S(2)}) collective-permute-start(bf16[48,896]{1,0:T(8,128)(2,1)S(1)} %get-tuple-element.60), channel_id=1, source_target_pairs={{0,8},{8,0},{16,24},{24,16},{1,9},{9,1},{17,25},{25,17},{2,10},{10... | collective-permute-start | bytes 258056 | tf_op jit(solution)/shard_map/ppermute | solution.py:435
  19.0 5.9 %collective-permute-start.14 = (bf16[48,896]{1,0:T(8,128)(2,1)S(1)}, bf16[48,896]{1,0:T(8,128)(2,1)S(1)}, u32[]{:S(2)}, u32[]{:S(2)}) collective-permute-start(bf16[48,896]{1,0:T(8,128)(2,1)S(1)} %get-tuple-element.61), channel_id=1, source_target_pairs={{0,16},{8,24},{16,0},{24,8},{1,17},{9,25},{17,1},{25,9},{2,18},{10... | collective-permute-start | bytes 258056 | tf_op jit(solution)/shard_map/ppermute | solution.py:435
  20.5 5.6 %collective-permute-start.15 = (bf16[48,896]{1,0:T(8,128)(2,1)S(1)}, bf16[48,896]{1,0:T(8,128)(2,1)S(1)}, u32[]{:S(2)}, u32[]{:S(2)}) collective-permute-start(bf16[48,896]{1,0:T(8,128)(2,1)S(1)} %get-tuple-element.62), channel_id=1, source_target_pairs={{0,24},{8,16},{16,8},{24,0},{1,25},{9,17},{17,9},{25,1},{2,26},{10... | collective-permute-start | bytes 258056 | tf_op jit(solution)/shard_map/ppermute | solution.py:435
  26.9 3.5 %collective-permute-start.16 = (bf16[4,1,192,256]{3,2,1,0:T(8,128)(2,1)S(1)}, bf16[4,1,192,256]{3,2,1,0:T(8,128)(2,1)S(1)}, u32[]{:S(2)}, u32[]{:S(2)}) collective-permute-start(bf16[4,1,192,256]{3,2,1,0:T(8,128)(2,1)S(1)} %get-tuple-element.64), channel_id=1, source_target_pairs={{0,1},{1,0},{2,3},{3,2},{4,5},{5,4},{6,7},{7,6},{8,9},{9,8},{10,11... | collective-permute-start | bytes 1179656 | tf_op jit(solution)/shard_map/ppermute | solution.py:405
  28.6 11.8 %collective-permute-start.5 = (bf16[1,2,192,256]{3,2,1,0:T(8,128)(2,1)S(1)}, bf16[1,2,192,256]{3,2,1,0:T(8,128)(2,1)S(1)}, u32[]{:S(2)}, u32[]{:S(2)}) collective-permute-start(bf16[1,2,192,256]{3,2,1,0:T(8,128)(2,1)S(1)} %slice.38), channel_id=1, source_target_pairs={{0,4},{1,3},{2,6},{3,1},{4,0},{5,7},{6,2},{7,5},{8,12},{9,11},{10,... | collective-permute-start | bytes 589832 | tf_op jit(solution)/shard_map/ppermute | solution.py:402
  31.2 33.7 %copy-start = (s32[128,1]{0,1:T(1,128)S(1)}, s32[128,1]{0,1:T(1,128)}, u32[]{:S(2)}) copy-start(s32[128,1]{0,1:T(1,128)} %param.9) | copy-start | bytes 1540
  31.2 33.7 %copy-start.1 = (bf16[128,1]{0,1:T(2,128)(2,1)S(1)}, bf16[128,1]{0,1:T(2,128)(2,1)}, u32[]{:S(2)}) copy-start(bf16[128,1]{0,1:T(2,128)(2,1)} %param.8) | copy-start | bytes 772
  31.2 9.3 %collective-permute-start.17 = (bf16[2,1,192,256]{3,2,1,0:T(8,128)(2,1)S(1)}, bf16[2,1,192,256]{3,2,1,0:T(8,128)(2,1)S(1)}, u32[]{:S(2)}, u32[]{:S(2)}) collective-permute-start(bf16[2,1,192,256]{3,2,1,0:T(8,128)(2,1)S(1)} %get-tuple-element.66), channel_id=1, source_target_pairs={{0,2},{1,5},{2,0},{3,7},{4,6},{5,1},{6,4},{7,3},{8,10},{9,13},{10,... | collective-permute-start | bytes 589832 | tf_op jit(solution)/shard_map/ppermute | solution.py:402
  40.5 6.0 %collective-permute-start.18 = (bf16[1,1,192,256]{3,2,1,0:T(8,128)(2,1)S(1)}, bf16[1,1,192,256]{3,2,1,0:T(8,128)(2,1)S(1)}, u32[]{:S(2)}, u32[]{:S(2)}) collective-permute-start(bf16[1,1,192,256]{3,2,1,0:T(8,128)(2,1)S(1)} %slice.39), channel_id=1, source_target_pairs={{0,4},{1,3},{2,6},{3,1},{4,0},{5,7},{6,2},{7,5},{8,12},{9,11},{10,... | collective-permute-start | bytes 294920 | tf_op jit(solution)/shard_map/ppermute | solution.py:402
  42.4 9.1 %collective-permute-start.6 = (bf16[1,1,192,256]{3,2,1,0:T(8,128)(2,1)S(1)}, bf16[1,1,192,256]{3,2,1,0:T(8,128)(2,1)S(1)}, u32[]{:S(2)}, u32[]{:S(2)}) collective-permute-start(bf16[1,1,192,256]{3,2,1,0:T(8,128)(2,1)S(1)} %bitcast.35), channel_id=1, source_target_pairs={{0,4},{1,5},{2,6},{3,7},{4,0},{5,1},{6,2},{7,3},{8,12},{9,13},{10,... | collective-permute-start | bytes 294920 | tf_op jit(solution)/shard_map/ppermute | solution.py:402
  46.6 9.1 %collective-permute-start.22 = (bf16[1,1,192,256]{3,2,1,0:T(8,128)(2,1)S(1)}, bf16[1,1,192,256]{3,2,1,0:T(8,128)(2,1)S(1)}, u32[]{:S(2)}, u32[]{:S(2)}) collective-permute-start(bf16[1,1,192,256]{3,2,1,0:T(8,128)(2,1)S(1)} %get-tuple-element.77), channel_id=1, source_target_pairs={{0,4},{1,3},{2,6},{3,1},{4,0},{5,7},{6,2},{7,5},{8,12},{9,11},{10,... | collective-permute-start | bytes 294920 | tf_op jit(solution)/shard_map/ppermute | solution.py:402
  51.4 12.9 %collective-permute-start.7 = (bf16[2,1,192,256]{3,2,1,0:T(8,128)(2,1)S(1)}, bf16[2,1,192,256]{3,2,1,0:T(8,128)(2,1)S(1)}, u32[]{:S(2)}, u32[]{:S(2)}) collective-permute-start(bf16[2,1,192,256]{3,2,1,0:T(8,128)(2,1)S(1)} %pad_maximum_fusion.refs_0_), channel_id=1, source_target_pairs={{0,2},{1,3},{2,0},{3,1},{4,6},{5,7},{6,4},{7,5},{8,10},{9,11},{10,... | collective-permute-start | bytes 589832 | tf_op jit(solution)/shard_map/ppermute | solution.py:402
  53.9 11.2 %collective-permute-start.9 = (bf16[2,1,192,256]{3,2,1,0:T(8,128)(2,1)S(1)}, bf16[2,1,192,256]{3,2,1,0:T(8,128)(2,1)S(1)}, u32[]{:S(2)}, u32[]{:S(2)}) collective-permute-start(bf16[2,1,192,256]{3,2,1,0:T(8,128)(2,1)S(1)} %pad_maximum_fusion.refs_0_), channel_id=1, source_target_pairs={{0,1},{1,0},{2,3},{3,2},{4,5},{5,4},{6,7},{7,6},{8,9},{9,8},{10,11... | collective-permute-start | bytes 589832 | tf_op jit(solution)/shard_map/ppermute | solution.py:405
  53.9 10.3 %collective-permute-start.19 = (bf16[1,1,192,256]{3,2,1,0:T(8,128)(2,1)S(1)}, bf16[1,1,192,256]{3,2,1,0:T(8,128)(2,1)S(1)}, u32[]{:S(2)}, u32[]{:S(2)}) collective-permute-start(bf16[1,1,192,256]{3,2,1,0:T(8,128)(2,1)S(1)} %get-tuple-element.78), channel_id=1, source_target_pairs={{0,4},{1,5},{2,6},{3,7},{4,0},{5,1},{6,2},{7,3},{8,12},{9,13},{10,... | collective-permute-start | bytes 294920 | tf_op jit(solution)/shard_map/ppermute | solution.py:402
  55.7 9.5 %collective-permute-start.23 = (bf16[2,1,192,256]{3,2,1,0:T(8,128)(2,1)S(1)}, bf16[2,1,192,256]{3,2,1,0:T(8,128)(2,1)S(1)}, u32[]{:S(2)}, u32[]{:S(2)}) collective-permute-start(bf16[2,1,192,256]{3,2,1,0:T(8,128)(2,1)S(1)} %pad_maximum_fusion.2.refs_0_), channel_id=1, source_target_pairs={{0,2},{1,5},{2,0},{3,7},{4,6},{5,1},{6,4},{7,3},{8,10},{9,13},{10,... | collective-permute-start | bytes 589832 | tf_op jit(solution)/shard_map/ppermute | solution.py:402
  64.2 6.5 %collective-permute-start.20 = (bf16[2,1,192,256]{3,2,1,0:T(8,128)(2,1)S(1)}, bf16[2,1,192,256]{3,2,1,0:T(8,128)(2,1)S(1)}, u32[]{:S(2)}, u32[]{:S(2)}) collective-permute-start(bf16[2,1,192,256]{3,2,1,0:T(8,128)(2,1)S(1)} %pad_maximum_fusion.1.refs_2_.refs_0_), channel_id=1, source_target_pairs={{0,2},{1,3},{2,0},{3,1},{4,6},{5,7},{6,4},{7,5},{8,10},{9,11},{10,... | collective-permute-start | bytes 589832 | tf_op jit(solution)/shard_map/ppermute | solution.py:402
  64.3 6.4 %collective-permute-start.26 = (bf16[2,1,192,256]{3,2,1,0:T(8,128)(2,1)S(1)}, bf16[2,1,192,256]{3,2,1,0:T(8,128)(2,1)S(1)}, u32[]{:S(2)}, u32[]{:S(2)}) collective-permute-start(bf16[2,1,192,256]{3,2,1,0:T(8,128)(2,1)S(1)} %pad_maximum_fusion.2.refs_0_), channel_id=1, source_target_pairs={{0,1},{1,0},{2,3},{3,2},{4,5},{5,4},{6,7},{7,6},{8,9},{9,8},{10,11... | collective-permute-start | bytes 589832 | tf_op jit(solution)/shard_map/ppermute | solution.py:405
  64.4 8.8 %collective-permute-start.8 = (bf16[2,1,192,256]{3,2,1,0:T(8,128)(2,1)S(1)}, bf16[2,1,192,256]{3,2,1,0:T(8,128)(2,1)S(1)}, u32[]{:S(2)}, u32[]{:S(2)}) collective-permute-start(bf16[2,1,192,256]{3,2,1,0:T(8,128)(2,1)S(1)} %collective-permute-done.7.refs_0_), channel_id=1, source_target_pairs={{0,1},{1,0},{2,3},{3,2},{4,5},{5,4},{6,7},{7,6},{8,9},{9,8},{10,11... | collective-permute-start | bytes 589832 | tf_op jit(solution)/shard_map/ppermute | solution.py:405
  65.1 12.8 %collective-permute-start.25 = (bf16[2,1,192,256]{3,2,1,0:T(8,128)(2,1)S(1)}, bf16[2,1,192,256]{3,2,1,0:T(8,128)(2,1)S(1)}, u32[]{:S(2)}, u32[]{:S(2)}) collective-permute-start(bf16[2,1,192,256]{3,2,1,0:T(8,128)(2,1)S(1)} %pad_maximum_fusion.1.refs_2_.refs_0_), channel_id=1, source_target_pairs={{0,1},{1,0},{2,3},{3,2},{4,5},{5,4},{6,7},{7,6},{8,9},{9,8},{10,11... | collective-permute-start | bytes 589832 | tf_op jit(solution)/shard_map/ppermute | solution.py:405
  65.3 13.8 %collective-permute-start.24 = (bf16[2,1,192,256]{3,2,1,0:T(8,128)(2,1)S(1)}, bf16[2,1,192,256]{3,2,1,0:T(8,128)(2,1)S(1)}, u32[]{:S(2)}, u32[]{:S(2)}) collective-permute-start(bf16[2,1,192,256]{3,2,1,0:T(8,128)(2,1)S(1)} %collective-permute-done.23.refs_0_.refs_4_), channel_id=1, source_target_pairs={{0,1},{1,0},{2,3},{3,2},{4,5},{5,4},{6,7},{7,6},{8,9},{9,8},{10,11... | collective-permute-start | bytes 589832 | tf_op jit(solution)/shard_map/ppermute | solution.py:405
  70.7 9.7 %collective-permute-start.21 = (bf16[2,1,192,256]{3,2,1,0:T(8,128)(2,1)S(1)}, bf16[2,1,192,256]{3,2,1,0:T(8,128)(2,1)S(1)}, u32[]{:S(2)}, u32[]{:S(2)}) collective-permute-start(bf16[2,1,192,256]{3,2,1,0:T(8,128)(2,1)S(1)} %collective-permute-done.20.refs_0_.refs_2_), channel_id=1, source_target_pairs={{0,1},{1,0},{2,3},{3,2},{4,5},{5,4},{6,7},{7,6},{8,9},{9,8},{10,11... | collective-permute-start | bytes 589832 | tf_op jit(solution)/shard_map/ppermute | solution.py:405
  73.8 9.9 %collective-permute-start.10 = (bf16[48,896]{1,0:T(8,128)(2,1)S(1)}, bf16[48,896]{1,0:T(8,128)(2,1)S(1)}, u32[]{:S(2)}, u32[]{:S(2)}) collective-permute-start(bf16[48,896]{1,0:T(8,128)(2,1)S(1)} %get-tuple-element.56), channel_id=1, source_target_pairs={{0,8},{8,0},{16,24},{24,16},{1,9},{9,1},{17,25},{25,17},{2,10},{10... | collective-permute-start | bytes 258056 | tf_op jit(solution)/shard_map/ppermute | solution.py:435
  74.7 13.0 %collective-permute-start.11 = (bf16[48,896]{1,0:T(8,128)(2,1)S(1)}, bf16[48,896]{1,0:T(8,128)(2,1)S(1)}, u32[]{:S(2)}, u32[]{:S(2)}) collective-permute-start(bf16[48,896]{1,0:T(8,128)(2,1)S(1)} %get-tuple-element.57), channel_id=1, source_target_pairs={{0,16},{8,24},{16,0},{24,8},{1,17},{9,25},{17,1},{25,9},{2,18},{10... | collective-permute-start | bytes 258056 | tf_op jit(solution)/shard_map/ppermute | solution.py:435
  77.9 9.9 %collective-permute-start.12 = (bf16[48,896]{1,0:T(8,128)(2,1)S(1)}, bf16[48,896]{1,0:T(8,128)(2,1)S(1)}, u32[]{:S(2)}, u32[]{:S(2)}) collective-permute-start(bf16[48,896]{1,0:T(8,128)(2,1)S(1)} %get-tuple-element.58), channel_id=1, source_target_pairs={{0,24},{8,16},{16,8},{24,0},{1,25},{9,17},{17,9},{25,1},{2,26},{10... | collective-permute-start | bytes 258056 | tf_op jit(solution)/shard_map/ppermute | solution.py:435
  81.2 6.6 %collective-permute-start.27 = (bf16[48,896]{1,0:T(8,128)(2,1)S(1)}, bf16[48,896]{1,0:T(8,128)(2,1)S(1)}, u32[]{:S(2)}, u32[]{:S(2)}) collective-permute-start(bf16[48,896]{1,0:T(8,128)(2,1)S(1)} %get-tuple-element.70), channel_id=1, source_target_pairs={{0,8},{8,0},{16,24},{24,16},{1,9},{9,1},{17,25},{25,17},{2,10},{10... | collective-permute-start | bytes 258056 | tf_op jit(solution)/shard_map/ppermute | solution.py:435
  82.2 5.6 %collective-permute-start.28 = (bf16[48,896]{1,0:T(8,128)(2,1)S(1)}, bf16[48,896]{1,0:T(8,128)(2,1)S(1)}, u32[]{:S(2)}, u32[]{:S(2)}) collective-permute-start(bf16[48,896]{1,0:T(8,128)(2,1)S(1)} %get-tuple-element.71), channel_id=1, source_target_pairs={{0,16},{8,24},{16,0},{24,8},{1,17},{9,25},{17,1},{25,9},{2,18},{10... | collective-permute-start | bytes 258056 | tf_op jit(solution)/shard_map/ppermute | solution.py:435
  83.7 5.4 %collective-permute-start.29 = (bf16[48,896]{1,0:T(8,128)(2,1)S(1)}, bf16[48,896]{1,0:T(8,128)(2,1)S(1)}, u32[]{:S(2)}, u32[]{:S(2)}) collective-permute-start(bf16[48,896]{1,0:T(8,128)(2,1)S(1)} %get-tuple-element.72), channel_id=1, source_target_pairs={{0,24},{8,16},{16,8},{24,0},{1,25},{9,17},{17,9},{25,1},{2,26},{10... | collective-permute-start | bytes 258056 | tf_op jit(solution)/shard_map/ppermute | solution.py:435

commit v7 on v6

--- a/solution.py
+++ b/solution.py
@@ -330,50 +330,56 @@
     )
 
 
-def weight_grads(groups, joined, unit, count, down, onto=(), after=()):
-    total, width = joined.shape
-    pieces = [(i, *piece) for i, group in enumerate(groups) for piece in group]
+def weight_grads(groups, unit, count, onto=(), after=()):
+    pieces = [(i, *piece) for i, group in enumerate(groups) for piece in group[0]]
     units = [u for _, _, _, u in pieces]
-    k, n = len(pieces), len(groups)
-    steps = sum(u.shape[0] for u in units)
-    shape = (1, count * unit, width) if down else (1, width, count * unit)
+    rows = [group[1] for group in groups]
+    downs = [group[2] for group in groups]
+    (total, width), k, n = rows[0].shape, len(pieces), len(groups)
+    steps = [sum(u.shape[0] for i, _, _, u in pieces if downs[i] == d) for d in (False, True)]
+    shapes = [(1, count * unit, width) if d else (1, width, count * unit) for d in downs]
 
     def kernel(*refs):
-        u_refs, x_ref = refs[:k], refs[k]
-        out_refs = refs[k + 1 + len(onto) :][:n]
-        turned, held, sems = refs[-3:]
-        if not down:
-            turned[...] = x_ref[...].T
-        waits = []
+        u_refs, row_refs = refs[:k], refs[k : k + n]
+        out_refs = refs[k + n + len(onto) :][:n]
+        turned, across, along, sems = refs[-4:]
+        source = None
+        waits, used = [], [0, 0]
         for (i, block, first, _), u_ref in zip(pieces, u_refs):
+            down = downs[i]
+            if not down and source is not rows[i]:
+                source = rows[i]
+                turned[...] = row_refs[i][...].T
             for j in range(u_ref.shape[0]):
                 at = pl.ds(pl.multiple_of(block(first + j) * unit, unit), unit)
-                slot = len(waits)
+                held = (along if down else across).at[used[down]]
+                used[down] += 1
                 if down:
-                    held[slot] = mm(u_ref[j, 0], x_ref[...], TN).astype(BF16)
+                    held[...] = mm(u_ref[j, 0], row_refs[i][...], TN).astype(BF16)
                     target = out_refs[i].at[0, at, :]
                 else:
-                    held[slot] = mm(turned[...], u_ref[j, 0]).astype(BF16)
+                    held[...] = mm(turned[...], u_ref[j, 0]).astype(BF16)
                     target = out_refs[i].at[0, :, at]
-                waits.append(pltpu.make_async_copy(held.at[slot], target, sems.at[slot]))
-                waits[slot].start()
+                waits.append(pltpu.make_async_copy(held, target, sems.at[len(waits)]))
+                waits[-1].start()
         for wait in waits:
             wait.wait()
 
     return call(
         kernel,
-        [spec(shape)] * n,
+        [spec(shape) for shape in shapes],
         [ANY] * n,
-        [*units, joined, *onto],
-        [VMEM] * (k + 1) + [ANY] * len(onto),
+        [*units, *rows, *onto],
+        [VMEM] * (k + n) + [ANY] * len(onto),
         [
-            pltpu.VMEM((8, 128) if down else (width, total), BF16),
-            pltpu.VMEM((steps, unit, width) if down else (steps, width, unit), BF16),
-            pltpu.SemaphoreType.DMA((steps,)),
+            pltpu.VMEM((width, total) if steps[0] else (8, 128), BF16),
+            pltpu.VMEM((steps[0], width, unit) if steps[0] else (1, 8, 128), BF16),
+            pltpu.VMEM((steps[1], unit, width) if steps[1] else (1, 8, 128), BF16),
+            pltpu.SemaphoreType.DMA((sum(steps),)),
         ],
         after,
-        2 * steps * total * width * unit,
-        {k + 1 + i: n - len(onto) + i for i in range(len(onto))},
+        2 * sum(steps) * total * width * unit,
+        {k + n + i: n - len(onto) + i for i in range(len(onto))},
     )
 
 
@@ -488,15 +494,18 @@
     (part,) = unit_rows(((weight_down, hidden_early),), unit, True)
     out = unit_rows(((weight_down, hidden_late),), unit, True, part, slot)
     out_back = expert_swap(out)
-    grad_w_down = weight_grads((hidden_early,), dy_all, unit, parts, True)
-    (grad_w_down,) = weight_grads((hidden_late,), dy_all, unit, parts, True, grad_w_down)
-
+    grad_w_down = weight_grads(((hidden_early, dy_all, True),), unit, parts)
     (part,) = unit_rows(((weight_up, up_early),), unit, False)
     (part,) = unit_rows(((weight_up, up_late), (weight_gate, gate_early)), unit, False, part)
     back = unit_rows(((weight_gate, gate_late),), unit, False, part, slot)
     grad_back = expert_swap(back)
-    grad_w_up = weight_grads((up_early,), x_all, unit, parts, False)
-    grad_w_gate, grad_w_up = weight_grads((gate_all, up_late), x_all, unit, parts, False, grad_w_up)
+    grad_w_up = weight_grads(((up_early, x_all, False),), unit, parts)
+    grad_w_gate, grad_w_up, grad_w_down = weight_grads(
+        ((gate_all, x_all, False), (up_late, x_all, False), (hidden_late, dy_all, True)),
+        unit,
+        parts,
+        (*grad_w_up, *grad_w_down),
+    )
     mixed, grad_tokens = collect(
         (gated, plain), ([out[0]] + out_back, [back[0]] + grad_back)
     )

time: 90.3 us -> 87.6 us (0.970)
  waiting for transfers between devices: 33 us -> 32 us
    ppermute x10, waiting for transfers between devices: 23.7 us -> 27.6 us  [step_swap(): return lax.ppermute(x, 'tensor', pairs)]
    ppermute x12, waiting for transfers between devices: 6.95 us -> 4.35 us  [expert_swap(): out.append(lax.ppermute(rows[m - skipped], 'expert', pairs))]
    ppermute x8, waiting for transfers between devices: 2.29 us -> 0.08 us  [core_swap(): return lax.ppermute(x, 'tensor', [(d, d ^ 1) for d in range(parts)])]
    pallas_call x17 -> x16, Pallas kernels: 22.5 us -> 21.6 us  [call(): pl.pallas_call(body, out_shape=list(outs), in_specs=list(in_specs) + [ANY...]
  transfers between devices with their start and end apart: 30 -> 30, of which waited for: 12 -> 15; matrix products, arithmetic and copies ran while one was open for 0% -> 1% of each run, Pallas kernels for 20% -> 20%
where the time goes in v7:
time: 87.6 us; the launch traced here: 87.5 us
  starting transfers between devices  32.5 us (37%)
  waiting for transfers between devices  32 us (37%)
  Pallas kernels  21.6 us (25%)
  between operations  0.92 us (1%)
    ppermute x10, waiting for transfers between devices, step_swap(): return lax.ppermute(x, 'tensor', pairs)  27.6 us
    pallas_call x16, Pallas kernels, call(): pl.pallas_call(body, out_shape=list(outs), in_specs=list(in_specs) + [ANY...  21.6 us
    ppermute x10, starting transfers between devices, step_swap(): return lax.ppermute(x, 'tensor', pairs)  16.5 us
    ppermute x12, starting transfers between devices, expert_swap(): out.append(lax.ppermute(rows[m - skipped], 'expert', pairs))  15.3 us
    ppermute x12, waiting for transfers between devices, expert_swap(): out.append(lax.ppermute(rows[m - skipped], 'expert', pairs))  4.35 us
  transfers between devices with their start and end apart: 30, of which 15 were waited for; matrix products, arithmetic and copies ran while one was open for 1% of the time, Pallas kernels for 20%

profile of v7, /device:TPU:0, one launch (start us, length us, event | category | flops | bytes accessed | tf_op | source)
XLA Modules:
  0.0 87.5 jit_solution(11417553837755881252)
XLA Ops:
  0.6 1.5 %shard_map.110 = (bf16[48,896]{1,0:T(8,128)(2,1)S(1)}, bf16[48,896]{1,0:T(8,128)(2,1)S(1)}, bf16[48,896]{1,0:T(8,128)(2,1)S(1)}, bf16[48,896]{1,0:T(8,128)(2,1)S...) custom-call(s32[1,128]{1,0:T(1,128)} %bitcast.28, ...), custom_call_target="tpu_custom_call" | custom-call | flops 88080384 | bytes 1147648 | tf_op jit(solution)/shard_map/pallas_call | solution.py:107
  2.2 3.1 %collective-permute-start.1 = (bf16[48,896]{1,0:T(8,128)(2,1)S(1)}, bf16[48,896]{1,0:T(8,128)(2,1)S(1)}, u32[]{:S(2)}, u32[]{:S(2)}) collective-permute-start(bf16[48,896]{1,0:T(8,128)(2,1)S(1)} %get-tuple-element.47), channel_id=1, source_target_pairs={{0,16},{8,24},{16,0},{24,8},{1,17},{9,25},{17,1},{25,9},{2,18},{10... | collective-permute-start | bytes 258056 | tf_op jit(solution)/shard_map/ppermute | solution.py:441
  5.2 1.4 %collective-permute-start.2 = (bf16[48,896]{1,0:T(8,128)(2,1)S(1)}, bf16[48,896]{1,0:T(8,128)(2,1)S(1)}, u32[]{:S(2)}, u32[]{:S(2)}) collective-permute-start(bf16[48,896]{1,0:T(8,128)(2,1)S(1)} %get-tuple-element.48), channel_id=1, source_target_pairs={{0,24},{8,16},{16,8},{24,0},{1,25},{9,17},{17,9},{25,1},{2,26},{10... | collective-permute-start | bytes 258056 | tf_op jit(solution)/shard_map/ppermute | solution.py:441
  6.6 0.1 collective-permute-start
  6.8 4.2 %shard_map.111 = (bf16[896,2048]{1,0:T(8,128)(2,1)S(1)}, bf16[896,2048]{1,0:T(8,128)(2,1)S(1)}, bf16[2048,896]{1,0:T(8,128)(2,1)S(1)}) custom-call(bf16[896,2048]{1,0:T(8,128)(2,1)} %bitcast.32, bf16[896,2048]{1,0:T(8,128)(2,1)} %bitcast.33, bf16[2048,896]{1,0:T(8,128)(2,1)} %bitcast.34, bf16[48,896]{1,0:T(8,128)(2,1)S(1)} %get-tuple-element.42.refs_3_), custom_call_target="tpu_custom_call" | custom-call | bytes 22020096 | tf_op jit(solution)/shard_map/pallas_call | solution.py:107
  11.0 0.3 collective-permute-done.2.refs_3_
  11.3 0.0 collective-permute-done.refs_1_
  11.3 1.0 %shard_map.113 = (bf16[4,2,192,256]{3,2,1,0:T(8,128)(2,1)S(1)}, bf16[192,896]{1,0:T(8,128)(2,1)S(1)}) custom-call(bf16[48,896]{1,0:T(8,128)(2,1)S(1)} %get-tuple-element.46.refs_0_, bf16[48,896]{1,0:T(8,128)(2,1)S(1)} %collective-permute-done.refs_1_, bf16[48,896]{1,0:T(8,128)(2,1)S(1)} %collective-permute-done.1.refs_2_, ...), custom_call_target="tpu_custom_call" | custom-call | flops 704643072 | bytes 8814592 | tf_op jit(solution)/shard_map/pallas_call | solution.py:107
  12.3 0.1 collective-permute-start.3
  12.4 1.7 %collective-permute-start.13 = (bf16[48,896]{1,0:T(8,128)(2,1)S(1)}, bf16[48,896]{1,0:T(8,128)(2,1)S(1)}, u32[]{:S(2)}, u32[]{:S(2)}) collective-permute-start(bf16[48,896]{1,0:T(8,128)(2,1)S(1)} %get-tuple-element.61), channel_id=1, source_target_pairs={{0,8},{8,0},{16,24},{24,16},{1,9},{9,1},{17,25},{25,17},{2,10},{10... | collective-permute-start | bytes 258056 | tf_op jit(solution)/shard_map/ppermute | solution.py:441
  14.1 1.5 %collective-permute-start.14 = (bf16[48,896]{1,0:T(8,128)(2,1)S(1)}, bf16[48,896]{1,0:T(8,128)(2,1)S(1)}, u32[]{:S(2)}, u32[]{:S(2)}) collective-permute-start(bf16[48,896]{1,0:T(8,128)(2,1)S(1)} %get-tuple-element.62), channel_id=1, source_target_pairs={{0,16},{8,24},{16,0},{24,8},{1,17},{9,25},{17,1},{25,9},{2,18},{10... | collective-permute-start | bytes 258056 | tf_op jit(solution)/shard_map/ppermute | solution.py:441
  15.6 0.3 collective-permute-start.15
  16.0 1.0 %shard_map.114 = (bf16[2,2,192,256]{3,2,1,0:T(8,128)(2,1)S(1)}, f32[2,2,192,256]{3,2,1,0:T(8,128)S(1)}) custom-call(bf16[192,896]{1,0:T(8,128)(2,1)S(1)} %get-tuple-element.50.refs_0_.refs_2_.refs_8_.refs_9_, bf16[896,2048]{1,0:T(8,128)(2,1)S(1)} %get-tuple-element.43.refs_2_.refs_4_.refs_1_.refs_5_, ...), custom_call_target="tpu_custom_call" | custom-call | flops 704643072 | bytes 9650176 | tf_op jit(solution)/shard_map/pallas_call | solution.py:107
  17.0 0.4 collective-permute-done.13.refs_1_
  17.4 2.3 %collective-permute-done.14.refs_2_ = bf16[48,896]{1,0:T(8,128)(2,1)S(1)} collective-permute-done((bf16[48,896]{1,0:T(8,128)(2,1)S(1)}, bf16[48,896]{1,0:T(8,128)(2,1)S(1)}, u32[]{:S(2)}, u32[]{:S(2)}) %collective-permute-start.14) | collective-permute-done | bytes 86048 | tf_op jit(solution)/shard_map/ppermute | solution.py:441
  19.6 1.4 %collective-permute-done.15.refs_3_ = bf16[48,896]{1,0:T(8,128)(2,1)S(1)} collective-permute-done((bf16[48,896]{1,0:T(8,128)(2,1)S(1)}, bf16[48,896]{1,0:T(8,128)(2,1)S(1)}, u32[]{:S(2)}, u32[]{:S(2)}) %collective-permute-start.15) | collective-permute-done | bytes 86048 | tf_op jit(solution)/shard_map/ppermute | solution.py:441
  21.0 0.8 shard_map.117
  21.8 0.1 collective-permute-start.16
  21.9 1.6 %collective-permute-start.4 = (bf16[2,2,192,256]{3,2,1,0:T(8,128)(2,1)S(1)}, bf16[2,2,192,256]{3,2,1,0:T(8,128)(2,1)S(1)}, u32[]{:S(2)}, u32[]{:S(2)}) collective-permute-start(bf16[2,2,192,256]{3,2,1,0:T(8,128)(2,1)S(1)} %get-tuple-element.53.refs_5_), channel_id=1, source_target_pairs={{0,2},{1,5},{2,0},{3,7},{4,6},{5,1},{6,4},{7,3},{8,10},{9,13},{10,... | collective-permute-start | bytes 1179656 | tf_op jit(solution)/shard_map/ppermute | solution.py:408
  23.5 0.1 collective-permute-done.16.refs_2_
  23.6 0.8 shard_map.118
  24.4 1.6 %collective-permute-start.17 = (bf16[2,1,192,256]{3,2,1,0:T(8,128)(2,1)S(1)}, bf16[2,1,192,256]{3,2,1,0:T(8,128)(2,1)S(1)}, u32[]{:S(2)}, u32[]{:S(2)}) collective-permute-start(bf16[2,1,192,256]{3,2,1,0:T(8,128)(2,1)S(1)} %get-tuple-element.67), channel_id=1, source_target_pairs={{0,2},{1,5},{2,0},{3,7},{4,6},{5,1},{6,4},{7,3},{8,10},{9,13},{10,... | collective-permute-start | bytes 589832 | tf_op jit(solution)/shard_map/ppermute | solution.py:408
  26.0 7.8 %collective-permute-done.4 = bf16[2,2,192,256]{3,2,1,0:T(8,128)(2,1)S(1)} collective-permute-done((bf16[2,2,192,256]{3,2,1,0:T(8,128)(2,1)S(1)}, bf16[2,2,192,256]{3,2,1,0:T(8,128)(2,1)S(1)}, u32[]{:S(2)}, u32[]{:S(2)}) %collective-permute-start.4) | collective-permute-done | bytes 393248 | tf_op jit(solution)/shard_map/ppermute | solution.py:408
  33.9 0.1 convert_add_fusion
  34.0 2.7 %collective-permute-start.5 = (bf16[1,2,192,256]{3,2,1,0:T(8,128)(2,1)S(1)}, bf16[1,2,192,256]{3,2,1,0:T(8,128)(2,1)S(1)}, u32[]{:S(2)}, u32[]{:S(2)}) collective-permute-start(bf16[1,2,192,256]{3,2,1,0:T(8,128)(2,1)S(1)} %slice.38), channel_id=1, source_target_pairs={{0,4},{1,3},{2,6},{3,1},{4,0},{5,7},{6,2},{7,5},{8,12},{9,11},{10,... | collective-permute-start | bytes 589832 | tf_op jit(solution)/shard_map/ppermute | solution.py:408
  36.7 3.6 %collective-permute-done.17 = bf16[2,1,192,256]{3,2,1,0:T(8,128)(2,1)S(1)} collective-permute-done((bf16[2,1,192,256]{3,2,1,0:T(8,128)(2,1)S(1)}, bf16[2,1,192,256]{3,2,1,0:T(8,128)(2,1)S(1)}, u32[]{:S(2)}, u32[]{:S(2)}) %collective-permute-start.17) | collective-permute-done | bytes 196640 | tf_op jit(solution)/shard_map/ppermute | solution.py:408
  40.4 0.4 collective-permute-start.18
  40.8 1.2 %collective-permute-done.5 = bf16[1,2,192,256]{3,2,1,0:T(8,128)(2,1)S(1)} collective-permute-done((bf16[1,2,192,256]{3,2,1,0:T(8,128)(2,1)S(1)}, bf16[1,2,192,256]{3,2,1,0:T(8,128)(2,1)S(1)}, u32[]{:S(2)}, u32[]{:S(2)}) %collective-permute-start.5) | collective-permute-done | bytes 196640 | tf_op jit(solution)/shard_map/ppermute | solution.py:408
  42.1 0.1 multiply_convert_fusion.2
  42.2 3.4 %collective-permute-start.6 = (bf16[1,1,192,256]{3,2,1,0:T(8,128)(2,1)S(1)}, bf16[1,1,192,256]{3,2,1,0:T(8,128)(2,1)S(1)}, u32[]{:S(2)}, u32[]{:S(2)}) collective-permute-start(bf16[1,1,192,256]{3,2,1,0:T(8,128)(2,1)S(1)} %bitcast.35), channel_id=1, source_target_pairs={{0,4},{1,5},{2,6},{3,7},{4,0},{5,1},{6,2},{7,3},{8,12},{9,13},{10,... | collective-permute-start | bytes 294920 | tf_op jit(solution)/shard_map/ppermute | solution.py:408
  45.6 2.8 %collective-permute-done.18 = bf16[1,1,192,256]{3,2,1,0:T(8,128)(2,1)S(1)} collective-permute-done((bf16[1,1,192,256]{3,2,1,0:T(8,128)(2,1)S(1)}, bf16[1,1,192,256]{3,2,1,0:T(8,128)(2,1)S(1)}, u32[]{:S(2)}, u32[]{:S(2)}) %collective-permute-start.18) | collective-permute-done | bytes 98336 | tf_op jit(solution)/shard_map/ppermute | solution.py:408
  48.4 0.1 fusion.1
  48.5 0.1 collective-permute-start.22
  48.6 2.2 %collective-permute-done.6 = bf16[1,1,192,256]{3,2,1,0:T(8,128)(2,1)S(1)} collective-permute-done((bf16[1,1,192,256]{3,2,1,0:T(8,128)(2,1)S(1)}, bf16[1,1,192,256]{3,2,1,0:T(8,128)(2,1)S(1)}, u32[]{:S(2)}, u32[]{:S(2)}) %collective-permute-start.6) | collective-permute-done | bytes 98336 | tf_op jit(solution)/shard_map/ppermute | solution.py:408
  50.8 0.1 collective-permute-start.9
  50.9 0.5 collective-permute-start.7
  51.4 2.3 %collective-permute-start.19 = (bf16[1,1,192,256]{3,2,1,0:T(8,128)(2,1)S(1)}, bf16[1,1,192,256]{3,2,1,0:T(8,128)(2,1)S(1)}, u32[]{:S(2)}, u32[]{:S(2)}) collective-permute-start(bf16[1,1,192,256]{3,2,1,0:T(8,128)(2,1)S(1)} %get-tuple-element.80), channel_id=1, source_target_pairs={{0,4},{1,5},{2,6},{3,7},{4,0},{5,1},{6,2},{7,3},{8,12},{9,13},{10,... | collective-permute-start | bytes 294920 | tf_op jit(solution)/shard_map/ppermute | solution.py:408
  53.7 0.4 collective-permute-done.22
  54.1 0.3 collective-permute-start.23
  54.4 4.5 %collective-permute-done.19 = bf16[1,1,192,256]{3,2,1,0:T(8,128)(2,1)S(1)} collective-permute-done((bf16[1,1,192,256]{3,2,1,0:T(8,128)(2,1)S(1)}, bf16[1,1,192,256]{3,2,1,0:T(8,128)(2,1)S(1)}, u32[]{:S(2)}, u32[]{:S(2)}) %collective-permute-start.19) | collective-permute-done | bytes 98336 | tf_op jit(solution)/shard_map/ppermute | solution.py:408
  58.9 3.5 %collective-permute-start.20 = (bf16[2,1,192,256]{3,2,1,0:T(8,128)(2,1)S(1)}, bf16[2,1,192,256]{3,2,1,0:T(8,128)(2,1)S(1)}, u32[]{:S(2)}, u32[]{:S(2)}) collective-permute-start(bf16[2,1,192,256]{3,2,1,0:T(8,128)(2,1)S(1)} %pad_maximum_fusion.1.refs_2_.refs_0_), channel_id=1, source_target_pairs={{0,2},{1,3},{2,0},{3,1},{4,6},{5,7},{6,4},{7,5},{8,10},{9,11},{10,... | collective-permute-start | bytes 589832 | tf_op jit(solution)/shard_map/ppermute | solution.py:408
  62.4 0.4 collective-permute-done.7.refs_0_.refs_6_
  62.8 0.1 collective-permute-start.8
  62.9 0.0 collective-permute-done.9.refs_1_
  62.9 0.4 collective-permute-start.25
  63.3 3.4 %collective-permute-done.23.refs_0_.refs_4_ = bf16[2,1,192,256]{3,2,1,0:T(8,128)(2,1)S(1)} collective-permute-done((bf16[2,1,192,256]{3,2,1,0:T(8,128)(2,1)S(1)}, bf16[2,1,192,256]{3,2,1,0:T(8,128)(2,1)S(1)}, u32[]{:S(2)}, u32[]{:S(2)}) %collective-permute-start.23) | collective-permute-done | bytes 196640 | tf_op jit(solution)/shard_map/ppermute | solution.py:408
  66.7 0.0 collective-permute-start.24
  66.7 0.2 shard_map.112
  67.0 0.6 shard_map.115.refs_3_
  67.6 1.2 %collective-permute-done.20.refs_0_.refs_2_ = bf16[2,1,192,256]{3,2,1,0:T(8,128)(2,1)S(1)} collective-permute-done((bf16[2,1,192,256]{3,2,1,0:T(8,128)(2,1)S(1)}, bf16[2,1,192,256]{3,2,1,0:T(8,128)(2,1)S(1)}, u32[]{:S(2)}, u32[]{:S(2)}) %collective-permute-start.20) | collective-permute-done | bytes 196640 | tf_op jit(solution)/shard_map/ppermute | solution.py:408
  68.8 1.6 %shard_map.124.refs_12_ = bf16[1,2048,896]{2,1,0:T(8,128)(2,1)} custom-call(bf16[2,1,192,256]{3,2,1,0:T(8,128)(2,1)S(1)} %pad_maximum_fusion.refs_0_, bf16[2,1,192,256]{3,2,1,0:T(8,128)(2,1)S(1)} %collective-permute-done.9.refs_1_, bf16[192,896]{1,0:T(8,128)(2,1)S(1)} %get-tuple-element.64.refs_0_.refs_2_.refs_10_), custom_call_target="tpu_custom_call" | custom-call | flops 352321536 | bytes 4407296 | tf_op jit(solution)/shard_map/pallas_call | solution.py:107
  70.4 0.8 shard_map.119.refs_6_
  71.2 1.7 %shard_map.123.refs_11_ = bf16[1,896,2048]{2,1,0:T(8,128)(2,1)} custom-call(bf16[2,1,192,256]{3,2,1,0:T(8,128)(2,1)S(1)} %pad_maximum_fusion.2.refs_0_, bf16[2,1,192,256]{3,2,1,0:T(8,128)(2,1)S(1)} %collective-permute-done.26.refs_1_, bf16[192,896]{1,0:T(8,128)(2,1)S(1)} %get-tuple-element.50.refs_0_.refs_2_.refs_8_.refs_9_), custom_call_target="tpu_custom_call" | custom-call | flops 352321536 | bytes 4407296 | tf_op jit(solution)/shard_map/pallas_call | solution.py:107
  72.9 0.6 shard_map.116
  73.6 0.8 collective-permute-start.10
  74.4 0.8 collective-permute-start.11
  75.2 1.9 %collective-permute-start.12 = (bf16[48,896]{1,0:T(8,128)(2,1)S(1)}, bf16[48,896]{1,0:T(8,128)(2,1)S(1)}, u32[]{:S(2)}, u32[]{:S(2)}) collective-permute-start(bf16[48,896]{1,0:T(8,128)(2,1)S(1)} %get-tuple-element.59), channel_id=1, source_target_pairs={{0,24},{8,16},{16,8},{24,0},{1,25},{9,17},{17,9},{25,1},{2,26},{10... | collective-permute-start | bytes 258056 | tf_op jit(solution)/shard_map/ppermute | solution.py:441
  77.1 1.4 %shard_map.120.refs_3_ = f32[192,896]{1,0:T(8,128)S(1)} custom-call(bf16[2,1,192,256]{3,2,1,0:T(8,128)(2,1)S(1)} %collective-permute-done.23.refs_0_.refs_4_, bf16[2,1,192,256]{3,2,1,0:T(8,128)(2,1)S(1)} %collective-permute-done.24.refs_1_.refs_5_, bf16[2,1,192,256]{3,2,1,0:T(8,128)(2,1)S(1)} %pad_maximum_fusion.1.refs_2_.refs_0_, ...), custom_call_target="tpu_custom_call" | custom-call | flops 704643072 | bytes 9502720 | tf_op jit(solution)/shard_map/pallas_call | solution.py:107
  78.5 0.8 shard_map.121
  79.3 0.8 collective-permute-start.27
  80.1 0.8 collective-permute-start.28
  81.0 1.9 %collective-permute-start.29 = (bf16[48,896]{1,0:T(8,128)(2,1)S(1)}, bf16[48,896]{1,0:T(8,128)(2,1)S(1)}, u32[]{:S(2)}, u32[]{:S(2)}) collective-permute-start(bf16[48,896]{1,0:T(8,128)(2,1)S(1)} %get-tuple-element.73), channel_id=1, source_target_pairs={{0,24},{8,16},{16,8},{24,0},{1,25},{9,17},{17,9},{25,1},{2,26},{10... | collective-permute-start | bytes 258056 | tf_op jit(solution)/shard_map/ppermute | solution.py:441
  82.9 3.6 %shard_map.125 = (bf16[1,896,2048]{2,1,0:T(8,128)(2,1)}, bf16[1,896,2048]{2,1,0:T(8,128)(2,1)}, bf16[1,2048,896]{2,1,0:T(8,128)(2,1)}) custom-call(bf16[2,1,192,256]{3,2,1,0:T(8,128)(2,1)S(1)} %pad_maximum_fusion.1.refs_2_.refs_0_, ...), custom_call_target="tpu_custom_call", output_to_operand_aliasing={{1}: (11, {}), {2}: (12, {})} | custom-call | flops 1409286144 | bytes 20955136 | tf_op jit(solution)/shard_map/pallas_call | solution.py:107
  86.5 1.0 %shard_map.122 = (bf16[128,896]{1,0:T(8,128)(2,1)}, bf16[128,896]{1,0:T(8,128)(2,1)}) custom-call(bf16[128,192]{1,0:T(8,128)(2,1)S(1)} %get-tuple-element.44.refs_0_, bf16[128,192]{1,0:T(8,128)(2,1)S(1)} %get-tuple-element.45.refs_1_, bf16[48,896]{1,0:T(8,128)(2,1)S(1)} %get-tuple-element.56.refs_2_, bf16[48,896]{1,0:T(8,128)(2,1)S(1)} %collective-permute-done.10.refs_3_, ...), custom_call_target="tpu_custom_call" | custom-call | flops 88080384 | bytes 1245184 | tf_op jit(solution)/shard_map/pallas_call | solution.py:107
  (27 shorter events, 0.2 us)
Async XLA Ops:
  2.2 8.8 %collective-permute-start.1 = (bf16[48,896]{1,0:T(8,128)(2,1)S(1)}, bf16[48,896]{1,0:T(8,128)(2,1)S(1)}, u32[]{:S(2)}, u32[]{:S(2)}) collective-permute-start(bf16[48,896]{1,0:T(8,128)(2,1)S(1)} %get-tuple-element.47), channel_id=1, source_target_pairs={{0,16},{8,24},{16,0},{24,8},{1,17},{9,25},{17,1},{25,9},{2,18},{10... | collective-permute-start | bytes 258056 | tf_op jit(solution)/shard_map/ppermute | solution.py:441
  5.2 6.1 %collective-permute-start.2 = (bf16[48,896]{1,0:T(8,128)(2,1)S(1)}, bf16[48,896]{1,0:T(8,128)(2,1)S(1)}, u32[]{:S(2)}, u32[]{:S(2)}) collective-permute-start(bf16[48,896]{1,0:T(8,128)(2,1)S(1)} %get-tuple-element.48), channel_id=1, source_target_pairs={{0,24},{8,16},{16,8},{24,0},{1,25},{9,17},{17,9},{25,1},{2,26},{10... | collective-permute-start | bytes 258056 | tf_op jit(solution)/shard_map/ppermute | solution.py:441
  6.6 4.7 %collective-permute-start = (bf16[48,896]{1,0:T(8,128)(2,1)S(1)}, bf16[48,896]{1,0:T(8,128)(2,1)S(1)}, u32[]{:S(2)}, u32[]{:S(2)}) collective-permute-start(bf16[48,896]{1,0:T(8,128)(2,1)S(1)} %get-tuple-element.42.refs_3_), channel_id=1, source_target_pairs={{0,8},{8,0},{16,24},{24,16},{1,9},{9,1},{17,25},{25,17},{2,10},{10... | collective-permute-start | bytes 258056 | tf_op jit(solution)/shard_map/ppermute | solution.py:441
  12.3 3.6 %collective-permute-start.3 = (bf16[4,2,192,256]{3,2,1,0:T(8,128)(2,1)S(1)}, bf16[4,2,192,256]{3,2,1,0:T(8,128)(2,1)S(1)}, u32[]{:S(2)}, u32[]{:S(2)}) collective-permute-start(bf16[4,2,192,256]{3,2,1,0:T(8,128)(2,1)S(1)} %get-tuple-element.51), channel_id=1, source_target_pairs={{0,1},{1,0},{2,3},{3,2},{4,5},{5,4},{6,7},{7,6},{8,9},{9,8},{10,11... | collective-permute-start | bytes 2359304 | tf_op jit(solution)/shard_map/ppermute | solution.py:411
  12.4 4.9 %collective-permute-start.13 = (bf16[48,896]{1,0:T(8,128)(2,1)S(1)}, bf16[48,896]{1,0:T(8,128)(2,1)S(1)}, u32[]{:S(2)}, u32[]{:S(2)}) collective-permute-start(bf16[48,896]{1,0:T(8,128)(2,1)S(1)} %get-tuple-element.61), channel_id=1, source_target_pairs={{0,8},{8,0},{16,24},{24,16},{1,9},{9,1},{17,25},{25,17},{2,10},{10... | collective-permute-start | bytes 258056 | tf_op jit(solution)/shard_map/ppermute | solution.py:441
  14.1 5.5 %collective-permute-start.14 = (bf16[48,896]{1,0:T(8,128)(2,1)S(1)}, bf16[48,896]{1,0:T(8,128)(2,1)S(1)}, u32[]{:S(2)}, u32[]{:S(2)}) collective-permute-start(bf16[48,896]{1,0:T(8,128)(2,1)S(1)} %get-tuple-element.62), channel_id=1, source_target_pairs={{0,16},{8,24},{16,0},{24,8},{1,17},{9,25},{17,1},{25,9},{2,18},{10... | collective-permute-start | bytes 258056 | tf_op jit(solution)/shard_map/ppermute | solution.py:441
  15.6 5.4 %collective-permute-start.15 = (bf16[48,896]{1,0:T(8,128)(2,1)S(1)}, bf16[48,896]{1,0:T(8,128)(2,1)S(1)}, u32[]{:S(2)}, u32[]{:S(2)}) collective-permute-start(bf16[48,896]{1,0:T(8,128)(2,1)S(1)} %get-tuple-element.63), channel_id=1, source_target_pairs={{0,24},{8,16},{16,8},{24,0},{1,25},{9,17},{17,9},{25,1},{2,26},{10... | collective-permute-start | bytes 258056 | tf_op jit(solution)/shard_map/ppermute | solution.py:441
  21.8 1.8 %collective-permute-start.16 = (bf16[4,1,192,256]{3,2,1,0:T(8,128)(2,1)S(1)}, bf16[4,1,192,256]{3,2,1,0:T(8,128)(2,1)S(1)}, u32[]{:S(2)}, u32[]{:S(2)}) collective-permute-start(bf16[4,1,192,256]{3,2,1,0:T(8,128)(2,1)S(1)} %get-tuple-element.65), channel_id=1, source_target_pairs={{0,1},{1,0},{2,3},{3,2},{4,5},{5,4},{6,7},{7,6},{8,9},{9,8},{10,11... | collective-permute-start | bytes 1179656 | tf_op jit(solution)/shard_map/ppermute | solution.py:411
  21.9 12.0 %collective-permute-start.4 = (bf16[2,2,192,256]{3,2,1,0:T(8,128)(2,1)S(1)}, bf16[2,2,192,256]{3,2,1,0:T(8,128)(2,1)S(1)}, u32[]{:S(2)}, u32[]{:S(2)}) collective-permute-start(bf16[2,2,192,256]{3,2,1,0:T(8,128)(2,1)S(1)} %get-tuple-element.53.refs_5_), channel_id=1, source_target_pairs={{0,2},{1,5},{2,0},{3,7},{4,6},{5,1},{6,4},{7,3},{8,10},{9,13},{10,... | collective-permute-start | bytes 1179656 | tf_op jit(solution)/shard_map/ppermute | solution.py:408
  24.4 16.0 %collective-permute-start.17 = (bf16[2,1,192,256]{3,2,1,0:T(8,128)(2,1)S(1)}, bf16[2,1,192,256]{3,2,1,0:T(8,128)(2,1)S(1)}, u32[]{:S(2)}, u32[]{:S(2)}) collective-permute-start(bf16[2,1,192,256]{3,2,1,0:T(8,128)(2,1)S(1)} %get-tuple-element.67), channel_id=1, source_target_pairs={{0,2},{1,5},{2,0},{3,7},{4,6},{5,1},{6,4},{7,3},{8,10},{9,13},{10,... | collective-permute-start | bytes 589832 | tf_op jit(solution)/shard_map/ppermute | solution.py:408
  33.9 32.9 %copy-start = (s32[128,1]{0,1:T(1,128)S(1)}, s32[128,1]{0,1:T(1,128)}, u32[]{:S(2)}) copy-start(s32[128,1]{0,1:T(1,128)} %param.9) | copy-start | bytes 1540
  33.9 32.9 %copy-start.1 = (bf16[128,1]{0,1:T(2,128)(2,1)S(1)}, bf16[128,1]{0,1:T(2,128)(2,1)}, u32[]{:S(2)}) copy-start(bf16[128,1]{0,1:T(2,128)(2,1)} %param.8) | copy-start | bytes 772
  34.0 8.0 %collective-permute-start.5 = (bf16[1,2,192,256]{3,2,1,0:T(8,128)(2,1)S(1)}, bf16[1,2,192,256]{3,2,1,0:T(8,128)(2,1)S(1)}, u32[]{:S(2)}, u32[]{:S(2)}) collective-permute-start(bf16[1,2,192,256]{3,2,1,0:T(8,128)(2,1)S(1)} %slice.38), channel_id=1, source_target_pairs={{0,4},{1,3},{2,6},{3,1},{4,0},{5,7},{6,2},{7,5},{8,12},{9,11},{10,... | collective-permute-start | bytes 589832 | tf_op jit(solution)/shard_map/ppermute | solution.py:408
  40.4 8.0 %collective-permute-start.18 = (bf16[1,1,192,256]{3,2,1,0:T(8,128)(2,1)S(1)}, bf16[1,1,192,256]{3,2,1,0:T(8,128)(2,1)S(1)}, u32[]{:S(2)}, u32[]{:S(2)}) collective-permute-start(bf16[1,1,192,256]{3,2,1,0:T(8,128)(2,1)S(1)} %slice.39), channel_id=1, source_target_pairs={{0,4},{1,3},{2,6},{3,1},{4,0},{5,7},{6,2},{7,5},{8,12},{9,11},{10,... | collective-permute-start | bytes 294920 | tf_op jit(solution)/shard_map/ppermute | solution.py:408
  42.2 8.6 %collective-permute-start.6 = (bf16[1,1,192,256]{3,2,1,0:T(8,128)(2,1)S(1)}, bf16[1,1,192,256]{3,2,1,0:T(8,128)(2,1)S(1)}, u32[]{:S(2)}, u32[]{:S(2)}) collective-permute-start(bf16[1,1,192,256]{3,2,1,0:T(8,128)(2,1)S(1)} %bitcast.35), channel_id=1, source_target_pairs={{0,4},{1,5},{2,6},{3,7},{4,0},{5,1},{6,2},{7,3},{8,12},{9,13},{10,... | collective-permute-start | bytes 294920 | tf_op jit(solution)/shard_map/ppermute | solution.py:408
  48.5 5.6 %collective-permute-start.22 = (bf16[1,1,192,256]{3,2,1,0:T(8,128)(2,1)S(1)}, bf16[1,1,192,256]{3,2,1,0:T(8,128)(2,1)S(1)}, u32[]{:S(2)}, u32[]{:S(2)}) collective-permute-start(bf16[1,1,192,256]{3,2,1,0:T(8,128)(2,1)S(1)} %get-tuple-element.79), channel_id=1, source_target_pairs={{0,4},{1,3},{2,6},{3,1},{4,0},{5,7},{6,2},{7,5},{8,12},{9,11},{10,... | collective-permute-start | bytes 294920 | tf_op jit(solution)/shard_map/ppermute | solution.py:408
  50.8 12.1 %collective-permute-start.9 = (bf16[2,1,192,256]{3,2,1,0:T(8,128)(2,1)S(1)}, bf16[2,1,192,256]{3,2,1,0:T(8,128)(2,1)S(1)}, u32[]{:S(2)}, u32[]{:S(2)}) collective-permute-start(bf16[2,1,192,256]{3,2,1,0:T(8,128)(2,1)S(1)} %pad_maximum_fusion.refs_0_), channel_id=1, source_target_pairs={{0,1},{1,0},{2,3},{3,2},{4,5},{5,4},{6,7},{7,6},{8,9},{9,8},{10,11... | collective-permute-start | bytes 589832 | tf_op jit(solution)/shard_map/ppermute | solution.py:411
  50.9 11.9 %collective-permute-start.7 = (bf16[2,1,192,256]{3,2,1,0:T(8,128)(2,1)S(1)}, bf16[2,1,192,256]{3,2,1,0:T(8,128)(2,1)S(1)}, u32[]{:S(2)}, u32[]{:S(2)}) collective-permute-start(bf16[2,1,192,256]{3,2,1,0:T(8,128)(2,1)S(1)} %pad_maximum_fusion.refs_0_), channel_id=1, source_target_pairs={{0,2},{1,3},{2,0},{3,1},{4,6},{5,7},{6,4},{7,5},{8,10},{9,11},{10,... | collective-permute-start | bytes 589832 | tf_op jit(solution)/shard_map/ppermute | solution.py:408
  51.4 7.4 %collective-permute-start.19 = (bf16[1,1,192,256]{3,2,1,0:T(8,128)(2,1)S(1)}, bf16[1,1,192,256]{3,2,1,0:T(8,128)(2,1)S(1)}, u32[]{:S(2)}, u32[]{:S(2)}) collective-permute-start(bf16[1,1,192,256]{3,2,1,0:T(8,128)(2,1)S(1)} %get-tuple-element.80), channel_id=1, source_target_pairs={{0,4},{1,5},{2,6},{3,7},{4,0},{5,1},{6,2},{7,3},{8,12},{9,13},{10,... | collective-permute-start | bytes 294920 | tf_op jit(solution)/shard_map/ppermute | solution.py:408
  54.1 12.6 %collective-permute-start.23 = (bf16[2,1,192,256]{3,2,1,0:T(8,128)(2,1)S(1)}, bf16[2,1,192,256]{3,2,1,0:T(8,128)(2,1)S(1)}, u32[]{:S(2)}, u32[]{:S(2)}) collective-permute-start(bf16[2,1,192,256]{3,2,1,0:T(8,128)(2,1)S(1)} %pad_maximum_fusion.2.refs_0_), channel_id=1, source_target_pairs={{0,2},{1,5},{2,0},{3,7},{4,6},{5,1},{6,4},{7,3},{8,10},{9,13},{10,... | collective-permute-start | bytes 589832 | tf_op jit(solution)/shard_map/ppermute | solution.py:408
  58.9 9.9 %collective-permute-start.20 = (bf16[2,1,192,256]{3,2,1,0:T(8,128)(2,1)S(1)}, bf16[2,1,192,256]{3,2,1,0:T(8,128)(2,1)S(1)}, u32[]{:S(2)}, u32[]{:S(2)}) collective-permute-start(bf16[2,1,192,256]{3,2,1,0:T(8,128)(2,1)S(1)} %pad_maximum_fusion.1.refs_2_.refs_0_), channel_id=1, source_target_pairs={{0,2},{1,3},{2,0},{3,1},{4,6},{5,7},{6,4},{7,5},{8,10},{9,11},{10,... | collective-permute-start | bytes 589832 | tf_op jit(solution)/shard_map/ppermute | solution.py:408
  62.4 8.1 %collective-permute-start.26 = (bf16[2,1,192,256]{3,2,1,0:T(8,128)(2,1)S(1)}, bf16[2,1,192,256]{3,2,1,0:T(8,128)(2,1)S(1)}, u32[]{:S(2)}, u32[]{:S(2)}) collective-permute-start(bf16[2,1,192,256]{3,2,1,0:T(8,128)(2,1)S(1)} %pad_maximum_fusion.2.refs_0_), channel_id=1, source_target_pairs={{0,1},{1,0},{2,3},{3,2},{4,5},{5,4},{6,7},{7,6},{8,9},{9,8},{10,11... | collective-permute-start | bytes 589832 | tf_op jit(solution)/shard_map/ppermute | solution.py:411
  62.8 10.2 %collective-permute-start.8 = (bf16[2,1,192,256]{3,2,1,0:T(8,128)(2,1)S(1)}, bf16[2,1,192,256]{3,2,1,0:T(8,128)(2,1)S(1)}, u32[]{:S(2)}, u32[]{:S(2)}) collective-permute-start(bf16[2,1,192,256]{3,2,1,0:T(8,128)(2,1)S(1)} %collective-permute-done.7.refs_0_.refs_6_), channel_id=1, source_target_pairs={{0,1},{1,0},{2,3},{3,2},{4,5},{5,4},{6,7},{7,6},{8,9},{9,8},{10,11... | collective-permute-start | bytes 589832 | tf_op jit(solution)/shard_map/ppermute | solution.py:411
  62.9 12.3 %collective-permute-start.25 = (bf16[2,1,192,256]{3,2,1,0:T(8,128)(2,1)S(1)}, bf16[2,1,192,256]{3,2,1,0:T(8,128)(2,1)S(1)}, u32[]{:S(2)}, u32[]{:S(2)}) collective-permute-start(bf16[2,1,192,256]{3,2,1,0:T(8,128)(2,1)S(1)} %pad_maximum_fusion.1.refs_2_.refs_0_), channel_id=1, source_target_pairs={{0,1},{1,0},{2,3},{3,2},{4,5},{5,4},{6,7},{7,6},{8,9},{9,8},{10,11... | collective-permute-start | bytes 589832 | tf_op jit(solution)/shard_map/ppermute | solution.py:411
  66.7 10.4 %collective-permute-start.24 = (bf16[2,1,192,256]{3,2,1,0:T(8,128)(2,1)S(1)}, bf16[2,1,192,256]{3,2,1,0:T(8,128)(2,1)S(1)}, u32[]{:S(2)}, u32[]{:S(2)}) collective-permute-start(bf16[2,1,192,256]{3,2,1,0:T(8,128)(2,1)S(1)} %collective-permute-done.23.refs_0_.refs_4_), channel_id=1, source_target_pairs={{0,1},{1,0},{2,3},{3,2},{4,5},{5,4},{6,7},{7,6},{8,9},{9,8},{10,11... | collective-permute-start | bytes 589832 | tf_op jit(solution)/shard_map/ppermute | solution.py:411
  68.8 9.7 %collective-permute-start.21 = (bf16[2,1,192,256]{3,2,1,0:T(8,128)(2,1)S(1)}, bf16[2,1,192,256]{3,2,1,0:T(8,128)(2,1)S(1)}, u32[]{:S(2)}, u32[]{:S(2)}) collective-permute-start(bf16[2,1,192,256]{3,2,1,0:T(8,128)(2,1)S(1)} %collective-permute-done.20.refs_0_.refs_2_), channel_id=1, source_target_pairs={{0,1},{1,0},{2,3},{3,2},{4,5},{5,4},{6,7},{7,6},{8,9},{9,8},{10,11... | collective-permute-start | bytes 589832 | tf_op jit(solution)/shard_map/ppermute | solution.py:411
  73.6 7.4 %collective-permute-start.10 = (bf16[48,896]{1,0:T(8,128)(2,1)S(1)}, bf16[48,896]{1,0:T(8,128)(2,1)S(1)}, u32[]{:S(2)}, u32[]{:S(2)}) collective-permute-start(bf16[48,896]{1,0:T(8,128)(2,1)S(1)} %get-tuple-element.57), channel_id=1, source_target_pairs={{0,8},{8,0},{16,24},{24,16},{1,9},{9,1},{17,25},{25,17},{2,10},{10... | collective-permute-start | bytes 258056 | tf_op jit(solution)/shard_map/ppermute | solution.py:441
  74.4 12.0 %collective-permute-start.11 = (bf16[48,896]{1,0:T(8,128)(2,1)S(1)}, bf16[48,896]{1,0:T(8,128)(2,1)S(1)}, u32[]{:S(2)}, u32[]{:S(2)}) collective-permute-start(bf16[48,896]{1,0:T(8,128)(2,1)S(1)} %get-tuple-element.58), channel_id=1, source_target_pairs={{0,16},{8,24},{16,0},{24,8},{1,17},{9,25},{17,1},{25,9},{2,18},{10... | collective-permute-start | bytes 258056 | tf_op jit(solution)/shard_map/ppermute | solution.py:441
  75.2 11.2 %collective-permute-start.12 = (bf16[48,896]{1,0:T(8,128)(2,1)S(1)}, bf16[48,896]{1,0:T(8,128)(2,1)S(1)}, u32[]{:S(2)}, u32[]{:S(2)}) collective-permute-start(bf16[48,896]{1,0:T(8,128)(2,1)S(1)} %get-tuple-element.59), channel_id=1, source_target_pairs={{0,24},{8,16},{16,8},{24,0},{1,25},{9,17},{17,9},{25,1},{2,26},{10... | collective-permute-start | bytes 258056 | tf_op jit(solution)/shard_map/ppermute | solution.py:441
  79.3 7.1 %collective-permute-start.27 = (bf16[48,896]{1,0:T(8,128)(2,1)S(1)}, bf16[48,896]{1,0:T(8,128)(2,1)S(1)}, u32[]{:S(2)}, u32[]{:S(2)}) collective-permute-start(bf16[48,896]{1,0:T(8,128)(2,1)S(1)} %get-tuple-element.71), channel_id=1, source_target_pairs={{0,8},{8,0},{16,24},{24,16},{1,9},{9,1},{17,25},{25,17},{2,10},{10... | collective-permute-start | bytes 258056 | tf_op jit(solution)/shard_map/ppermute | solution.py:441
  80.1 6.3 %collective-permute-start.28 = (bf16[48,896]{1,0:T(8,128)(2,1)S(1)}, bf16[48,896]{1,0:T(8,128)(2,1)S(1)}, u32[]{:S(2)}, u32[]{:S(2)}) collective-permute-start(bf16[48,896]{1,0:T(8,128)(2,1)S(1)} %get-tuple-element.72), channel_id=1, source_target_pairs={{0,16},{8,24},{16,0},{24,8},{1,17},{9,25},{17,1},{25,9},{2,18},{10... | collective-permute-start | bytes 258056 | tf_op jit(solution)/shard_map/ppermute | solution.py:441
  81.0 5.5 %collective-permute-start.29 = (bf16[48,896]{1,0:T(8,128)(2,1)S(1)}, bf16[48,896]{1,0:T(8,128)(2,1)S(1)}, u32[]{:S(2)}, u32[]{:S(2)}) collective-permute-start(bf16[48,896]{1,0:T(8,128)(2,1)S(1)} %get-tuple-element.73), channel_id=1, source_target_pairs={{0,24},{8,16},{16,8},{24,0},{1,25},{9,17},{17,9},{25,1},{2,26},{10... | collective-permute-start | bytes 258056 | tf_op jit(solution)/shard_map/ppermute | solution.py:441
